TPU v7x, 256 devices: a whole 4x4x8 slice. The times are simulated.
256 devices in a mesh: dp: 16 (over y, x_hi, core), seq: 16 (over x_lo, z).
Axes of the slice: x: 4 (x_hi: 2, x_lo: 2; x = x_hi * 2 + x_lo), y: 4, z: 8, core: 2. Of those that a mesh axis runs over, the one named last changes fastest.
Arguments:
- frames: bfloat16 [16, 2048, 1024], P('dp', 'seq'), may hold values from -6 to 6
- cotangent: bfloat16 [16, 2048, 1024], P('dp', 'seq'), may hold values from -6 to 6
- w_qkv: bfloat16 [1024, 3072], replicated, may hold values from -3 to 3
- w_out: bfloat16 [1024, 1024], replicated, may hold values from -0.1875 to 0.1875
- w_conv: float32 [31, 1024], replicated, may hold values from -1 to 1
- lengths: int32 [16], P('dp'), may hold values from 512 to 2048, as said below
Outputs:
- output: bfloat16 [16, 2048, 1024], P('dp', 'seq')
- input_grad: bfloat16 [16, 2048, 1024], P('dp', 'seq')
- qkv_grad: float32 [1024, 3, 1024], P('dp', None, 'seq')
- out_grad: float32 [1024, 1024], P(('dp', 'seq'))
- conv_grad: float32 [31, 1024], replicated
Inputs may be any that keep to these rules, and one draw needn't show every extreme that they name: `lengths`: at least one utterance has all 2048 frames valid.
All inputs are finite; a program needn't handle non-finite values.
Results may differ from a plain program's by a relative error of at most 0.017.
The roundings to bfloat16 on the way count: a program that leaves them out, or rounds other values in their place, can miss the bound.
Values may be sent and summed in bfloat16 or wider, within the bound.
No kernel may reach another device: no remote copies, remote signals or barrier semaphores. Data moves between devices by JAX's collectives and lax.ppermute only.
A program may use at most 128 MiB of HBM per device.

v0:
```python
import math

import jax
import jax.numpy as jnp
from jax import lax
from jax.sharding import PartitionSpec as P

HEADS = 16
KW = 31


def extended(block, sides, width):
    for axis, dim in sides:
        count = lax.axis_size(axis)
        forward = [(i, i + 1) for i in range(count - 1)]
        backward = [(target, source) for source, target in forward]
        low = lax.ppermute(
            lax.slice_in_dim(block, block.shape[dim] - width, None, axis=dim), axis, forward
        )
        high = lax.ppermute(lax.slice_in_dim(block, 0, width, axis=dim), axis, backward)
        block = jnp.concatenate([low, block, high], axis=dim)
    return block


def layer_norm(inputs):
    center = inputs - jnp.mean(inputs, axis=-1, keepdims=True)
    spread = jnp.mean(center * center, axis=-1, keepdims=True)
    return center * lax.rsqrt(spread + 1e-05)


def norm_backward(inputs, upstream):
    unused_out, pullback = jax.vjp(layer_norm, inputs)
    return pullback(upstream)[0]


def block_probs(query_block, key_rows, key_keep, score_scale):
    scores = (
        lax.dot_general(
            query_block, key_rows, (((1,), (1,)), ((), ())), preferred_element_type=jnp.float32
        )
        * score_scale
    )
    scores = jnp.where(key_keep[None, :], scores, -1000000000.0)
    row_peak = jnp.max(scores, axis=-1, keepdims=True)
    expo_rows = jnp.exp(scores - row_peak)
    return expo_rows / jnp.sum(expo_rows, axis=-1, keepdims=True)


def attention_forward(query_rows, key_rows, value_rows, key_keep):
    length_all, head_dim = query_rows.shape
    block_size = min(512, length_all)
    score_scale = 1.0 / math.sqrt(head_dim)

    def one_block(query_block):
        probabilities = block_probs(query_block, key_rows, key_keep, score_scale)
        return jnp.dot(
            probabilities.astype(jnp.bfloat16), value_rows, preferred_element_type=jnp.float32
        ).astype(jnp.bfloat16)

    blocked = query_rows.reshape(length_all // block_size, block_size, head_dim)
    return lax.map(one_block, blocked).reshape(length_all, head_dim)


def attention_backward(query_rows, key_rows, value_rows, grad_rows, key_keep):
    length_all, head_dim = query_rows.shape
    block_size = min(512, length_all)
    block_count = length_all // block_size
    score_scale = 1.0 / math.sqrt(head_dim)

    def one_block(running, block_items):
        key_grad, value_grad = running
        query_block, grad_block = block_items
        probabilities = block_probs(query_block, key_rows, key_keep, score_scale)
        prob_grad = lax.dot_general(
            grad_block, value_rows, (((1,), (1,)), ((), ())), preferred_element_type=jnp.float32
        )
        score_grad = (
            probabilities
            * (prob_grad - jnp.sum(prob_grad * probabilities, axis=-1, keepdims=True))
            * score_scale
        ).astype(jnp.bfloat16)
        query_grad = jnp.dot(score_grad, key_rows, preferred_element_type=jnp.float32)
        key_grad = key_grad + lax.dot_general(
            score_grad, query_block, (((0,), (0,)), ((), ())), preferred_element_type=jnp.float32
        )
        value_grad = value_grad + lax.dot_general(
            probabilities.astype(jnp.bfloat16),
            grad_block,
            (((0,), (0,)), ((), ())),
            preferred_element_type=jnp.float32,
        )
        return ((key_grad, value_grad), query_grad)

    zero_rows = jnp.zeros((length_all, head_dim), jnp.float32)
    blocked_q = query_rows.reshape(block_count, block_size, head_dim)
    blocked_g = grad_rows.reshape(block_count, block_size, head_dim)
    (key_grad, value_grad), query_grad = lax.scan(
        one_block, (zero_rows, zero_rows), (blocked_q, blocked_g)
    )
    return (
        query_grad.reshape(length_all, head_dim).astype(jnp.bfloat16),
        key_grad.astype(jnp.bfloat16),
        value_grad.astype(jnp.bfloat16),
    )


def conv_apply(padded, kernel, row_count):
    result = jnp.zeros((row_count, padded.shape[1]), jnp.float32)
    for offset in range(kernel.shape[0]):
        result = result + kernel[offset][None, :] * padded[offset : offset + row_count].astype(
            jnp.float32
        )
    return result


def conv_adjoint(padded_grad, kernel, row_count):
    taps_count = kernel.shape[0]
    result = jnp.zeros((row_count, padded_grad.shape[1]), jnp.float32)
    for offset in range(taps_count):
        first = taps_count - 1 - offset
        result = result + kernel[offset][None, :] * padded_grad[first : first + row_count]
    return result


def conv_kernel_grad(padded, conv_back, taps_count):
    row_count = conv_back.shape[0]
    pieces = [
        jnp.sum(padded[offset : offset + row_count].astype(jnp.float32) * conv_back, axis=0)
        for offset in range(taps_count)
    ]
    return jnp.stack(pieces, axis=0)


def local(frames, cotangent, w_qkv, w_out, w_conv, lengths):
    seq_count = lax.axis_size("seq")
    data_count = lax.axis_size("dp")
    frame_count = frames.shape[1]
    model_width = frames.shape[2]
    head_count = HEADS
    head_dim = model_width // head_count
    local_heads = head_count // seq_count
    length_all = frame_count * seq_count
    half_width = KW // 2
    length = lengths[0]
    first_frame = lax.axis_index("seq") * frame_count
    row_keep = first_frame + jnp.arange(frame_count, dtype=jnp.int32) < length
    keep_col = row_keep.astype(jnp.float32)[:, None]
    key_keep = jnp.arange(length_all, dtype=jnp.int32) < length
    inputs = frames[0].astype(jnp.float32)
    normed = layer_norm(inputs).astype(jnp.bfloat16)
    joined_proj = jnp.dot(normed, w_qkv, preferred_element_type=jnp.float32).astype(jnp.bfloat16)
    joined_proj = joined_proj.reshape(frame_count, 3, head_count, head_dim)
    head_layout = lax.all_to_all(joined_proj, "seq", split_axis=2, concat_axis=0, tiled=True)
    per_head = jnp.transpose(head_layout, (1, 2, 0, 3))

    def head_forward(head_set):
        return attention_forward(head_set[0], head_set[1], head_set[2], key_keep)

    attended_heads = lax.map(head_forward, (per_head[0], per_head[1], per_head[2]))
    attended_frames = jnp.transpose(attended_heads, (1, 0, 2))
    attended = lax.all_to_all(
        attended_frames, "seq", split_axis=0, concat_axis=1, tiled=True
    ).reshape(frame_count, model_width)
    residual = (inputs + jnp.dot(attended, w_out, preferred_element_type=jnp.float32)).astype(
        jnp.bfloat16
    )
    residual_float = residual.astype(jnp.float32)
    conv_in = (layer_norm(residual_float) * keep_col).astype(jnp.bfloat16)
    padded = extended(conv_in, (("seq", 0),), half_width)
    conv_out = conv_apply(padded, w_conv, frame_count)
    sigmoid_gate = jax.nn.sigmoid(conv_out)
    output = (residual_float + conv_out * sigmoid_gate).astype(jnp.bfloat16)
    grad_float = cotangent[0].astype(jnp.float32)
    conv_back = grad_float * (sigmoid_gate + conv_out * sigmoid_gate * (1.0 - sigmoid_gate))
    padded_back = extended(conv_back.astype(jnp.bfloat16), (("seq", 0),), half_width).astype(
        conv_back.dtype
    )
    conv_in_grad = conv_adjoint(padded_back, w_conv, frame_count)
    grad_scale = 1.0 / math.sqrt(data_count * length_all)
    kernel_total = lax.psum(conv_kernel_grad(padded, conv_back, KW), ("dp", "seq")) * grad_scale
    residual_grad = grad_float + norm_backward(residual_float, conv_in_grad * keep_col)
    grad_round = residual_grad.astype(jnp.bfloat16)
    out_total = lax.psum_scatter(
        lax.dot_general(
            attended, grad_round, (((0,), (0,)), ((), ())), preferred_element_type=jnp.float32
        ),
        ("dp", "seq"),
        scatter_dimension=0,
        tiled=True,
    )
    attended_grad = lax.dot_general(
        grad_round, w_out, (((1,), (1,)), ((), ())), preferred_element_type=jnp.float32
    ).astype(jnp.bfloat16)
    attended_grad = attended_grad.reshape(frame_count, head_count, head_dim)
    head_grads = jnp.transpose(
        lax.all_to_all(attended_grad, "seq", split_axis=1, concat_axis=0, tiled=True), (1, 0, 2)
    )

    def head_backward(head_set):
        return attention_backward(head_set[0], head_set[1], head_set[2], head_set[3], key_keep)

    query_grad, key_grad, value_grad = lax.map(
        head_backward, (per_head[0], per_head[1], per_head[2], head_grads)
    )
    head_stack = jnp.stack([query_grad, key_grad, value_grad], axis=0)
    stacked_grad = jnp.transpose(head_stack, (2, 0, 1, 3))
    joined_grad = lax.all_to_all(
        stacked_grad, "seq", split_axis=0, concat_axis=2, tiled=True
    ).reshape(frame_count, 3 * model_width)
    head_columns = jnp.transpose(head_stack, (0, 2, 1, 3)).reshape(
        3, length_all, local_heads * head_dim
    )
    qkv_local = jnp.einsum(
        "nd,knc->dkc",
        lax.all_gather(normed, "seq", axis=0, tiled=True),
        head_columns,
        preferred_element_type=jnp.float32,
    )
    qkv_total = lax.psum_scatter(
        qkv_local.astype(jnp.bfloat16), "dp", scatter_dimension=0, tiled=True
    ).astype(jnp.float32)
    normed_grad = lax.dot_general(
        joined_grad, w_qkv, (((1,), (1,)), ((), ())), preferred_element_type=jnp.float32
    )
    input_grad = (residual_grad + norm_backward(inputs, normed_grad)).astype(jnp.bfloat16)
    return (
        output[None],
        input_grad[None],
        qkv_total * grad_scale,
        out_total * grad_scale,
        kernel_total,
    )


def solution(mesh):
    placed = (P("dp", "seq", None), P("dp", "seq", None), P(), P(), P(), P("dp"))
    return jax.shard_map(
        local,
        mesh=mesh,
        in_specs=placed,
        out_specs=(
            P("dp", "seq", None),
            P("dp", "seq", None),
            P("dp", None, "seq"),
            P(("dp", "seq"), None),
            P(),
        ),
        check_vma=False,
    )
```

profile of v0, /device:TPU:32, one launch (start us, length us, event | category | flops | bytes accessed | tf_op | source)
XLA Modules:
  0.0 542.4 jit_solution(80853840937764842)
XLA Ops:
  12.7 3.9 convolution_convert_fusion
  17.7 2.1 copy.58
  19.8 9.5 %all-to-all-start = ((bf16[128,3,16,64]{0,3,1,2:T(8,128)(2,1)}), bf16[128,3,16,64]{0,3,1,2:T(8,128)(2,1)S(1)}, u32[]{:S(2)}, u32[]{:S(2)}) async-start(bf16[128,3,16,64]{0,3,1,2:T(8,128)(2,1)} %copy.58), calls=%async_computation | async-start | bytes 1572864 | tf_op jit(solution)/shard_map/all_to_all | solution.py:153
  29.3 20.8 %all-to-all-done = bf16[128,3,16,64]{0,3,1,2:T(8,128)(2,1)S(1)} async-done(((bf16[128,3,16,64]{0,3,1,2:T(8,128)(2,1)}), bf16[128,3,16,64]{0,3,1,2:T(8,128)(2,1)S(1)}, u32[]{:S(2)}, u32[]{:S(2)}) %all-to-all-start) | async-done | bytes 786464 | tf_op jit(solution)/shard_map/all_to_all | solution.py:153
  53.5 17.2 %while.44 = (s32[]{:T(128)}, bf16[4,512,64]{1,2,0:T(8,128)(2,1)}, bf16[4,512,64]{2,1,0:T(8,128)(2,1)S(1)}, bf16[2048,64]{1,0:T(8,128)(2,1)S(1)}, bf16[2048,64]{1,0:T(8,128)(2,1)}, /*index=5*/s32[]{:T(128)}, s32[]{:T(128)}) while((s32[]{:T(128)}, bf16[4,512,64]{1,2,0:T(8,128)(2,1)}, bf16[4,512,64]{2,1,0:T(8,128)(2,1)S(1)}, ...), condition=%wide.region_5.6_spmd.clone, body=%wide.region_2.5_spmd.clone.sunk | while | flops 281052160 | bytes 14633585 | solution.py:61
  70.8 2.2 copy.79
  73.0 4.1 reshape.133
  77.6 13.4 %reduce.1 = bf16[2048,64]{1,0:T(8,128)(2,1)} reduce(bf16[2048,1,64]{2,1,0:T(2,128)(2,1)} %reshape.133, bf16[]{:T(256)} %broadcast.193), dimensions={1}, to_apply=%reshape.133.reduce_sub_computation | reduce | bytes 524290 | tf_op jit(solution)/shard_map/transpose | solution.py:160
  91.0 2.1 reshape.134
  93.1 5.1 all-to-all-start.1
  100.3 8.3 %all-to-all-done.1 = bf16[16,2,4096]{2,1,0:T(2,128)(2,1)} async-done(((bf16[16,2,4096]{2,1,0:T(2,128)(2,1)}), bf16[16,2,4096]{2,1,0:T(2,128)(2,1)}, u32[]{:S(2)}, u32[]{:S(2)}) %all-to-all-start.1) | async-done | bytes 262176 | tf_op jit(solution)/shard_map/all_to_all | solution.py:161
  108.5 3.4 reshape.135
  111.9 3.4 copy.65
  117.5 2.8 collective-permute-start
  120.3 3.0 collective-permute-start.1
  126.3 4.2 fusion.112
  131.6 2.7 collective-permute-start.2
  134.3 3.1 collective-permute-start.3
  137.5 2.6 collective-permute-done.3
  140.2 3.2 multiply_reduce_fusion.1
  147.7 7.9 %all-to-all-start.2 = ((bf16[128,16,64]{0,2,1:T(8,128)(2,1)}), bf16[128,16,64]{0,2,1:T(8,128)(2,1)}, u32[]{:S(2)}, u32[]{:S(2)}) async-start(bf16[128,16,64]{0,2,1:T(8,128)(2,1)} %bitcast.44), calls=%async_computation.2 | async-start | bytes 524288 | tf_op jit(solution)/shard_map/all_to_all | solution.py:196
  156.4 8.4 %all-to-all-done.2 = bf16[128,16,64]{0,2,1:T(8,128)(2,1)} async-done(((bf16[128,16,64]{0,2,1:T(8,128)(2,1)}), bf16[128,16,64]{0,2,1:T(8,128)(2,1)}, u32[]{:S(2)}, u32[]{:S(2)}) %all-to-all-start.2) | async-done | bytes 262176 | tf_op jit(solution)/shard_map/all_to_all | solution.py:196
  164.8 2.0 copy.80
  166.8 66.8 %while.45 = (s32[]{:T(128)}, f32[2048,64]{0,1:T(8,128)S(1)}, f32[2048,64]{0,1:T(8,128)}, bf16[4,512,64]{1,2,0:T(8,128)(2,1)}, bf16[4,512,64]{2,1,0:T(8,128)(2,1)...) while((s32[]{:T(128)}, f32[2048,64]{0,1:T(8,128)S(1)}, ...), condition=%wide.region_14.15_spmd.clone, body=%wide.region_10.14_spmd.clone.sunk | while | flops 698876416 | bytes 73831120 | solution.py:97
  169.2 2.0 copy-done.1
  172.1 4.3 convolution_add_fusion.6
  176.4 2.3 multiply_reduce_fusion.4
  185.7 2.0 copy-done.1
  188.7 4.5 convolution_add_fusion.6
  193.2 2.3 multiply_reduce_fusion.4
  202.5 2.0 copy-done.1
  205.4 4.5 convolution_add_fusion.6
  209.9 2.3 multiply_reduce_fusion.4
  219.2 2.0 copy-done.1
  222.2 4.5 convolution_add_fusion.6
  226.7 2.3 multiply_reduce_fusion.4
  237.5 2.0 fusion.146
  239.7 4.1 copy.74
  243.7 4.2 reshape.136
  247.9 4.3 all-to-all-start.3
  254.2 4.0 stack.140
  258.2 3.6 fusion.189
  262.1 6.2 %all-to-all-done.3 = bf16[16,2,12288]{2,1,0:T(2,128)(2,1)} async-done(((bf16[16,2,12288]{2,1,0:T(2,128)(2,1)}), bf16[16,2,12288]{2,1,0:T(2,128)(2,1)}, u32[]{:S(2)}, u32[]{:S(2)}) %all-to-all-start.3) | async-done | bytes 786464 | tf_op jit(solution)/shard_map/all_to_all | solution.py:207
  268.3 4.2 reshape.137
  272.5 3.9 copy.82
  276.4 5.4 fusion.51
  282.1 5.8 %fusion.38 = bf16[1024,3,64]{2,0,1:T(8,128)(2,1)} fusion(bf16[2048,1024]{1,0:T(8,128)(2,1)} %all-gather.2.cloned.1.call-done, bf16[1,1,2048,64]{2,3,0,1:T(8,128)(2,1)} %copy-done.16, bf16[1,1,2048,64]{2,3,0,1:T(8,128)(2,1)} %copy-done.17, bf16[1,1,2048,64]{2,3,0,1:T(8,128)(2,1)} %convert_element_type.263), kind=kOutput, calls=%fused_computation.76 | convolution fusion | flops 807862272 | bytes 5373952 | tf_op jit(solution)/shard_map/nd,knc->dkc/dot_general | solution.py:213
  289.8 240.7 %all-reduce.4.cloned.1.call-done = (f32[1024,1024]{1,0:T(8,128)}, f32[31,1024]{1,0:T(8,128)}) async-done(((f32[1024,1024]{1,0:T(8,128)}, f32[31,1024]{1,0:T(8,128)}), (f32[1024,1024]{1,0:T(8,128)}, f32[31,1024]{1,0:T(8,128)})) %all-reduce.4.cloned.1.call-update) | async-done | bytes 4321296
  (243 shorter events, 83.6 us)
Async XLA Ops:
  8.0 108.5 %copy-start = (bf16[1024,1024]{1,0:T(8,128)(2,1)S(1)}, bf16[1024,1024]{1,0:T(8,128)(2,1)}, u32[]{:S(2)}) copy-start(bf16[1024,1024]{1,0:T(8,128)(2,1)} %param.13) | copy-start | bytes 6291460
  19.8 30.3 %all-to-all-start = ((bf16[128,3,16,64]{0,3,1,2:T(8,128)(2,1)}), bf16[128,3,16,64]{0,3,1,2:T(8,128)(2,1)S(1)}, u32[]{:S(2)}, u32[]{:S(2)}) async-start(bf16[128,3,16,64]{0,3,1,2:T(8,128)(2,1)} %copy.58), calls=%async_computation | async-start | bytes 1572864 | tf_op jit(solution)/shard_map/all_to_all | solution.py:153
  70.8 45.6 %copy-start.4 = (bf16[4,512,64]{2,1,0:T(8,128)(2,1)}, bf16[4,512,64]{2,1,0:T(8,128)(2,1)S(1)}, u32[]{:S(2)}) copy-start(bf16[4,512,64]{2,1,0:T(8,128)(2,1)S(1)} %get-tuple-element.516) | copy-start | bytes 786436
  70.8 28.7 %copy-start.20 = (f32[31,1024]{1,0:T(8,128)S(1)}, f32[31,1024]{1,0:T(8,128)}, u32[]{:S(2)}) copy-start(f32[31,1024]{1,0:T(8,128)} %param.14) | copy-start | bytes 380932
  73.0 43.5 %copy-start.3 = (bf16[1,128,1024]{2,1,0:T(8,128)(2,1)S(1)}, bf16[1,128,1024]{2,1,0:T(8,128)(2,1)}, u32[]{:S(2)}) copy-start(bf16[1,128,1024]{2,1,0:T(8,128)(2,1)} %param.10) | copy-start | bytes 786436
  93.1 15.4 %all-to-all-start.1 = ((bf16[16,2,4096]{2,1,0:T(2,128)(2,1)}), bf16[16,2,4096]{2,1,0:T(2,128)(2,1)}, u32[]{:S(2)}, u32[]{:S(2)}) async-start(bf16[16,2,4096]{2,1,0:T(2,128)(2,1)} %reshape.134), calls=%async_computation.1 | async-start | bytes 524288 | tf_op jit(solution)/shard_map/all_to_all | solution.py:161
  100.1 17.2 %copy-start.56 = (f32[128]{0:T(128)S(1)}, f32[128]{0:T(128)}, u32[]{:S(2)}) copy-start(f32[128]{0:T(128)} %compare_convert_fusion) | copy-start | bytes 1540
  100.1 26.1 %copy-start.21 = (f32[1,1024]{1,0:T(1,128)S(1)}, f32[1,1024]{1,0:T(1,128)}, u32[]{:S(2)}) copy-start(f32[1,1024]{1,0:T(1,128)} %get-tuple-element.316) | copy-start | bytes 12292
  100.1 26.0 %copy-start.22 = (f32[1,1024]{1,0:T(1,128)S(1)}, f32[1,1024]{1,0:T(1,128)}, u32[]{:S(2)}) copy-start(f32[1,1024]{1,0:T(1,128)} %get-tuple-element.317) | copy-start | bytes 12292
  100.1 26.0 %copy-start.23 = (f32[1,1024]{1,0:T(1,128)S(1)}, f32[1,1024]{1,0:T(1,128)}, u32[]{:S(2)}) copy-start(f32[1,1024]{1,0:T(1,128)} %get-tuple-element.318) | copy-start | bytes 12292
  100.1 26.0 %copy-start.24 = (f32[1,1024]{1,0:T(1,128)S(1)}, f32[1,1024]{1,0:T(1,128)}, u32[]{:S(2)}) copy-start(f32[1,1024]{1,0:T(1,128)} %get-tuple-element.319) | copy-start | bytes 12292
  100.2 26.0 %copy-start.25 = (f32[1,1024]{1,0:T(1,128)S(1)}, f32[1,1024]{1,0:T(1,128)}, u32[]{:S(2)}) copy-start(f32[1,1024]{1,0:T(1,128)} %get-tuple-element.320) | copy-start | bytes 12292
  100.2 26.0 %copy-start.26 = (f32[1,1024]{1,0:T(1,128)S(1)}, f32[1,1024]{1,0:T(1,128)}, u32[]{:S(2)}) copy-start(f32[1,1024]{1,0:T(1,128)} %get-tuple-element.321) | copy-start | bytes 12292
  100.2 26.0 %copy-start.27 = (f32[1,1024]{1,0:T(1,128)S(1)}, f32[1,1024]{1,0:T(1,128)}, u32[]{:S(2)}) copy-start(f32[1,1024]{1,0:T(1,128)} %get-tuple-element.322) | copy-start | bytes 12292
  100.2 26.0 %copy-start.28 = (f32[1,1024]{1,0:T(1,128)S(1)}, f32[1,1024]{1,0:T(1,128)}, u32[]{:S(2)}) copy-start(f32[1,1024]{1,0:T(1,128)} %get-tuple-element.323) | copy-start | bytes 12292
  100.2 26.0 %copy-start.29 = (f32[1,1024]{1,0:T(1,128)S(1)}, f32[1,1024]{1,0:T(1,128)}, u32[]{:S(2)}) copy-start(f32[1,1024]{1,0:T(1,128)} %get-tuple-element.324) | copy-start | bytes 12292
  100.2 26.0 %copy-start.30 = (f32[1,1024]{1,0:T(1,128)S(1)}, f32[1,1024]{1,0:T(1,128)}, u32[]{:S(2)}) copy-start(f32[1,1024]{1,0:T(1,128)} %get-tuple-element.325) | copy-start | bytes 12292
  100.2 26.0 %copy-start.31 = (f32[1,1024]{1,0:T(1,128)S(1)}, f32[1,1024]{1,0:T(1,128)}, u32[]{:S(2)}) copy-start(f32[1,1024]{1,0:T(1,128)} %get-tuple-element.326) | copy-start | bytes 12292
  100.2 26.0 %copy-start.32 = (f32[1,1024]{1,0:T(1,128)S(1)}, f32[1,1024]{1,0:T(1,128)}, u32[]{:S(2)}) copy-start(f32[1,1024]{1,0:T(1,128)} %get-tuple-element.327) | copy-start | bytes 12292
  100.2 26.0 %copy-start.33 = (f32[1,1024]{1,0:T(1,128)S(1)}, f32[1,1024]{1,0:T(1,128)}, u32[]{:S(2)}) copy-start(f32[1,1024]{1,0:T(1,128)} %get-tuple-element.328) | copy-start | bytes 12292
  100.2 26.0 %copy-start.34 = (f32[1,1024]{1,0:T(1,128)S(1)}, f32[1,1024]{1,0:T(1,128)}, u32[]{:S(2)}) copy-start(f32[1,1024]{1,0:T(1,128)} %get-tuple-element.329) | copy-start | bytes 12292
  100.3 26.0 %copy-start.35 = (f32[1,1024]{1,0:T(1,128)S(1)}, f32[1,1024]{1,0:T(1,128)}, u32[]{:S(2)}) copy-start(f32[1,1024]{1,0:T(1,128)} %get-tuple-element.330) | copy-start | bytes 12292
  116.5 23.8 %copy-start.57 = (f32[128]{0:T(128)S(1)}, f32[128]{0:T(128)}, u32[]{:S(2)}) copy-start(f32[128]{0:T(128)} %compare_convert_fusion) | copy-start | bytes 1540
  117.5 20.0 %copy-start.7 = (bf16[128,1024]{1,0:T(8,128)(2,1)}, bf16[128,1024]{1,0:T(8,128)(2,1)S(1)}, u32[]{:S(2)}) copy-start(bf16[128,1024]{1,0:T(8,128)(2,1)S(1)} %multiply_convert_fusion.1) | copy-start | bytes 786436
  117.5 7.0 %collective-permute-start = (bf16[15,1024]{1,0:T(8,128)(2,1)S(1)}, bf16[15,1024]{1,0:T(8,128)(2,1)S(1)}, u32[]{:S(2)}, u32[]{:S(2)}) collective-permute-start(bf16[15,1024]{1,0:T(8,128)(2,1)S(1)} %get-tuple-element.310), channel_id=1, source_target_pairs={{0,1},{1,2},{2,3},{3,4},{4,5},{5,6},{6,7},{7,8},{8,9},{9,10},{10,1... | collective-permute-start | bytes 92168 | tf_op jit(solution)/shard_map/ppermute | solution.py:17
  120.3 5.8 %collective-permute-start.1 = (bf16[15,1024]{1,0:T(8,128)(2,1)S(1)}, bf16[15,1024]{1,0:T(8,128)(2,1)S(1)}, u32[]{:S(2)}, u32[]{:S(2)}) collective-permute-start(bf16[15,1024]{1,0:T(8,128)(2,1)S(1)} %get-tuple-element.311), channel_id=1, source_target_pairs={{1,0},{2,1},{3,2},{4,3},{5,4},{6,5},{7,6},{8,7},{9,8},{10,9},{11,1... | collective-permute-start | bytes 92168 | tf_op jit(solution)/shard_map/ppermute | solution.py:20
  131.6 5.9 %collective-permute-start.2 = (bf16[15,1024]{1,0:T(8,128)(2,1)S(1)}, bf16[15,1024]{1,0:T(8,128)(2,1)S(1)}, u32[]{:S(2)}, u32[]{:S(2)}) collective-permute-start(bf16[15,1024]{1,0:T(8,128)(2,1)S(1)} %get-tuple-element.308), channel_id=1, source_target_pairs={{0,1},{1,2},{2,3},{3,4},{4,5},{5,6},{6,7},{7,8},{8,9},{9,10},{10,1... | collective-permute-start | bytes 92168 | tf_op jit(solution)/shard_map/ppermute | solution.py:17
  134.3 5.8 %collective-permute-start.3 = (bf16[15,1024]{1,0:T(8,128)(2,1)S(1)}, bf16[15,1024]{1,0:T(8,128)(2,1)S(1)}, u32[]{:S(2)}, u32[]{:S(2)}) collective-permute-start(bf16[15,1024]{1,0:T(8,128)(2,1)S(1)} %get-tuple-element.309), channel_id=1, source_target_pairs={{1,0},{2,1},{3,2},{4,3},{5,4},{6,5},{7,6},{8,7},{9,8},{10,9},{11,1... | collective-permute-start | bytes 92168 | tf_op jit(solution)/shard_map/ppermute | solution.py:20
  147.7 17.0 %all-to-all-start.2 = ((bf16[128,16,64]{0,2,1:T(8,128)(2,1)}), bf16[128,16,64]{0,2,1:T(8,128)(2,1)}, u32[]{:S(2)}, u32[]{:S(2)}) async-start(bf16[128,16,64]{0,2,1:T(8,128)(2,1)} %bitcast.44), calls=%async_computation.2 | async-start | bytes 524288 | tf_op jit(solution)/shard_map/all_to_all | solution.py:196
  155.6 126.4 %all-gather.2.cloned.1.call-start = ((), (), s32[]{:S(2)}) async-start(), calls=%async_computation.5 | async-start | bytes 4456448 | tf_op jit(solution)/shard_map/all_gather | solution.py:215
  237.5 14.8 %copy-start.6 = (f32[128,1024]{1,0:T(8,128)S(1)}, f32[128,1024]{1,0:T(8,128)}, u32[]{:S(2)}) copy-start(f32[128,1024]{1,0:T(8,128)} %copy-done.5) | copy-start | bytes 1572868
  237.5 14.8 %copy-start.8 = (bf16[128,1024]{1,0:T(8,128)(2,1)S(1)}, bf16[128,1024]{1,0:T(8,128)(2,1)}, u32[]{:S(2)}) copy-start(bf16[128,1024]{1,0:T(8,128)(2,1)} %copy-done.7) | copy-start | bytes 786436
  239.5 14.5 %copy-start.40 = (f32[1024]{0:T(1024)S(1)}, f32[1024]{0:T(1024)}, u32[]{:S(2)}) copy-start(f32[1024]{0:T(1024)} %get-tuple-element.232) | copy-start | bytes 12292
  239.6 14.5 %copy-start.41 = (f32[1024]{0:T(1024)S(1)}, f32[1024]{0:T(1024)}, u32[]{:S(2)}) copy-start(f32[1024]{0:T(1024)} %get-tuple-element.233) | copy-start | bytes 12292
  239.6 14.5 %copy-start.42 = (f32[1024]{0:T(1024)S(1)}, f32[1024]{0:T(1024)}, u32[]{:S(2)}) copy-start(f32[1024]{0:T(1024)} %get-tuple-element.234) | copy-start | bytes 12292
  239.6 14.5 %copy-start.43 = (f32[1024]{0:T(1024)S(1)}, f32[1024]{0:T(1024)}, u32[]{:S(2)}) copy-start(f32[1024]{0:T(1024)} %get-tuple-element.235) | copy-start | bytes 12292
  239.6 14.5 %copy-start.44 = (f32[1024]{0:T(1024)S(1)}, f32[1024]{0:T(1024)}, u32[]{:S(2)}) copy-start(f32[1024]{0:T(1024)} %get-tuple-element.236) | copy-start | bytes 12292
  239.6 14.5 %copy-start.45 = (f32[1024]{0:T(1024)S(1)}, f32[1024]{0:T(1024)}, u32[]{:S(2)}) copy-start(f32[1024]{0:T(1024)} %get-tuple-element.237) | copy-start | bytes 12292
  239.6 14.5 %copy-start.46 = (f32[1024]{0:T(1024)S(1)}, f32[1024]{0:T(1024)}, u32[]{:S(2)}) copy-start(f32[1024]{0:T(1024)} %get-tuple-element.238) | copy-start | bytes 12292
  239.6 14.5 %copy-start.47 = (f32[1024]{0:T(1024)S(1)}, f32[1024]{0:T(1024)}, u32[]{:S(2)}) copy-start(f32[1024]{0:T(1024)} %get-tuple-element.239) | copy-start | bytes 12292
  239.6 14.5 %copy-start.48 = (f32[1024]{0:T(1024)S(1)}, f32[1024]{0:T(1024)}, u32[]{:S(2)}) copy-start(f32[1024]{0:T(1024)} %get-tuple-element.240) | copy-start | bytes 12292
  239.6 14.5 %copy-start.49 = (f32[1024]{0:T(1024)S(1)}, f32[1024]{0:T(1024)}, u32[]{:S(2)}) copy-start(f32[1024]{0:T(1024)} %get-tuple-element.241) | copy-start | bytes 12292
  239.6 14.5 %copy-start.50 = (f32[1024]{0:T(1024)S(1)}, f32[1024]{0:T(1024)}, u32[]{:S(2)}) copy-start(f32[1024]{0:T(1024)} %get-tuple-element.242) | copy-start | bytes 12292
  239.7 18.5 %copy-start.14 = (bf16[128,1024]{1,0:T(8,128)(2,1)S(1)}, bf16[128,1024]{1,0:T(8,128)(2,1)}, u32[]{:S(2)}) copy-start(bf16[128,1024]{1,0:T(8,128)(2,1)} %copy-done.13) | copy-start | bytes 786436
  247.9 20.3 %all-to-all-start.3 = ((bf16[16,2,12288]{2,1,0:T(2,128)(2,1)}), bf16[16,2,12288]{2,1,0:T(2,128)(2,1)}, u32[]{:S(2)}, u32[]{:S(2)}) async-start(bf16[16,2,12288]{2,1,0:T(2,128)(2,1)} %reshape.136), calls=%async_computation.3 | async-start | bytes 1572864 | tf_op jit(solution)/shard_map/all_to_all | solution.py:207
  252.2 278.3 %all-reduce.4.cloned.1.call-start = ((), (), s32[]{:S(2)}) async-start(), calls=%async_computation.7 | async-start | bytes 8650752
  261.8 14.5 %copy-start.53 = (f32[128]{0:T(128)S(1)}, f32[128]{0:T(128)}, u32[]{:S(2)}) copy-start(f32[128]{0:T(128)} %copy-done.52) | copy-start | bytes 1540
  261.9 271.7 %reduce-scatter.2.cloned.1.call-start = ((), (), s32[]{:S(2)}) async-start(), calls=%async_computation.6 | async-start | bytes 835584 | tf_op jit(solution)/shard_map/reduce_scatter | solution.py:219
  (37 other events, 184.0 us)
Sparse Core Ops, SparseCore 0:
  158.3 76.9 all-gather.1
  288.0 71.8 reduce-scatter.1
Sparse Core Ops, SparseCore 1:
  261.9 268.6 all-reduce.3
where the time goes:
time: 547 us; the launch traced here: 542 us
  waiting for transfers between devices  289 us (53%)
  matrix products  76.4 us (14%)
  local copies, waits for them, and re-layouts  62.1 us (11%)
  other arithmetic  58.4 us (11%)
  starting transfers between devices  38.8 us (7%)
  between operations  17 us (3%)
    unnamed x4, waiting for transfers between devices  241 us
    unnamed x125, local copies, waits for them, and re-layouts  23 us
    all_to_all x1, waiting for transfers between devices, local(): lax.all_to_all(joined_proj, 'seq', split_axis=2, concat_axis=0, tiled=True)  20.8 us
    dot_general x4, matrix products, one_block(): lax.dot_general(probabilities.astype(jnp.bfloat16), grad_block, (((0,), (...  17.8 us
    transpose x1, other arithmetic, local(): attended_frames = jnp.transpose(attended_heads, (1, 0, 2))  13.4 us
  transfers between devices with their start and end apart: 11, of which 7 were waited for; matrix products, arithmetic and copies ran while one was open for 20% of the time, Pallas kernels for 0%

commit v1 on v0

v1 whole, which is shorter than its diff:
```python
import math

import jax
import jax.numpy as jnp
from jax import lax
from jax.experimental import pallas as pl
from jax.experimental.pallas import tpu as pltpu
from jax.sharding import PartitionSpec as P

HEADS = 16
KW = 31
HD = 64
HALO = 32
QB = 256
KB = 256
F32 = jnp.float32
BF16 = jnp.bfloat16
LIMIT = 56 * 1024 * 1024


def dot(a, b, ca=1, cb=0):
    return lax.dot_general(a, b, (((ca,), (cb,)), ((), ())), preferred_element_type=F32)


def normalize(rows):
    center = rows - jnp.mean(rows, axis=-1, keepdims=True)
    scale = lax.rsqrt(jnp.mean(center * center, axis=-1, keepdims=True) + 1e-05)
    return center * scale, scale


def normalize_back(unit, scale, upstream):
    return scale * (
        upstream
        - jnp.mean(upstream, axis=-1, keepdims=True)
        - unit * jnp.mean(upstream * unit, axis=-1, keepdims=True)
    )


def params(**kw):
    return pltpu.CompilerParams(vmem_limit_bytes=LIMIT, **kw)


def whole(shape):
    return pl.BlockSpec(shape, lambda *_: (0,) * len(shape))


def halves(exact):
    top = exact.astype(BF16)
    rest = (exact - top.astype(F32)).astype(BF16)
    return jnp.concatenate([top, rest], axis=1)


def joined_halves(pair):
    return pair[:, : pair.shape[1] // 2] + pair[:, pair.shape[1] // 2 :]


SMEM = pl.BlockSpec(memory_space=pltpu.SMEM)


def project_kernel(frames_ref, weight_ref, normed_ref, send_ref):
    @pl.when(pl.program_id(0) == 0)
    def _():
        unit, _ = normalize(frames_ref[...].astype(F32))
        normed_ref[...] = unit.astype(BF16)

    part = dot(normed_ref[...], weight_ref[...]).astype(BF16)
    send_ref[...] = part.T.reshape(send_ref.shape)


def project(frames, w_qkv):
    rows, width = frames.shape
    cols = 512
    per = cols // HD
    groups = HEADS // per
    return pl.pallas_call(
        project_kernel,
        grid=(3 * groups,),
        in_specs=[whole(frames.shape), pl.BlockSpec((width, cols), lambda j: (0, j))],
        out_specs=[
            whole(frames.shape),
            pl.BlockSpec((per, HD, rows), lambda j: (j % groups, j // groups, 0)),
        ],
        out_shape=[
            jax.ShapeDtypeStruct(frames.shape, BF16),
            jax.ShapeDtypeStruct((HEADS, 3 * HD, rows), BF16),
        ],
        compiler_params=params(),
        name="project",
    )(frames, w_qkv)


def load_heads(length, heads_ref, query, keys, count, rows):
    extra = lax.broadcasted_iota(jnp.int32, (HD, rows), 0)
    frame = lax.broadcasted_iota(jnp.int32, (HD, rows), 1)
    for i in range(count):
        cols = slice(i * rows, (i + 1) * rows)
        query[0:HD, cols] = (heads_ref[i, 0:HD, :].astype(F32) * 0.125).astype(BF16)
        query[HD : 2 * HD, cols] = jnp.where(extra == 0, 1.0, 0.0).astype(BF16)
        masked = jnp.logical_and(extra == 0, frame + i * rows >= length)
        mask = jnp.where(masked, -1e30, 0.0).astype(BF16)
        joined = jnp.concatenate([heads_ref[i, HD : 2 * HD, :], mask], axis=0)
        keys[cols, :] = joined.T


def attend_kernel(
    scalars, heads_ref, send_ref, own_ref, out_ref, lse_ref, query, keys, value, scores
):
    count, _, rows = heads_ref.shape
    total = count * rows
    load_heads(scalars[0], heads_ref, query, keys, count, rows)
    for i in range(count):
        value[:, i * rows : (i + 1) * rows] = heads_ref[i, 2 * HD : 3 * HD, :]

    def one_block(block, carry):
        cols = pl.ds(pl.multiple_of(block * QB, QB), QB)
        query_cols = query[:, cols]
        peak = None
        for k in range(total // KB):
            part = dot(keys[k * KB : (k + 1) * KB, :], query_cols)
            scores[k * KB : (k + 1) * KB, :] = part
            top = jnp.max(part.reshape(KB // 8, 8, QB), axis=0)
            peak = top if peak is None else jnp.maximum(peak, top)
        peak = jnp.max(peak, axis=0, keepdims=True)
        total_row = jnp.zeros((8, QB), F32)
        acc = jnp.zeros((HD, QB), F32)
        for k in range(total // KB):
            expo = jnp.exp(scores[k * KB : (k + 1) * KB, :] - peak)
            total_row = total_row + jnp.sum(expo.reshape(KB // 8, 8, QB), axis=0)
            acc = acc + dot(value[:, k * KB : (k + 1) * KB], expo.astype(BF16))
        total_row = jnp.sum(total_row, axis=0, keepdims=True)
        result = acc / total_row
        out_ref[:, cols] = result
        own_ref[:, cols] = result.astype(BF16)
        lse_ref[:, cols] = peak + jnp.log(total_row)
        return carry

    lax.fori_loop(0, total // QB, one_block, 0)
    none = jnp.zeros((HD, HALO), F32)
    for i in range(count):
        send_ref[i, 0:HD, :] = own_ref[:, i * rows : (i + 1) * rows]
        low = out_ref[:, i * rows - HALO : i * rows] if i else none
        high = out_ref[:, (i + 1) * rows : (i + 1) * rows + HALO] if i < count - 1 else none
        sides = jnp.concatenate([low, high], axis=1)
        packed = jnp.concatenate([sides[0 : HD // 2], sides[HD // 2 :]], axis=1)
        send_ref[i, HD : HD + HD // 2, :] = packed.astype(BF16)


def attend(scalars, heads):
    count, _, rows = heads.shape
    total = count * rows
    return pl.pallas_call(
        attend_kernel,
        in_specs=[SMEM, pl.BlockSpec(memory_space=pltpu.VMEM)],
        out_shape=[
            jax.ShapeDtypeStruct((count, HD + HD // 2, rows), BF16),
            jax.ShapeDtypeStruct((HD, total), BF16),
            jax.ShapeDtypeStruct((HD, total), F32),
            jax.ShapeDtypeStruct((1, total), F32),
        ],
        scratch_shapes=[
            pltpu.VMEM((2 * HD, total), BF16),
            pltpu.VMEM((total, 2 * HD), BF16),
            pltpu.VMEM((HD, total), BF16),
            pltpu.VMEM((total, QB), F32),
        ],
        compiler_params=params(),
        name="attend",
    )(scalars, heads)


def middle_kernel(
    scalars,
    att_ref,
    frames_ref,
    frames_side,
    grads_ref,
    grads_side,
    w_out_ref,
    w_conv_ref,
    output_ref,
    res_grad_ref,
    send_ref,
    taps_ref,
    conv_in,
    grad_all,
    residual,
    window,
    window_back,
    conv_grad,
):
    rows, width = frames_ref.shape
    heads = att_ref.shape[0]
    length = scalars[0]
    first = scalars[1]
    zero = scalars[2]
    half = HD // 2
    body = slice(HALO, HALO + rows)

    attended = att_ref[:, 0:HD, :].reshape(width, rows).T
    main = frames_ref[...].astype(F32) + dot(attended, w_out_ref[...])
    packed = att_ref[:, HD : HD + half, :].reshape(heads * half, rows).T
    split_w = w_out_ref[...].reshape(heads, 2, half, width)
    side = dot(packed[0 : 2 * HALO], split_w[:, 0].reshape(heads * half, width))
    side = side + dot(packed[2 * HALO :], split_w[:, 1].reshape(heads * half, width))
    side = frames_side[...].astype(F32) + side

    def keep_of(count, start):
        frame = lax.broadcasted_iota(jnp.int32, (count, 1), 0) + start
        return jnp.where(jnp.logical_and(frame >= 0, frame < length), 1.0, 0.0)

    main = main.astype(BF16).astype(F32)
    residual[...] = main
    unit, scale = normalize(main)
    keep = keep_of(rows, first)
    conv_in[body, :] = (unit * keep).astype(BF16).astype(F32)
    unit_side, _ = normalize(side.astype(BF16).astype(F32))
    low = unit_side[0:HALO] * keep_of(HALO, first - HALO)
    high = unit_side[HALO:] * keep_of(HALO, first + rows)
    conv_in[0:HALO, :] = low.astype(BF16).astype(F32)
    conv_in[HALO + rows :, :] = high.astype(BF16).astype(F32)
    grad_all[0:HALO, :] = grads_side[0:HALO, :].astype(F32)
    grad_all[body, :] = grads_ref[...].astype(F32)
    grad_all[HALO + rows :, :] = grads_side[HALO:, :].astype(F32)

    reach = rows + HALO
    edge = HALO // 2

    def one_chunk(chunk, carry):
        lanes = pl.ds(pl.multiple_of(chunk * 128, 128), 128)
        window[...] = conv_in[:, lanes]
        acc = jnp.zeros((reach, 128), F32)
        for j in range(KW):
            acc = acc + w_conv_ref[j : j + 1, lanes] * window[pl.ds(zero + (1 + j), reach), :]
        gate = jax.nn.sigmoid(acc)
        back = grad_all[edge : edge + reach, lanes] * (gate + acc * gate * (1.0 - gate))
        window_back[...] = back
        gated = acc[edge : edge + rows] * gate[edge : edge + rows]
        output_ref[:, lanes] = (residual[:, lanes] + gated).astype(BF16)
        own = window_back[edge : edge + rows, :]
        acc = jnp.zeros((rows, 128), F32)
        for j in range(KW):
            acc = acc + w_conv_ref[j : j + 1, lanes] * window_back[
                pl.ds(zero + (KW - j), rows), :
            ]
            moved = window[pl.ds(zero + (edge + 1 + j), rows), :]
            taps_ref[j : j + 1, lanes] = jnp.sum(moved * own, axis=0, keepdims=True)
        taps_ref[KW : KW + 1, lanes] = jnp.zeros((1, 128), F32)
        conv_grad[:, lanes] = acc
        return carry

    lax.fori_loop(0, width // 128, one_chunk, 0)
    res_grad = grads_ref[...].astype(F32) + normalize_back(unit, scale, conv_grad[...] * keep)
    res_grad_ref[...] = res_grad
    rounded = res_grad.astype(BF16)
    columns = rounded.T
    send_ref[:, 0:HD, :] = dot(w_out_ref[...], columns).astype(BF16).reshape(heads, HD, rows)
    send_ref[:, HD : 2 * HD, :] = columns.reshape(heads, HD, rows)
    for h in range(heads):
        send_ref[h, 2 * HD :, :] = halves(taps_ref[:, h * HD : (h + 1) * HD])


def middle(scalars, att, frames, frames_side, grads, grads_side, w_out, w_conv):
    rows, width = frames.shape
    vmem = pl.BlockSpec(memory_space=pltpu.VMEM)
    return pl.pallas_call(
        middle_kernel,
        in_specs=[SMEM] + [vmem] * 7,
        out_shape=[
            jax.ShapeDtypeStruct((rows, width), BF16),
            jax.ShapeDtypeStruct((rows, width), F32),
            jax.ShapeDtypeStruct((HEADS, 2 * HD + KW + 1, rows), BF16),
        ],
        scratch_shapes=[
            pltpu.VMEM((KW + 1, width), F32),
            pltpu.VMEM((rows + 2 * HALO, width), F32),
            pltpu.VMEM((rows + 2 * HALO, width), F32),
            pltpu.VMEM((rows, width), F32),
            pltpu.VMEM((rows + 2 * HALO, 128), F32),
            pltpu.VMEM((rows + HALO, 128), F32),
            pltpu.VMEM((rows, width), F32),
        ],
        compiler_params=params(),
        name="middle",
    )(scalars, att, frames, frames_side, grads, grads_side, w_out, w_conv)


def attend_back_kernel(
    scalars, heads_ref, grads_ref, out_ref, lse_ref, send_ref,
    query, keys, value_t, grad_t, query_rows, grad_rows, query_grad, probs, score_grads,
):
    count, _, rows = heads_ref.shape
    total = count * rows
    load_heads(scalars[0], heads_ref, query, keys, count, rows)
    for i in range(count):
        cols = slice(i * rows, (i + 1) * rows)
        block = grads_ref[i, 0:HD, :]
        grad_t[:, cols] = block
        both = jnp.concatenate([query[0:HD, cols], block], axis=0).T
        query_rows[cols, :] = both[:, 0:HD]
        grad_rows[cols, :] = both[:, HD:]
        value_t[cols, :] = heads_ref[i, 2 * HD : 3 * HD, :].T
    query_grad[...] = jnp.zeros_like(query_grad)
    lse = lse_ref[...]
    delta = jnp.sum(grad_t[...].astype(F32) * out_ref[...], axis=0, keepdims=True)

    def one_block(block, carry):
        span = pl.ds(pl.multiple_of(block * KB, KB), KB)
        key_rows = keys[span, :]
        value_rows = value_t[span, :]
        for q in range(total // QB):
            cols = slice(q * QB, (q + 1) * QB)
            prob = jnp.exp(dot(key_rows, query[:, cols]) - lse[:, cols])
            prob_grad = dot(value_rows, grad_t[:, cols])
            probs[:, cols] = prob.astype(BF16)
            score_grads[:, cols] = (prob * (prob_grad - delta[:, cols])).astype(BF16)
        key_grad = dot(score_grads[...], query_rows[...])
        value_grad = dot(probs[...], grad_rows[...])
        key_cols = key_rows[:, 0:HD].T
        query_grad[...] += dot(key_cols, score_grads[...])
        joined = jnp.concatenate([key_grad, value_grad], axis=1).T.astype(BF16)
        for i in range(KB // rows):
            send_ref[block * (KB // rows) + i, HD : 3 * HD, :] = joined[:, i * rows : (i + 1) * rows]
        return carry

    lax.fori_loop(0, total // KB, one_block, 0)
    for i in range(count):
        cols = slice(i * rows, (i + 1) * rows)
        send_ref[i, 0:HD, :] = (query_grad[:, cols] * 0.125).astype(BF16)


def attend_back(scalars, heads, grads, out, lse):
    count, _, rows = heads.shape
    total = count * rows
    vmem = pl.BlockSpec(memory_space=pltpu.VMEM)
    return pl.pallas_call(
        attend_back_kernel,
        in_specs=[SMEM] + [vmem] * 4,
        out_shape=jax.ShapeDtypeStruct(heads.shape, BF16),
        scratch_shapes=[
            pltpu.VMEM((2 * HD, total), BF16),
            pltpu.VMEM((total, 2 * HD), BF16),
            pltpu.VMEM((total, HD), BF16),
            pltpu.VMEM((HD, total), BF16),
            pltpu.VMEM((total, HD), BF16),
            pltpu.VMEM((total, HD), BF16),
            pltpu.VMEM((HD, total), F32),
            pltpu.VMEM((KB, total), BF16),
            pltpu.VMEM((KB, total), BF16),
        ],
        compiler_params=params(),
        name="attend_back",
    )(scalars, heads, grads, out, lse)


def input_grad_kernel(joined_ref, weight_ref, frames_ref, res_grad_ref, out_ref, joined, grads):
    step = pl.program_id(0)
    heads = joined_ref.shape[0]

    @pl.when(step == 0)
    def _():
        for h in range(heads):
            for t in range(3):
                row = (t * heads + h) * HD
                joined[row : row + HD, :] = joined_ref[h, t * HD : (t + 1) * HD, :]

    block = weight_ref.shape[0]
    start = pl.multiple_of(step * block, block)
    grads[pl.ds(start, block), :] = dot(weight_ref[...], joined[...])

    @pl.when(step == pl.num_programs(0) - 1)
    def _():
        unit, scale = normalize(frames_ref[...].astype(F32))
        back = normalize_back(unit, scale, grads[...].T)
        out_ref[...] = (res_grad_ref[...] + back).astype(BF16)


def input_gradient(joined, w_qkv, frames, res_grad):
    rows, width = frames.shape
    block = 256
    return pl.pallas_call(
        input_grad_kernel,
        grid=(width // block,),
        in_specs=[
            whole(joined.shape),
            pl.BlockSpec((block, w_qkv.shape[1]), lambda j: (j, 0)),
            whole(frames.shape),
            whole(frames.shape),
        ],
        out_specs=whole(frames.shape),
        out_shape=jax.ShapeDtypeStruct(frames.shape, BF16),
        scratch_shapes=[
            pltpu.VMEM((w_qkv.shape[1], rows), BF16),
            pltpu.VMEM((width, rows), F32),
        ],
        compiler_params=params(),
        name="input_gradient",
    )(joined, w_qkv, frames, res_grad)


def parts_kernel(grads_ref, back_ref, normed_ref, att_ref, send_ref, columns, back_rows):
    count, wide, rows = grads_ref.shape
    slow = pl.program_id(0)
    fast = send_ref.shape[0]

    @pl.when(slow == 0)
    def _():
        taps = jnp.zeros((KW + 1, rows), F32)
        for i in range(count):
            columns[:, i * rows : (i + 1) * rows] = grads_ref[i]
            back_rows[i * rows : (i + 1) * rows, :] = back_ref[i, HD : 2 * HD, :].T
            taps = taps + back_ref[i, 2 * HD :, :].astype(F32)
        pair = halves(joined_halves(taps))
        for i in range(fast):
            send_ref[i, TAPS:, :] = pair

    part = dot(columns[...], normed_ref[...])
    outer = dot(att_ref[...], back_rows[...])
    each = part.shape[1] // fast
    for i in range(fast):
        piece = part[:, i * each : (i + 1) * each]
        first = pl.multiple_of(slow * CUT, CUT)
        send_ref[i, pl.ds(first, wide // 2), :] = jnp.concatenate(
            [piece[0 : wide // 2], piece[wide // 2 :]], axis=1
        ).astype(BF16)
        piece = outer[i * each : (i + 1) * each, :]
        send_ref[i, pl.ds(first + wide // 2, each // 2), :] = jnp.concatenate(
            [piece[0 : each // 2], piece[each // 2 :]], axis=1
        ).astype(BF16)


CUT = 128
FAST = 4
SLOW = 4
TAPS = SLOW * CUT


def gradient_parts(grads, back, normed_all, att_all):
    count, wide, rows = grads.shape
    total, width = normed_all.shape
    return pl.pallas_call(
        parts_kernel,
        grid=(SLOW,),
        in_specs=[
            whole(grads.shape),
            whole(back.shape),
            pl.BlockSpec((total, width // SLOW), lambda j: (0, j)),
            pl.BlockSpec((width // SLOW, total), lambda j: (j, 0)),
        ],
        out_specs=whole((FAST, TAPS + KW + 1, 128)),
        out_shape=jax.ShapeDtypeStruct((FAST, TAPS + KW + 1, 128), BF16),
        scratch_shapes=[pltpu.VMEM((wide, total), BF16), pltpu.VMEM((total, HD), BF16)],
        compiler_params=params(),
        name="gradient_parts",
    )(grads, back, normed_all, att_all)


def fold_fast_kernel(scalars, own_ref, one, two, three, out_ref):
    own = own_ref[scalars[3]]
    for i in range(SLOW):
        cut = slice(i * CUT, (i + 1) * CUT)
        total = own[cut].astype(F32) + one[cut, :].astype(F32)
        total = total + (two[cut, :].astype(F32) + three[cut, :].astype(F32))
        out_ref[i, 0:CUT, :] = total.astype(BF16)
    cut = slice(TAPS, TAPS + KW + 1)
    total = own[cut].astype(F32) + one[cut, :].astype(F32)
    total = total + (two[cut, :].astype(F32) + three[cut, :].astype(F32))
    pair = halves(joined_halves(total))
    for i in range(SLOW):
        out_ref[i, CUT:, :] = pair


def fold_fast(scalars, own, others):
    vmem = pl.BlockSpec(memory_space=pltpu.VMEM)
    return pl.pallas_call(
        fold_fast_kernel,
        in_specs=[SMEM] + [vmem] * 4,
        out_shape=jax.ShapeDtypeStruct((SLOW, CUT + KW + 1, 128), BF16),
        compiler_params=params(),
        name="fold_fast",
    )(scalars, own, *others)


def fold_slow_kernel(scalars, own_ref, one, two, three, qkv_ref, send_ref, *, scale):
    total = own_ref[scalars[4]].astype(F32) + one[...].astype(F32)
    total = (total + (two[...].astype(F32) + three[...].astype(F32))) * scale
    wide = 3 * HD // 2
    whole_rows = total[0:wide].T
    qkv_ref[:, 0:wide] = whole_rows[0:HD]
    qkv_ref[:, wide:] = whole_rows[HD:]
    outer = total[wide:CUT]
    rows = jnp.concatenate([outer[:, 0:HD], outer[:, HD:]], axis=0)
    taps = joined_halves(total[CUT:])
    half = (KW + 1) // 2
    pair = jnp.concatenate([taps[0:half], taps[half:]], axis=1)
    count = send_ref.shape[0]
    each = HD // count
    for i in range(count):
        piece = rows[i * each : (i + 1) * each]
        send_ref[i, 0:half, :] = pair
        send_ref[i, half : half + each, 0:HD] = piece
        send_ref[i, half : half + each, HD:] = piece
        send_ref[i, half + each :, :] = jnp.zeros((8 - each, 128), F32)


def fold_slow(scalars, own, others, seq_count, scale):
    vmem = pl.BlockSpec(memory_space=pltpu.VMEM)
    return pl.pallas_call(
        lambda *refs: fold_slow_kernel(*refs, scale=scale),
        in_specs=[SMEM] + [vmem] * 4,
        out_shape=[
            jax.ShapeDtypeStruct((HD, 3 * HD), F32),
            jax.ShapeDtypeStruct((seq_count, 24, 128), F32),
        ],
        compiler_params=params(),
        name="fold_slow",
    )(scalars, own, *others)


def finish_kernel(recv_ref, out_ref, taps_ref):
    count = recv_ref.shape[0]
    each = out_ref.shape[0]
    half = (KW + 1) // 2
    for i in range(count // 2):
        a = recv_ref[2 * i]
        b = recv_ref[2 * i + 1]
        lanes = slice(i * 2 * HD, (i + 1) * 2 * HD)
        out_ref[:, lanes] = jnp.concatenate(
            [a[half : half + each, 0:HD], b[half : half + each, HD:]], axis=1
        )
        taps_ref[0:half, lanes] = jnp.concatenate([a[0:half, 0:HD], b[0:half, 0:HD]], axis=1)
        taps_ref[half:KW, lanes] = jnp.concatenate(
            [a[0 : half - 1, HD:], b[0 : half - 1, HD:]], axis=1
        )


def finish(recv, width):
    count = recv.shape[0]
    vmem = pl.BlockSpec(memory_space=pltpu.VMEM)
    return pl.pallas_call(
        finish_kernel,
        in_specs=[vmem],
        out_shape=[
            jax.ShapeDtypeStruct((HD // count, width), F32),
            jax.ShapeDtypeStruct((KW, width), F32),
        ],
        compiler_params=params(),
        name="finish",
    )(recv)


def exchange(blocks, index, partner):
    pairs = lambda k: [(d, partner(d, k)) for d in range(FAST * SLOW)]
    received = []
    for k in range(1, 4):
        block = lax.dynamic_index_in_dim(blocks, index ^ k, 0, keepdims=False)
        received.append(lax.ppermute(block, "dp", pairs(k)))
    return received


def local(frames, cotangent, w_qkv, w_out, w_conv, lengths):
    seq_count = lax.axis_size("seq")
    data_count = lax.axis_size("dp")
    rows, width = frames.shape[1:]
    first = lax.axis_index("seq") * rows
    grad_scale = 1.0 / math.sqrt(data_count * rows * seq_count)
    position = lax.axis_index("dp")
    fast = position % FAST
    slow = position // FAST
    scalars = jnp.stack([lengths[0], first, jnp.zeros((), jnp.int32), fast, slow])
    x = frames[0]
    g = cotangent[0]

    forward = [(i, i + 1) for i in range(seq_count - 1)]
    backward = [(i + 1, i) for i in range(seq_count - 1)]
    low = lax.ppermute(jnp.concatenate([x[-HALO:], g[-HALO:]], axis=0), "seq", forward)
    high = lax.ppermute(jnp.concatenate([x[:HALO], g[:HALO]], axis=0), "seq", backward)
    x_side = jnp.concatenate([low[:HALO], high[:HALO]], axis=0)
    g_side = jnp.concatenate([low[HALO:], high[HALO:]], axis=0)

    normed, send = project(x, w_qkv)
    heads = lax.all_to_all(send, "seq", 0, 0, tiled=True)
    normed_all = lax.all_gather(normed, "seq", axis=0, tiled=True)
    send, own, out, lse = attend(scalars, heads)
    att = lax.all_to_all(send, "seq", 0, 0, tiled=True)
    att_all = lax.all_gather(own, "seq", axis=0, tiled=True)
    output, res_grad, send = middle(scalars, att, x, x_side, g, g_side, w_out, w_conv)
    back = lax.all_to_all(send, "seq", 0, 0, tiled=True)
    send = attend_back(scalars, heads, back, out, lse)
    joined = lax.all_to_all(send, "seq", 0, 0, tiled=True)
    parts = gradient_parts(send, back, normed_all, att_all)
    others = exchange(parts, fast, lambda d, k: d ^ k)
    parts = fold_fast(scalars, parts, others)
    others = exchange(parts, slow, lambda d, k: d ^ (FAST * k))
    qkv, send = fold_slow(scalars, parts, others, seq_count, grad_scale)
    input_grad = input_gradient(joined, w_qkv, x, res_grad)
    out_total, taps_total = finish(lax.all_to_all(send, "seq", 0, 0, tiled=True), width)
    return (
        output[None],
        input_grad[None],
        qkv.reshape(width // data_count, 3, HD),
        out_total,
        taps_total,
    )


def solution(mesh):
    placed = (P("dp", "seq", None), P("dp", "seq", None), P(), P(), P(), P("dp"))
    return jax.shard_map(
        local,
        mesh=mesh,
        in_specs=placed,
        out_specs=(
            P("dp", "seq", None),
            P("dp", "seq", None),
            P("dp", None, "seq"),
            P(("dp", "seq"), None),
            P(),
        ),
        check_vma=False,
    )
```

time: 547 us -> 259 us (0.47)
  waiting for transfers between devices: 289 us -> 106 us
  matrix products: 76.4 us -> 0 us
  Pallas kernels: 0 us -> 62.6 us
  other arithmetic: 58.4 us -> 0.75 us
  local copies, waits for them, and re-layouts: 62.1 us -> 7.07 us
  blocking collectives: 0 us -> 25.6 us
    unnamed x4 -> x2, waiting for transfers between devices: 241 us -> 0.03 us
    dot_general x34 -> x0, matrix products: 76.4 us -> none  [the longest x4 17.8 us: one_block(): lax.dot_general(probabilities.astype(jnp.bfloat16), grad_block, (((0,), (...]
    pallas_call x0 -> x9, Pallas kernels: none -> 62.6 us  [the longest x1 14.8 us: attend_back(): pl.pallas_call(attend_back_kernel, in_specs=[SMEM] + [vmem] * 4, out_shap...]
    all_gather x1 -> x2, waiting for transfers between devices: 0.02 us -> 55.3 us  [the longest x1 55.3 us: local(): att_all = lax.all_gather(own, 'seq', axis=0, tiled=True)]
    all_to_all x0 -> x1, blocking collectives: none -> 25.6 us  [local(): back = lax.all_to_all(send, 'seq', 0, 0, tiled=True)]
    reduce_sum x18 -> x0, other arithmetic: 21.5 us -> none  [the longest x8 7.48 us: block_probs(): return expo_rows / jnp.sum(expo_rows, axis=-1, keepdims=True)]
    ppermute x4 -> x8, waiting for transfers between devices: 4.3 us -> 25.1 us  [the longest x1 12.8 us: local(): lax.ppermute(jnp.concatenate([x[:HALO], g[:HALO]], axis=0), 'seq', backward)]
    unnamed x125 -> x27, local copies, waits for them, and re-layouts: 23 us -> 4.37 us
  transfers between devices with their start and end apart: 11 -> 14, of which waited for: 7 -> 8; matrix products, arithmetic and copies ran while one was open for 20% -> 2% of each run, Pallas kernels for 0% -> 21%
where the time goes in v1:
time: 259 us; the launch traced here: 258 us
  waiting for transfers between devices  106 us (41%)
  Pallas kernels  62.6 us (24%)
  starting transfers between devices  40.7 us (16%)
  blocking collectives  25.6 us (10%)
  between operations  14.9 us (6%)
  local copies, waits for them, and re-layouts  7.07 us (3%)
    all_gather x1, waiting for transfers between devices, local(): att_all = lax.all_gather(own, 'seq', axis=0, tiled=True)  55.3 us
    all_to_all x1, blocking collectives, local(): back = lax.all_to_all(send, 'seq', 0, 0, tiled=True)  25.6 us
    all_to_all x1, waiting for transfers between devices, local(): heads = lax.all_to_all(send, 'seq', 0, 0, tiled=True)  24.6 us
    pallas_call x1, Pallas kernels, attend_back(): pl.pallas_call(attend_back_kernel, in_specs=[SMEM] + [vmem] * 4, out_shap...  14.8 us
    ppermute x1, waiting for transfers between devices, local(): lax.ppermute(jnp.concatenate([x[:HALO], g[:HALO]], axis=0), 'seq', backward)  12.8 us
    pallas_call x1, Pallas kernels, attend(): pl.pallas_call(attend_kernel, in_specs=[SMEM, pl.BlockSpec(memory_space=p...  12.8 us
    ppermute x6, waiting for transfers between devices, exchange(): received.append(lax.ppermute(block, 'dp', pairs(k)))  12.3 us
    all_to_all x1, starting transfers between devices, local(): heads = lax.all_to_all(send, 'seq', 0, 0, tiled=True)  9.52 us
  transfers between devices with their start and end apart: 14, of which 8 were waited for; matrix products, arithmetic and copies ran while one was open for 2% of the time, Pallas kernels for 21%

profile of v1, /device:TPU:32, one launch (start us, length us, event | category | flops | bytes accessed | tf_op | source)
XLA Modules:
  0.0 257.8 jit_solution(10600128154656821002)
XLA Ops:
  7.2 0.0 all-gather.3.cloned.1.call-start
  7.2 0.0 copy-start.1
  7.2 0.0 copy-start.5
  7.2 6.9 %project.1 = (bf16[128,1024]{1,0:T(8,128)(2,1)}, bf16[16,192,128]{2,1,0:T(8,128)(2,1)}) custom-call(bf16[128,1024]{1,0:T(8,128)(2,1)} %bitcast.28, bf16[1024,3072]{1,0:T(8,128)(2,1)} %weight_ref.3), custom_call_target="tpu_custom_call" | custom-call | tf_op jit(solution)/shard_map/project/pallas_call | solution.py:75
  14.2 0.0 all-gather.3.cloned.1.call-update
  14.2 9.5 %all-to-all-start = ((bf16[16,192,128]{2,1,0:T(8,128)(2,1)}), bf16[16,192,128]{2,1,0:T(8,128)(2,1)S(1)}, u32[]{:S(2)}, u32[]{:S(2)}) async-start(bf16[16,192,128]{2,1,0:T(8,128)(2,1)} %get-tuple-element.18), calls=%async_computation | async-start | bytes 1572864 | tf_op jit(solution)/shard_map/all_to_all | solution.py:581
  23.7 0.0 all-gather.5.cloned.1.call-start
  24.4 0.7 stack.15.scalars.refs_0_
  25.1 24.6 %all-to-all-done.heads_ref = bf16[16,192,128]{2,1,0:T(8,128)(2,1)S(1)} async-done(((bf16[16,192,128]{2,1,0:T(8,128)(2,1)}), bf16[16,192,128]{2,1,0:T(8,128)(2,1)S(1)}, u32[]{:S(2)}, u32[]{:S(2)}) %all-to-all-start) | async-done | bytes 786464 | tf_op jit(solution)/shard_map/all_to_all | solution.py:581
  49.7 0.9 copy-done
  50.6 12.8 %attend.1 = (bf16[16,96,128]{2,1,0:T(8,128)(2,1)}, bf16[64,2048]{1,0:T(8,128)(2,1)}, f32[64,2048]{1,0:T(8,128)}, f32[1,2048]{1,0:T(1,128)}) custom-call(s32[5]{0:T(128)} %stack.15.scalars.refs_0_, bf16[16,192,128]{2,1,0:T(8,128)(2,1)} %copy-done), custom_call_target="tpu_custom_call" | custom-call | tf_op jit(solution)/shard_map/attend/pallas_call | solution.py:151
  63.4 0.0 all-gather.5.cloned.1.call-update
  63.5 7.0 %all-to-all-start.1 = ((bf16[16,96,128]{2,1,0:T(8,128)(2,1)}), bf16[16,96,128]{2,1,0:T(8,128)(2,1)S(1)}, u32[]{:S(2)}, u32[]{:S(2)}) async-start(bf16[16,96,128]{2,1,0:T(8,128)(2,1)} %get-tuple-element.19), calls=%async_computation.1 | async-start | bytes 786432 | tf_op jit(solution)/shard_map/all_to_all | solution.py:584
  70.5 2.0 collective-permute-start.1
  72.6 3.8 %collective-permute-start = (bf16[64,1024]{1,0:T(8,128)(2,1)S(1)}, bf16[64,1024]{1,0:T(8,128)(2,1)S(1)}, u32[]{:S(2)}, u32[]{:S(2)}) collective-permute-start(bf16[64,1024]{1,0:T(8,128)(2,1)S(1)} %pad_maximum_fusion), channel_id=1, source_target_pairs={{0,1},{1,2},{2,3},{3,4},{4,5},{5,6},{6,7},{7,8},{8,9},{9,10},{10,1... | collective-permute-start | bytes 393224 | tf_op jit(solution)/shard_map/ppermute | solution.py:575
  76.4 12.8 %collective-permute-done.1 = bf16[64,1024]{1,0:T(8,128)(2,1)S(1)} collective-permute-done((bf16[64,1024]{1,0:T(8,128)(2,1)S(1)}, bf16[64,1024]{1,0:T(8,128)(2,1)S(1)}, u32[]{:S(2)}, u32[]{:S(2)}) %collective-permute-start.1) | collective-permute-done | bytes 131104 | tf_op jit(solution)/shard_map/ppermute | solution.py:576
  89.3 0.7 pad_maximum_fusion.2
  90.0 0.0 all-to-all-done.1.att_ref
  90.0 0.8 copy-done.3
  90.8 9.0 %middle.1 = (bf16[128,1024]{1,0:T(8,128)(2,1)}, f32[128,1024]{1,0:T(8,128)}, bf16[16,160,128]{2,1,0:T(8,128)(2,1)}) custom-call(s32[5]{0:T(128)} %stack.15.scalars.refs_0_, bf16[16,96,128]{2,1,0:T(8,128)(2,1)} %copy-done.3, bf16[128,1024]{1,0:T(8,128)(2,1)} %bitcast.29, bf16[64,1024]{1,0:T(8,128)(2,1)} %get-tuple-element.55.frames_side, ...), custom_call_target="tpu_custom_call" | custom-call | tf_op jit(solution)/shard_map/middle/pallas_call | solution.py:265
  99.8 25.6 %all_to_all.25.grads_ref.back_ref = bf16[16,160,128]{2,1,0:T(8,128)(2,1)} all-to-all(bf16[16,160,128]{2,1,0:T(8,128)(2,1)} %get-tuple-element.21), channel_id=1, replica_groups=mesh['dp'=16,'seq'=16] {'seq'}, dimensions={0} | all-to-all | bytes 1310720 | tf_op jit(solution)/shard_map/all_to_all | solution.py:587
  125.4 14.8 %attend_back.1.grads_ref = bf16[16,192,128]{2,1,0:T(8,128)(2,1)} custom-call(s32[5]{0:T(128)} %stack.15.scalars.refs_0_, bf16[16,192,128]{2,1,0:T(8,128)(2,1)} %copy-done, bf16[16,160,128]{2,1,0:T(8,128)(2,1)} %all_to_all.25.grads_ref.back_ref, f32[64,2048]{1,0:T(8,128)} %get-tuple-element.22.out_ref, f32[1,2048]{1,0:T(1,128)} %get-tuple-element.23.lse_ref), custom_call_target="tpu_custom_call" | custom-call | tf_op jit(solution)/shard_map/attend_back/pallas_call | solution.py:335
  140.2 4.1 %all-to-all-start.3 = ((bf16[16,192,128]{2,1,0:T(8,128)(2,1)}), bf16[16,192,128]{2,1,0:T(8,128)(2,1)S(1)}, u32[]{:S(2)}, u32[]{:S(2)}) async-start(bf16[16,192,128]{2,1,0:T(8,128)(2,1)} %attend_back.1.grads_ref), calls=%async_computation.3 | async-start | bytes 1572864 | tf_op jit(solution)/shard_map/all_to_all | solution.py:589
  144.3 0.0 all-gather.3.cloned.1.call-done.normed_ref
  144.3 55.3 %all-gather.5.cloned.1.call-done.att_ref = bf16[1024,2048]{1,0:T(8,128)(2,1)} async-done(((bf16[64,2048]{1,0:T(8,128)(2,1)}), bf16[1024,2048]{1,0:T(8,128)(2,1)}) %all-gather.5.cloned.1.call-update) | async-done | bytes 4194320 | tf_op jit(solution)/shard_map/all_gather | solution.py:585
  199.6 7.1 %gradient_parts.1.own_ref = bf16[4,544,128]{2,1,0:T(8,128)(2,1)} custom-call(bf16[16,192,128]{2,1,0:T(8,128)(2,1)} %attend_back.1.grads_ref, bf16[16,160,128]{2,1,0:T(8,128)(2,1)} %all_to_all.25.grads_ref.back_ref, bf16[2048,1024]{1,0:T(8,128)(2,1)} %all-gather.3.cloned.1.call-done.normed_ref, bf16[1024,2048]{1,0:T(8,128)(2,1)} %all-gather.5.cloned.1.call-done.att_ref), custom_call_target="tpu_custom_call" | custom-call | tf_op jit(solution)/shard_map/gradient_parts/pallas_call | solution.py:440
  206.6 1.1 dynamic-slice_bitcast_fusion
  207.7 0.1 collective-permute-start.2
  207.8 3.4 %collective-permute-start.3 = (bf16[544,128]{1,0:T(8,128)(2,1)S(1)}, bf16[544,128]{1,0:T(8,128)(2,1)S(1)}, u32[]{:S(2)}, u32[]{:S(2)}) collective-permute-start(bf16[544,128]{1,0:T(8,128)(2,1)S(1)} %get-tuple-element.42), channel_id=1, source_target_pairs={{0,32},{16,48},{32,0},{48,16},{64,96},{80,112},{96,64},{112,80},{1... | collective-permute-start | bytes 417800 | tf_op jit(solution)/shard_map/ppermute | solution.py:556
  211.2 0.1 collective-permute-start.4
  211.2 4.2 %collective-permute-done.3.two = bf16[544,128]{1,0:T(8,128)(2,1)S(1)} collective-permute-done((bf16[544,128]{1,0:T(8,128)(2,1)S(1)}, bf16[544,128]{1,0:T(8,128)(2,1)S(1)}, u32[]{:S(2)}, u32[]{:S(2)}) %collective-permute-start.3) | collective-permute-done | bytes 139296 | tf_op jit(solution)/shard_map/ppermute | solution.py:556
  215.4 2.9 %collective-permute-done.4.three = bf16[544,128]{1,0:T(8,128)(2,1)S(1)} collective-permute-done((bf16[544,128]{1,0:T(8,128)(2,1)S(1)}, bf16[544,128]{1,0:T(8,128)(2,1)S(1)}, u32[]{:S(2)}, u32[]{:S(2)}) %collective-permute-start.4) | collective-permute-done | bytes 139296 | tf_op jit(solution)/shard_map/ppermute | solution.py:556
  218.3 0.7 copy-done.8
  219.0 2.0 fold_fast.1.refs_1_
  221.0 0.8 dynamic-slice_bitcast_fusion.3
  221.8 1.9 collective-permute-start.5
  223.7 3.0 %collective-permute-start.6 = (bf16[160,128]{1,0:T(8,128)(2,1)S(1)}, bf16[160,128]{1,0:T(8,128)(2,1)S(1)}, u32[]{:S(2)}, u32[]{:S(2)}) collective-permute-start(bf16[160,128]{1,0:T(8,128)(2,1)S(1)} %get-tuple-element.49), channel_id=1, source_target_pairs={{0,128},{16,144},{32,160},{48,176},{64,192},{80,208},{96,224},{112... | collective-permute-start | bytes 122888 | tf_op jit(solution)/shard_map/ppermute | solution.py:556
  226.7 2.5 collective-permute-done.6.refs_3_
  229.2 2.7 %collective-permute-done.7.refs_4_ = bf16[160,128]{1,0:T(8,128)(2,1)S(1)} collective-permute-done((bf16[160,128]{1,0:T(8,128)(2,1)S(1)}, bf16[160,128]{1,0:T(8,128)(2,1)S(1)}, u32[]{:S(2)}, u32[]{:S(2)}) %collective-permute-start.7) | collective-permute-done | bytes 40992 | tf_op jit(solution)/shard_map/ppermute | solution.py:556
  231.9 0.6 copy-done.12
  232.5 1.8 fold_slow.1
  234.4 5.8 %all-to-all-start.4 = ((f32[16,24,128]{2,1,0:T(8,128)}), f32[16,24,128]{2,1,0:T(8,128)S(1)}, u32[]{:S(2)}, u32[]{:S(2)}) async-start(f32[16,24,128]{2,1,0:T(8,128)} %get-tuple-element.28), calls=%async_computation.4 | async-start | bytes 393216 | tf_op jit(solution)/shard_map/all_to_all | solution.py:596
  240.2 6.4 %input_gradient.1 = bf16[128,1024]{1,0:T(8,128)(2,1)} custom-call(bf16[16,192,128]{2,1,0:T(8,128)(2,1)} %copy-done.2, bf16[1024,3072]{1,0:T(8,128)(2,1)} %weight_ref.3, bf16[128,1024]{1,0:T(8,128)(2,1)} %bitcast.30, f32[128,1024]{1,0:T(8,128)} %get-tuple-element.24.res_grad_ref), custom_call_target="tpu_custom_call" | custom-call | tf_op jit(solution)/shard_map/input_gradient/pallas_call | solution.py:380
  246.6 0.1 copy.12
  246.7 0.7 copy.13
  247.5 1.2 all-to-all-done.4.recv_ref
  248.6 0.7 copy-done.4
  249.3 1.7 finish.1
  (30 shorter events, 0.1 us)
Async XLA Ops:
  7.2 137.1 %all-gather.3.cloned.1.call-start = ((), (), s32[]{:S(2)}) async-start(), calls=%async_computation.5 | async-start | bytes 4456448 | tf_op jit(solution)/shard_map/all_gather | solution.py:582
  7.2 56.2 %copy-start.1 = (bf16[1,128,1024]{2,1,0:T(8,128)(2,1)S(1)}, bf16[1,128,1024]{2,1,0:T(8,128)(2,1)}, u32[]{:S(2)}) copy-start(bf16[1,128,1024]{2,1,0:T(8,128)(2,1)} %param.6) | copy-start | bytes 786436
  7.2 56.3 %copy-start.5 = (bf16[1,128,1024]{2,1,0:T(8,128)(2,1)S(1)}, bf16[1,128,1024]{2,1,0:T(8,128)(2,1)}, u32[]{:S(2)}) copy-start(bf16[1,128,1024]{2,1,0:T(8,128)(2,1)} %param.7) | copy-start | bytes 786436
  14.2 35.5 %all-to-all-start = ((bf16[16,192,128]{2,1,0:T(8,128)(2,1)}), bf16[16,192,128]{2,1,0:T(8,128)(2,1)S(1)}, u32[]{:S(2)}, u32[]{:S(2)}) async-start(bf16[16,192,128]{2,1,0:T(8,128)(2,1)} %get-tuple-element.18), calls=%async_computation | async-start | bytes 1572864 | tf_op jit(solution)/shard_map/all_to_all | solution.py:581
  23.7 175.9 %all-gather.5.cloned.1.call-start = ((), (), s32[]{:S(2)}) async-start(), calls=%async_computation.6 | async-start | bytes 4456448 | tf_op jit(solution)/shard_map/all_gather | solution.py:585
  49.7 0.9 copy-start
  63.5 26.5 %all-to-all-start.1 = ((bf16[16,96,128]{2,1,0:T(8,128)(2,1)}), bf16[16,96,128]{2,1,0:T(8,128)(2,1)S(1)}, u32[]{:S(2)}, u32[]{:S(2)}) async-start(bf16[16,96,128]{2,1,0:T(8,128)(2,1)} %get-tuple-element.19), calls=%async_computation.1 | async-start | bytes 786432 | tf_op jit(solution)/shard_map/all_to_all | solution.py:584
  70.5 18.7 %collective-permute-start.1 = (bf16[64,1024]{1,0:T(8,128)(2,1)S(1)}, bf16[64,1024]{1,0:T(8,128)(2,1)S(1)}, u32[]{:S(2)}, u32[]{:S(2)}) collective-permute-start(bf16[64,1024]{1,0:T(8,128)(2,1)S(1)} %pad_maximum_fusion.1), channel_id=1, source_target_pairs={{1,0},{2,1},{3,2},{4,3},{5,4},{6,5},{7,6},{8,7},{9,8},{10,9},{11,1... | collective-permute-start | bytes 393224 | tf_op jit(solution)/shard_map/ppermute | solution.py:576
  72.6 16.7 %collective-permute-start = (bf16[64,1024]{1,0:T(8,128)(2,1)S(1)}, bf16[64,1024]{1,0:T(8,128)(2,1)S(1)}, u32[]{:S(2)}, u32[]{:S(2)}) collective-permute-start(bf16[64,1024]{1,0:T(8,128)(2,1)S(1)} %pad_maximum_fusion), channel_id=1, source_target_pairs={{0,1},{1,2},{2,3},{3,4},{4,5},{5,6},{6,7},{7,8},{8,9},{9,10},{10,1... | collective-permute-start | bytes 393224 | tf_op jit(solution)/shard_map/ppermute | solution.py:575
  90.0 0.8 copy-start.3
  140.2 94.2 %all-to-all-start.3 = ((bf16[16,192,128]{2,1,0:T(8,128)(2,1)}), bf16[16,192,128]{2,1,0:T(8,128)(2,1)S(1)}, u32[]{:S(2)}, u32[]{:S(2)}) async-start(bf16[16,192,128]{2,1,0:T(8,128)(2,1)} %attend_back.1.grads_ref), calls=%async_computation.3 | async-start | bytes 1572864 | tf_op jit(solution)/shard_map/all_to_all | solution.py:589
  207.7 3.5 %collective-permute-start.2 = (bf16[544,128]{1,0:T(8,128)(2,1)S(1)}, bf16[544,128]{1,0:T(8,128)(2,1)S(1)}, u32[]{:S(2)}, u32[]{:S(2)}) collective-permute-start(bf16[544,128]{1,0:T(8,128)(2,1)S(1)} %get-tuple-element.43), channel_id=1, source_target_pairs={{0,16},{16,0},{32,48},{48,32},{64,80},{80,64},{96,112},{112,96},{1... | collective-permute-start | bytes 417800 | tf_op jit(solution)/shard_map/ppermute | solution.py:556
  207.8 7.6 %collective-permute-start.3 = (bf16[544,128]{1,0:T(8,128)(2,1)S(1)}, bf16[544,128]{1,0:T(8,128)(2,1)S(1)}, u32[]{:S(2)}, u32[]{:S(2)}) collective-permute-start(bf16[544,128]{1,0:T(8,128)(2,1)S(1)} %get-tuple-element.42), channel_id=1, source_target_pairs={{0,32},{16,48},{32,0},{48,16},{64,96},{80,112},{96,64},{112,80},{1... | collective-permute-start | bytes 417800 | tf_op jit(solution)/shard_map/ppermute | solution.py:556
  211.2 7.1 %collective-permute-start.4 = (bf16[544,128]{1,0:T(8,128)(2,1)S(1)}, bf16[544,128]{1,0:T(8,128)(2,1)S(1)}, u32[]{:S(2)}, u32[]{:S(2)}) collective-permute-start(bf16[544,128]{1,0:T(8,128)(2,1)S(1)} %get-tuple-element.41), channel_id=1, source_target_pairs={{0,48},{16,32},{32,16},{48,0},{64,112},{80,96},{96,80},{112,64},{1... | collective-permute-start | bytes 417800 | tf_op jit(solution)/shard_map/ppermute | solution.py:556
  211.2 7.1 %copy-start.6 = (bf16[544,128]{1,0:T(8,128)(2,1)}, bf16[544,128]{1,0:T(8,128)(2,1)S(1)}, u32[]{:S(2)}) copy-start(bf16[544,128]{1,0:T(8,128)(2,1)S(1)} %collective-permute-done.2.one) | copy-start | bytes 417796
  215.4 2.9 %copy-start.7 = (bf16[544,128]{1,0:T(8,128)(2,1)}, bf16[544,128]{1,0:T(8,128)(2,1)S(1)}, u32[]{:S(2)}) copy-start(bf16[544,128]{1,0:T(8,128)(2,1)S(1)} %collective-permute-done.3.two) | copy-start | bytes 417796
  218.3 0.7 copy-start.8
  221.8 4.9 %collective-permute-start.5 = (bf16[160,128]{1,0:T(8,128)(2,1)S(1)}, bf16[160,128]{1,0:T(8,128)(2,1)S(1)}, u32[]{:S(2)}, u32[]{:S(2)}) collective-permute-start(bf16[160,128]{1,0:T(8,128)(2,1)S(1)} %get-tuple-element.50), channel_id=1, source_target_pairs={{0,64},{16,80},{32,96},{48,112},{64,0},{80,16},{96,32},{112,48},{1... | collective-permute-start | bytes 122888 | tf_op jit(solution)/shard_map/ppermute | solution.py:556
  223.7 5.5 %collective-permute-start.6 = (bf16[160,128]{1,0:T(8,128)(2,1)S(1)}, bf16[160,128]{1,0:T(8,128)(2,1)S(1)}, u32[]{:S(2)}, u32[]{:S(2)}) collective-permute-start(bf16[160,128]{1,0:T(8,128)(2,1)S(1)} %get-tuple-element.49), channel_id=1, source_target_pairs={{0,128},{16,144},{32,160},{48,176},{64,192},{80,208},{96,224},{112... | collective-permute-start | bytes 122888 | tf_op jit(solution)/shard_map/ppermute | solution.py:556
  226.7 5.2 %collective-permute-start.7 = (bf16[160,128]{1,0:T(8,128)(2,1)S(1)}, bf16[160,128]{1,0:T(8,128)(2,1)S(1)}, u32[]{:S(2)}, u32[]{:S(2)}) collective-permute-start(bf16[160,128]{1,0:T(8,128)(2,1)S(1)} %get-tuple-element.48), channel_id=1, source_target_pairs={{0,192},{16,208},{32,224},{48,240},{64,128},{80,144},{96,160},{112... | collective-permute-start | bytes 122888 | tf_op jit(solution)/shard_map/ppermute | solution.py:556
  226.7 5.2 %copy-start.10 = (bf16[160,128]{1,0:T(8,128)(2,1)}, bf16[160,128]{1,0:T(8,128)(2,1)S(1)}, u32[]{:S(2)}) copy-start(bf16[160,128]{1,0:T(8,128)(2,1)S(1)} %collective-permute-done.5.refs_2_) | copy-start | bytes 122884
  229.2 2.7 %copy-start.11 = (bf16[160,128]{1,0:T(8,128)(2,1)}, bf16[160,128]{1,0:T(8,128)(2,1)S(1)}, u32[]{:S(2)}) copy-start(bf16[160,128]{1,0:T(8,128)(2,1)S(1)} %collective-permute-done.6.refs_3_) | copy-start | bytes 122884
  231.9 0.6 copy-start.12
  234.4 5.8 %copy-start.2 = (bf16[16,192,128]{2,1,0:T(8,128)(2,1)}, bf16[16,192,128]{2,1,0:T(8,128)(2,1)S(1)}, u32[]{:S(2)}) copy-start(bf16[16,192,128]{2,1,0:T(8,128)(2,1)S(1)} %all-to-all-done.3.joined_ref) | copy-start | bytes 2359300
  234.4 12.2 %copy-start.9 = (f32[64,192]{1,0:T(8,128)S(1)}, f32[64,192]{1,0:T(8,128)}, u32[]{:S(2)}) copy-start(f32[64,192]{1,0:T(8,128)} %get-tuple-element.27) | copy-start | bytes 147460
  234.4 14.2 %all-to-all-start.4 = ((f32[16,24,128]{2,1,0:T(8,128)}), f32[16,24,128]{2,1,0:T(8,128)S(1)}, u32[]{:S(2)}, u32[]{:S(2)}) async-start(f32[16,24,128]{2,1,0:T(8,128)} %get-tuple-element.28), calls=%async_computation.4 | async-start | bytes 393216 | tf_op jit(solution)/shard_map/all_to_all | solution.py:596
  248.6 0.7 copy-start.4
Sparse Core Ops, SparseCore 0:
  14.3 93.9 all-gather.2
  110.1 89.4 all-gather.4

commit v2 on v1

--- a/solution.py
+++ b/solution.py
@@ -38,6 +38,10 @@
 
 def params(**kw):
     return pltpu.CompilerParams(vmem_limit_bytes=LIMIT, **kw)
+
+
+def cost(flops, moved, expos=0):
+    return pl.CostEstimate(flops=flops, bytes_accessed=moved, transcendentals=expos)
 
 
 def whole(shape):
@@ -103,7 +107,7 @@
 
 
 def attend_kernel(
-    scalars, heads_ref, send_ref, own_ref, out_ref, lse_ref, query, keys, value, scores
+    scalars, heads_ref, send_ref, out_ref, lse_ref, query, keys, value, scores
 ):
     count, _, rows = heads_ref.shape
     total = count * rows
@@ -128,16 +132,14 @@
             total_row = total_row + jnp.sum(expo.reshape(KB // 8, 8, QB), axis=0)
             acc = acc + dot(value[:, k * KB : (k + 1) * KB], expo.astype(BF16))
         total_row = jnp.sum(total_row, axis=0, keepdims=True)
-        result = acc / total_row
-        out_ref[:, cols] = result
-        own_ref[:, cols] = result.astype(BF16)
+        out_ref[:, cols] = acc / total_row
         lse_ref[:, cols] = peak + jnp.log(total_row)
         return carry
 
     lax.fori_loop(0, total // QB, one_block, 0)
     none = jnp.zeros((HD, HALO), F32)
     for i in range(count):
-        send_ref[i, 0:HD, :] = own_ref[:, i * rows : (i + 1) * rows]
+        send_ref[i, 0:HD, :] = out_ref[:, i * rows : (i + 1) * rows].astype(BF16)
         low = out_ref[:, i * rows - HALO : i * rows] if i else none
         high = out_ref[:, (i + 1) * rows : (i + 1) * rows + HALO] if i < count - 1 else none
         sides = jnp.concatenate([low, high], axis=1)
@@ -153,7 +155,6 @@
         in_specs=[SMEM, pl.BlockSpec(memory_space=pltpu.VMEM)],
         out_shape=[
             jax.ShapeDtypeStruct((count, HD + HD // 2, rows), BF16),
-            jax.ShapeDtypeStruct((HD, total), BF16),
             jax.ShapeDtypeStruct((HD, total), F32),
             jax.ShapeDtypeStruct((1, total), F32),
         ],
@@ -164,6 +165,7 @@
             pltpu.VMEM((total, QB), F32),
         ],
         compiler_params=params(),
+        cost_estimate=cost(2 * 2 * total * total * 256, heads.size * 2, total * total),
         name="attend",
     )(scalars, heads)
 
@@ -179,6 +181,7 @@
     w_conv_ref,
     output_ref,
     res_grad_ref,
+    round_ref,
     send_ref,
     taps_ref,
     conv_in,
@@ -252,11 +255,11 @@
     res_grad = grads_ref[...].astype(F32) + normalize_back(unit, scale, conv_grad[...] * keep)
     res_grad_ref[...] = res_grad
     rounded = res_grad.astype(BF16)
-    columns = rounded.T
-    send_ref[:, 0:HD, :] = dot(w_out_ref[...], columns).astype(BF16).reshape(heads, HD, rows)
-    send_ref[:, HD : 2 * HD, :] = columns.reshape(heads, HD, rows)
+    round_ref[...] = rounded
+    back = dot(w_out_ref[...], rounded, 1, 1).astype(BF16)
+    send_ref[:, 0:HD, :] = back.reshape(heads, HD, rows)
     for h in range(heads):
-        send_ref[h, 2 * HD :, :] = halves(taps_ref[:, h * HD : (h + 1) * HD])
+        send_ref[h, HD:, :] = halves(taps_ref[:, h * HD : (h + 1) * HD])
 
 
 def middle(scalars, att, frames, frames_side, grads, grads_side, w_out, w_conv):
@@ -268,7 +271,8 @@
         out_shape=[
             jax.ShapeDtypeStruct((rows, width), BF16),
             jax.ShapeDtypeStruct((rows, width), F32),
-            jax.ShapeDtypeStruct((HEADS, 2 * HD + KW + 1, rows), BF16),
+            jax.ShapeDtypeStruct((rows, width), BF16),
+            jax.ShapeDtypeStruct((HEADS, HD + KW + 1, rows), BF16),
         ],
         scratch_shapes=[
             pltpu.VMEM((KW + 1, width), F32),
@@ -348,6 +352,7 @@
             pltpu.VMEM((KB, total), BF16),
         ],
         compiler_params=params(),
+        cost_estimate=cost(5 * 2 * total * total * 256, heads.size * 4, total * total),
         name="attend_back",
     )(scalars, heads, grads, out, lse)
 
@@ -397,147 +402,181 @@
     )(joined, w_qkv, frames, res_grad)
 
 
-def parts_kernel(grads_ref, back_ref, normed_ref, att_ref, send_ref, columns, back_rows):
+CUT = 96
+FAST = 4
+SLOW = 4
+TAPS = SLOW * CUT
+OUT = 8 * HD
+
+
+def out_part_kernel(scalars, att_ref, round_ref, *send_refs):
+    lanes = send_refs[0].shape[2]
+    for k, send_ref in enumerate(send_refs):
+        part = dot(att_ref[scalars[3] ^ k, 0:HD, :], round_ref[...])
+        for c in range(part.shape[1] // lanes):
+            piece = part[:, c * lanes : (c + 1) * lanes]
+            send_ref[0, c * HD : (c + 1) * HD, :] = piece.astype(BF16)
+
+
+def out_part(scalars, att, rounded):
+    heads, wide, rows = att.shape
+    return pl.pallas_call(
+        out_part_kernel,
+        grid=(SLOW,),
+        in_specs=[
+            SMEM,
+            pl.BlockSpec((FAST, wide, rows), lambda j: (j, 0, 0)),
+            whole(rounded.shape),
+        ],
+        out_specs=[pl.BlockSpec((1, OUT, 128), lambda j: (j, 0, 0))] * FAST,
+        out_shape=[jax.ShapeDtypeStruct((SLOW, OUT, 128), BF16)] * FAST,
+        compiler_params=params(),
+        cost_estimate=cost(2 * heads * HD * 256 * rounded.shape[1], heads * HD * rounded.shape[1] * 2),
+        name="out_part",
+    )(scalars, att, rounded)
+
+
+def parts_kernel(scalars, grads_ref, back_ref, normed_ref, *rest):
+    send_refs, columns, pieces = rest[:FAST], rest[FAST], rest[FAST + 1]
     count, wide, rows = grads_ref.shape
     slow = pl.program_id(0)
-    fast = send_ref.shape[0]
 
     @pl.when(slow == 0)
     def _():
         taps = jnp.zeros((KW + 1, rows), F32)
         for i in range(count):
             columns[:, i * rows : (i + 1) * rows] = grads_ref[i]
-            back_rows[i * rows : (i + 1) * rows, :] = back_ref[i, HD : 2 * HD, :].T
-            taps = taps + back_ref[i, 2 * HD :, :].astype(F32)
+            taps = taps + back_ref[i, HD:, :].astype(F32)
         pair = halves(joined_halves(taps))
-        for i in range(fast):
-            send_ref[i, TAPS:, :] = pair
+        for send_ref in send_refs:
+            send_ref[TAPS:, :] = pair
 
     part = dot(columns[...], normed_ref[...])
-    outer = dot(att_ref[...], back_rows[...])
-    each = part.shape[1] // fast
-    for i in range(fast):
+    each = part.shape[1] // FAST
+    for i in range(FAST):
         piece = part[:, i * each : (i + 1) * each]
-        first = pl.multiple_of(slow * CUT, CUT)
-        send_ref[i, pl.ds(first, wide // 2), :] = jnp.concatenate(
-            [piece[0 : wide // 2], piece[wide // 2 :]], axis=1
-        ).astype(BF16)
-        piece = outer[i * each : (i + 1) * each, :]
-        send_ref[i, pl.ds(first + wide // 2, each // 2), :] = jnp.concatenate(
-            [piece[0 : each // 2], piece[each // 2 :]], axis=1
-        ).astype(BF16)
-
-
-CUT = 128
-FAST = 4
-SLOW = 4
-TAPS = SLOW * CUT
-
-
-def gradient_parts(grads, back, normed_all, att_all):
+        pieces[i] = jnp.concatenate([piece[0:CUT], piece[CUT:]], axis=1).astype(BF16)
+    for k, send_ref in enumerate(send_refs):
+        send_ref[pl.ds(pl.multiple_of(slow * CUT, CUT), CUT), :] = pieces[scalars[3] ^ k]
+
+
+def gradient_parts(scalars, grads, back, normed_all):
     count, wide, rows = grads.shape
     total, width = normed_all.shape
     return pl.pallas_call(
         parts_kernel,
         grid=(SLOW,),
         in_specs=[
+            SMEM,
             whole(grads.shape),
             whole(back.shape),
             pl.BlockSpec((total, width // SLOW), lambda j: (0, j)),
-            pl.BlockSpec((width // SLOW, total), lambda j: (j, 0)),
-        ],
-        out_specs=whole((FAST, TAPS + KW + 1, 128)),
-        out_shape=jax.ShapeDtypeStruct((FAST, TAPS + KW + 1, 128), BF16),
-        scratch_shapes=[pltpu.VMEM((wide, total), BF16), pltpu.VMEM((total, HD), BF16)],
-        compiler_params=params(),
+        ],
+        out_specs=[whole((TAPS + KW + 1, 128))] * FAST,
+        out_shape=[jax.ShapeDtypeStruct((TAPS + KW + 1, 128), BF16)] * FAST,
+        scratch_shapes=[pltpu.VMEM((wide, total), BF16), pltpu.VMEM((FAST, CUT, 128), BF16)],
+        compiler_params=params(),
+        cost_estimate=cost(2 * 256 * total * width, total * width * 2),
         name="gradient_parts",
-    )(grads, back, normed_all, att_all)
-
-
-def fold_fast_kernel(scalars, own_ref, one, two, three, out_ref):
-    own = own_ref[scalars[3]]
+    )(scalars, grads, back, normed_all)
+
+
+def sum_four(own, one, two, three):
+    return (own.astype(F32) + one.astype(F32)) + (two.astype(F32) + three.astype(F32))
+
+
+def fold_out_kernel(scalars, one, two, three, four, *send_refs):
+    for k, send_ref in enumerate(send_refs):
+        i = scalars[4] ^ k
+        send_ref[...] = sum_four(one[i], two[i], three[i], four[i]).astype(BF16)
+
+
+def fold_out(scalars, blocks):
+    vmem = pl.BlockSpec(memory_space=pltpu.VMEM)
+    return pl.pallas_call(
+        fold_out_kernel,
+        in_specs=[SMEM] + [vmem] * 4,
+        out_shape=[jax.ShapeDtypeStruct((OUT, 128), BF16)] * SLOW,
+        compiler_params=params(),
+        cost_estimate=cost(0, 5 * SLOW * OUT * 128 * 2),
+        name="fold_out",
+    )(scalars, *blocks)
+
+
+def fold_fast_kernel(scalars, one, two, three, four, *rest):
+    send_refs, pieces = rest[:SLOW], rest[SLOW]
+    total = sum_four(one[...], two[...], three[...], four[...])
+    pair = halves(joined_halves(total[TAPS:]))
     for i in range(SLOW):
-        cut = slice(i * CUT, (i + 1) * CUT)
-        total = own[cut].astype(F32) + one[cut, :].astype(F32)
-        total = total + (two[cut, :].astype(F32) + three[cut, :].astype(F32))
-        out_ref[i, 0:CUT, :] = total.astype(BF16)
-    cut = slice(TAPS, TAPS + KW + 1)
-    total = own[cut].astype(F32) + one[cut, :].astype(F32)
-    total = total + (two[cut, :].astype(F32) + three[cut, :].astype(F32))
-    pair = halves(joined_halves(total))
-    for i in range(SLOW):
-        out_ref[i, CUT:, :] = pair
-
-
-def fold_fast(scalars, own, others):
+        pieces[i] = total[i * CUT : (i + 1) * CUT].astype(BF16)
+    for k, send_ref in enumerate(send_refs):
+        send_ref[0:CUT, :] = pieces[scalars[4] ^ k]
+        send_ref[CUT:, :] = pair
+
+
+def fold_fast(scalars, blocks):
     vmem = pl.BlockSpec(memory_space=pltpu.VMEM)
     return pl.pallas_call(
         fold_fast_kernel,
         in_specs=[SMEM] + [vmem] * 4,
-        out_shape=jax.ShapeDtypeStruct((SLOW, CUT + KW + 1, 128), BF16),
+        out_shape=[jax.ShapeDtypeStruct((CUT + KW + 1, 128), BF16)] * SLOW,
+        scratch_shapes=[pltpu.VMEM((SLOW, CUT, 128), BF16)],
         compiler_params=params(),
         name="fold_fast",
-    )(scalars, own, *others)
-
-
-def fold_slow_kernel(scalars, own_ref, one, two, three, qkv_ref, send_ref, *, scale):
-    total = own_ref[scalars[4]].astype(F32) + one[...].astype(F32)
-    total = (total + (two[...].astype(F32) + three[...].astype(F32))) * scale
-    wide = 3 * HD // 2
-    whole_rows = total[0:wide].T
-    qkv_ref[:, 0:wide] = whole_rows[0:HD]
-    qkv_ref[:, wide:] = whole_rows[HD:]
-    outer = total[wide:CUT]
-    rows = jnp.concatenate([outer[:, 0:HD], outer[:, HD:]], axis=0)
-    taps = joined_halves(total[CUT:])
-    half = (KW + 1) // 2
-    pair = jnp.concatenate([taps[0:half], taps[half:]], axis=1)
+    )(scalars, *blocks)
+
+
+def fold_slow_kernel(*refs, scale):
+    qkv_ref, send_ref = refs[8:]
+    total = sum_four(*(ref[...] for ref in refs[0:4]))
+    model_rows = (total[0:CUT] * scale).T
+    qkv_ref[:, 0:CUT] = model_rows[0:HD]
+    qkv_ref[:, CUT:] = model_rows[HD:]
+    pair = halves(joined_halves(total[CUT:]))
+    outer = sum_four(*(ref[...] for ref in refs[4:8]))
     count = send_ref.shape[0]
     each = HD // count
     for i in range(count):
-        piece = rows[i * each : (i + 1) * each]
-        send_ref[i, 0:half, :] = pair
-        send_ref[i, half : half + each, 0:HD] = piece
-        send_ref[i, half : half + each, HD:] = piece
-        send_ref[i, half + each :, :] = jnp.zeros((8 - each, 128), F32)
-
-
-def fold_slow(scalars, own, others, seq_count, scale):
+        pieces = [outer[c * HD + i * each : c * HD + (i + 1) * each] for c in range(OUT // HD)]
+        send_ref[i, 0 : OUT // count, :] = jnp.concatenate(pieces, axis=0).astype(BF16)
+        send_ref[i, OUT // count :, :] = pair
+
+
+def fold_slow(blocks, out_blocks, seq_count, scale):
     vmem = pl.BlockSpec(memory_space=pltpu.VMEM)
     return pl.pallas_call(
         lambda *refs: fold_slow_kernel(*refs, scale=scale),
-        in_specs=[SMEM] + [vmem] * 4,
+        in_specs=[vmem] * 8,
         out_shape=[
             jax.ShapeDtypeStruct((HD, 3 * HD), F32),
-            jax.ShapeDtypeStruct((seq_count, 24, 128), F32),
+            jax.ShapeDtypeStruct((seq_count, OUT // seq_count + KW + 1, 128), BF16),
         ],
         compiler_params=params(),
         name="fold_slow",
-    )(scalars, own, *others)
-
-
-def finish_kernel(recv_ref, out_ref, taps_ref):
+    )(*blocks, *out_blocks)
+
+
+def finish_kernel(recv_ref, out_ref, taps_ref, *, scale):
     count = recv_ref.shape[0]
     each = out_ref.shape[0]
-    half = (KW + 1) // 2
+    wide = OUT // count
+    total = recv_ref[0, 0:wide, :].astype(F32)
+    for i in range(1, count):
+        total = total + recv_ref[i, 0:wide, :].astype(F32)
+    total = total * scale
+    for c in range(OUT // HD):
+        out_ref[:, c * 128 : (c + 1) * 128] = total[c * each : (c + 1) * each]
     for i in range(count // 2):
-        a = recv_ref[2 * i]
-        b = recv_ref[2 * i + 1]
-        lanes = slice(i * 2 * HD, (i + 1) * 2 * HD)
-        out_ref[:, lanes] = jnp.concatenate(
-            [a[half : half + each, 0:HD], b[half : half + each, HD:]], axis=1
-        )
-        taps_ref[0:half, lanes] = jnp.concatenate([a[0:half, 0:HD], b[0:half, 0:HD]], axis=1)
-        taps_ref[half:KW, lanes] = jnp.concatenate(
-            [a[0 : half - 1, HD:], b[0 : half - 1, HD:]], axis=1
-        )
-
-
-def finish(recv, width):
+        both = [joined_halves(recv_ref[2 * i + k, wide:, :].astype(F32)) for k in range(2)]
+        both = jnp.concatenate(both, axis=1) * scale
+        taps_ref[:, i * 2 * HD : (i + 1) * 2 * HD] = both[0:KW]
+
+
+def finish(recv, width, scale):
     count = recv.shape[0]
     vmem = pl.BlockSpec(memory_space=pltpu.VMEM)
     return pl.pallas_call(
-        finish_kernel,
+        lambda *refs: finish_kernel(*refs, scale=scale),
         in_specs=[vmem],
         out_shape=[
             jax.ShapeDtypeStruct((HD // count, width), F32),
@@ -548,13 +587,10 @@
     )(recv)
 
 
-def exchange(blocks, index, partner):
-    pairs = lambda k: [(d, partner(d, k)) for d in range(FAST * SLOW)]
-    received = []
-    for k in range(1, 4):
-        block = lax.dynamic_index_in_dim(blocks, index ^ k, 0, keepdims=False)
-        received.append(lax.ppermute(block, "dp", pairs(k)))
-    return received
+def exchange(blocks, step):
+    pairs = lambda k: [(d, d ^ (step * k)) for d in range(FAST * SLOW)]
+    moved = [lax.ppermute(block, "dp", pairs(k)) for k, block in enumerate(blocks) if k]
+    return [blocks[0]] + moved
 
 
 def local(frames, cotangent, w_qkv, w_out, w_conv, lengths):
@@ -580,20 +616,22 @@
     normed, send = project(x, w_qkv)
     heads = lax.all_to_all(send, "seq", 0, 0, tiled=True)
     normed_all = lax.all_gather(normed, "seq", axis=0, tiled=True)
-    send, own, out, lse = attend(scalars, heads)
+    send, out, lse = attend(scalars, heads)
     att = lax.all_to_all(send, "seq", 0, 0, tiled=True)
-    att_all = lax.all_gather(own, "seq", axis=0, tiled=True)
-    output, res_grad, send = middle(scalars, att, x, x_side, g, g_side, w_out, w_conv)
+    output, res_grad, rounded, send = middle(scalars, att, x, x_side, g, g_side, w_out, w_conv)
     back = lax.all_to_all(send, "seq", 0, 0, tiled=True)
+    outer = out_part(scalars, att, rounded)
+    back, outer = lax.optimization_barrier((back, outer))
+    outer = exchange(outer, 1)
     send = attend_back(scalars, heads, back, out, lse)
     joined = lax.all_to_all(send, "seq", 0, 0, tiled=True)
-    parts = gradient_parts(send, back, normed_all, att_all)
-    others = exchange(parts, fast, lambda d, k: d ^ k)
-    parts = fold_fast(scalars, parts, others)
-    others = exchange(parts, slow, lambda d, k: d ^ (FAST * k))
-    qkv, send = fold_slow(scalars, parts, others, seq_count, grad_scale)
+    parts = exchange(gradient_parts(scalars, send, back, normed_all), 1)
+    outer = exchange(fold_out(scalars, outer), FAST)
+    parts = exchange(fold_fast(scalars, parts), FAST)
+    qkv, send = fold_slow(parts, outer, seq_count, grad_scale)
     input_grad = input_gradient(joined, w_qkv, x, res_grad)
-    out_total, taps_total = finish(lax.all_to_all(send, "seq", 0, 0, tiled=True), width)
+    recv = lax.all_to_all(send, "seq", 0, 0, tiled=True)
+    out_total, taps_total = finish(recv, width, grad_scale)
     return (
         output[None],
         input_grad[None],

time: 259 us -> 227 us (0.88)
  waiting for transfers between devices: 106 us -> 79.4 us
  blocking collectives: 25.6 us -> 0 us
  starting transfers between devices: 40.7 us -> 56.6 us
  Pallas kernels: 62.6 us -> 67.3 us
    all_gather x1 -> x0, waiting for transfers between devices: 55.3 us -> none  [local(): att_all = lax.all_gather(own, 'seq', axis=0, tiled=True)]
    all_to_all x1 -> x0, blocking collectives: 25.6 us -> none  [local(): back = lax.all_to_all(send, 'seq', 0, 0, tiled=True)]
    ppermute x6 -> x12, waiting for transfers between devices: 12.3 us -> 31.4 us  [exchange(): lax.ppermute(block, 'dp', pairs(k))]
    ppermute x1, waiting for transfers between devices: 0.01 us -> 12.6 us  [local(): lax.ppermute(jnp.concatenate([x[-HALO:], g[-HALO:]], axis=0), 'seq', forw...]
    ppermute x1, waiting for transfers between devices: 12.8 us -> 0.28 us  [local(): lax.ppermute(jnp.concatenate([x[:HALO], g[:HALO]], axis=0), 'seq', backward)]
    all_to_all x1 -> x2, waiting for transfers between devices: 1.15 us -> 10.4 us  [the longest x1 7.62 us: local(): back = lax.all_to_all(send, 'seq', 0, 0, tiled=True)]
    all_to_all x1 -> x2, starting transfers between devices: 5.79 us -> 14 us  [the longest x1 7.08 us: local(): recv = lax.all_to_all(send, 'seq', 0, 0, tiled=True)]
    ppermute x6 -> x12, starting transfers between devices: 8.39 us -> 15.5 us  [exchange(): lax.ppermute(block, 'dp', pairs(k))]
  transfers between devices with their start and end apart: 14 -> 20, of which waited for: 8 -> 10; matrix products, arithmetic and copies ran while one was open for 2% -> 1% of each run, Pallas kernels for 21% -> 26%
where the time goes in v2:
time: 227 us; the launch traced here: 226 us
  waiting for transfers between devices  79.4 us (35%)
  Pallas kernels  67.3 us (30%)
  starting transfers between devices  56.6 us (25%)
  between operations  14.9 us (7%)
  local copies, waits for them, and re-layouts  6.75 us (3%)
    ppermute x12, waiting for transfers between devices, exchange(): lax.ppermute(block, 'dp', pairs(k))  31.4 us
    all_to_all x1, waiting for transfers between devices, local(): heads = lax.all_to_all(send, 'seq', 0, 0, tiled=True)  24.7 us
    ppermute x12, starting transfers between devices, exchange(): lax.ppermute(block, 'dp', pairs(k))  15.5 us
    pallas_call x1, Pallas kernels, attend_back(): pl.pallas_call(attend_back_kernel, in_specs=[SMEM] + [vmem] * 4, out_shap...  14.8 us
    pallas_call x1, Pallas kernels, attend(): pl.pallas_call(attend_kernel, in_specs=[SMEM, pl.BlockSpec(memory_space=p...  12.8 us
    ppermute x1, waiting for transfers between devices, local(): lax.ppermute(jnp.concatenate([x[-HALO:], g[-HALO:]], axis=0), 'seq', forw...  12.6 us
    all_to_all x1, starting transfers between devices, local(): heads = lax.all_to_all(send, 'seq', 0, 0, tiled=True)  9.52 us
    pallas_call x1, Pallas kernels, middle(): pl.pallas_call(middle_kernel, in_specs=[SMEM] + [vmem] * 7, out_shape=[ja...  8.85 us
  transfers between devices with their start and end apart: 20, of which 10 were waited for; matrix products, arithmetic and copies ran while one was open for 1% of the time, Pallas kernels for 26%

profile of v2, /device:TPU:32, one launch (start us, length us, event | category | flops | bytes accessed | tf_op | source)
XLA Modules:
  0.0 225.7 jit_solution(14551192756293293510)
XLA Ops:
  7.2 7.0 %project.1 = (bf16[128,1024]{1,0:T(8,128)(2,1)}, bf16[16,192,128]{2,1,0:T(8,128)(2,1)}) custom-call(bf16[128,1024]{1,0:T(8,128)(2,1)} %bitcast.16, bf16[1024,3072]{1,0:T(8,128)(2,1)} %weight_ref.3), custom_call_target="tpu_custom_call" | custom-call | tf_op jit(solution)/shard_map/project/pallas_call | solution.py:79
  14.2 9.5 %all-to-all-start = ((bf16[16,192,128]{2,1,0:T(8,128)(2,1)}), bf16[16,192,128]{2,1,0:T(8,128)(2,1)S(1)}, u32[]{:S(2)}, u32[]{:S(2)}) async-start(bf16[16,192,128]{2,1,0:T(8,128)(2,1)} %get-tuple-element.39), calls=%async_computation | async-start | bytes 1572864 | tf_op jit(solution)/shard_map/all_to_all | solution.py:617
  24.4 0.6 stack.15.scalars
  25.1 24.7 %all-to-all-done.heads_ref = bf16[16,192,128]{2,1,0:T(8,128)(2,1)S(1)} async-done(((bf16[16,192,128]{2,1,0:T(8,128)(2,1)}), bf16[16,192,128]{2,1,0:T(8,128)(2,1)S(1)}, u32[]{:S(2)}, u32[]{:S(2)}) %all-to-all-start) | async-done | bytes 786464 | tf_op jit(solution)/shard_map/all_to_all | solution.py:617
  49.7 0.9 copy-done.5
  50.6 12.8 %attend.1 = (bf16[16,96,128]{2,1,0:T(8,128)(2,1)}, f32[64,2048]{1,0:T(8,128)}, f32[1,2048]{1,0:T(1,128)}) custom-call(s32[5]{0:T(128)} %stack.15.scalars, bf16[16,192,128]{2,1,0:T(8,128)(2,1)} %copy-done.5), custom_call_target="tpu_custom_call" | custom-call | flops 4294967296 | bytes 786432 | tf_op jit(solution)/shard_map/attend/pallas_call | solution.py:153
  63.4 7.0 %all-to-all-start.1 = ((bf16[16,96,128]{2,1,0:T(8,128)(2,1)}), bf16[16,96,128]{2,1,0:T(8,128)(2,1)S(1)}, u32[]{:S(2)}, u32[]{:S(2)}) async-start(bf16[16,96,128]{2,1,0:T(8,128)(2,1)} %get-tuple-element.40), calls=%async_computation.1 | async-start | bytes 786432 | tf_op jit(solution)/shard_map/all_to_all | solution.py:620
  70.4 3.4 %collective-permute-start = (bf16[64,1024]{1,0:T(8,128)(2,1)S(1)}, bf16[64,1024]{1,0:T(8,128)(2,1)S(1)}, u32[]{:S(2)}, u32[]{:S(2)}) collective-permute-start(bf16[64,1024]{1,0:T(8,128)(2,1)S(1)} %pad_maximum_fusion), channel_id=1, source_target_pairs={{0,1},{1,2},{2,3},{3,4},{4,5},{5,6},{6,7},{7,8},{8,9},{9,10},{10,1... | collective-permute-start | bytes 393224 | tf_op jit(solution)/shard_map/ppermute | solution.py:611
  73.8 2.5 %collective-permute-start.1 = (bf16[64,1024]{1,0:T(8,128)(2,1)S(1)}, bf16[64,1024]{1,0:T(8,128)(2,1)S(1)}, u32[]{:S(2)}, u32[]{:S(2)}) collective-permute-start(bf16[64,1024]{1,0:T(8,128)(2,1)S(1)} %pad_maximum_fusion.1), channel_id=1, source_target_pairs={{1,0},{2,1},{3,2},{4,3},{5,4},{6,5},{7,6},{8,7},{9,8},{10,9},{11,1... | collective-permute-start | bytes 393224 | tf_op jit(solution)/shard_map/ppermute | solution.py:612
  76.3 12.6 %collective-permute-done = bf16[64,1024]{1,0:T(8,128)(2,1)S(1)} collective-permute-done((bf16[64,1024]{1,0:T(8,128)(2,1)S(1)}, bf16[64,1024]{1,0:T(8,128)(2,1)S(1)}, u32[]{:S(2)}, u32[]{:S(2)}) %collective-permute-start) | collective-permute-done | bytes 131104 | tf_op jit(solution)/shard_map/ppermute | solution.py:611
  89.0 0.3 collective-permute-done.1
  89.3 0.7 pad_maximum_fusion.2
  90.0 0.7 copy-done.2
  90.7 8.9 %middle.1 = (bf16[128,1024]{1,0:T(8,128)(2,1)}, f32[128,1024]{1,0:T(8,128)}, bf16[128,1024]{1,0:T(8,128)(2,1)}, bf16[16,96,128]{2,1,0:T(8,128)(2,1)}) custom-call(s32[5]{0:T(128)} %stack.15.scalars, bf16[16,96,128]{2,1,0:T(8,128)(2,1)} %copy-done.2, bf16[128,1024]{1,0:T(8,128)(2,1)} %bitcast.17, bf16[64,1024]{1,0:T(8,128)(2,1)} %get-tuple-element.91.frames_side, ...), custom_call_target="tpu_custom_call" | custom-call | tf_op jit(solution)/shard_map/middle/pallas_call | solution.py:268
  99.6 6.9 %all-to-all-start.2 = ((bf16[16,96,128]{2,1,0:T(8,128)(2,1)}), bf16[16,96,128]{2,1,0:T(8,128)(2,1)S(1)}, u32[]{:S(2)}, u32[]{:S(2)}) async-start(bf16[16,96,128]{2,1,0:T(8,128)(2,1)} %get-tuple-element.42), calls=%async_computation.2 | async-start | bytes 786432 | tf_op jit(solution)/shard_map/all_to_all | solution.py:622
  106.5 3.9 %out_part.1 = (bf16[4,512,128]{2,1,0:T(8,128)(2,1)}, bf16[4,512,128]{2,1,0:T(8,128)(2,1)}, bf16[4,512,128]{2,1,0:T(8,128)(2,1)}, bf16[4,512,128]{2,1,0:T(8,128)(2,1)}) custom-call(s32[5]{0:T(128)} %stack.15.scalars, bf16[16,96,128]{2,1,0:T(8,128)(2,1)} %copy-done.2, bf16[128,1024]{1,0:T(8,128)(2,1)} %get-tuple-element.43.round_ref), custom_call_target="tpu_custom_call" | custom-call | flops 536870912 | bytes 2097152 | tf_op jit(solution)/shard_map/out_part/pallas_call | solution.py:423
  110.4 7.6 %all-to-all-done.2.grads_ref.back_ref = bf16[16,96,128]{2,1,0:T(8,128)(2,1)S(1)} async-done(((bf16[16,96,128]{2,1,0:T(8,128)(2,1)}), bf16[16,96,128]{2,1,0:T(8,128)(2,1)S(1)}, u32[]{:S(2)}, u32[]{:S(2)}) %all-to-all-start.2) | async-done | bytes 393248 | tf_op jit(solution)/shard_map/all_to_all | solution.py:622
  118.1 0.8 copy-done.3
  118.8 14.8 %attend_back.1.grads_ref = bf16[16,192,128]{2,1,0:T(8,128)(2,1)} custom-call(s32[5]{0:T(128)} %stack.15.scalars, bf16[16,192,128]{2,1,0:T(8,128)(2,1)} %copy-done.5, bf16[16,96,128]{2,1,0:T(8,128)(2,1)} %copy-done.3, f32[64,2048]{1,0:T(8,128)} %get-tuple-element.49.out_ref, f32[1,2048]{1,0:T(1,128)} %get-tuple-element.50.lse_ref), custom_call_target="tpu_custom_call" | custom-call | flops 10737418240 | bytes 1572864 | tf_op jit(solution)/shard_map/attend_back/pallas_call | solution.py:339
  133.6 4.8 %all-to-all-start.3 = ((bf16[16,192,128]{2,1,0:T(8,128)(2,1)}), bf16[16,192,128]{2,1,0:T(8,128)(2,1)S(1)}, u32[]{:S(2)}, u32[]{:S(2)}) async-start(bf16[16,192,128]{2,1,0:T(8,128)(2,1)} %attend_back.1.grads_ref), calls=%async_computation.3 | async-start | bytes 1572864 | tf_op jit(solution)/shard_map/all_to_all | solution.py:627
  138.4 0.6 collective-permute-start.10
  138.9 2.1 collective-permute-start.8
  141.1 0.9 collective-permute-start.9
  142.0 5.3 %gradient_parts.1 = (bf16[416,128]{1,0:T(8,128)(2,1)}, bf16[416,128]{1,0:T(8,128)(2,1)}, bf16[416,128]{1,0:T(8,128)(2,1)}, bf16[416,128]{1,0:T(8,128)(2,1)}) custom-call(s32[5]{0:T(128)} %stack.15.scalars, bf16[16,192,128]{2,1,0:T(8,128)(2,1)} %attend_back.1.grads_ref, bf16[16,96,128]{2,1,0:T(8,128)(2,1)} %copy-done.3, ...), custom_call_target="tpu_custom_call" | custom-call | flops 1073741824 | bytes 4194304 | tf_op jit(solution)/shard_map/gradient_parts/pallas_call | solution.py:466
  147.4 14.2 %collective-permute-done.10.four = bf16[4,512,128]{2,1,0:T(8,128)(2,1)S(1)} collective-permute-done((bf16[4,512,128]{2,1,0:T(8,128)(2,1)}, bf16[4,512,128]{2,1,0:T(8,128)(2,1)S(1)}, u32[]{:S(2)}, u32[]{:S(2)}) %collective-permute-start.10) | collective-permute-done | bytes 524320 | tf_op jit(solution)/shard_map/ppermute | solution.py:592
  161.6 11.5 %collective-permute-done.9.three = bf16[4,512,128]{2,1,0:T(8,128)(2,1)S(1)} collective-permute-done((bf16[4,512,128]{2,1,0:T(8,128)(2,1)S(1)}, bf16[4,512,128]{2,1,0:T(8,128)(2,1)S(1)}, u32[]{:S(2)}, u32[]{:S(2)}) %collective-permute-start.9) | collective-permute-done | bytes 524320 | tf_op jit(solution)/shard_map/ppermute | solution.py:592
  173.1 0.8 copy-done.9
  173.9 2.4 %fold_out.1 = (bf16[512,128]{1,0:T(8,128)(2,1)}, bf16[512,128]{1,0:T(8,128)(2,1)}, bf16[512,128]{1,0:T(8,128)(2,1)}, bf16[512,128]{1,0:T(8,128)(2,1)}) custom-call(s32[5]{0:T(128)} %stack.15.scalars, bf16[4,512,128]{2,1,0:T(8,128)(2,1)} %get-tuple-element.61.one, bf16[4,512,128]{2,1,0:T(8,128)(2,1)} %copy-done.8, bf16[4,512,128]{2,1,0:T(8,128)(2,1)} %copy-done.9, ...), custom_call_target="tpu_custom_call" | custom-call | bytes 2621440 | tf_op jit(solution)/shard_map/fold_out/pallas_call | solution.py:496
  176.3 1.7 collective-permute-start.11
  178.1 2.2 collective-permute-start.4
  180.2 2.9 %collective-permute-start.12 = (bf16[512,128]{1,0:T(8,128)(2,1)}, bf16[512,128]{1,0:T(8,128)(2,1)S(1)}, u32[]{:S(2)}, u32[]{:S(2)}) collective-permute-start(bf16[512,128]{1,0:T(8,128)(2,1)} %get-tuple-element.67), channel_id=1, source_target_pairs={{0,128},{16,144},{32,160},{48,176},{64,192},{80,208},{96,224},{112... | collective-permute-start | bytes 393224 | tf_op jit(solution)/shard_map/ppermute | solution.py:592
  183.1 0.3 collective-permute-start.13
  183.5 1.7 collective-permute-done.3.three
  185.1 0.6 copy-done.14
  185.8 1.9 fold_fast.1
  187.7 0.5 collective-permute-start.5
  188.2 2.9 %collective-permute-start.6 = (bf16[128,128]{1,0:T(8,128)(2,1)}, bf16[128,128]{1,0:T(8,128)(2,1)S(1)}, u32[]{:S(2)}, u32[]{:S(2)}) collective-permute-start(bf16[128,128]{1,0:T(8,128)(2,1)} %get-tuple-element.59), channel_id=1, source_target_pairs={{0,128},{16,144},{32,160},{48,176},{64,192},{80,208},{96,224},{112... | collective-permute-start | bytes 98312 | tf_op jit(solution)/shard_map/ppermute | solution.py:592
  191.1 1.3 collective-permute-start.7
  192.4 1.8 collective-permute-done.6.refs_2_
  194.2 2.3 %collective-permute-done.7.refs_3_ = bf16[128,128]{1,0:T(8,128)(2,1)S(1)} collective-permute-done((bf16[128,128]{1,0:T(8,128)(2,1)}, bf16[128,128]{1,0:T(8,128)(2,1)S(1)}, u32[]{:S(2)}, u32[]{:S(2)}) %collective-permute-start.7) | collective-permute-done | bytes 32800 | tf_op jit(solution)/shard_map/ppermute | solution.py:592
  196.5 0.6 copy-done.19
  197.1 2.2 fold_slow.1
  199.2 7.1 %all-to-all-start.4 = ((bf16[16,64,128]{2,1,0:T(8,128)(2,1)}), bf16[16,64,128]{2,1,0:T(8,128)(2,1)S(1)}, u32[]{:S(2)}, u32[]{:S(2)}) async-start(bf16[16,64,128]{2,1,0:T(8,128)(2,1)} %get-tuple-element.70), calls=%async_computation.4 | async-start | bytes 524288 | tf_op jit(solution)/shard_map/all_to_all | solution.py:633
  206.3 6.4 %input_gradient.1 = bf16[128,1024]{1,0:T(8,128)(2,1)} custom-call(bf16[16,192,128]{2,1,0:T(8,128)(2,1)} %copy-done.1, bf16[1024,3072]{1,0:T(8,128)(2,1)} %weight_ref.3, bf16[128,1024]{1,0:T(8,128)(2,1)} %bitcast.18, f32[128,1024]{1,0:T(8,128)} %get-tuple-element.51.res_grad_ref), custom_call_target="tpu_custom_call" | custom-call | tf_op jit(solution)/shard_map/input_gradient/pallas_call | solution.py:385
  212.9 0.7 copy.13
  213.6 2.8 %all-to-all-done.4.refs_0_ = bf16[16,64,128]{2,1,0:T(8,128)(2,1)S(1)} async-done(((bf16[16,64,128]{2,1,0:T(8,128)(2,1)}), bf16[16,64,128]{2,1,0:T(8,128)(2,1)S(1)}, u32[]{:S(2)}, u32[]{:S(2)}) %all-to-all-start.4) | async-done | bytes 262176 | tf_op jit(solution)/shard_map/all_to_all | solution.py:633
  216.4 0.7 copy-done.4
  217.1 1.8 finish.1
  (58 shorter events, 0.3 us)
Async XLA Ops:
  7.2 134.9 %all-gather.2.cloned.1.call-start = ((), (), s32[]{:S(2)}) async-start(), calls=%async_computation.5 | async-start | bytes 4456448 | tf_op jit(solution)/shard_map/all_gather | solution.py:618
  7.2 17.8 %copy-start = (bf16[1,128,1024]{2,1,0:T(8,128)(2,1)S(1)}, bf16[1,128,1024]{2,1,0:T(8,128)(2,1)}, u32[]{:S(2)}) copy-start(bf16[1,128,1024]{2,1,0:T(8,128)(2,1)} %param.6) | copy-start | bytes 786436
  7.2 17.8 %copy-start.6 = (bf16[1,128,1024]{2,1,0:T(8,128)(2,1)S(1)}, bf16[1,128,1024]{2,1,0:T(8,128)(2,1)}, u32[]{:S(2)}) copy-start(bf16[1,128,1024]{2,1,0:T(8,128)(2,1)} %param.7) | copy-start | bytes 786436
  14.2 35.5 %all-to-all-start = ((bf16[16,192,128]{2,1,0:T(8,128)(2,1)}), bf16[16,192,128]{2,1,0:T(8,128)(2,1)S(1)}, u32[]{:S(2)}, u32[]{:S(2)}) async-start(bf16[16,192,128]{2,1,0:T(8,128)(2,1)} %get-tuple-element.39), calls=%async_computation | async-start | bytes 1572864 | tf_op jit(solution)/shard_map/all_to_all | solution.py:617
  49.7 0.9 copy-start.5
  63.4 26.6 %all-to-all-start.1 = ((bf16[16,96,128]{2,1,0:T(8,128)(2,1)}), bf16[16,96,128]{2,1,0:T(8,128)(2,1)S(1)}, u32[]{:S(2)}, u32[]{:S(2)}) async-start(bf16[16,96,128]{2,1,0:T(8,128)(2,1)} %get-tuple-element.40), calls=%async_computation.1 | async-start | bytes 786432 | tf_op jit(solution)/shard_map/all_to_all | solution.py:620
  70.4 18.5 %collective-permute-start = (bf16[64,1024]{1,0:T(8,128)(2,1)S(1)}, bf16[64,1024]{1,0:T(8,128)(2,1)S(1)}, u32[]{:S(2)}, u32[]{:S(2)}) collective-permute-start(bf16[64,1024]{1,0:T(8,128)(2,1)S(1)} %pad_maximum_fusion), channel_id=1, source_target_pairs={{0,1},{1,2},{2,3},{3,4},{4,5},{5,6},{6,7},{7,8},{8,9},{9,10},{10,1... | collective-permute-start | bytes 393224 | tf_op jit(solution)/shard_map/ppermute | solution.py:611
  73.8 15.4 %collective-permute-start.1 = (bf16[64,1024]{1,0:T(8,128)(2,1)S(1)}, bf16[64,1024]{1,0:T(8,128)(2,1)S(1)}, u32[]{:S(2)}, u32[]{:S(2)}) collective-permute-start(bf16[64,1024]{1,0:T(8,128)(2,1)S(1)} %pad_maximum_fusion.1), channel_id=1, source_target_pairs={{1,0},{2,1},{3,2},{4,3},{5,4},{6,5},{7,6},{8,7},{9,8},{10,9},{11,1... | collective-permute-start | bytes 393224 | tf_op jit(solution)/shard_map/ppermute | solution.py:612
  90.0 0.7 copy-start.2
  99.6 18.5 %all-to-all-start.2 = ((bf16[16,96,128]{2,1,0:T(8,128)(2,1)}), bf16[16,96,128]{2,1,0:T(8,128)(2,1)S(1)}, u32[]{:S(2)}, u32[]{:S(2)}) async-start(bf16[16,96,128]{2,1,0:T(8,128)(2,1)} %get-tuple-element.42), calls=%async_computation.2 | async-start | bytes 786432 | tf_op jit(solution)/shard_map/all_to_all | solution.py:622
  118.1 0.8 copy-start.3
  118.8 20.1 %copy-start.21 = (bf16[4,512,128]{2,1,0:T(8,128)(2,1)S(1)}, bf16[4,512,128]{2,1,0:T(8,128)(2,1)}, u32[]{:S(2)}) copy-start(bf16[4,512,128]{2,1,0:T(8,128)(2,1)} %get-tuple-element.62) | copy-start | bytes 1572868
  118.8 22.2 %copy-start.20 = (bf16[4,512,128]{2,1,0:T(8,128)(2,1)S(1)}, bf16[4,512,128]{2,1,0:T(8,128)(2,1)}, u32[]{:S(2)}) copy-start(bf16[4,512,128]{2,1,0:T(8,128)(2,1)} %get-tuple-element.63) | copy-start | bytes 1572868
  133.6 65.6 %all-to-all-start.3 = ((bf16[16,192,128]{2,1,0:T(8,128)(2,1)}), bf16[16,192,128]{2,1,0:T(8,128)(2,1)S(1)}, u32[]{:S(2)}, u32[]{:S(2)}) async-start(bf16[16,192,128]{2,1,0:T(8,128)(2,1)} %attend_back.1.grads_ref), calls=%async_computation.3 | async-start | bytes 1572864 | tf_op jit(solution)/shard_map/all_to_all | solution.py:627
  138.4 23.2 %collective-permute-start.10 = (bf16[4,512,128]{2,1,0:T(8,128)(2,1)}, bf16[4,512,128]{2,1,0:T(8,128)(2,1)S(1)}, u32[]{:S(2)}, u32[]{:S(2)}) collective-permute-start(bf16[4,512,128]{2,1,0:T(8,128)(2,1)} %get-tuple-element.64), channel_id=1, source_target_pairs={{0,48},{16,32},{32,16},{48,0},{64,112},{80,96},{96,80},{112,64},{1... | collective-permute-start | bytes 1572872 | tf_op jit(solution)/shard_map/ppermute | solution.py:592
  138.9 22.6 %collective-permute-start.8 = (bf16[4,512,128]{2,1,0:T(8,128)(2,1)S(1)}, bf16[4,512,128]{2,1,0:T(8,128)(2,1)S(1)}, u32[]{:S(2)}, u32[]{:S(2)}) collective-permute-start(bf16[4,512,128]{2,1,0:T(8,128)(2,1)S(1)} %copy-done.21), channel_id=1, source_target_pairs={{0,16},{16,0},{32,48},{48,32},{64,80},{80,64},{96,112},{112,96},{1... | collective-permute-start | bytes 1572872 | tf_op jit(solution)/shard_map/ppermute | solution.py:592
  141.1 32.0 %collective-permute-start.9 = (bf16[4,512,128]{2,1,0:T(8,128)(2,1)S(1)}, bf16[4,512,128]{2,1,0:T(8,128)(2,1)S(1)}, u32[]{:S(2)}, u32[]{:S(2)}) collective-permute-start(bf16[4,512,128]{2,1,0:T(8,128)(2,1)S(1)} %copy-done.20), channel_id=1, source_target_pairs={{0,32},{16,48},{32,0},{48,16},{64,96},{80,112},{96,64},{112,80},{1... | collective-permute-start | bytes 1572872 | tf_op jit(solution)/shard_map/ppermute | solution.py:592
  147.4 35.8 %collective-permute-start.2 = (bf16[416,128]{1,0:T(8,128)(2,1)}, bf16[416,128]{1,0:T(8,128)(2,1)S(1)}, u32[]{:S(2)}, u32[]{:S(2)}) collective-permute-start(bf16[416,128]{1,0:T(8,128)(2,1)} %get-tuple-element.54), channel_id=1, source_target_pairs={{0,16},{16,0},{32,48},{48,32},{64,80},{80,64},{96,112},{112,96},{1... | collective-permute-start | bytes 319496 | tf_op jit(solution)/shard_map/ppermute | solution.py:592
  161.6 11.5 %copy-start.7 = (bf16[4,512,128]{2,1,0:T(8,128)(2,1)}, bf16[4,512,128]{2,1,0:T(8,128)(2,1)S(1)}, u32[]{:S(2)}) copy-start(bf16[4,512,128]{2,1,0:T(8,128)(2,1)S(1)} %collective-permute-done.10.four) | copy-start | bytes 1572868
  161.6 11.5 %copy-start.8 = (bf16[4,512,128]{2,1,0:T(8,128)(2,1)}, bf16[4,512,128]{2,1,0:T(8,128)(2,1)S(1)}, u32[]{:S(2)}) copy-start(bf16[4,512,128]{2,1,0:T(8,128)(2,1)S(1)} %collective-permute-done.8.two) | copy-start | bytes 1572868
  173.1 0.8 copy-start.9
  176.3 14.7 %collective-permute-start.11 = (bf16[512,128]{1,0:T(8,128)(2,1)}, bf16[512,128]{1,0:T(8,128)(2,1)S(1)}, u32[]{:S(2)}, u32[]{:S(2)}) collective-permute-start(bf16[512,128]{1,0:T(8,128)(2,1)} %get-tuple-element.66), channel_id=1, source_target_pairs={{0,64},{16,80},{32,96},{48,112},{64,0},{80,16},{96,32},{112,48},{1... | collective-permute-start | bytes 393224 | tf_op jit(solution)/shard_map/ppermute | solution.py:592
  178.1 7.0 %collective-permute-start.3 = (bf16[416,128]{1,0:T(8,128)(2,1)}, bf16[416,128]{1,0:T(8,128)(2,1)S(1)}, u32[]{:S(2)}, u32[]{:S(2)}) collective-permute-start(bf16[416,128]{1,0:T(8,128)(2,1)} %get-tuple-element.55), channel_id=1, source_target_pairs={{0,32},{16,48},{32,0},{48,16},{64,96},{80,112},{96,64},{112,80},{1... | collective-permute-start | bytes 319496 | tf_op jit(solution)/shard_map/ppermute | solution.py:592
  178.1 7.0 %collective-permute-start.4 = (bf16[416,128]{1,0:T(8,128)(2,1)}, bf16[416,128]{1,0:T(8,128)(2,1)S(1)}, u32[]{:S(2)}, u32[]{:S(2)}) collective-permute-start(bf16[416,128]{1,0:T(8,128)(2,1)} %get-tuple-element.56), channel_id=1, source_target_pairs={{0,48},{16,32},{32,16},{48,0},{64,112},{80,96},{96,80},{112,64},{1... | collective-permute-start | bytes 319496 | tf_op jit(solution)/shard_map/ppermute | solution.py:592
  180.2 12.1 %collective-permute-start.12 = (bf16[512,128]{1,0:T(8,128)(2,1)}, bf16[512,128]{1,0:T(8,128)(2,1)S(1)}, u32[]{:S(2)}, u32[]{:S(2)}) collective-permute-start(bf16[512,128]{1,0:T(8,128)(2,1)} %get-tuple-element.67), channel_id=1, source_target_pairs={{0,128},{16,144},{32,160},{48,176},{64,192},{80,208},{96,224},{112... | collective-permute-start | bytes 393224 | tf_op jit(solution)/shard_map/ppermute | solution.py:592
  183.1 2.0 copy-start.13
  183.1 9.2 %collective-permute-start.13 = (bf16[512,128]{1,0:T(8,128)(2,1)}, bf16[512,128]{1,0:T(8,128)(2,1)S(1)}, u32[]{:S(2)}, u32[]{:S(2)}) collective-permute-start(bf16[512,128]{1,0:T(8,128)(2,1)} %get-tuple-element.68), channel_id=1, source_target_pairs={{0,192},{16,208},{32,224},{48,240},{64,128},{80,144},{96,160},{112... | collective-permute-start | bytes 393224 | tf_op jit(solution)/shard_map/ppermute | solution.py:592
  185.1 0.7 copy-start.14
  185.1 0.7 copy-start.15
  187.7 4.7 %collective-permute-start.5 = (bf16[128,128]{1,0:T(8,128)(2,1)}, bf16[128,128]{1,0:T(8,128)(2,1)S(1)}, u32[]{:S(2)}, u32[]{:S(2)}) collective-permute-start(bf16[128,128]{1,0:T(8,128)(2,1)} %get-tuple-element.58), channel_id=1, source_target_pairs={{0,64},{16,80},{32,96},{48,112},{64,0},{80,16},{96,32},{112,48},{1... | collective-permute-start | bytes 98312 | tf_op jit(solution)/shard_map/ppermute | solution.py:592
  188.2 6.0 %collective-permute-start.6 = (bf16[128,128]{1,0:T(8,128)(2,1)}, bf16[128,128]{1,0:T(8,128)(2,1)S(1)}, u32[]{:S(2)}, u32[]{:S(2)}) collective-permute-start(bf16[128,128]{1,0:T(8,128)(2,1)} %get-tuple-element.59), channel_id=1, source_target_pairs={{0,128},{16,144},{32,160},{48,176},{64,192},{80,208},{96,224},{112... | collective-permute-start | bytes 98312 | tf_op jit(solution)/shard_map/ppermute | solution.py:592
  191.1 5.4 %copy-start.10 = (bf16[512,128]{1,0:T(8,128)(2,1)}, bf16[512,128]{1,0:T(8,128)(2,1)S(1)}, u32[]{:S(2)}) copy-start(bf16[512,128]{1,0:T(8,128)(2,1)S(1)} %collective-permute-done.11.refs_5_) | copy-start | bytes 393220
  191.1 5.4 %collective-permute-start.7 = (bf16[128,128]{1,0:T(8,128)(2,1)}, bf16[128,128]{1,0:T(8,128)(2,1)S(1)}, u32[]{:S(2)}, u32[]{:S(2)}) collective-permute-start(bf16[128,128]{1,0:T(8,128)(2,1)} %get-tuple-element.60), channel_id=1, source_target_pairs={{0,192},{16,208},{32,224},{48,240},{64,128},{80,144},{96,160},{112... | collective-permute-start | bytes 98312 | tf_op jit(solution)/shard_map/ppermute | solution.py:592
  192.4 4.1 %copy-start.11 = (bf16[512,128]{1,0:T(8,128)(2,1)}, bf16[512,128]{1,0:T(8,128)(2,1)S(1)}, u32[]{:S(2)}) copy-start(bf16[512,128]{1,0:T(8,128)(2,1)S(1)} %collective-permute-done.12.refs_6_) | copy-start | bytes 393220
  192.4 4.1 %copy-start.12 = (bf16[512,128]{1,0:T(8,128)(2,1)}, bf16[512,128]{1,0:T(8,128)(2,1)S(1)}, u32[]{:S(2)}) copy-start(bf16[512,128]{1,0:T(8,128)(2,1)S(1)} %collective-permute-done.13.refs_7_) | copy-start | bytes 393220
  192.4 4.1 %copy-start.17 = (bf16[128,128]{1,0:T(8,128)(2,1)}, bf16[128,128]{1,0:T(8,128)(2,1)S(1)}, u32[]{:S(2)}) copy-start(bf16[128,128]{1,0:T(8,128)(2,1)S(1)} %collective-permute-done.5.refs_1_) | copy-start | bytes 98308
  194.2 2.3 %copy-start.18 = (bf16[128,128]{1,0:T(8,128)(2,1)}, bf16[128,128]{1,0:T(8,128)(2,1)S(1)}, u32[]{:S(2)}) copy-start(bf16[128,128]{1,0:T(8,128)(2,1)S(1)} %collective-permute-done.6.refs_2_) | copy-start | bytes 98308
  196.5 0.6 copy-start.19
  199.2 7.1 %copy-start.1 = (bf16[16,192,128]{2,1,0:T(8,128)(2,1)}, bf16[16,192,128]{2,1,0:T(8,128)(2,1)S(1)}, u32[]{:S(2)}) copy-start(bf16[16,192,128]{2,1,0:T(8,128)(2,1)S(1)} %all-to-all-done.3.joined_ref) | copy-start | bytes 2359300
  199.2 17.1 %all-to-all-start.4 = ((bf16[16,64,128]{2,1,0:T(8,128)(2,1)}), bf16[16,64,128]{2,1,0:T(8,128)(2,1)S(1)}, u32[]{:S(2)}, u32[]{:S(2)}) async-start(bf16[16,64,128]{2,1,0:T(8,128)(2,1)} %get-tuple-element.70), calls=%async_computation.4 | async-start | bytes 524288 | tf_op jit(solution)/shard_map/all_to_all | solution.py:633
  206.3 6.5 %copy-start.16 = (f32[64,192]{1,0:T(8,128)S(1)}, f32[64,192]{1,0:T(8,128)}, u32[]{:S(2)}) copy-start(f32[64,192]{1,0:T(8,128)} %get-tuple-element.69) | copy-start | bytes 147460
  216.4 0.7 copy-start.4
Sparse Core Ops, SparseCore 0:
  14.3 94.4 all-gather.1

commit v3 on v2

--- a/solution.py
+++ b/solution.py
@@ -409,31 +409,31 @@
 OUT = 8 * HD
 
 
-def out_part_kernel(scalars, att_ref, round_ref, *send_refs):
-    lanes = send_refs[0].shape[2]
-    for k, send_ref in enumerate(send_refs):
-        part = dot(att_ref[scalars[3] ^ k, 0:HD, :], round_ref[...])
+def out_part_kernel(att_ref, round_ref, send_ref):
+    fast, _, _, lanes = send_ref.shape
+    rows = att_ref.shape[2]
+    part = dot(att_ref[:, 0:HD, :].reshape(fast * HD, rows), round_ref[...])
+    for i in range(fast):
         for c in range(part.shape[1] // lanes):
-            piece = part[:, c * lanes : (c + 1) * lanes]
-            send_ref[0, c * HD : (c + 1) * HD, :] = piece.astype(BF16)
-
-
-def out_part(scalars, att, rounded):
+            piece = part[i * HD : (i + 1) * HD, c * lanes : (c + 1) * lanes]
+            send_ref[i, 0, c * HD : (c + 1) * HD, :] = piece.astype(BF16)
+
+
+def out_part(att, rounded):
     heads, wide, rows = att.shape
     return pl.pallas_call(
         out_part_kernel,
         grid=(SLOW,),
         in_specs=[
-            SMEM,
             pl.BlockSpec((FAST, wide, rows), lambda j: (j, 0, 0)),
             whole(rounded.shape),
         ],
-        out_specs=[pl.BlockSpec((1, OUT, 128), lambda j: (j, 0, 0))] * FAST,
-        out_shape=[jax.ShapeDtypeStruct((SLOW, OUT, 128), BF16)] * FAST,
+        out_specs=pl.BlockSpec((FAST, 1, OUT, 128), lambda j: (0, j, 0, 0)),
+        out_shape=jax.ShapeDtypeStruct((FAST, SLOW, OUT, 128), BF16),
         compiler_params=params(),
         cost_estimate=cost(2 * heads * HD * 256 * rounded.shape[1], heads * HD * rounded.shape[1] * 2),
         name="out_part",
-    )(scalars, att, rounded)
+    )(att, rounded)
 
 
 def parts_kernel(scalars, grads_ref, back_ref, normed_ref, *rest):
@@ -485,24 +485,6 @@
     return (own.astype(F32) + one.astype(F32)) + (two.astype(F32) + three.astype(F32))
 
 
-def fold_out_kernel(scalars, one, two, three, four, *send_refs):
-    for k, send_ref in enumerate(send_refs):
-        i = scalars[4] ^ k
-        send_ref[...] = sum_four(one[i], two[i], three[i], four[i]).astype(BF16)
-
-
-def fold_out(scalars, blocks):
-    vmem = pl.BlockSpec(memory_space=pltpu.VMEM)
-    return pl.pallas_call(
-        fold_out_kernel,
-        in_specs=[SMEM] + [vmem] * 4,
-        out_shape=[jax.ShapeDtypeStruct((OUT, 128), BF16)] * SLOW,
-        compiler_params=params(),
-        cost_estimate=cost(0, 5 * SLOW * OUT * 128 * 2),
-        name="fold_out",
-    )(scalars, *blocks)
-
-
 def fold_fast_kernel(scalars, one, two, three, four, *rest):
     send_refs, pieces = rest[:SLOW], rest[SLOW]
     total = sum_four(one[...], two[...], three[...], four[...])
@@ -527,13 +509,13 @@
 
 
 def fold_slow_kernel(*refs, scale):
-    qkv_ref, send_ref = refs[8:]
+    outer_ref, qkv_ref, send_ref = refs[4:]
     total = sum_four(*(ref[...] for ref in refs[0:4]))
     model_rows = (total[0:CUT] * scale).T
     qkv_ref[:, 0:CUT] = model_rows[0:HD]
     qkv_ref[:, CUT:] = model_rows[HD:]
     pair = halves(joined_halves(total[CUT:]))
-    outer = sum_four(*(ref[...] for ref in refs[4:8]))
+    outer = outer_ref[0].astype(F32)
     count = send_ref.shape[0]
     each = HD // count
     for i in range(count):
@@ -542,18 +524,18 @@
         send_ref[i, OUT // count :, :] = pair
 
 
-def fold_slow(blocks, out_blocks, seq_count, scale):
+def fold_slow(blocks, outer, seq_count, scale):
     vmem = pl.BlockSpec(memory_space=pltpu.VMEM)
     return pl.pallas_call(
         lambda *refs: fold_slow_kernel(*refs, scale=scale),
-        in_specs=[vmem] * 8,
+        in_specs=[vmem] * 5,
         out_shape=[
             jax.ShapeDtypeStruct((HD, 3 * HD), F32),
             jax.ShapeDtypeStruct((seq_count, OUT // seq_count + KW + 1, 128), BF16),
         ],
         compiler_params=params(),
         name="fold_slow",
-    )(*blocks, *out_blocks)
+    )(*blocks, outer)
 
 
 def finish_kernel(recv_ref, out_ref, taps_ref, *, scale):
@@ -620,13 +602,20 @@
     att = lax.all_to_all(send, "seq", 0, 0, tiled=True)
     output, res_grad, rounded, send = middle(scalars, att, x, x_side, g, g_side, w_out, w_conv)
     back = lax.all_to_all(send, "seq", 0, 0, tiled=True)
-    outer = out_part(scalars, att, rounded)
-    back, outer = lax.optimization_barrier((back, outer))
-    outer = exchange(outer, 1)
+    near = [[FAST * i + j for j in range(FAST)] for i in range(SLOW)]
+    far = [[FAST * i + j for i in range(SLOW)] for j in range(FAST)]
+    outer = out_part(att, rounded)
+    back, outer, normed_all = lax.optimization_barrier((back, outer, normed_all))
+    outer = lax.psum_scatter(
+        outer, "dp", scatter_dimension=0, axis_index_groups=near, tiled=True
+    )
     send = attend_back(scalars, heads, back, out, lse)
     joined = lax.all_to_all(send, "seq", 0, 0, tiled=True)
+    outer, after = lax.optimization_barrier((outer, send))
+    outer = lax.psum_scatter(
+        outer[0], "dp", scatter_dimension=0, axis_index_groups=far, tiled=True
+    )
     parts = exchange(gradient_parts(scalars, send, back, normed_all), 1)
-    outer = exchange(fold_out(scalars, outer), FAST)
     parts = exchange(fold_fast(scalars, parts), FAST)
     qkv, send = fold_slow(parts, outer, seq_count, grad_scale)
     input_grad = input_gradient(joined, w_qkv, x, res_grad)

time: 227 us -> 221 us (0.974)
  starting transfers between devices: 56.6 us -> 49.2 us
  waiting for transfers between devices: 79.4 us -> 85.1 us
  Pallas kernels: 67.3 us -> 64.6 us
    reduce_scatter x0 -> x2, waiting for transfers between devices: none -> 27 us  [the longest x1 27 us: local(): lax.psum_scatter(outer, 'dp', scatter_dimension=0, axis_index_groups=near...]
    ppermute x12 -> x6, waiting for transfers between devices: 31.4 us -> 10.9 us  [exchange(): lax.ppermute(block, 'dp', pairs(k))]
    ppermute x1, waiting for transfers between devices: 12.6 us -> 0.01 us  [local(): lax.ppermute(jnp.concatenate([x[-HALO:], g[-HALO:]], axis=0), 'seq', forw...]
    ppermute x1, waiting for transfers between devices: 0.28 us -> 12.9 us  [local(): lax.ppermute(jnp.concatenate([x[:HALO], g[:HALO]], axis=0), 'seq', backward)]
    ppermute x12 -> x6, starting transfers between devices: 15.5 us -> 8.23 us  [exchange(): lax.ppermute(block, 'dp', pairs(k))]
    pallas_call x2 -> x1, Pallas kernels: 6.37 us -> 4.06 us  [out_part(): pl.pallas_call(out_part_kernel, grid=(SLOW,), in_specs=[pl.BlockSpec((FAS...]
    unnamed x45 -> x29, local copies, waits for them, and re-layouts: 5.99 us -> 5.16 us
  transfers between devices with their start and end apart: 20 -> 16, of which waited for: 10 -> 9; matrix products, arithmetic and copies ran while one was open for 1% -> 1% of each run, Pallas kernels for 26% -> 25%
where the time goes in v3:
time: 221 us; the launch traced here: 220 us
  waiting for transfers between devices  85.1 us (39%)
  Pallas kernels  64.6 us (29%)
  starting transfers between devices  49.2 us (22%)
  between operations  14.5 us (7%)
  local copies, waits for them, and re-layouts  5.97 us (3%)
    reduce_scatter x1, waiting for transfers between devices, local(): lax.psum_scatter(outer, 'dp', scatter_dimension=0, axis_index_groups=near...  27 us
    all_to_all x1, waiting for transfers between devices, local(): heads = lax.all_to_all(send, 'seq', 0, 0, tiled=True)  24.6 us
    pallas_call x1, Pallas kernels, attend_back(): pl.pallas_call(attend_back_kernel, in_specs=[SMEM] + [vmem] * 4, out_shap...  14.7 us
    ppermute x1, waiting for transfers between devices, local(): lax.ppermute(jnp.concatenate([x[:HALO], g[:HALO]], axis=0), 'seq', backward)  12.9 us
    pallas_call x1, Pallas kernels, attend(): pl.pallas_call(attend_kernel, in_specs=[SMEM, pl.BlockSpec(memory_space=p...  12.8 us
    ppermute x6, waiting for transfers between devices, exchange(): lax.ppermute(block, 'dp', pairs(k))  10.9 us
    all_to_all x1, starting transfers between devices, local(): heads = lax.all_to_all(send, 'seq', 0, 0, tiled=True)  9.53 us
    pallas_call x1, Pallas kernels, middle(): pl.pallas_call(middle_kernel, in_specs=[SMEM] + [vmem] * 7, out_shape=[ja...  8.84 us
  transfers between devices with their start and end apart: 16, of which 9 were waited for; matrix products, arithmetic and copies ran while one was open for 1% of the time, Pallas kernels for 25%

profile of v3, /device:TPU:32, one launch (start us, length us, event | category | flops | bytes accessed | tf_op | source)
XLA Modules:
  0.0 220.1 jit_solution(8284278302497875636)
XLA Ops:
  7.2 0.0 all-gather.2.cloned.1.call-start
  7.2 0.0 copy-start.1
  7.2 7.0 %project.1 = (bf16[128,1024]{1,0:T(8,128)(2,1)}, bf16[16,192,128]{2,1,0:T(8,128)(2,1)}) custom-call(bf16[128,1024]{1,0:T(8,128)(2,1)} %bitcast.17, bf16[1024,3072]{1,0:T(8,128)(2,1)} %weight_ref.3), custom_call_target="tpu_custom_call" | custom-call | tf_op jit(solution)/shard_map/project/pallas_call | solution.py:79
  14.2 0.0 all-gather.2.cloned.1.call-update
  14.2 9.5 %all-to-all-start = ((bf16[16,192,128]{2,1,0:T(8,128)(2,1)}), bf16[16,192,128]{2,1,0:T(8,128)(2,1)S(1)}, u32[]{:S(2)}, u32[]{:S(2)}) async-start(bf16[16,192,128]{2,1,0:T(8,128)(2,1)} %get-tuple-element.30), calls=%async_computation | async-start | bytes 1572864 | tf_op jit(solution)/shard_map/all_to_all | solution.py:599
  24.4 0.7 stack.15.scalars
  25.1 24.6 %all-to-all-done.heads_ref = bf16[16,192,128]{2,1,0:T(8,128)(2,1)S(1)} async-done(((bf16[16,192,128]{2,1,0:T(8,128)(2,1)}), bf16[16,192,128]{2,1,0:T(8,128)(2,1)S(1)}, u32[]{:S(2)}, u32[]{:S(2)}) %all-to-all-start) | async-done | bytes 786464 | tf_op jit(solution)/shard_map/all_to_all | solution.py:599
  49.7 0.9 copy-done.5
  50.7 12.8 %attend.1 = (bf16[16,96,128]{2,1,0:T(8,128)(2,1)}, f32[64,2048]{1,0:T(8,128)}, f32[1,2048]{1,0:T(1,128)}) custom-call(s32[5]{0:T(128)} %stack.15.scalars, bf16[16,192,128]{2,1,0:T(8,128)(2,1)} %copy-done.5), custom_call_target="tpu_custom_call" | custom-call | flops 4294967296 | bytes 786432 | tf_op jit(solution)/shard_map/attend/pallas_call | solution.py:153
  63.5 7.0 %all-to-all-start.1 = ((bf16[16,96,128]{2,1,0:T(8,128)(2,1)}), bf16[16,96,128]{2,1,0:T(8,128)(2,1)S(1)}, u32[]{:S(2)}, u32[]{:S(2)}) async-start(bf16[16,96,128]{2,1,0:T(8,128)(2,1)} %get-tuple-element.31), calls=%async_computation.1 | async-start | bytes 786432 | tf_op jit(solution)/shard_map/all_to_all | solution.py:602
  70.5 2.0 collective-permute-start.1
  72.5 3.8 %collective-permute-start = (bf16[64,1024]{1,0:T(8,128)(2,1)S(1)}, bf16[64,1024]{1,0:T(8,128)(2,1)S(1)}, u32[]{:S(2)}, u32[]{:S(2)}) collective-permute-start(bf16[64,1024]{1,0:T(8,128)(2,1)S(1)} %pad_maximum_fusion), channel_id=1, source_target_pairs={{0,1},{1,2},{2,3},{3,4},{4,5},{5,6},{6,7},{7,8},{8,9},{9,10},{10,1... | collective-permute-start | bytes 393224 | tf_op jit(solution)/shard_map/ppermute | solution.py:593
  76.4 12.9 %collective-permute-done.1 = bf16[64,1024]{1,0:T(8,128)(2,1)S(1)} collective-permute-done((bf16[64,1024]{1,0:T(8,128)(2,1)S(1)}, bf16[64,1024]{1,0:T(8,128)(2,1)S(1)}, u32[]{:S(2)}, u32[]{:S(2)}) %collective-permute-start.1) | collective-permute-done | bytes 131104 | tf_op jit(solution)/shard_map/ppermute | solution.py:594
  89.3 0.7 pad_maximum_fusion.2
  90.0 0.8 copy-done
  90.8 8.8 %middle.1 = (bf16[128,1024]{1,0:T(8,128)(2,1)}, f32[128,1024]{1,0:T(8,128)}, bf16[128,1024]{1,0:T(8,128)(2,1)}, bf16[16,96,128]{2,1,0:T(8,128)(2,1)}) custom-call(s32[5]{0:T(128)} %stack.15.scalars, bf16[16,96,128]{2,1,0:T(8,128)(2,1)} %copy-done, bf16[128,1024]{1,0:T(8,128)(2,1)} %bitcast.18, bf16[64,1024]{1,0:T(8,128)(2,1)} %get-tuple-element.73.frames_side, ...), custom_call_target="tpu_custom_call" | custom-call | tf_op jit(solution)/shard_map/middle/pallas_call | solution.py:268
  99.6 6.9 %all-to-all-start.2 = ((bf16[16,96,128]{2,1,0:T(8,128)(2,1)}), bf16[16,96,128]{2,1,0:T(8,128)(2,1)S(1)}, u32[]{:S(2)}, u32[]{:S(2)}) async-start(bf16[16,96,128]{2,1,0:T(8,128)(2,1)} %get-tuple-element.33), calls=%async_computation.2 | async-start | bytes 786432 | tf_op jit(solution)/shard_map/all_to_all | solution.py:604
  106.6 0.0 reduce-scatter.3.cloned.1.call-start
  106.6 4.1 %out_part.1 = bf16[4,4,512,128]{3,2,1,0:T(8,128)(2,1)} custom-call(bf16[16,96,128]{2,1,0:T(8,128)(2,1)} %copy-done, bf16[128,1024]{1,0:T(8,128)(2,1)} %get-tuple-element.34.round_ref), custom_call_target="tpu_custom_call" | custom-call | flops 536870912 | bytes 2097152 | tf_op jit(solution)/shard_map/out_part/pallas_call | solution.py:424
  110.7 7.2 %all-to-all-done.2.grads_ref.back_ref = bf16[16,96,128]{2,1,0:T(8,128)(2,1)S(1)} async-done(((bf16[16,96,128]{2,1,0:T(8,128)(2,1)}), bf16[16,96,128]{2,1,0:T(8,128)(2,1)S(1)}, u32[]{:S(2)}, u32[]{:S(2)}) %all-to-all-start.2) | async-done | bytes 393248 | tf_op jit(solution)/shard_map/all_to_all | solution.py:604
  117.9 0.0 reduce-scatter.3.cloned.1.call-update
  117.9 0.7 copy-done.3
  118.6 14.7 %attend_back.1.grads_ref = bf16[16,192,128]{2,1,0:T(8,128)(2,1)} custom-call(s32[5]{0:T(128)} %stack.15.scalars, bf16[16,192,128]{2,1,0:T(8,128)(2,1)} %copy-done.5, bf16[16,96,128]{2,1,0:T(8,128)(2,1)} %copy-done.3, f32[64,2048]{1,0:T(8,128)} %get-tuple-element.37.out_ref, f32[1,2048]{1,0:T(1,128)} %get-tuple-element.38.lse_ref), custom_call_target="tpu_custom_call" | custom-call | flops 10737418240 | bytes 1572864 | tf_op jit(solution)/shard_map/attend_back/pallas_call | solution.py:339
  133.3 4.7 %all-to-all-start.3 = ((bf16[16,192,128]{2,1,0:T(8,128)(2,1)}), bf16[16,192,128]{2,1,0:T(8,128)(2,1)S(1)}, u32[]{:S(2)}, u32[]{:S(2)}) async-start(bf16[16,192,128]{2,1,0:T(8,128)(2,1)} %attend_back.1.grads_ref), calls=%async_computation.3 | async-start | bytes 1572864 | tf_op jit(solution)/shard_map/all_to_all | solution.py:613
  138.0 0.0 reduce-scatter.5.cloned.1.call-start
  138.1 27.0 %reduce-scatter.3.cloned.1.call-done = bf16[1,4,512,128]{3,2,1,0:T(8,128)(2,1)} async-done(((bf16[4,4,512,128]{3,2,1,0:T(8,128)(2,1)}), bf16[1,4,512,128]{3,2,1,0:T(8,128)(2,1)}) %reduce-scatter.3.cloned.1.call-update) | async-done | bytes 524304 | tf_op jit(solution)/shard_map/reduce_scatter | solution.py:609
  165.1 0.0 reduce-scatter.5.cloned.1.call-update
  165.1 5.3 %gradient_parts.1 = (bf16[416,128]{1,0:T(8,128)(2,1)}, bf16[416,128]{1,0:T(8,128)(2,1)}, bf16[416,128]{1,0:T(8,128)(2,1)}, bf16[416,128]{1,0:T(8,128)(2,1)}) custom-call(s32[5]{0:T(128)} %stack.15.scalars, bf16[16,192,128]{2,1,0:T(8,128)(2,1)} %attend_back.1.grads_ref, bf16[16,96,128]{2,1,0:T(8,128)(2,1)} %copy-done.3, ...), custom_call_target="tpu_custom_call" | custom-call | flops 1073741824 | bytes 4194304 | tf_op jit(solution)/shard_map/gradient_parts/pallas_call | solution.py:466
  170.4 0.1 collective-permute-start.2
  170.5 0.6 collective-permute-start.3
  171.1 2.7 %collective-permute-start.4 = (bf16[416,128]{1,0:T(8,128)(2,1)}, bf16[416,128]{1,0:T(8,128)(2,1)S(1)}, u32[]{:S(2)}, u32[]{:S(2)}) collective-permute-start(bf16[416,128]{1,0:T(8,128)(2,1)} %get-tuple-element.44), channel_id=1, source_target_pairs={{0,48},{16,32},{32,16},{48,0},{64,112},{80,96},{96,80},{112,64},{1... | collective-permute-start | bytes 319496 | tf_op jit(solution)/shard_map/ppermute | solution.py:574
  173.8 4.2 %collective-permute-done.3.three = bf16[416,128]{1,0:T(8,128)(2,1)S(1)} collective-permute-done((bf16[416,128]{1,0:T(8,128)(2,1)}, bf16[416,128]{1,0:T(8,128)(2,1)S(1)}, u32[]{:S(2)}, u32[]{:S(2)}) %collective-permute-start.3) | collective-permute-done | bytes 106528 | tf_op jit(solution)/shard_map/ppermute | solution.py:574
  178.0 1.4 collective-permute-done.4.four
  179.4 0.6 copy-done.9
  180.0 1.8 fold_fast.1
  181.9 1.9 collective-permute-start.5
  183.7 3.0 %collective-permute-start.6 = (bf16[128,128]{1,0:T(8,128)(2,1)}, bf16[128,128]{1,0:T(8,128)(2,1)S(1)}, u32[]{:S(2)}, u32[]{:S(2)}) collective-permute-start(bf16[128,128]{1,0:T(8,128)(2,1)} %get-tuple-element.47), channel_id=1, source_target_pairs={{0,128},{16,144},{32,160},{48,176},{64,192},{80,208},{96,224},{112... | collective-permute-start | bytes 98312 | tf_op jit(solution)/shard_map/ppermute | solution.py:574
  186.7 3.1 %collective-permute-done.6.refs_2_ = bf16[128,128]{1,0:T(8,128)(2,1)S(1)} collective-permute-done((bf16[128,128]{1,0:T(8,128)(2,1)}, bf16[128,128]{1,0:T(8,128)(2,1)S(1)}, u32[]{:S(2)}, u32[]{:S(2)}) %collective-permute-start.6) | collective-permute-done | bytes 32800 | tf_op jit(solution)/shard_map/ppermute | solution.py:574
  189.9 2.2 %collective-permute-done.7.refs_3_ = bf16[128,128]{1,0:T(8,128)(2,1)S(1)} collective-permute-done((bf16[128,128]{1,0:T(8,128)(2,1)}, bf16[128,128]{1,0:T(8,128)(2,1)S(1)}, u32[]{:S(2)}, u32[]{:S(2)}) %collective-permute-start.7) | collective-permute-done | bytes 32800 | tf_op jit(solution)/shard_map/ppermute | solution.py:574
  192.1 0.6 copy-done.13
  192.7 1.9 fold_slow.1
  194.6 6.8 %all-to-all-start.4 = ((bf16[16,64,128]{2,1,0:T(8,128)(2,1)}), bf16[16,64,128]{2,1,0:T(8,128)(2,1)S(1)}, u32[]{:S(2)}, u32[]{:S(2)}) async-start(bf16[16,64,128]{2,1,0:T(8,128)(2,1)} %get-tuple-element.52), calls=%async_computation.6 | async-start | bytes 524288 | tf_op jit(solution)/shard_map/all_to_all | solution.py:622
  201.4 6.4 %input_gradient.1 = bf16[128,1024]{1,0:T(8,128)(2,1)} custom-call(bf16[16,192,128]{2,1,0:T(8,128)(2,1)} %copy-done.2, bf16[1024,3072]{1,0:T(8,128)(2,1)} %weight_ref.3, bf16[128,1024]{1,0:T(8,128)(2,1)} %bitcast.19, f32[128,1024]{1,0:T(8,128)} %get-tuple-element.39.res_grad_ref), custom_call_target="tpu_custom_call" | custom-call | tf_op jit(solution)/shard_map/input_gradient/pallas_call | solution.py:385
  207.8 0.1 copy.12
  207.9 0.7 copy.13
  208.6 2.4 %all-to-all-done.4.refs_0_ = bf16[16,64,128]{2,1,0:T(8,128)(2,1)S(1)} async-done(((bf16[16,64,128]{2,1,0:T(8,128)(2,1)}), bf16[16,64,128]{2,1,0:T(8,128)(2,1)S(1)}, u32[]{:S(2)}, u32[]{:S(2)}) %all-to-all-start.4) | async-done | bytes 262176 | tf_op jit(solution)/shard_map/all_to_all | solution.py:622
  211.1 0.7 copy-done.4
  211.8 1.8 finish.1
  (35 shorter events, 0.1 us)
Async XLA Ops:
  7.2 110.7 %all-gather.2.cloned.1.call-start = ((), (), s32[]{:S(2)}) async-start(), calls=%async_computation.7 | async-start | bytes 4456448 | tf_op jit(solution)/shard_map/all_gather | solution.py:600
  7.2 17.9 %copy-start.1 = (bf16[1,128,1024]{2,1,0:T(8,128)(2,1)S(1)}, bf16[1,128,1024]{2,1,0:T(8,128)(2,1)}, u32[]{:S(2)}) copy-start(bf16[1,128,1024]{2,1,0:T(8,128)(2,1)} %param.6) | copy-start | bytes 786436
  7.2 17.9 %copy-start.6 = (bf16[1,128,1024]{2,1,0:T(8,128)(2,1)S(1)}, bf16[1,128,1024]{2,1,0:T(8,128)(2,1)}, u32[]{:S(2)}) copy-start(bf16[1,128,1024]{2,1,0:T(8,128)(2,1)} %param.7) | copy-start | bytes 786436
  14.2 35.5 %all-to-all-start = ((bf16[16,192,128]{2,1,0:T(8,128)(2,1)}), bf16[16,192,128]{2,1,0:T(8,128)(2,1)S(1)}, u32[]{:S(2)}, u32[]{:S(2)}) async-start(bf16[16,192,128]{2,1,0:T(8,128)(2,1)} %get-tuple-element.30), calls=%async_computation | async-start | bytes 1572864 | tf_op jit(solution)/shard_map/all_to_all | solution.py:599
  49.7 0.9 copy-start.5
  63.5 26.5 %all-to-all-start.1 = ((bf16[16,96,128]{2,1,0:T(8,128)(2,1)}), bf16[16,96,128]{2,1,0:T(8,128)(2,1)S(1)}, u32[]{:S(2)}, u32[]{:S(2)}) async-start(bf16[16,96,128]{2,1,0:T(8,128)(2,1)} %get-tuple-element.31), calls=%async_computation.1 | async-start | bytes 786432 | tf_op jit(solution)/shard_map/all_to_all | solution.py:602
  70.5 18.8 %collective-permute-start.1 = (bf16[64,1024]{1,0:T(8,128)(2,1)S(1)}, bf16[64,1024]{1,0:T(8,128)(2,1)S(1)}, u32[]{:S(2)}, u32[]{:S(2)}) collective-permute-start(bf16[64,1024]{1,0:T(8,128)(2,1)S(1)} %pad_maximum_fusion.1), channel_id=1, source_target_pairs={{1,0},{2,1},{3,2},{4,3},{5,4},{6,5},{7,6},{8,7},{9,8},{10,9},{11,1... | collective-permute-start | bytes 393224 | tf_op jit(solution)/shard_map/ppermute | solution.py:594
  72.5 16.7 %collective-permute-start = (bf16[64,1024]{1,0:T(8,128)(2,1)S(1)}, bf16[64,1024]{1,0:T(8,128)(2,1)S(1)}, u32[]{:S(2)}, u32[]{:S(2)}) collective-permute-start(bf16[64,1024]{1,0:T(8,128)(2,1)S(1)} %pad_maximum_fusion), channel_id=1, source_target_pairs={{0,1},{1,2},{2,3},{3,4},{4,5},{5,6},{6,7},{7,8},{8,9},{9,10},{10,1... | collective-permute-start | bytes 393224 | tf_op jit(solution)/shard_map/ppermute | solution.py:593
  90.0 0.8 copy-start
  99.6 18.2 %all-to-all-start.2 = ((bf16[16,96,128]{2,1,0:T(8,128)(2,1)}), bf16[16,96,128]{2,1,0:T(8,128)(2,1)S(1)}, u32[]{:S(2)}, u32[]{:S(2)}) async-start(bf16[16,96,128]{2,1,0:T(8,128)(2,1)} %get-tuple-element.33), calls=%async_computation.2 | async-start | bytes 786432 | tf_op jit(solution)/shard_map/all_to_all | solution.py:604
  106.6 58.5 %reduce-scatter.3.cloned.1.call-start = ((), (), s32[]{:S(2)}) async-start(), calls=%async_computation.8 | async-start | bytes 2621440 | tf_op jit(solution)/shard_map/reduce_scatter | solution.py:609
  117.9 0.7 copy-start.3
  133.3 61.3 %all-to-all-start.3 = ((bf16[16,192,128]{2,1,0:T(8,128)(2,1)}), bf16[16,192,128]{2,1,0:T(8,128)(2,1)S(1)}, u32[]{:S(2)}, u32[]{:S(2)}) async-start(bf16[16,192,128]{2,1,0:T(8,128)(2,1)} %attend_back.1.grads_ref), calls=%async_computation.3 | async-start | bytes 1572864 | tf_op jit(solution)/shard_map/all_to_all | solution.py:613
  138.0 54.1 %reduce-scatter.5.cloned.1.call-start = ((), (), s32[]{:S(2)}) async-start(), calls=%async_computation.9 | async-start | bytes 655360 | tf_op jit(solution)/shard_map/reduce_scatter | solution.py:615
  170.4 3.4 %collective-permute-start.2 = (bf16[416,128]{1,0:T(8,128)(2,1)}, bf16[416,128]{1,0:T(8,128)(2,1)S(1)}, u32[]{:S(2)}, u32[]{:S(2)}) collective-permute-start(bf16[416,128]{1,0:T(8,128)(2,1)} %get-tuple-element.42), channel_id=1, source_target_pairs={{0,16},{16,0},{32,48},{48,32},{64,80},{80,64},{96,112},{112,96},{1... | collective-permute-start | bytes 319496 | tf_op jit(solution)/shard_map/ppermute | solution.py:574
  170.5 7.5 %collective-permute-start.3 = (bf16[416,128]{1,0:T(8,128)(2,1)}, bf16[416,128]{1,0:T(8,128)(2,1)S(1)}, u32[]{:S(2)}, u32[]{:S(2)}) collective-permute-start(bf16[416,128]{1,0:T(8,128)(2,1)} %get-tuple-element.43), channel_id=1, source_target_pairs={{0,32},{16,48},{32,0},{48,16},{64,96},{80,112},{96,64},{112,80},{1... | collective-permute-start | bytes 319496 | tf_op jit(solution)/shard_map/ppermute | solution.py:574
  171.1 8.3 %collective-permute-start.4 = (bf16[416,128]{1,0:T(8,128)(2,1)}, bf16[416,128]{1,0:T(8,128)(2,1)S(1)}, u32[]{:S(2)}, u32[]{:S(2)}) collective-permute-start(bf16[416,128]{1,0:T(8,128)(2,1)} %get-tuple-element.44), channel_id=1, source_target_pairs={{0,48},{16,32},{32,16},{48,0},{64,112},{80,96},{96,80},{112,64},{1... | collective-permute-start | bytes 319496 | tf_op jit(solution)/shard_map/ppermute | solution.py:574
  173.8 5.6 %copy-start.7 = (bf16[416,128]{1,0:T(8,128)(2,1)}, bf16[416,128]{1,0:T(8,128)(2,1)S(1)}, u32[]{:S(2)}) copy-start(bf16[416,128]{1,0:T(8,128)(2,1)S(1)} %collective-permute-done.2.two) | copy-start | bytes 319492
  178.0 1.4 copy-start.8
  179.4 0.6 copy-start.9
  181.9 4.9 %collective-permute-start.5 = (bf16[128,128]{1,0:T(8,128)(2,1)}, bf16[128,128]{1,0:T(8,128)(2,1)S(1)}, u32[]{:S(2)}, u32[]{:S(2)}) collective-permute-start(bf16[128,128]{1,0:T(8,128)(2,1)} %get-tuple-element.46), channel_id=1, source_target_pairs={{0,64},{16,80},{32,96},{48,112},{64,0},{80,16},{96,32},{112,48},{1... | collective-permute-start | bytes 98312 | tf_op jit(solution)/shard_map/ppermute | solution.py:574
  183.7 6.1 %collective-permute-start.6 = (bf16[128,128]{1,0:T(8,128)(2,1)}, bf16[128,128]{1,0:T(8,128)(2,1)S(1)}, u32[]{:S(2)}, u32[]{:S(2)}) collective-permute-start(bf16[128,128]{1,0:T(8,128)(2,1)} %get-tuple-element.47), channel_id=1, source_target_pairs={{0,128},{16,144},{32,160},{48,176},{64,192},{80,208},{96,224},{112... | collective-permute-start | bytes 98312 | tf_op jit(solution)/shard_map/ppermute | solution.py:574
  186.7 5.3 %collective-permute-start.7 = (bf16[128,128]{1,0:T(8,128)(2,1)}, bf16[128,128]{1,0:T(8,128)(2,1)S(1)}, u32[]{:S(2)}, u32[]{:S(2)}) collective-permute-start(bf16[128,128]{1,0:T(8,128)(2,1)} %get-tuple-element.48), channel_id=1, source_target_pairs={{0,192},{16,208},{32,224},{48,240},{64,128},{80,144},{96,160},{112... | collective-permute-start | bytes 98312 | tf_op jit(solution)/shard_map/ppermute | solution.py:574
  186.7 5.3 %copy-start.11 = (bf16[128,128]{1,0:T(8,128)(2,1)}, bf16[128,128]{1,0:T(8,128)(2,1)S(1)}, u32[]{:S(2)}) copy-start(bf16[128,128]{1,0:T(8,128)(2,1)S(1)} %collective-permute-done.5.refs_1_) | copy-start | bytes 98308
  189.9 2.2 %copy-start.12 = (bf16[128,128]{1,0:T(8,128)(2,1)}, bf16[128,128]{1,0:T(8,128)(2,1)S(1)}, u32[]{:S(2)}) copy-start(bf16[128,128]{1,0:T(8,128)(2,1)S(1)} %collective-permute-done.6.refs_2_) | copy-start | bytes 98308
  192.1 0.6 copy-start.13
  194.6 6.8 %copy-start.2 = (bf16[16,192,128]{2,1,0:T(8,128)(2,1)}, bf16[16,192,128]{2,1,0:T(8,128)(2,1)S(1)}, u32[]{:S(2)}) copy-start(bf16[16,192,128]{2,1,0:T(8,128)(2,1)S(1)} %all-to-all-done.3.joined_ref) | copy-start | bytes 2359300
  194.6 16.5 %all-to-all-start.4 = ((bf16[16,64,128]{2,1,0:T(8,128)(2,1)}), bf16[16,64,128]{2,1,0:T(8,128)(2,1)S(1)}, u32[]{:S(2)}, u32[]{:S(2)}) async-start(bf16[16,64,128]{2,1,0:T(8,128)(2,1)} %get-tuple-element.52), calls=%async_computation.6 | async-start | bytes 524288 | tf_op jit(solution)/shard_map/all_to_all | solution.py:622
  201.3 6.5 %copy-start.10 = (f32[64,192]{1,0:T(8,128)S(1)}, f32[64,192]{1,0:T(8,128)}, u32[]{:S(2)}) copy-start(f32[64,192]{1,0:T(8,128)} %get-tuple-element.51) | copy-start | bytes 147460
  211.1 0.7 copy-start.4
Sparse Core Ops, SparseCore 0:
  14.3 93.9 all-gather.1
  118.0 47.0 reduce-scatter.2
  167.8 23.2 reduce-scatter.4

commit v4 on v2

--- a/solution.py
+++ b/solution.py
@@ -42,6 +42,10 @@
 
 def cost(flops, moved, expos=0):
     return pl.CostEstimate(flops=flops, bytes_accessed=moved, transcendentals=expos)
+
+
+def local_memory(array):
+    return pltpu.with_memory_space_constraint(array, pltpu.VMEM)
 
 
 def whole(shape):
@@ -386,7 +390,7 @@
         input_grad_kernel,
         grid=(width // block,),
         in_specs=[
-            whole(joined.shape),
+            pl.BlockSpec(memory_space=pltpu.VMEM),
             pl.BlockSpec((block, w_qkv.shape[1]), lambda j: (j, 0)),
             whole(frames.shape),
             whole(frames.shape),
@@ -399,7 +403,7 @@
         ],
         compiler_params=params(),
         name="input_gradient",
-    )(joined, w_qkv, frames, res_grad)
+    )(local_memory(joined), w_qkv, frames, res_grad)
 
 
 CUT = 96
@@ -410,12 +414,13 @@
 
 
 def out_part_kernel(scalars, att_ref, round_ref, *send_refs):
-    lanes = send_refs[0].shape[2]
+    lanes = send_refs[0].shape[3]
     for k, send_ref in enumerate(send_refs):
-        part = dot(att_ref[scalars[3] ^ k, 0:HD, :], round_ref[...])
-        for c in range(part.shape[1] // lanes):
-            piece = part[:, c * lanes : (c + 1) * lanes]
-            send_ref[0, c * HD : (c + 1) * HD, :] = piece.astype(BF16)
+        for p in range(FAST // 2):
+            part = dot(att_ref[2 * p + (scalars[5] ^ k), 0:HD, :], round_ref[...])
+            for c in range(part.shape[1] // lanes):
+                piece = part[:, c * lanes : (c + 1) * lanes]
+                send_ref[0, p, c * HD : (c + 1) * HD, :] = piece.astype(BF16)
 
 
 def out_part(scalars, att, rounded):
@@ -428,8 +433,8 @@
             pl.BlockSpec((FAST, wide, rows), lambda j: (j, 0, 0)),
             whole(rounded.shape),
         ],
-        out_specs=[pl.BlockSpec((1, OUT, 128), lambda j: (j, 0, 0))] * FAST,
-        out_shape=[jax.ShapeDtypeStruct((SLOW, OUT, 128), BF16)] * FAST,
+        out_specs=[pl.BlockSpec((1, FAST // 2, OUT, 128), lambda j: (j, 0, 0, 0))] * 2,
+        out_shape=[jax.ShapeDtypeStruct((SLOW, FAST // 2, OUT, 128), BF16)] * 2,
         compiler_params=params(),
         cost_estimate=cost(2 * heads * HD * 256 * rounded.shape[1], heads * HD * rounded.shape[1] * 2),
         name="out_part",
@@ -485,9 +490,27 @@
     return (own.astype(F32) + one.astype(F32)) + (two.astype(F32) + three.astype(F32))
 
 
+def fold_core_kernel(scalars, one, two, *send_refs):
+    for k, send_ref in enumerate(send_refs):
+        i = scalars[4] ^ k
+        send_ref[...] = (one[i].astype(F32) + two[i].astype(F32)).astype(BF16)
+
+
+def fold_core(scalars, blocks):
+    vmem = pl.BlockSpec(memory_space=pltpu.VMEM)
+    return pl.pallas_call(
+        fold_core_kernel,
+        in_specs=[SMEM] + [vmem] * 2,
+        out_shape=[jax.ShapeDtypeStruct((FAST // 2, OUT, 128), BF16)] * SLOW,
+        compiler_params=params(),
+        cost_estimate=cost(0, 3 * SLOW * FAST // 2 * OUT * 128 * 2),
+        name="fold_core",
+    )(scalars, *blocks)
+
+
 def fold_out_kernel(scalars, one, two, three, four, *send_refs):
     for k, send_ref in enumerate(send_refs):
-        i = scalars[4] ^ k
+        i = scalars[6] ^ k
         send_ref[...] = sum_four(one[i], two[i], three[i], four[i]).astype(BF16)
 
 
@@ -496,9 +519,9 @@
     return pl.pallas_call(
         fold_out_kernel,
         in_specs=[SMEM] + [vmem] * 4,
-        out_shape=[jax.ShapeDtypeStruct((OUT, 128), BF16)] * SLOW,
-        compiler_params=params(),
-        cost_estimate=cost(0, 5 * SLOW * OUT * 128 * 2),
+        out_shape=[jax.ShapeDtypeStruct((OUT, 128), BF16)] * 2,
+        compiler_params=params(),
+        cost_estimate=cost(0, 5 * OUT * 128 * 4),
         name="fold_out",
     )(scalars, *blocks)
 
@@ -527,13 +550,13 @@
 
 
 def fold_slow_kernel(*refs, scale):
-    qkv_ref, send_ref = refs[8:]
+    qkv_ref, send_ref = refs[6:]
     total = sum_four(*(ref[...] for ref in refs[0:4]))
     model_rows = (total[0:CUT] * scale).T
     qkv_ref[:, 0:CUT] = model_rows[0:HD]
     qkv_ref[:, CUT:] = model_rows[HD:]
     pair = halves(joined_halves(total[CUT:]))
-    outer = sum_four(*(ref[...] for ref in refs[4:8]))
+    outer = refs[4][...].astype(F32) + refs[5][...].astype(F32)
     count = send_ref.shape[0]
     each = HD // count
     for i in range(count):
@@ -546,7 +569,7 @@
     vmem = pl.BlockSpec(memory_space=pltpu.VMEM)
     return pl.pallas_call(
         lambda *refs: fold_slow_kernel(*refs, scale=scale),
-        in_specs=[vmem] * 8,
+        in_specs=[vmem] * 6,
         out_shape=[
             jax.ShapeDtypeStruct((HD, 3 * HD), F32),
             jax.ShapeDtypeStruct((seq_count, OUT // seq_count + KW + 1, 128), BF16),
@@ -589,7 +612,9 @@
 
 def exchange(blocks, step):
     pairs = lambda k: [(d, d ^ (step * k)) for d in range(FAST * SLOW)]
-    moved = [lax.ppermute(block, "dp", pairs(k)) for k, block in enumerate(blocks) if k]
+    moved = [
+        local_memory(lax.ppermute(block, "dp", pairs(k))) for k, block in enumerate(blocks) if k
+    ]
     return [blocks[0]] + moved
 
 
@@ -602,7 +627,8 @@
     position = lax.axis_index("dp")
     fast = position % FAST
     slow = position // FAST
-    scalars = jnp.stack([lengths[0], first, jnp.zeros((), jnp.int32), fast, slow])
+    place = [fast, slow, fast % 2, fast // 2]
+    scalars = jnp.stack([lengths[0], first, jnp.zeros((), jnp.int32)] + place)
     x = frames[0]
     g = cotangent[0]
 
@@ -615,23 +641,23 @@
 
     normed, send = project(x, w_qkv)
     heads = lax.all_to_all(send, "seq", 0, 0, tiled=True)
+    heads_near = local_memory(heads)
     normed_all = lax.all_gather(normed, "seq", axis=0, tiled=True)
-    send, out, lse = attend(scalars, heads)
-    att = lax.all_to_all(send, "seq", 0, 0, tiled=True)
+    send, out, lse = attend(scalars, heads_near)
+    att = local_memory(lax.all_to_all(send, "seq", 0, 0, tiled=True))
     output, res_grad, rounded, send = middle(scalars, att, x, x_side, g, g_side, w_out, w_conv)
     back = lax.all_to_all(send, "seq", 0, 0, tiled=True)
-    outer = out_part(scalars, att, rounded)
-    back, outer = lax.optimization_barrier((back, outer))
-    outer = exchange(outer, 1)
-    send = attend_back(scalars, heads, back, out, lse)
+    back, outer = lax.optimization_barrier((back, out_part(scalars, att, rounded)))
+    outer = exchange(fold_core(scalars, exchange(outer, 1)), FAST)
+    send = attend_back(scalars, heads, local_memory(back), out, lse)
     joined = lax.all_to_all(send, "seq", 0, 0, tiled=True)
     parts = exchange(gradient_parts(scalars, send, back, normed_all), 1)
-    outer = exchange(fold_out(scalars, outer), FAST)
+    outer = exchange(fold_out(scalars, outer), 2)
     parts = exchange(fold_fast(scalars, parts), FAST)
     qkv, send = fold_slow(parts, outer, seq_count, grad_scale)
     input_grad = input_gradient(joined, w_qkv, x, res_grad)
     recv = lax.all_to_all(send, "seq", 0, 0, tiled=True)
-    out_total, taps_total = finish(recv, width, grad_scale)
+    out_total, taps_total = finish(local_memory(recv), width, grad_scale)
     return (
         output[None],
         input_grad[None],

time: 227 us -> 200 us (0.88)
  waiting for transfers between devices: 79.4 us -> 58.7 us
  local copies, waits for them, and re-layouts: 6.75 us -> 1.54 us
    ppermute x12 -> x11, waiting for transfers between devices: 31.4 us -> 10.7 us  [exchange(): lax.ppermute(block, 'dp', pairs(k))]
    unnamed x45 -> x13, local copies, waits for them, and re-layouts: 5.99 us -> 0.77 us
    pallas_call x1 -> x2, Pallas kernels: 6.43 us -> 8.62 us  [the longest x1 6.22 us: input_gradient(): pl.pallas_call(input_grad_kernel, grid=(width // block,), in_specs=[pl.Bl...]
    ppermute x12 -> x11, starting transfers between devices: 15.5 us -> 15 us  [exchange(): lax.ppermute(block, 'dp', pairs(k))]
  transfers between devices with their start and end apart: 20 -> 19, of which waited for: 10 -> 9; matrix products, arithmetic and copies ran while one was open for 1% -> 1% of each run, Pallas kernels for 26% -> 29%
where the time goes in v4:
time: 200 us; the launch traced here: 199 us
  Pallas kernels  66.4 us (33%)
  waiting for transfers between devices  58.7 us (29%)
  starting transfers between devices  57 us (28%)
  between operations  14.8 us (7%)
    all_to_all x1, waiting for transfers between devices, local(): heads = lax.all_to_all(send, 'seq', 0, 0, tiled=True)  24.7 us
    ppermute x11, starting transfers between devices, exchange(): lax.ppermute(block, 'dp', pairs(k))  15 us
    pallas_call x1, Pallas kernels, attend_back(): pl.pallas_call(attend_back_kernel, in_specs=[SMEM] + [vmem] * 4, out_shap...  14.7 us
    ppermute x1, waiting for transfers between devices, local(): lax.ppermute(jnp.concatenate([x[-HALO:], g[-HALO:]], axis=0), 'seq', forw...  12.8 us
    pallas_call x1, Pallas kernels, attend(): pl.pallas_call(attend_kernel, in_specs=[SMEM, pl.BlockSpec(memory_space=p...  12.3 us
    ppermute x11, waiting for transfers between devices, exchange(): lax.ppermute(block, 'dp', pairs(k))  10.7 us
    all_to_all x1, starting transfers between devices, local(): heads = lax.all_to_all(send, 'seq', 0, 0, tiled=True)  9.53 us
    pallas_call x1, Pallas kernels, middle(): pl.pallas_call(middle_kernel, in_specs=[SMEM] + [vmem] * 7, out_shape=[ja...  8.86 us
  transfers between devices with their start and end apart: 19, of which 9 were waited for; matrix products, arithmetic and copies ran while one was open for 1% of the time, Pallas kernels for 29%

profile of v4, /device:TPU:32, one launch (start us, length us, event | category | flops | bytes accessed | tf_op | source)
XLA Modules:
  0.0 199.2 jit_solution(13970249928240647705)
XLA Ops:
  7.2 0.0 all-gather.2.cloned.1.call-start
  7.2 0.0 copy-start.2
  7.2 0.0 copy-start.3
  7.2 6.9 %project.1 = (bf16[128,1024]{1,0:T(8,128)(2,1)}, bf16[16,192,128]{2,1,0:T(8,128)(2,1)}) custom-call(bf16[128,1024]{1,0:T(8,128)(2,1)} %bitcast.18, bf16[1024,3072]{1,0:T(8,128)(2,1)} %weight_ref.3), custom_call_target="tpu_custom_call" | custom-call | tf_op jit(solution)/shard_map/project/pallas_call | solution.py:83
  14.2 0.0 all-gather.2.cloned.1.call-update
  14.2 9.5 %all-to-all-start = ((bf16[16,192,128]{2,1,0:T(8,128)(2,1)}), bf16[16,192,128]{2,1,0:T(8,128)(2,1)S(1)}, u32[]{:S(2)}, u32[]{:S(2)}) async-start(bf16[16,192,128]{2,1,0:T(8,128)(2,1)} %get-tuple-element.37), calls=%async_computation | async-start | bytes 1572864 | tf_op jit(solution)/shard_map/all_to_all | solution.py:643
  24.4 0.6 stack.23.scalars
  25.1 24.7 %all-to-all-done.heads_ref = bf16[16,192,128]{2,1,0:T(8,128)(2,1)S(1)} async-done(((bf16[16,192,128]{2,1,0:T(8,128)(2,1)}), bf16[16,192,128]{2,1,0:T(8,128)(2,1)S(1)}, u32[]{:S(2)}, u32[]{:S(2)}) %all-to-all-start) | async-done | bytes 786464 | tf_op jit(solution)/shard_map/all_to_all | solution.py:643
  49.7 12.3 %attend.1 = (bf16[16,96,128]{2,1,0:T(8,128)(2,1)}, f32[64,2048]{1,0:T(8,128)}, f32[1,2048]{1,0:T(1,128)}) custom-call(s32[7]{0:T(128)} %stack.23.scalars, bf16[16,192,128]{2,1,0:T(8,128)(2,1)S(1)} %all-to-all-done.heads_ref), custom_call_target="tpu_custom_call" | custom-call | flops 4294967296 | bytes 786432 | tf_op jit(solution)/shard_map/attend/pallas_call | solution.py:157
  62.1 7.0 %all-to-all-start.1 = ((bf16[16,96,128]{2,1,0:T(8,128)(2,1)}), bf16[16,96,128]{2,1,0:T(8,128)(2,1)S(1)}, u32[]{:S(2)}, u32[]{:S(2)}) async-start(bf16[16,96,128]{2,1,0:T(8,128)(2,1)} %get-tuple-element.38), calls=%async_computation.1 | async-start | bytes 786432 | tf_op jit(solution)/shard_map/all_to_all | solution.py:647
  69.1 3.4 %collective-permute-start = (bf16[64,1024]{1,0:T(8,128)(2,1)S(1)}, bf16[64,1024]{1,0:T(8,128)(2,1)S(1)}, u32[]{:S(2)}, u32[]{:S(2)}) collective-permute-start(bf16[64,1024]{1,0:T(8,128)(2,1)S(1)} %pad_maximum_fusion), channel_id=1, source_target_pairs={{0,1},{1,2},{2,3},{3,4},{4,5},{5,6},{6,7},{7,8},{8,9},{9,10},{10,1... | collective-permute-start | bytes 393224 | tf_op jit(solution)/shard_map/ppermute | solution.py:637
  72.5 2.5 %collective-permute-start.1 = (bf16[64,1024]{1,0:T(8,128)(2,1)S(1)}, bf16[64,1024]{1,0:T(8,128)(2,1)S(1)}, u32[]{:S(2)}, u32[]{:S(2)}) collective-permute-start(bf16[64,1024]{1,0:T(8,128)(2,1)S(1)} %pad_maximum_fusion.1), channel_id=1, source_target_pairs={{1,0},{2,1},{3,2},{4,3},{5,4},{6,5},{7,6},{8,7},{9,8},{10,9},{11,1... | collective-permute-start | bytes 393224 | tf_op jit(solution)/shard_map/ppermute | solution.py:638
  74.9 12.8 %collective-permute-done = bf16[64,1024]{1,0:T(8,128)(2,1)S(1)} collective-permute-done((bf16[64,1024]{1,0:T(8,128)(2,1)S(1)}, bf16[64,1024]{1,0:T(8,128)(2,1)S(1)}, u32[]{:S(2)}, u32[]{:S(2)}) %collective-permute-start) | collective-permute-done | bytes 131104 | tf_op jit(solution)/shard_map/ppermute | solution.py:637
  87.8 0.0 collective-permute-done.1
  87.8 0.7 pad_maximum_fusion.2
  88.5 8.9 %middle.1 = (bf16[128,1024]{1,0:T(8,128)(2,1)}, f32[128,1024]{1,0:T(8,128)}, bf16[128,1024]{1,0:T(8,128)(2,1)}, bf16[16,96,128]{2,1,0:T(8,128)(2,1)}) custom-call(s32[7]{0:T(128)} %stack.23.scalars, bf16[16,96,128]{2,1,0:T(8,128)(2,1)S(1)} %all-to-all-done.1.att_ref, bf16[128,1024]{1,0:T(8,128)(2,1)} %bitcast.19, ...), custom_call_target="tpu_custom_call" | custom-call | tf_op jit(solution)/shard_map/middle/pallas_call | solution.py:272
  97.4 7.3 %all-to-all-start.2 = ((bf16[16,96,128]{2,1,0:T(8,128)(2,1)}), bf16[16,96,128]{2,1,0:T(8,128)(2,1)S(1)}, u32[]{:S(2)}, u32[]{:S(2)}) async-start(bf16[16,96,128]{2,1,0:T(8,128)(2,1)} %get-tuple-element.40), calls=%async_computation.2 | async-start | bytes 786432 | tf_op jit(solution)/shard_map/all_to_all | solution.py:649
  104.6 3.4 %out_part.1 = (bf16[4,2,512,128]{3,2,1,0:T(8,128)(2,1)}, bf16[4,2,512,128]{3,2,1,0:T(8,128)(2,1)}) custom-call(s32[7]{0:T(128)} %stack.23.scalars, bf16[16,96,128]{2,1,0:T(8,128)(2,1)S(1)} %all-to-all-done.1.att_ref, bf16[128,1024]{1,0:T(8,128)(2,1)} %get-tuple-element.41.round_ref), custom_call_target="tpu_custom_call" | custom-call | flops 536870912 | bytes 2097152 | tf_op jit(solution)/shard_map/out_part/pallas_call | solution.py:428
  108.0 8.5 %all-to-all-done.2.grads_ref.back_ref = bf16[16,96,128]{2,1,0:T(8,128)(2,1)S(1)} async-done(((bf16[16,96,128]{2,1,0:T(8,128)(2,1)}), bf16[16,96,128]{2,1,0:T(8,128)(2,1)S(1)}, u32[]{:S(2)}, u32[]{:S(2)}) %all-to-all-start.2) | async-done | bytes 393248 | tf_op jit(solution)/shard_map/all_to_all | solution.py:649
  116.6 14.7 %attend_back.1.grads_ref = bf16[16,192,128]{2,1,0:T(8,128)(2,1)} custom-call(s32[7]{0:T(128)} %stack.23.scalars, bf16[16,192,128]{2,1,0:T(8,128)(2,1)} %copy-done.1, bf16[16,96,128]{2,1,0:T(8,128)(2,1)S(1)} %all-to-all-done.2.grads_ref.back_ref, f32[64,2048]{1,0:T(8,128)} %get-tuple-element.45.out_ref, f32[1,2048]{1,0:T(1,128)} %get-tuple-element.46.lse_ref), custom_call_target="tpu_custom_call" | custom-call | flops 10737418240 | bytes 1572864 | tf_op jit(solution)/shard_map/attend_back/pallas_call | solution.py:343
  131.3 4.8 %all-to-all-start.3 = ((bf16[16,192,128]{2,1,0:T(8,128)(2,1)}), bf16[16,192,128]{2,1,0:T(8,128)(2,1)S(1)}, u32[]{:S(2)}, u32[]{:S(2)}) async-start(bf16[16,192,128]{2,1,0:T(8,128)(2,1)} %attend_back.1.grads_ref), calls=%async_computation.3 | async-start | bytes 1572864 | tf_op jit(solution)/shard_map/all_to_all | solution.py:653
  136.1 0.1 collective-permute-start.8
  136.2 2.6 %collective-permute-done.8.two = bf16[4,2,512,128]{3,2,1,0:T(8,128)(2,1)S(1)} collective-permute-done((bf16[4,2,512,128]{3,2,1,0:T(8,128)(2,1)S(1)}, bf16[4,2,512,128]{3,2,1,0:T(8,128)(2,1)S(1)}, u32[]{:S(2)}, u32[]{:S(2)}) %collective-permute-start.8) | collective-permute-done | bytes 1048608 | tf_op jit(solution)/shard_map/ppermute | solution.py:616
  138.9 2.4 %fold_core.1 = (bf16[2,512,128]{2,1,0:T(8,128)(2,1)}, bf16[2,512,128]{2,1,0:T(8,128)(2,1)}, bf16[2,512,128]{2,1,0:T(8,128)(2,1)}, bf16[2,512,128]{2,1,0:T(8,128)(2,1)}) custom-call(s32[7]{0:T(128)} %stack.23.scalars, bf16[4,2,512,128]{3,2,1,0:T(8,128)(2,1)} %get-tuple-element.57.one, bf16[4,2,512,128]{3,2,1,0:T(8,128)(2,1)S(1)} %collective-permute-done.8.two), custom_call_target="tpu_custom_call" | custom-call | bytes 3145728 | tf_op jit(solution)/shard_map/fold_core/pallas_call | solution.py:501
  141.3 3.6 %collective-permute-start.10 = (bf16[2,512,128]{2,1,0:T(8,128)(2,1)}, bf16[2,512,128]{2,1,0:T(8,128)(2,1)S(1)}, u32[]{:S(2)}, u32[]{:S(2)}) collective-permute-start(bf16[2,512,128]{2,1,0:T(8,128)(2,1)} %get-tuple-element.61), channel_id=1, source_target_pairs={{0,128},{16,144},{32,160},{48,176},{64,192},{80,208},{96,224},{112... | collective-permute-start | bytes 786440 | tf_op jit(solution)/shard_map/ppermute | solution.py:616
  144.9 0.7 collective-permute-start.11
  145.6 5.4 %gradient_parts.1 = (bf16[416,128]{1,0:T(8,128)(2,1)}, bf16[416,128]{1,0:T(8,128)(2,1)}, bf16[416,128]{1,0:T(8,128)(2,1)}, bf16[416,128]{1,0:T(8,128)(2,1)}) custom-call(s32[7]{0:T(128)} %stack.23.scalars, bf16[16,192,128]{2,1,0:T(8,128)(2,1)} %attend_back.1.grads_ref, bf16[16,96,128]{2,1,0:T(8,128)(2,1)} %copy-done, ...), custom_call_target="tpu_custom_call" | custom-call | flops 1073741824 | bytes 4194304 | tf_op jit(solution)/shard_map/gradient_parts/pallas_call | solution.py:471
  151.0 0.0 collective-permute-start.2
  151.0 3.1 %collective-permute-start.3 = (bf16[416,128]{1,0:T(8,128)(2,1)}, bf16[416,128]{1,0:T(8,128)(2,1)S(1)}, u32[]{:S(2)}, u32[]{:S(2)}) collective-permute-start(bf16[416,128]{1,0:T(8,128)(2,1)} %get-tuple-element.51), channel_id=1, source_target_pairs={{0,32},{16,48},{32,0},{48,16},{64,96},{80,112},{96,64},{112,80},{1... | collective-permute-start | bytes 319496 | tf_op jit(solution)/shard_map/ppermute | solution.py:616
  154.1 0.3 collective-permute-start.4
  154.4 3.0 %collective-permute-done.11.four = bf16[2,512,128]{2,1,0:T(8,128)(2,1)S(1)} collective-permute-done((bf16[2,512,128]{2,1,0:T(8,128)(2,1)}, bf16[2,512,128]{2,1,0:T(8,128)(2,1)S(1)}, u32[]{:S(2)}, u32[]{:S(2)}) %collective-permute-start.11) | collective-permute-done | bytes 262176 | tf_op jit(solution)/shard_map/ppermute | solution.py:616
  157.3 0.3 collective-permute-done.9.two
  157.7 1.7 fold_out.1
  159.4 2.6 %collective-permute-start.12 = (bf16[512,128]{1,0:T(8,128)(2,1)}, bf16[512,128]{1,0:T(8,128)(2,1)S(1)}, u32[]{:S(2)}, u32[]{:S(2)}) collective-permute-start(bf16[512,128]{1,0:T(8,128)(2,1)} %get-tuple-element.64), channel_id=1, source_target_pairs={{0,32},{16,48},{32,0},{48,16},{64,96},{80,112},{96,64},{112,80},{1... | collective-permute-start | bytes 393224 | tf_op jit(solution)/shard_map/ppermute | solution.py:616
  162.0 1.7 fold_fast.1
  163.7 1.2 collective-permute-start.5
  165.0 2.9 %collective-permute-start.6 = (bf16[128,128]{1,0:T(8,128)(2,1)}, bf16[128,128]{1,0:T(8,128)(2,1)S(1)}, u32[]{:S(2)}, u32[]{:S(2)}) collective-permute-start(bf16[128,128]{1,0:T(8,128)(2,1)} %get-tuple-element.55), channel_id=1, source_target_pairs={{0,128},{16,144},{32,160},{48,176},{64,192},{80,208},{96,224},{112... | collective-permute-start | bytes 98312 | tf_op jit(solution)/shard_map/ppermute | solution.py:616
  167.8 0.6 collective-permute-start.7
  168.4 0.0 collective-permute-done.12.refs_5_
  168.4 2.2 %collective-permute-done.6.refs_2_ = bf16[128,128]{1,0:T(8,128)(2,1)S(1)} collective-permute-done((bf16[128,128]{1,0:T(8,128)(2,1)}, bf16[128,128]{1,0:T(8,128)(2,1)S(1)}, u32[]{:S(2)}, u32[]{:S(2)}) %collective-permute-start.6) | collective-permute-done | bytes 32800 | tf_op jit(solution)/shard_map/ppermute | solution.py:616
  170.6 2.6 %collective-permute-done.7.refs_3_ = bf16[128,128]{1,0:T(8,128)(2,1)S(1)} collective-permute-done((bf16[128,128]{1,0:T(8,128)(2,1)}, bf16[128,128]{1,0:T(8,128)(2,1)S(1)}, u32[]{:S(2)}, u32[]{:S(2)}) %collective-permute-start.7) | collective-permute-done | bytes 32800 | tf_op jit(solution)/shard_map/ppermute | solution.py:616
  173.1 1.8 fold_slow.1
  175.0 7.5 %all-to-all-start.4 = ((bf16[16,64,128]{2,1,0:T(8,128)(2,1)}), bf16[16,64,128]{2,1,0:T(8,128)(2,1)S(1)}, u32[]{:S(2)}, u32[]{:S(2)}) async-start(bf16[16,64,128]{2,1,0:T(8,128)(2,1)} %get-tuple-element.66), calls=%async_computation.4 | async-start | bytes 524288 | tf_op jit(solution)/shard_map/all_to_all | solution.py:659
  182.5 6.2 %input_gradient.1 = bf16[128,1024]{1,0:T(8,128)(2,1)} custom-call(bf16[16,192,128]{2,1,0:T(8,128)(2,1)S(1)} %all-to-all-done.3.joined_ref, bf16[1024,3072]{1,0:T(8,128)(2,1)} %weight_ref.3, bf16[128,1024]{1,0:T(8,128)(2,1)} %bitcast.20, f32[128,1024]{1,0:T(8,128)} %get-tuple-element.47.res_grad_ref), custom_call_target="tpu_custom_call" | custom-call | tf_op jit(solution)/shard_map/input_gradient/pallas_call | solution.py:389
  188.7 0.1 copy.12
  188.8 0.7 copy.13
  189.6 2.0 all-to-all-done.4.refs_0_
  191.5 0.8 finish.1
  (25 shorter events, 0.1 us)
Async XLA Ops:
  7.2 138.4 %all-gather.2.cloned.1.call-start = ((), (), s32[]{:S(2)}) async-start(), calls=%async_computation.5 | async-start | bytes 4456448 | tf_op jit(solution)/shard_map/all_gather | solution.py:645
  7.2 17.8 %copy-start.2 = (bf16[1,128,1024]{2,1,0:T(8,128)(2,1)S(1)}, bf16[1,128,1024]{2,1,0:T(8,128)(2,1)}, u32[]{:S(2)}) copy-start(bf16[1,128,1024]{2,1,0:T(8,128)(2,1)} %param.6) | copy-start | bytes 786436
  7.2 17.8 %copy-start.3 = (bf16[1,128,1024]{2,1,0:T(8,128)(2,1)S(1)}, bf16[1,128,1024]{2,1,0:T(8,128)(2,1)}, u32[]{:S(2)}) copy-start(bf16[1,128,1024]{2,1,0:T(8,128)(2,1)} %param.7) | copy-start | bytes 786436
  14.2 35.5 %all-to-all-start = ((bf16[16,192,128]{2,1,0:T(8,128)(2,1)}), bf16[16,192,128]{2,1,0:T(8,128)(2,1)S(1)}, u32[]{:S(2)}, u32[]{:S(2)}) async-start(bf16[16,192,128]{2,1,0:T(8,128)(2,1)} %get-tuple-element.37), calls=%async_computation | async-start | bytes 1572864 | tf_op jit(solution)/shard_map/all_to_all | solution.py:643
  49.7 12.3 %copy-start.1 = (bf16[16,192,128]{2,1,0:T(8,128)(2,1)}, bf16[16,192,128]{2,1,0:T(8,128)(2,1)S(1)}, u32[]{:S(2)}) copy-start(bf16[16,192,128]{2,1,0:T(8,128)(2,1)S(1)} %all-to-all-done.heads_ref) | copy-start | bytes 2359300
  62.1 26.5 %all-to-all-start.1 = ((bf16[16,96,128]{2,1,0:T(8,128)(2,1)}), bf16[16,96,128]{2,1,0:T(8,128)(2,1)S(1)}, u32[]{:S(2)}, u32[]{:S(2)}) async-start(bf16[16,96,128]{2,1,0:T(8,128)(2,1)} %get-tuple-element.38), calls=%async_computation.1 | async-start | bytes 786432 | tf_op jit(solution)/shard_map/all_to_all | solution.py:647
  69.1 18.7 %collective-permute-start = (bf16[64,1024]{1,0:T(8,128)(2,1)S(1)}, bf16[64,1024]{1,0:T(8,128)(2,1)S(1)}, u32[]{:S(2)}, u32[]{:S(2)}) collective-permute-start(bf16[64,1024]{1,0:T(8,128)(2,1)S(1)} %pad_maximum_fusion), channel_id=1, source_target_pairs={{0,1},{1,2},{2,3},{3,4},{4,5},{5,6},{6,7},{7,8},{8,9},{9,10},{10,1... | collective-permute-start | bytes 393224 | tf_op jit(solution)/shard_map/ppermute | solution.py:637
  72.5 15.3 %collective-permute-start.1 = (bf16[64,1024]{1,0:T(8,128)(2,1)S(1)}, bf16[64,1024]{1,0:T(8,128)(2,1)S(1)}, u32[]{:S(2)}, u32[]{:S(2)}) collective-permute-start(bf16[64,1024]{1,0:T(8,128)(2,1)S(1)} %pad_maximum_fusion.1), channel_id=1, source_target_pairs={{1,0},{2,1},{3,2},{4,3},{5,4},{6,5},{7,6},{8,7},{9,8},{10,9},{11,1... | collective-permute-start | bytes 393224 | tf_op jit(solution)/shard_map/ppermute | solution.py:638
  97.4 19.2 %all-to-all-start.2 = ((bf16[16,96,128]{2,1,0:T(8,128)(2,1)}), bf16[16,96,128]{2,1,0:T(8,128)(2,1)S(1)}, u32[]{:S(2)}, u32[]{:S(2)}) async-start(bf16[16,96,128]{2,1,0:T(8,128)(2,1)} %get-tuple-element.40), calls=%async_computation.2 | async-start | bytes 786432 | tf_op jit(solution)/shard_map/all_to_all | solution.py:649
  116.6 14.7 %copy-start = (bf16[16,96,128]{2,1,0:T(8,128)(2,1)}, bf16[16,96,128]{2,1,0:T(8,128)(2,1)S(1)}, u32[]{:S(2)}) copy-start(bf16[16,96,128]{2,1,0:T(8,128)(2,1)S(1)} %all-to-all-done.2.grads_ref.back_ref) | copy-start | bytes 1179652
  116.6 19.6 %copy-start.5 = (bf16[4,2,512,128]{3,2,1,0:T(8,128)(2,1)S(1)}, bf16[4,2,512,128]{3,2,1,0:T(8,128)(2,1)}, u32[]{:S(2)}) copy-start(bf16[4,2,512,128]{3,2,1,0:T(8,128)(2,1)} %get-tuple-element.58) | copy-start | bytes 3145732
  131.3 43.7 %all-to-all-start.3 = ((bf16[16,192,128]{2,1,0:T(8,128)(2,1)}), bf16[16,192,128]{2,1,0:T(8,128)(2,1)S(1)}, u32[]{:S(2)}, u32[]{:S(2)}) async-start(bf16[16,192,128]{2,1,0:T(8,128)(2,1)} %attend_back.1.grads_ref), calls=%async_computation.3 | async-start | bytes 1572864 | tf_op jit(solution)/shard_map/all_to_all | solution.py:653
  136.1 2.7 %collective-permute-start.8 = (bf16[4,2,512,128]{3,2,1,0:T(8,128)(2,1)S(1)}, bf16[4,2,512,128]{3,2,1,0:T(8,128)(2,1)S(1)}, u32[]{:S(2)}, u32[]{:S(2)}) collective-permute-start(bf16[4,2,512,128]{3,2,1,0:T(8,128)(2,1)S(1)} %copy-done.5), channel_id=1, source_target_pairs={{0,16},{16,0},{32,48},{48,32},{64,80},{80,64},{96,112},{112,96},{1... | collective-permute-start | bytes 3145736 | tf_op jit(solution)/shard_map/ppermute | solution.py:616
  141.3 12.8 %collective-permute-start.10 = (bf16[2,512,128]{2,1,0:T(8,128)(2,1)}, bf16[2,512,128]{2,1,0:T(8,128)(2,1)S(1)}, u32[]{:S(2)}, u32[]{:S(2)}) collective-permute-start(bf16[2,512,128]{2,1,0:T(8,128)(2,1)} %get-tuple-element.61), channel_id=1, source_target_pairs={{0,128},{16,144},{32,160},{48,176},{64,192},{80,208},{96,224},{112... | collective-permute-start | bytes 786440 | tf_op jit(solution)/shard_map/ppermute | solution.py:616
  144.9 12.4 %collective-permute-start.11 = (bf16[2,512,128]{2,1,0:T(8,128)(2,1)}, bf16[2,512,128]{2,1,0:T(8,128)(2,1)S(1)}, u32[]{:S(2)}, u32[]{:S(2)}) collective-permute-start(bf16[2,512,128]{2,1,0:T(8,128)(2,1)} %get-tuple-element.62), channel_id=1, source_target_pairs={{0,192},{16,208},{32,224},{48,240},{64,128},{80,144},{96,160},{112... | collective-permute-start | bytes 786440 | tf_op jit(solution)/shard_map/ppermute | solution.py:616
  145.6 12.1 %collective-permute-start.9 = (bf16[2,512,128]{2,1,0:T(8,128)(2,1)}, bf16[2,512,128]{2,1,0:T(8,128)(2,1)S(1)}, u32[]{:S(2)}, u32[]{:S(2)}) collective-permute-start(bf16[2,512,128]{2,1,0:T(8,128)(2,1)} %get-tuple-element.60), channel_id=1, source_target_pairs={{0,64},{16,80},{32,96},{48,112},{64,0},{80,16},{96,32},{112,48},{1... | collective-permute-start | bytes 786440 | tf_op jit(solution)/shard_map/ppermute | solution.py:616
  151.0 11.0 %collective-permute-start.2 = (bf16[416,128]{1,0:T(8,128)(2,1)}, bf16[416,128]{1,0:T(8,128)(2,1)S(1)}, u32[]{:S(2)}, u32[]{:S(2)}) collective-permute-start(bf16[416,128]{1,0:T(8,128)(2,1)} %get-tuple-element.50), channel_id=1, source_target_pairs={{0,16},{16,0},{32,48},{48,32},{64,80},{80,64},{96,112},{112,96},{1... | collective-permute-start | bytes 319496 | tf_op jit(solution)/shard_map/ppermute | solution.py:616
  151.0 11.0 %collective-permute-start.3 = (bf16[416,128]{1,0:T(8,128)(2,1)}, bf16[416,128]{1,0:T(8,128)(2,1)S(1)}, u32[]{:S(2)}, u32[]{:S(2)}) collective-permute-start(bf16[416,128]{1,0:T(8,128)(2,1)} %get-tuple-element.51), channel_id=1, source_target_pairs={{0,32},{16,48},{32,0},{48,16},{64,96},{80,112},{96,64},{112,80},{1... | collective-permute-start | bytes 319496 | tf_op jit(solution)/shard_map/ppermute | solution.py:616
  154.1 7.9 %collective-permute-start.4 = (bf16[416,128]{1,0:T(8,128)(2,1)}, bf16[416,128]{1,0:T(8,128)(2,1)S(1)}, u32[]{:S(2)}, u32[]{:S(2)}) collective-permute-start(bf16[416,128]{1,0:T(8,128)(2,1)} %get-tuple-element.52), channel_id=1, source_target_pairs={{0,48},{16,32},{32,16},{48,0},{64,112},{80,96},{96,80},{112,64},{1... | collective-permute-start | bytes 319496 | tf_op jit(solution)/shard_map/ppermute | solution.py:616
  159.4 9.0 %collective-permute-start.12 = (bf16[512,128]{1,0:T(8,128)(2,1)}, bf16[512,128]{1,0:T(8,128)(2,1)S(1)}, u32[]{:S(2)}, u32[]{:S(2)}) collective-permute-start(bf16[512,128]{1,0:T(8,128)(2,1)} %get-tuple-element.64), channel_id=1, source_target_pairs={{0,32},{16,48},{32,0},{48,16},{64,96},{80,112},{96,64},{112,80},{1... | collective-permute-start | bytes 393224 | tf_op jit(solution)/shard_map/ppermute | solution.py:616
  163.7 4.7 %collective-permute-start.5 = (bf16[128,128]{1,0:T(8,128)(2,1)}, bf16[128,128]{1,0:T(8,128)(2,1)S(1)}, u32[]{:S(2)}, u32[]{:S(2)}) collective-permute-start(bf16[128,128]{1,0:T(8,128)(2,1)} %get-tuple-element.54), channel_id=1, source_target_pairs={{0,64},{16,80},{32,96},{48,112},{64,0},{80,16},{96,32},{112,48},{1... | collective-permute-start | bytes 98312 | tf_op jit(solution)/shard_map/ppermute | solution.py:616
  165.0 5.6 %collective-permute-start.6 = (bf16[128,128]{1,0:T(8,128)(2,1)}, bf16[128,128]{1,0:T(8,128)(2,1)S(1)}, u32[]{:S(2)}, u32[]{:S(2)}) collective-permute-start(bf16[128,128]{1,0:T(8,128)(2,1)} %get-tuple-element.55), channel_id=1, source_target_pairs={{0,128},{16,144},{32,160},{48,176},{64,192},{80,208},{96,224},{112... | collective-permute-start | bytes 98312 | tf_op jit(solution)/shard_map/ppermute | solution.py:616
  167.8 5.3 %collective-permute-start.7 = (bf16[128,128]{1,0:T(8,128)(2,1)}, bf16[128,128]{1,0:T(8,128)(2,1)S(1)}, u32[]{:S(2)}, u32[]{:S(2)}) collective-permute-start(bf16[128,128]{1,0:T(8,128)(2,1)} %get-tuple-element.56), channel_id=1, source_target_pairs={{0,192},{16,208},{32,224},{48,240},{64,128},{80,144},{96,160},{112... | collective-permute-start | bytes 98312 | tf_op jit(solution)/shard_map/ppermute | solution.py:616
  175.0 16.6 %all-to-all-start.4 = ((bf16[16,64,128]{2,1,0:T(8,128)(2,1)}), bf16[16,64,128]{2,1,0:T(8,128)(2,1)S(1)}, u32[]{:S(2)}, u32[]{:S(2)}) async-start(bf16[16,64,128]{2,1,0:T(8,128)(2,1)} %get-tuple-element.66), calls=%async_computation.4 | async-start | bytes 524288 | tf_op jit(solution)/shard_map/all_to_all | solution.py:659
  182.5 6.2 %copy-start.4 = (f32[64,192]{1,0:T(8,128)S(1)}, f32[64,192]{1,0:T(8,128)}, u32[]{:S(2)}) copy-start(f32[64,192]{1,0:T(8,128)} %get-tuple-element.65) | copy-start | bytes 147460
Sparse Core Ops, SparseCore 0:
  14.3 95.5 all-gather.1

commit v5 on v4

--- a/solution.py
+++ b/solution.py
@@ -16,6 +16,11 @@
 F32 = jnp.float32
 BF16 = jnp.bfloat16
 LIMIT = 56 * 1024 * 1024
+CUT = 96
+FAST = 4
+SLOW = 4
+TAPS = SLOW * CUT
+OUT = 8 * HD
 
 
 def dot(a, b, ca=1, cb=0):
@@ -185,8 +190,11 @@
     w_conv_ref,
     output_ref,
     res_grad_ref,
-    round_ref,
     send_ref,
+    pack_one,
+    pack_two,
+    pack_three,
+    pack_four,
     taps_ref,
     conv_in,
     grad_all,
@@ -259,7 +267,10 @@
     res_grad = grads_ref[...].astype(F32) + normalize_back(unit, scale, conv_grad[...] * keep)
     res_grad_ref[...] = res_grad
     rounded = res_grad.astype(BF16)
-    round_ref[...] = rounded
+    for k, pack_ref in enumerate((pack_one, pack_two, pack_three, pack_four)):
+        pack_ref[:, 0:width] = rounded
+        picked = [att_ref[FAST * i + (scalars[3] ^ k), 0:HD, :] for i in range(SLOW)]
+        pack_ref[:, width:] = jnp.concatenate(picked, axis=0).T
     back = dot(w_out_ref[...], rounded, 1, 1).astype(BF16)
     send_ref[:, 0:HD, :] = back.reshape(heads, HD, rows)
     for h in range(heads):
@@ -275,9 +286,9 @@
         out_shape=[
             jax.ShapeDtypeStruct((rows, width), BF16),
             jax.ShapeDtypeStruct((rows, width), F32),
-            jax.ShapeDtypeStruct((rows, width), BF16),
             jax.ShapeDtypeStruct((HEADS, HD + KW + 1, rows), BF16),
-        ],
+        ]
+        + [jax.ShapeDtypeStruct((rows, width + SLOW * HD), BF16)] * FAST,
         scratch_shapes=[
             pltpu.VMEM((KW + 1, width), F32),
             pltpu.VMEM((rows + 2 * HALO, width), F32),
@@ -406,39 +417,30 @@
     )(local_memory(joined), w_qkv, frames, res_grad)
 
 
-CUT = 96
-FAST = 4
-SLOW = 4
-TAPS = SLOW * CUT
-OUT = 8 * HD
-
-
-def out_part_kernel(scalars, att_ref, round_ref, *send_refs):
-    lanes = send_refs[0].shape[3]
+def out_part_kernel(scalars, one, two, three, four, *rest):
+    send_refs, part = rest[:SLOW], rest[SLOW]
+    width = send_refs[0].shape[0] // HD * 128
+    packs = (one, two, three, four)
+    left = jnp.concatenate([ref[:, width:] for ref in packs], axis=0)
+    right = jnp.concatenate([ref[:, 0:width] for ref in packs], axis=0)
+    part[...] = dot(left.T, right)
     for k, send_ref in enumerate(send_refs):
-        for p in range(FAST // 2):
-            part = dot(att_ref[2 * p + (scalars[5] ^ k), 0:HD, :], round_ref[...])
-            for c in range(part.shape[1] // lanes):
-                piece = part[:, c * lanes : (c + 1) * lanes]
-                send_ref[0, p, c * HD : (c + 1) * HD, :] = piece.astype(BF16)
-
-
-def out_part(scalars, att, rounded):
-    heads, wide, rows = att.shape
+        rows = pl.ds(pl.multiple_of((scalars[4] ^ k) * HD, HD), HD)
+        for c in range(width // 128):
+            send_ref[c * HD : (c + 1) * HD, :] = part[rows, c * 128 : (c + 1) * 128].astype(BF16)
+
+
+def out_part(scalars, packs):
+    rows, wide = packs[0].shape
+    vmem = pl.BlockSpec(memory_space=pltpu.VMEM)
     return pl.pallas_call(
         out_part_kernel,
-        grid=(SLOW,),
-        in_specs=[
-            SMEM,
-            pl.BlockSpec((FAST, wide, rows), lambda j: (j, 0, 0)),
-            whole(rounded.shape),
-        ],
-        out_specs=[pl.BlockSpec((1, FAST // 2, OUT, 128), lambda j: (j, 0, 0, 0))] * 2,
-        out_shape=[jax.ShapeDtypeStruct((SLOW, FAST // 2, OUT, 128), BF16)] * 2,
-        compiler_params=params(),
-        cost_estimate=cost(2 * heads * HD * 256 * rounded.shape[1], heads * HD * rounded.shape[1] * 2),
+        in_specs=[SMEM] + [vmem] * 4,
+        out_shape=[jax.ShapeDtypeStruct((OUT, 128), BF16)] * SLOW,
+        scratch_shapes=[pltpu.VMEM((SLOW * HD, wide - SLOW * HD), F32)],
+        compiler_params=params(),
         name="out_part",
-    )(scalars, att, rounded)
+    )(scalars, *packs)
 
 
 def parts_kernel(scalars, grads_ref, back_ref, normed_ref, *rest):
@@ -490,42 +492,6 @@
     return (own.astype(F32) + one.astype(F32)) + (two.astype(F32) + three.astype(F32))
 
 
-def fold_core_kernel(scalars, one, two, *send_refs):
-    for k, send_ref in enumerate(send_refs):
-        i = scalars[4] ^ k
-        send_ref[...] = (one[i].astype(F32) + two[i].astype(F32)).astype(BF16)
-
-
-def fold_core(scalars, blocks):
-    vmem = pl.BlockSpec(memory_space=pltpu.VMEM)
-    return pl.pallas_call(
-        fold_core_kernel,
-        in_specs=[SMEM] + [vmem] * 2,
-        out_shape=[jax.ShapeDtypeStruct((FAST // 2, OUT, 128), BF16)] * SLOW,
-        compiler_params=params(),
-        cost_estimate=cost(0, 3 * SLOW * FAST // 2 * OUT * 128 * 2),
-        name="fold_core",
-    )(scalars, *blocks)
-
-
-def fold_out_kernel(scalars, one, two, three, four, *send_refs):
-    for k, send_ref in enumerate(send_refs):
-        i = scalars[6] ^ k
-        send_ref[...] = sum_four(one[i], two[i], three[i], four[i]).astype(BF16)
-
-
-def fold_out(scalars, blocks):
-    vmem = pl.BlockSpec(memory_space=pltpu.VMEM)
-    return pl.pallas_call(
-        fold_out_kernel,
-        in_specs=[SMEM] + [vmem] * 4,
-        out_shape=[jax.ShapeDtypeStruct((OUT, 128), BF16)] * 2,
-        compiler_params=params(),
-        cost_estimate=cost(0, 5 * OUT * 128 * 4),
-        name="fold_out",
-    )(scalars, *blocks)
-
-
 def fold_fast_kernel(scalars, one, two, three, four, *rest):
     send_refs, pieces = rest[:SLOW], rest[SLOW]
     total = sum_four(one[...], two[...], three[...], four[...])
@@ -550,13 +516,13 @@
 
 
 def fold_slow_kernel(*refs, scale):
-    qkv_ref, send_ref = refs[6:]
+    qkv_ref, send_ref = refs[8:]
     total = sum_four(*(ref[...] for ref in refs[0:4]))
     model_rows = (total[0:CUT] * scale).T
     qkv_ref[:, 0:CUT] = model_rows[0:HD]
     qkv_ref[:, CUT:] = model_rows[HD:]
     pair = halves(joined_halves(total[CUT:]))
-    outer = refs[4][...].astype(F32) + refs[5][...].astype(F32)
+    outer = sum_four(*(ref[...] for ref in refs[4:8]))
     count = send_ref.shape[0]
     each = HD // count
     for i in range(count):
@@ -569,7 +535,7 @@
     vmem = pl.BlockSpec(memory_space=pltpu.VMEM)
     return pl.pallas_call(
         lambda *refs: fold_slow_kernel(*refs, scale=scale),
-        in_specs=[vmem] * 6,
+        in_specs=[vmem] * 8,
         out_shape=[
             jax.ShapeDtypeStruct((HD, 3 * HD), F32),
             jax.ShapeDtypeStruct((seq_count, OUT // seq_count + KW + 1, 128), BF16),
@@ -627,7 +593,7 @@
     position = lax.axis_index("dp")
     fast = position % FAST
     slow = position // FAST
-    place = [fast, slow, fast % 2, fast // 2]
+    place = [fast, slow]
     scalars = jnp.stack([lengths[0], first, jnp.zeros((), jnp.int32)] + place)
     x = frames[0]
     g = cotangent[0]
@@ -645,14 +611,13 @@
     normed_all = lax.all_gather(normed, "seq", axis=0, tiled=True)
     send, out, lse = attend(scalars, heads_near)
     att = local_memory(lax.all_to_all(send, "seq", 0, 0, tiled=True))
-    output, res_grad, rounded, send = middle(scalars, att, x, x_side, g, g_side, w_out, w_conv)
+    output, res_grad, send, *packs = middle(scalars, att, x, x_side, g, g_side, w_out, w_conv)
     back = lax.all_to_all(send, "seq", 0, 0, tiled=True)
-    back, outer = lax.optimization_barrier((back, out_part(scalars, att, rounded)))
-    outer = exchange(fold_core(scalars, exchange(outer, 1)), FAST)
+    back, packs = lax.optimization_barrier((back, exchange(packs, 1)))
     send = attend_back(scalars, heads, local_memory(back), out, lse)
     joined = lax.all_to_all(send, "seq", 0, 0, tiled=True)
     parts = exchange(gradient_parts(scalars, send, back, normed_all), 1)
-    outer = exchange(fold_out(scalars, outer), 2)
+    outer = exchange(out_part(scalars, packs), FAST)
     parts = exchange(fold_fast(scalars, parts), FAST)
     qkv, send = fold_slow(parts, outer, seq_count, grad_scale)
     input_grad = input_gradient(joined, w_qkv, x, res_grad)

time: 200 us -> 208 us (1.040)
  waiting for transfers between devices: 58.7 us -> 67.1 us
  Pallas kernels: 66.4 us -> 61.4 us
  starting transfers between devices: 57 us -> 60.7 us
    ppermute x11 -> x12, waiting for transfers between devices: 10.7 us -> 27.2 us  [exchange(): lax.ppermute(block, 'dp', pairs(k))]
    all_to_all x1, waiting for transfers between devices: 8.54 us -> 0.01 us  [local(): back = lax.all_to_all(send, 'seq', 0, 0, tiled=True)]
    pallas_call x3 -> x1, Pallas kernels: 7.53 us -> 2.25 us  [out_part(): pl.pallas_call(out_part_kernel, in_specs=[SMEM] + [vmem] * 4, out_shape=[...]
    all_to_all x1, starting transfers between devices: 4.84 us -> 7.66 us  [local(): joined = lax.all_to_all(send, 'seq', 0, 0, tiled=True)]
    ppermute x11 -> x12, starting transfers between devices: 15 us -> 15.9 us  [exchange(): lax.ppermute(block, 'dp', pairs(k))]
  transfers between devices with their start and end apart: 19 -> 20, of which waited for: 9 -> 10; matrix products, arithmetic and copies ran while one was open for 1% -> 1% of each run, Pallas kernels for 29% -> 26%
where the time goes in v5:
time: 208 us; the launch traced here: 206 us
  waiting for transfers between devices  67.1 us (32%)
  Pallas kernels  61.4 us (30%)
  starting transfers between devices  60.7 us (29%)
  between operations  14.8 us (7%)
    ppermute x12, waiting for transfers between devices, exchange(): lax.ppermute(block, 'dp', pairs(k))  27.2 us
    all_to_all x1, waiting for transfers between devices, local(): heads = lax.all_to_all(send, 'seq', 0, 0, tiled=True)  24.6 us
    ppermute x12, starting transfers between devices, exchange(): lax.ppermute(block, 'dp', pairs(k))  15.9 us
    pallas_call x1, Pallas kernels, attend_back(): pl.pallas_call(attend_back_kernel, in_specs=[SMEM] + [vmem] * 4, out_shap...  14.7 us
    ppermute x1, waiting for transfers between devices, local(): lax.ppermute(jnp.concatenate([x[-HALO:], g[-HALO:]], axis=0), 'seq', forw...  13.1 us
    pallas_call x1, Pallas kernels, attend(): pl.pallas_call(attend_kernel, in_specs=[SMEM, pl.BlockSpec(memory_space=p...  12.3 us
    all_to_all x1, starting transfers between devices, local(): heads = lax.all_to_all(send, 'seq', 0, 0, tiled=True)  9.52 us
    pallas_call x1, Pallas kernels, middle(): pl.pallas_call(middle_kernel, in_specs=[SMEM] + [vmem] * 7, out_shape=[ja...  9.15 us
  transfers between devices with their start and end apart: 20, of which 10 were waited for; matrix products, arithmetic and copies ran while one was open for 1% of the time, Pallas kernels for 26%

profile of v5, /device:TPU:32, one launch (start us, length us, event | category | flops | bytes accessed | tf_op | source)
XLA Modules:
  0.0 206.4 jit_solution(13753966402121106425)
XLA Ops:
  7.2 0.0 all-gather.2.cloned.1.call-start
  7.2 0.0 copy-start.2
  7.2 0.0 copy-start.3
  7.2 6.9 %project.1 = (bf16[128,1024]{1,0:T(8,128)(2,1)}, bf16[16,192,128]{2,1,0:T(8,128)(2,1)}) custom-call(bf16[128,1024]{1,0:T(8,128)(2,1)} %bitcast.16, bf16[1024,3072]{1,0:T(8,128)(2,1)} %weight_ref.3), custom_call_target="tpu_custom_call" | custom-call | tf_op jit(solution)/shard_map/project/pallas_call | solution.py:88
  14.2 0.0 all-gather.2.cloned.1.call-update
  14.2 9.5 %all-to-all-start = ((bf16[16,192,128]{2,1,0:T(8,128)(2,1)}), bf16[16,192,128]{2,1,0:T(8,128)(2,1)S(1)}, u32[]{:S(2)}, u32[]{:S(2)}) async-start(bf16[16,192,128]{2,1,0:T(8,128)(2,1)} %get-tuple-element.38), calls=%async_computation | async-start | bytes 1572864 | tf_op jit(solution)/shard_map/all_to_all | solution.py:609
  24.4 0.7 stack.15.scalars
  25.1 24.6 %all-to-all-done.heads_ref = bf16[16,192,128]{2,1,0:T(8,128)(2,1)S(1)} async-done(((bf16[16,192,128]{2,1,0:T(8,128)(2,1)}), bf16[16,192,128]{2,1,0:T(8,128)(2,1)S(1)}, u32[]{:S(2)}, u32[]{:S(2)}) %all-to-all-start) | async-done | bytes 786464 | tf_op jit(solution)/shard_map/all_to_all | solution.py:609
  49.7 12.3 %attend.1 = (bf16[16,96,128]{2,1,0:T(8,128)(2,1)}, f32[64,2048]{1,0:T(8,128)}, f32[1,2048]{1,0:T(1,128)}) custom-call(s32[5]{0:T(128)} %stack.15.scalars, bf16[16,192,128]{2,1,0:T(8,128)(2,1)S(1)} %all-to-all-done.heads_ref), custom_call_target="tpu_custom_call" | custom-call | flops 4294967296 | bytes 786432 | tf_op jit(solution)/shard_map/attend/pallas_call | solution.py:162
  62.0 7.0 %all-to-all-start.1 = ((bf16[16,96,128]{2,1,0:T(8,128)(2,1)}), bf16[16,96,128]{2,1,0:T(8,128)(2,1)S(1)}, u32[]{:S(2)}, u32[]{:S(2)}) async-start(bf16[16,96,128]{2,1,0:T(8,128)(2,1)} %get-tuple-element.39), calls=%async_computation.1 | async-start | bytes 786432 | tf_op jit(solution)/shard_map/all_to_all | solution.py:613
  69.0 3.4 %collective-permute-start = (bf16[64,1024]{1,0:T(8,128)(2,1)S(1)}, bf16[64,1024]{1,0:T(8,128)(2,1)S(1)}, u32[]{:S(2)}, u32[]{:S(2)}) collective-permute-start(bf16[64,1024]{1,0:T(8,128)(2,1)S(1)} %pad_maximum_fusion), channel_id=1, source_target_pairs={{0,1},{1,2},{2,3},{3,4},{4,5},{5,6},{6,7},{7,8},{8,9},{9,10},{10,1... | collective-permute-start | bytes 393224 | tf_op jit(solution)/shard_map/ppermute | solution.py:603
  72.4 2.5 %collective-permute-start.1 = (bf16[64,1024]{1,0:T(8,128)(2,1)S(1)}, bf16[64,1024]{1,0:T(8,128)(2,1)S(1)}, u32[]{:S(2)}, u32[]{:S(2)}) collective-permute-start(bf16[64,1024]{1,0:T(8,128)(2,1)S(1)} %pad_maximum_fusion.1), channel_id=1, source_target_pairs={{1,0},{2,1},{3,2},{4,3},{5,4},{6,5},{7,6},{8,7},{9,8},{10,9},{11,1... | collective-permute-start | bytes 393224 | tf_op jit(solution)/shard_map/ppermute | solution.py:604
  74.9 13.1 %collective-permute-done = bf16[64,1024]{1,0:T(8,128)(2,1)S(1)} collective-permute-done((bf16[64,1024]{1,0:T(8,128)(2,1)S(1)}, bf16[64,1024]{1,0:T(8,128)(2,1)S(1)}, u32[]{:S(2)}, u32[]{:S(2)}) %collective-permute-start) | collective-permute-done | bytes 131104 | tf_op jit(solution)/shard_map/ppermute | solution.py:603
  88.1 0.0 collective-permute-done.1
  88.1 0.7 pad_maximum_fusion.2
  88.8 0.0 all-to-all-done.1.att_ref
  88.8 9.2 %middle.1 = (bf16[128,1024]{1,0:T(8,128)(2,1)}, f32[128,1024]{1,0:T(8,128)}, bf16[16,96,128]{2,1,0:T(8,128)(2,1)}, bf16[128,1280]{1,0:T(8,128)(2,1)}, bf16[128,1...) custom-call(s32[5]{0:T(128)} %stack.15.scalars, ...), custom_call_target="tpu_custom_call" | custom-call | tf_op jit(solution)/shard_map/middle/pallas_call | solution.py:283
  98.0 6.9 %all-to-all-start.2 = ((bf16[16,96,128]{2,1,0:T(8,128)(2,1)}), bf16[16,96,128]{2,1,0:T(8,128)(2,1)S(1)}, u32[]{:S(2)}, u32[]{:S(2)}) async-start(bf16[16,96,128]{2,1,0:T(8,128)(2,1)} %get-tuple-element.41), calls=%async_computation.2 | async-start | bytes 786432 | tf_op jit(solution)/shard_map/all_to_all | solution.py:615
  104.8 2.8 %collective-permute-start.3 = (bf16[128,1280]{1,0:T(8,128)(2,1)}, bf16[128,1280]{1,0:T(8,128)(2,1)S(1)}, u32[]{:S(2)}, u32[]{:S(2)}) collective-permute-start(bf16[128,1280]{1,0:T(8,128)(2,1)} %get-tuple-element.44), channel_id=1, source_target_pairs={{0,32},{16,48},{32,0},{48,16},{64,96},{80,112},{96,64},{112,80},{1... | collective-permute-start | bytes 983048 | tf_op jit(solution)/shard_map/ppermute | solution.py:582
  107.7 0.5 collective-permute-start.4
  108.2 11.8 %collective-permute-done.3.three = bf16[128,1280]{1,0:T(8,128)(2,1)S(1)} collective-permute-done((bf16[128,1280]{1,0:T(8,128)(2,1)}, bf16[128,1280]{1,0:T(8,128)(2,1)S(1)}, u32[]{:S(2)}, u32[]{:S(2)}) %collective-permute-start.3) | collective-permute-done | bytes 327712 | tf_op jit(solution)/shard_map/ppermute | solution.py:582
  120.1 6.1 %collective-permute-done.4.four = bf16[128,1280]{1,0:T(8,128)(2,1)S(1)} collective-permute-done((bf16[128,1280]{1,0:T(8,128)(2,1)}, bf16[128,1280]{1,0:T(8,128)(2,1)S(1)}, u32[]{:S(2)}, u32[]{:S(2)}) %collective-permute-start.4) | collective-permute-done | bytes 327712 | tf_op jit(solution)/shard_map/ppermute | solution.py:582
  126.2 0.0 all-to-all-done.2.grads_ref.back_ref
  126.2 14.7 %attend_back.1.grads_ref = bf16[16,192,128]{2,1,0:T(8,128)(2,1)} custom-call(s32[5]{0:T(128)} %stack.15.scalars, bf16[16,192,128]{2,1,0:T(8,128)(2,1)} %copy-done.1, bf16[16,96,128]{2,1,0:T(8,128)(2,1)S(1)} %all-to-all-done.2.grads_ref.back_ref, f32[64,2048]{1,0:T(8,128)} %get-tuple-element.47.out_ref, f32[1,2048]{1,0:T(1,128)} %get-tuple-element.48.lse_ref), custom_call_target="tpu_custom_call" | custom-call | flops 10737418240 | bytes 1572864 | tf_op jit(solution)/shard_map/attend_back/pallas_call | solution.py:354
  141.0 7.7 %all-to-all-start.3 = ((bf16[16,192,128]{2,1,0:T(8,128)(2,1)}), bf16[16,192,128]{2,1,0:T(8,128)(2,1)S(1)}, u32[]{:S(2)}, u32[]{:S(2)}) async-start(bf16[16,192,128]{2,1,0:T(8,128)(2,1)} %attend_back.1.grads_ref), calls=%async_computation.3 | async-start | bytes 1572864 | tf_op jit(solution)/shard_map/all_to_all | solution.py:618
  148.6 0.0 all-gather.2.cloned.1.call-done.normed_ref
  148.6 5.3 %gradient_parts.1 = (bf16[416,128]{1,0:T(8,128)(2,1)}, bf16[416,128]{1,0:T(8,128)(2,1)}, bf16[416,128]{1,0:T(8,128)(2,1)}, bf16[416,128]{1,0:T(8,128)(2,1)}) custom-call(s32[5]{0:T(128)} %stack.15.scalars, bf16[16,192,128]{2,1,0:T(8,128)(2,1)} %attend_back.1.grads_ref, bf16[16,96,128]{2,1,0:T(8,128)(2,1)} %copy-done, ...), custom_call_target="tpu_custom_call" | custom-call | flops 1073741824 | bytes 4194304 | tf_op jit(solution)/shard_map/gradient_parts/pallas_call | solution.py:473
  154.0 2.3 %out_part.1 = (bf16[512,128]{1,0:T(8,128)(2,1)}, bf16[512,128]{1,0:T(8,128)(2,1)}, bf16[512,128]{1,0:T(8,128)(2,1)}, bf16[512,128]{1,0:T(8,128)(2,1)}) custom-call(s32[5]{0:T(128)} %stack.15.scalars, bf16[128,1280]{1,0:T(8,128)(2,1)} %get-tuple-element.59.one, bf16[128,1280]{1,0:T(8,128)(2,1)S(1)} %collective-permute-done.2.two, ...), custom_call_target="tpu_custom_call" | custom-call | tf_op jit(solution)/shard_map/out_part/pallas_call | solution.py:436
  156.2 1.6 collective-permute-start.11
  157.9 2.2 %collective-permute-start.6 = (bf16[416,128]{1,0:T(8,128)(2,1)}, bf16[416,128]{1,0:T(8,128)(2,1)S(1)}, u32[]{:S(2)}, u32[]{:S(2)}) collective-permute-start(bf16[416,128]{1,0:T(8,128)(2,1)} %get-tuple-element.53), channel_id=1, source_target_pairs={{0,32},{16,48},{32,0},{48,16},{64,96},{80,112},{96,64},{112,80},{1... | collective-permute-start | bytes 319496 | tf_op jit(solution)/shard_map/ppermute | solution.py:582
  160.1 0.9 collective-permute-start.7
  161.0 2.9 %collective-permute-start.12 = (bf16[512,128]{1,0:T(8,128)(2,1)}, bf16[512,128]{1,0:T(8,128)(2,1)S(1)}, u32[]{:S(2)}, u32[]{:S(2)}) collective-permute-start(bf16[512,128]{1,0:T(8,128)(2,1)} %get-tuple-element.65), channel_id=1, source_target_pairs={{0,128},{16,144},{32,160},{48,176},{64,192},{80,208},{96,224},{112... | collective-permute-start | bytes 393224 | tf_op jit(solution)/shard_map/ppermute | solution.py:582
  163.8 0.2 collective-permute-start.13
  164.0 4.1 %collective-permute-done.6.three = bf16[416,128]{1,0:T(8,128)(2,1)S(1)} collective-permute-done((bf16[416,128]{1,0:T(8,128)(2,1)}, bf16[416,128]{1,0:T(8,128)(2,1)S(1)}, u32[]{:S(2)}, u32[]{:S(2)}) %collective-permute-start.6) | collective-permute-done | bytes 106528 | tf_op jit(solution)/shard_map/ppermute | solution.py:582
  168.1 1.2 collective-permute-done.7.four
  169.4 1.7 fold_fast.1
  171.1 2.9 %collective-permute-start.10 = (bf16[128,128]{1,0:T(8,128)(2,1)}, bf16[128,128]{1,0:T(8,128)(2,1)S(1)}, u32[]{:S(2)}, u32[]{:S(2)}) collective-permute-start(bf16[128,128]{1,0:T(8,128)(2,1)} %get-tuple-element.58), channel_id=1, source_target_pairs={{0,192},{16,208},{32,224},{48,240},{64,128},{80,144},{96,160},{112... | collective-permute-start | bytes 98312 | tf_op jit(solution)/shard_map/ppermute | solution.py:582
  174.0 1.8 collective-permute-start.9
  175.8 0.8 collective-permute-done.10.refs_3_
  176.6 1.5 collective-permute-done.8.refs_1_
  178.1 1.5 collective-permute-done.9.refs_2_
  179.6 1.9 fold_slow.1
  181.6 8.0 %all-to-all-start.4 = ((bf16[16,64,128]{2,1,0:T(8,128)(2,1)}), bf16[16,64,128]{2,1,0:T(8,128)(2,1)S(1)}, u32[]{:S(2)}, u32[]{:S(2)}) async-start(bf16[16,64,128]{2,1,0:T(8,128)(2,1)} %get-tuple-element.68), calls=%async_computation.4 | async-start | bytes 524288 | tf_op jit(solution)/shard_map/all_to_all | solution.py:624
  189.5 6.2 %input_gradient.1 = bf16[128,1024]{1,0:T(8,128)(2,1)} custom-call(bf16[16,192,128]{2,1,0:T(8,128)(2,1)S(1)} %all-to-all-done.3.joined_ref, bf16[1024,3072]{1,0:T(8,128)(2,1)} %weight_ref.3, bf16[128,1024]{1,0:T(8,128)(2,1)} %bitcast.18, f32[128,1024]{1,0:T(8,128)} %get-tuple-element.49.res_grad_ref), custom_call_target="tpu_custom_call" | custom-call | tf_op jit(solution)/shard_map/input_gradient/pallas_call | solution.py:400
  195.7 0.1 copy.12
  195.8 0.7 copy.13
  196.6 2.1 %all-to-all-done.4.refs_0_ = bf16[16,64,128]{2,1,0:T(8,128)(2,1)S(1)} async-done(((bf16[16,64,128]{2,1,0:T(8,128)(2,1)}), bf16[16,64,128]{2,1,0:T(8,128)(2,1)S(1)}, u32[]{:S(2)}, u32[]{:S(2)}) %all-to-all-start.4) | async-done | bytes 262176 | tf_op jit(solution)/shard_map/all_to_all | solution.py:624
  198.7 0.8 finish.1
  (23 shorter events, 0.1 us)
Async XLA Ops:
  7.2 141.5 %all-gather.2.cloned.1.call-start = ((), (), s32[]{:S(2)}) async-start(), calls=%async_computation.5 | async-start | bytes 4456448 | tf_op jit(solution)/shard_map/all_gather | solution.py:611
  7.2 17.8 %copy-start.2 = (bf16[1,128,1024]{2,1,0:T(8,128)(2,1)S(1)}, bf16[1,128,1024]{2,1,0:T(8,128)(2,1)}, u32[]{:S(2)}) copy-start(bf16[1,128,1024]{2,1,0:T(8,128)(2,1)} %param.6) | copy-start | bytes 786436
  7.2 17.8 %copy-start.3 = (bf16[1,128,1024]{2,1,0:T(8,128)(2,1)S(1)}, bf16[1,128,1024]{2,1,0:T(8,128)(2,1)}, u32[]{:S(2)}) copy-start(bf16[1,128,1024]{2,1,0:T(8,128)(2,1)} %param.7) | copy-start | bytes 786436
  14.2 35.5 %all-to-all-start = ((bf16[16,192,128]{2,1,0:T(8,128)(2,1)}), bf16[16,192,128]{2,1,0:T(8,128)(2,1)S(1)}, u32[]{:S(2)}, u32[]{:S(2)}) async-start(bf16[16,192,128]{2,1,0:T(8,128)(2,1)} %get-tuple-element.38), calls=%async_computation | async-start | bytes 1572864 | tf_op jit(solution)/shard_map/all_to_all | solution.py:609
  49.7 12.3 %copy-start.1 = (bf16[16,192,128]{2,1,0:T(8,128)(2,1)}, bf16[16,192,128]{2,1,0:T(8,128)(2,1)S(1)}, u32[]{:S(2)}) copy-start(bf16[16,192,128]{2,1,0:T(8,128)(2,1)S(1)} %all-to-all-done.heads_ref) | copy-start | bytes 2359300
  62.0 26.8 %all-to-all-start.1 = ((bf16[16,96,128]{2,1,0:T(8,128)(2,1)}), bf16[16,96,128]{2,1,0:T(8,128)(2,1)S(1)}, u32[]{:S(2)}, u32[]{:S(2)}) async-start(bf16[16,96,128]{2,1,0:T(8,128)(2,1)} %get-tuple-element.39), calls=%async_computation.1 | async-start | bytes 786432 | tf_op jit(solution)/shard_map/all_to_all | solution.py:613
  69.0 19.0 %collective-permute-start = (bf16[64,1024]{1,0:T(8,128)(2,1)S(1)}, bf16[64,1024]{1,0:T(8,128)(2,1)S(1)}, u32[]{:S(2)}, u32[]{:S(2)}) collective-permute-start(bf16[64,1024]{1,0:T(8,128)(2,1)S(1)} %pad_maximum_fusion), channel_id=1, source_target_pairs={{0,1},{1,2},{2,3},{3,4},{4,5},{5,6},{6,7},{7,8},{8,9},{9,10},{10,1... | collective-permute-start | bytes 393224 | tf_op jit(solution)/shard_map/ppermute | solution.py:603
  72.4 15.6 %collective-permute-start.1 = (bf16[64,1024]{1,0:T(8,128)(2,1)S(1)}, bf16[64,1024]{1,0:T(8,128)(2,1)S(1)}, u32[]{:S(2)}, u32[]{:S(2)}) collective-permute-start(bf16[64,1024]{1,0:T(8,128)(2,1)S(1)} %pad_maximum_fusion.1), channel_id=1, source_target_pairs={{1,0},{2,1},{3,2},{4,3},{5,4},{6,5},{7,6},{8,7},{9,8},{10,9},{11,1... | collective-permute-start | bytes 393224 | tf_op jit(solution)/shard_map/ppermute | solution.py:604
  98.0 28.3 %all-to-all-start.2 = ((bf16[16,96,128]{2,1,0:T(8,128)(2,1)}), bf16[16,96,128]{2,1,0:T(8,128)(2,1)S(1)}, u32[]{:S(2)}, u32[]{:S(2)}) async-start(bf16[16,96,128]{2,1,0:T(8,128)(2,1)} %get-tuple-element.41), calls=%async_computation.2 | async-start | bytes 786432 | tf_op jit(solution)/shard_map/all_to_all | solution.py:615
  104.8 3.4 %collective-permute-start.2 = (bf16[128,1280]{1,0:T(8,128)(2,1)}, bf16[128,1280]{1,0:T(8,128)(2,1)S(1)}, u32[]{:S(2)}, u32[]{:S(2)}) collective-permute-start(bf16[128,1280]{1,0:T(8,128)(2,1)} %get-tuple-element.43), channel_id=1, source_target_pairs={{0,16},{16,0},{32,48},{48,32},{64,80},{80,64},{96,112},{112,96},{1... | collective-permute-start | bytes 983048 | tf_op jit(solution)/shard_map/ppermute | solution.py:582
  104.8 15.2 %collective-permute-start.3 = (bf16[128,1280]{1,0:T(8,128)(2,1)}, bf16[128,1280]{1,0:T(8,128)(2,1)S(1)}, u32[]{:S(2)}, u32[]{:S(2)}) collective-permute-start(bf16[128,1280]{1,0:T(8,128)(2,1)} %get-tuple-element.44), channel_id=1, source_target_pairs={{0,32},{16,48},{32,0},{48,16},{64,96},{80,112},{96,64},{112,80},{1... | collective-permute-start | bytes 983048 | tf_op jit(solution)/shard_map/ppermute | solution.py:582
  107.7 18.5 %collective-permute-start.4 = (bf16[128,1280]{1,0:T(8,128)(2,1)}, bf16[128,1280]{1,0:T(8,128)(2,1)S(1)}, u32[]{:S(2)}, u32[]{:S(2)}) collective-permute-start(bf16[128,1280]{1,0:T(8,128)(2,1)} %get-tuple-element.45), channel_id=1, source_target_pairs={{0,48},{16,32},{32,16},{48,0},{64,112},{80,96},{96,80},{112,64},{1... | collective-permute-start | bytes 983048 | tf_op jit(solution)/shard_map/ppermute | solution.py:582
  126.2 14.7 %copy-start = (bf16[16,96,128]{2,1,0:T(8,128)(2,1)}, bf16[16,96,128]{2,1,0:T(8,128)(2,1)S(1)}, u32[]{:S(2)}) copy-start(bf16[16,96,128]{2,1,0:T(8,128)(2,1)S(1)} %all-to-all-done.2.grads_ref.back_ref) | copy-start | bytes 1179652
  141.0 40.6 %all-to-all-start.3 = ((bf16[16,192,128]{2,1,0:T(8,128)(2,1)}), bf16[16,192,128]{2,1,0:T(8,128)(2,1)S(1)}, u32[]{:S(2)}, u32[]{:S(2)}) async-start(bf16[16,192,128]{2,1,0:T(8,128)(2,1)} %attend_back.1.grads_ref), calls=%async_computation.3 | async-start | bytes 1572864 | tf_op jit(solution)/shard_map/all_to_all | solution.py:618
  154.0 9.9 %collective-permute-start.5 = (bf16[416,128]{1,0:T(8,128)(2,1)}, bf16[416,128]{1,0:T(8,128)(2,1)S(1)}, u32[]{:S(2)}, u32[]{:S(2)}) collective-permute-start(bf16[416,128]{1,0:T(8,128)(2,1)} %get-tuple-element.52), channel_id=1, source_target_pairs={{0,16},{16,0},{32,48},{48,32},{64,80},{80,64},{96,112},{112,96},{1... | collective-permute-start | bytes 319496 | tf_op jit(solution)/shard_map/ppermute | solution.py:582
  156.2 17.8 %collective-permute-start.11 = (bf16[512,128]{1,0:T(8,128)(2,1)}, bf16[512,128]{1,0:T(8,128)(2,1)S(1)}, u32[]{:S(2)}, u32[]{:S(2)}) collective-permute-start(bf16[512,128]{1,0:T(8,128)(2,1)} %get-tuple-element.64), channel_id=1, source_target_pairs={{0,64},{16,80},{32,96},{48,112},{64,0},{80,16},{96,32},{112,48},{1... | collective-permute-start | bytes 393224 | tf_op jit(solution)/shard_map/ppermute | solution.py:582
  157.9 10.3 %collective-permute-start.6 = (bf16[416,128]{1,0:T(8,128)(2,1)}, bf16[416,128]{1,0:T(8,128)(2,1)S(1)}, u32[]{:S(2)}, u32[]{:S(2)}) collective-permute-start(bf16[416,128]{1,0:T(8,128)(2,1)} %get-tuple-element.53), channel_id=1, source_target_pairs={{0,32},{16,48},{32,0},{48,16},{64,96},{80,112},{96,64},{112,80},{1... | collective-permute-start | bytes 319496 | tf_op jit(solution)/shard_map/ppermute | solution.py:582
  160.1 9.3 %collective-permute-start.7 = (bf16[416,128]{1,0:T(8,128)(2,1)}, bf16[416,128]{1,0:T(8,128)(2,1)S(1)}, u32[]{:S(2)}, u32[]{:S(2)}) collective-permute-start(bf16[416,128]{1,0:T(8,128)(2,1)} %get-tuple-element.54), channel_id=1, source_target_pairs={{0,48},{16,32},{32,16},{48,0},{64,112},{80,96},{96,80},{112,64},{1... | collective-permute-start | bytes 319496 | tf_op jit(solution)/shard_map/ppermute | solution.py:582
  161.0 14.8 %collective-permute-start.12 = (bf16[512,128]{1,0:T(8,128)(2,1)}, bf16[512,128]{1,0:T(8,128)(2,1)S(1)}, u32[]{:S(2)}, u32[]{:S(2)}) collective-permute-start(bf16[512,128]{1,0:T(8,128)(2,1)} %get-tuple-element.65), channel_id=1, source_target_pairs={{0,128},{16,144},{32,160},{48,176},{64,192},{80,208},{96,224},{112... | collective-permute-start | bytes 393224 | tf_op jit(solution)/shard_map/ppermute | solution.py:582
  163.8 11.9 %collective-permute-start.13 = (bf16[512,128]{1,0:T(8,128)(2,1)}, bf16[512,128]{1,0:T(8,128)(2,1)S(1)}, u32[]{:S(2)}, u32[]{:S(2)}) collective-permute-start(bf16[512,128]{1,0:T(8,128)(2,1)} %get-tuple-element.66), channel_id=1, source_target_pairs={{0,192},{16,208},{32,224},{48,240},{64,128},{80,144},{96,160},{112... | collective-permute-start | bytes 393224 | tf_op jit(solution)/shard_map/ppermute | solution.py:582
  171.1 5.5 %collective-permute-start.10 = (bf16[128,128]{1,0:T(8,128)(2,1)}, bf16[128,128]{1,0:T(8,128)(2,1)S(1)}, u32[]{:S(2)}, u32[]{:S(2)}) collective-permute-start(bf16[128,128]{1,0:T(8,128)(2,1)} %get-tuple-element.58), channel_id=1, source_target_pairs={{0,192},{16,208},{32,224},{48,240},{64,128},{80,144},{96,160},{112... | collective-permute-start | bytes 98312 | tf_op jit(solution)/shard_map/ppermute | solution.py:582
  174.0 4.1 %collective-permute-start.8 = (bf16[128,128]{1,0:T(8,128)(2,1)}, bf16[128,128]{1,0:T(8,128)(2,1)S(1)}, u32[]{:S(2)}, u32[]{:S(2)}) collective-permute-start(bf16[128,128]{1,0:T(8,128)(2,1)} %get-tuple-element.56), channel_id=1, source_target_pairs={{0,64},{16,80},{32,96},{48,112},{64,0},{80,16},{96,32},{112,48},{1... | collective-permute-start | bytes 98312 | tf_op jit(solution)/shard_map/ppermute | solution.py:582
  174.0 5.6 %collective-permute-start.9 = (bf16[128,128]{1,0:T(8,128)(2,1)}, bf16[128,128]{1,0:T(8,128)(2,1)S(1)}, u32[]{:S(2)}, u32[]{:S(2)}) collective-permute-start(bf16[128,128]{1,0:T(8,128)(2,1)} %get-tuple-element.57), channel_id=1, source_target_pairs={{0,128},{16,144},{32,160},{48,176},{64,192},{80,208},{96,224},{112... | collective-permute-start | bytes 98312 | tf_op jit(solution)/shard_map/ppermute | solution.py:582
  181.6 17.1 %all-to-all-start.4 = ((bf16[16,64,128]{2,1,0:T(8,128)(2,1)}), bf16[16,64,128]{2,1,0:T(8,128)(2,1)S(1)}, u32[]{:S(2)}, u32[]{:S(2)}) async-start(bf16[16,64,128]{2,1,0:T(8,128)(2,1)} %get-tuple-element.68), calls=%async_computation.4 | async-start | bytes 524288 | tf_op jit(solution)/shard_map/all_to_all | solution.py:624
  189.5 6.2 %copy-start.4 = (f32[64,192]{1,0:T(8,128)S(1)}, f32[64,192]{1,0:T(8,128)}, u32[]{:S(2)}) copy-start(f32[64,192]{1,0:T(8,128)} %get-tuple-element.67) | copy-start | bytes 147460
Sparse Core Ops, SparseCore 0:
  14.3 94.1 all-gather.1

commit v6 on v5

--- a/solution.py
+++ b/solution.py
@@ -20,6 +20,7 @@
 FAST = 4
 SLOW = 4
 TAPS = SLOW * CUT
+PARTS = TAPS + KW + 1
 OUT = 8 * HD
 
 
@@ -269,8 +270,9 @@
     rounded = res_grad.astype(BF16)
     for k, pack_ref in enumerate((pack_one, pack_two, pack_three, pack_four)):
         pack_ref[:, 0:width] = rounded
-        picked = [att_ref[FAST * i + (scalars[3] ^ k), 0:HD, :] for i in range(SLOW)]
-        pack_ref[:, width:] = jnp.concatenate(picked, axis=0).T
+        first_head = pl.multiple_of((scalars[4] ^ k) * FAST, FAST)
+        picked = att_ref[pl.ds(first_head, FAST), 0:HD, :]
+        pack_ref[:, width:] = picked.reshape(FAST * HD, rows).T
     back = dot(w_out_ref[...], rounded, 1, 1).astype(BF16)
     send_ref[:, 0:HD, :] = back.reshape(heads, HD, rows)
     for h in range(heads):
@@ -288,7 +290,7 @@
             jax.ShapeDtypeStruct((rows, width), F32),
             jax.ShapeDtypeStruct((HEADS, HD + KW + 1, rows), BF16),
         ]
-        + [jax.ShapeDtypeStruct((rows, width + SLOW * HD), BF16)] * FAST,
+        + [jax.ShapeDtypeStruct((rows, width + FAST * HD), BF16)] * SLOW,
         scratch_shapes=[
             pltpu.VMEM((KW + 1, width), F32),
             pltpu.VMEM((rows + 2 * HALO, width), F32),
@@ -417,38 +419,14 @@
     )(local_memory(joined), w_qkv, frames, res_grad)
 
 
-def out_part_kernel(scalars, one, two, three, four, *rest):
-    send_refs, part = rest[:SLOW], rest[SLOW]
-    width = send_refs[0].shape[0] // HD * 128
+def parts_kernel(scalars, grads_ref, back_ref, normed_ref, one, two, three, four, *rest):
+    send_refs, columns, pieces, left, outer = rest[:FAST], *rest[FAST:]
     packs = (one, two, three, four)
-    left = jnp.concatenate([ref[:, width:] for ref in packs], axis=0)
-    right = jnp.concatenate([ref[:, 0:width] for ref in packs], axis=0)
-    part[...] = dot(left.T, right)
-    for k, send_ref in enumerate(send_refs):
-        rows = pl.ds(pl.multiple_of((scalars[4] ^ k) * HD, HD), HD)
-        for c in range(width // 128):
-            send_ref[c * HD : (c + 1) * HD, :] = part[rows, c * 128 : (c + 1) * 128].astype(BF16)
-
-
-def out_part(scalars, packs):
-    rows, wide = packs[0].shape
-    vmem = pl.BlockSpec(memory_space=pltpu.VMEM)
-    return pl.pallas_call(
-        out_part_kernel,
-        in_specs=[SMEM] + [vmem] * 4,
-        out_shape=[jax.ShapeDtypeStruct((OUT, 128), BF16)] * SLOW,
-        scratch_shapes=[pltpu.VMEM((SLOW * HD, wide - SLOW * HD), F32)],
-        compiler_params=params(),
-        name="out_part",
-    )(scalars, *packs)
-
-
-def parts_kernel(scalars, grads_ref, back_ref, normed_ref, *rest):
-    send_refs, columns, pieces = rest[:FAST], rest[FAST], rest[FAST + 1]
     count, wide, rows = grads_ref.shape
-    slow = pl.program_id(0)
-
-    @pl.when(slow == 0)
+    width = one.shape[1] - FAST * HD
+    step = pl.program_id(0)
+
+    @pl.when(step == 0)
     def _():
         taps = jnp.zeros((KW + 1, rows), F32)
         for i in range(count):
@@ -456,36 +434,50 @@
             taps = taps + back_ref[i, HD:, :].astype(F32)
         pair = halves(joined_halves(taps))
         for send_ref in send_refs:
-            send_ref[TAPS:, :] = pair
+            send_ref[TAPS:PARTS, :] = pair
+        left[...] = jnp.concatenate([ref[:, width:] for ref in packs], axis=0).T
 
     part = dot(columns[...], normed_ref[...])
     each = part.shape[1] // FAST
     for i in range(FAST):
         piece = part[:, i * each : (i + 1) * each]
         pieces[i] = jnp.concatenate([piece[0:CUT], piece[CUT:]], axis=1).astype(BF16)
+    block = width // SLOW
+    lanes = pl.ds(pl.multiple_of(step * block, block), block)
+    outer[...] = dot(left[...], jnp.concatenate([ref[:, lanes] for ref in packs], axis=0))
     for k, send_ref in enumerate(send_refs):
-        send_ref[pl.ds(pl.multiple_of(slow * CUT, CUT), CUT), :] = pieces[scalars[3] ^ k]
-
-
-def gradient_parts(scalars, grads, back, normed_all):
+        send_ref[pl.ds(pl.multiple_of(step * CUT, CUT), CUT), :] = pieces[scalars[3] ^ k]
+        own = pl.ds(pl.multiple_of((scalars[3] ^ k) * HD, HD), HD)
+        for c in range(block // 128):
+            at = pl.multiple_of(PARTS + (step * (block // 128) + c) * HD, 32)
+            send_ref[pl.ds(at, HD), :] = outer[own, c * 128 : (c + 1) * 128].astype(BF16)
+
+
+def gradient_parts(scalars, grads, back, normed_all, packs):
     count, wide, rows = grads.shape
     total, width = normed_all.shape
+    vmem = pl.BlockSpec(memory_space=pltpu.VMEM)
     return pl.pallas_call(
         parts_kernel,
         grid=(SLOW,),
         in_specs=[
             SMEM,
-            whole(grads.shape),
-            whole(back.shape),
+            vmem,
+            vmem,
             pl.BlockSpec((total, width // SLOW), lambda j: (0, j)),
-        ],
-        out_specs=[whole((TAPS + KW + 1, 128))] * FAST,
-        out_shape=[jax.ShapeDtypeStruct((TAPS + KW + 1, 128), BF16)] * FAST,
-        scratch_shapes=[pltpu.VMEM((wide, total), BF16), pltpu.VMEM((FAST, CUT, 128), BF16)],
-        compiler_params=params(),
-        cost_estimate=cost(2 * 256 * total * width, total * width * 2),
+        ]
+        + [vmem] * SLOW,
+        out_specs=[whole((PARTS + OUT, 128))] * FAST,
+        out_shape=[jax.ShapeDtypeStruct((PARTS + OUT, 128), BF16)] * FAST,
+        scratch_shapes=[
+            pltpu.VMEM((wide, total), BF16),
+            pltpu.VMEM((FAST, CUT, 128), BF16),
+            pltpu.VMEM((FAST * HD, SLOW * rows), BF16),
+            pltpu.VMEM((FAST * HD, width // SLOW), F32),
+        ],
+        compiler_params=params(),
         name="gradient_parts",
-    )(scalars, grads, back, normed_all)
+    )(scalars, grads, back, normed_all, *packs)
 
 
 def sum_four(own, one, two, three):
@@ -493,9 +485,10 @@
 
 
 def fold_fast_kernel(scalars, one, two, three, four, *rest):
-    send_refs, pieces = rest[:SLOW], rest[SLOW]
+    send_refs, outer_ref, pieces = rest[:SLOW], *rest[SLOW:]
     total = sum_four(one[...], two[...], three[...], four[...])
-    pair = halves(joined_halves(total[TAPS:]))
+    outer_ref[...] = total[PARTS:]
+    pair = halves(joined_halves(total[TAPS:PARTS]))
     for i in range(SLOW):
         pieces[i] = total[i * CUT : (i + 1) * CUT].astype(BF16)
     for k, send_ref in enumerate(send_refs):
@@ -508,7 +501,8 @@
     return pl.pallas_call(
         fold_fast_kernel,
         in_specs=[SMEM] + [vmem] * 4,
-        out_shape=[jax.ShapeDtypeStruct((CUT + KW + 1, 128), BF16)] * SLOW,
+        out_shape=[jax.ShapeDtypeStruct((CUT + KW + 1, 128), BF16)] * SLOW
+        + [jax.ShapeDtypeStruct((OUT, 128), F32)],
         scratch_shapes=[pltpu.VMEM((SLOW, CUT, 128), BF16)],
         compiler_params=params(),
         name="fold_fast",
@@ -516,13 +510,13 @@
 
 
 def fold_slow_kernel(*refs, scale):
-    qkv_ref, send_ref = refs[8:]
+    qkv_ref, send_ref = refs[5:]
     total = sum_four(*(ref[...] for ref in refs[0:4]))
     model_rows = (total[0:CUT] * scale).T
     qkv_ref[:, 0:CUT] = model_rows[0:HD]
     qkv_ref[:, CUT:] = model_rows[HD:]
     pair = halves(joined_halves(total[CUT:]))
-    outer = sum_four(*(ref[...] for ref in refs[4:8]))
+    outer = refs[4][...]
     count = send_ref.shape[0]
     each = HD // count
     for i in range(count):
@@ -531,18 +525,18 @@
         send_ref[i, OUT // count :, :] = pair
 
 
-def fold_slow(blocks, out_blocks, seq_count, scale):
+def fold_slow(blocks, outer, seq_count, scale):
     vmem = pl.BlockSpec(memory_space=pltpu.VMEM)
     return pl.pallas_call(
         lambda *refs: fold_slow_kernel(*refs, scale=scale),
-        in_specs=[vmem] * 8,
+        in_specs=[vmem] * 5,
         out_shape=[
             jax.ShapeDtypeStruct((HD, 3 * HD), F32),
             jax.ShapeDtypeStruct((seq_count, OUT // seq_count + KW + 1, 128), BF16),
         ],
         compiler_params=params(),
         name="fold_slow",
-    )(*blocks, *out_blocks)
+    )(*blocks, outer)
 
 
 def finish_kernel(recv_ref, out_ref, taps_ref, *, scale):
@@ -613,12 +607,12 @@
     att = local_memory(lax.all_to_all(send, "seq", 0, 0, tiled=True))
     output, res_grad, send, *packs = middle(scalars, att, x, x_side, g, g_side, w_out, w_conv)
     back = lax.all_to_all(send, "seq", 0, 0, tiled=True)
-    back, packs = lax.optimization_barrier((back, exchange(packs, 1)))
+    back, packs = lax.optimization_barrier((back, exchange(packs, FAST)))
     send = attend_back(scalars, heads, local_memory(back), out, lse)
     joined = lax.all_to_all(send, "seq", 0, 0, tiled=True)
-    parts = exchange(gradient_parts(scalars, send, back, normed_all), 1)
-    outer = exchange(out_part(scalars, packs), FAST)
-    parts = exchange(fold_fast(scalars, parts), FAST)
+    parts = exchange(gradient_parts(scalars, send, back, normed_all, packs), 1)
+    *parts, outer = fold_fast(scalars, parts)
+    parts = exchange(parts, FAST)
     qkv, send = fold_slow(parts, outer, seq_count, grad_scale)
     input_grad = input_gradient(joined, w_qkv, x, res_grad)
     recv = lax.all_to_all(send, "seq", 0, 0, tiled=True)

time: 208 us -> 208 us (level)
  waiting for transfers between devices: 67.1 us -> 72.8 us
  starting transfers between devices: 60.7 us -> 57.3 us
    ppermute x1, waiting for transfers between devices: 13.1 us -> 0.46 us  [local(): lax.ppermute(jnp.concatenate([x[-HALO:], g[-HALO:]], axis=0), 'seq', forw...]
    ppermute x1, waiting for transfers between devices: 0.01 us -> 12.6 us  [local(): lax.ppermute(jnp.concatenate([x[:HALO], g[:HALO]], axis=0), 'seq', backward)]
    ppermute x12 -> x9, waiting for transfers between devices: 27.2 us -> 32.8 us  [exchange(): lax.ppermute(block, 'dp', pairs(k))]
    ppermute x12 -> x9, starting transfers between devices: 15.9 us -> 12.8 us  [exchange(): lax.ppermute(block, 'dp', pairs(k))]
    pallas_call x2 -> x1, Pallas kernels: 7.58 us -> 5.96 us  [gradient_parts(): pl.pallas_call(parts_kernel, grid=(SLOW,), in_specs=[SMEM, vmem, vmem, pl...]
  transfers between devices with their start and end apart: 20 -> 17, of which waited for: 10 -> 11; matrix products, arithmetic and copies ran while one was open for 1% -> 1% of each run, Pallas kernels for 26% -> 25%
where the time goes in v6:
time: 208 us; the launch traced here: 207 us
  waiting for transfers between devices  72.8 us (35%)
  Pallas kernels  59.9 us (29%)
  starting transfers between devices  57.3 us (28%)
  between operations  14.8 us (7%)
    ppermute x9, waiting for transfers between devices, exchange(): lax.ppermute(block, 'dp', pairs(k))  32.8 us
    all_to_all x1, waiting for transfers between devices, local(): heads = lax.all_to_all(send, 'seq', 0, 0, tiled=True)  24.7 us
    pallas_call x1, Pallas kernels, attend_back(): pl.pallas_call(attend_back_kernel, in_specs=[SMEM] + [vmem] * 4, out_shap...  14.7 us
    ppermute x9, starting transfers between devices, exchange(): lax.ppermute(block, 'dp', pairs(k))  12.8 us
    ppermute x1, waiting for transfers between devices, local(): lax.ppermute(jnp.concatenate([x[:HALO], g[:HALO]], axis=0), 'seq', backward)  12.6 us
    pallas_call x1, Pallas kernels, attend(): pl.pallas_call(attend_kernel, in_specs=[SMEM, pl.BlockSpec(memory_space=p...  12.3 us
    all_to_all x1, starting transfers between devices, local(): heads = lax.all_to_all(send, 'seq', 0, 0, tiled=True)  9.52 us
    pallas_call x1, Pallas kernels, middle(): pl.pallas_call(middle_kernel, in_specs=[SMEM] + [vmem] * 7, out_shape=[ja...  9.17 us
  transfers between devices with their start and end apart: 17, of which 11 were waited for; matrix products, arithmetic and copies ran while one was open for 1% of the time, Pallas kernels for 25%

profile of v6, /device:TPU:32, one launch (start us, length us, event | category | flops | bytes accessed | tf_op | source)
XLA Modules:
  0.0 207.0 jit_solution(13554386070350704087)
XLA Ops:
  7.2 0.0 all-gather.2.cloned.1.call-start
  7.2 0.0 copy-start.2
  7.2 0.0 copy-start.3
  7.2 6.9 %project.1 = (bf16[128,1024]{1,0:T(8,128)(2,1)}, bf16[16,192,128]{2,1,0:T(8,128)(2,1)}) custom-call(bf16[128,1024]{1,0:T(8,128)(2,1)} %bitcast.16, bf16[1024,3072]{1,0:T(8,128)(2,1)} %weight_ref.3), custom_call_target="tpu_custom_call" | custom-call | tf_op jit(solution)/shard_map/project/pallas_call | solution.py:89
  14.2 0.0 all-gather.2.cloned.1.call-update
  14.2 9.5 %all-to-all-start = ((bf16[16,192,128]{2,1,0:T(8,128)(2,1)}), bf16[16,192,128]{2,1,0:T(8,128)(2,1)S(1)}, u32[]{:S(2)}, u32[]{:S(2)}) async-start(bf16[16,192,128]{2,1,0:T(8,128)(2,1)} %get-tuple-element.35), calls=%async_computation | async-start | bytes 1572864 | tf_op jit(solution)/shard_map/all_to_all | solution.py:603
  24.4 0.6 stack.15.scalars
  25.0 24.7 %all-to-all-done.heads_ref = bf16[16,192,128]{2,1,0:T(8,128)(2,1)S(1)} async-done(((bf16[16,192,128]{2,1,0:T(8,128)(2,1)}), bf16[16,192,128]{2,1,0:T(8,128)(2,1)S(1)}, u32[]{:S(2)}, u32[]{:S(2)}) %all-to-all-start) | async-done | bytes 786464 | tf_op jit(solution)/shard_map/all_to_all | solution.py:603
  49.7 12.3 %attend.1 = (bf16[16,96,128]{2,1,0:T(8,128)(2,1)}, f32[64,2048]{1,0:T(8,128)}, f32[1,2048]{1,0:T(1,128)}) custom-call(s32[5]{0:T(128)} %stack.15.scalars, bf16[16,192,128]{2,1,0:T(8,128)(2,1)S(1)} %all-to-all-done.heads_ref), custom_call_target="tpu_custom_call" | custom-call | flops 4294967296 | bytes 786432 | tf_op jit(solution)/shard_map/attend/pallas_call | solution.py:163
  62.0 7.0 %all-to-all-start.1 = ((bf16[16,96,128]{2,1,0:T(8,128)(2,1)}), bf16[16,96,128]{2,1,0:T(8,128)(2,1)S(1)}, u32[]{:S(2)}, u32[]{:S(2)}) async-start(bf16[16,96,128]{2,1,0:T(8,128)(2,1)} %get-tuple-element.36), calls=%async_computation.1 | async-start | bytes 786432 | tf_op jit(solution)/shard_map/all_to_all | solution.py:607
  69.0 2.0 collective-permute-start.1
  71.1 3.8 %collective-permute-start = (bf16[64,1024]{1,0:T(8,128)(2,1)S(1)}, bf16[64,1024]{1,0:T(8,128)(2,1)S(1)}, u32[]{:S(2)}, u32[]{:S(2)}) collective-permute-start(bf16[64,1024]{1,0:T(8,128)(2,1)S(1)} %pad_maximum_fusion), channel_id=1, source_target_pairs={{0,1},{1,2},{2,3},{3,4},{4,5},{5,6},{6,7},{7,8},{8,9},{9,10},{10,1... | collective-permute-start | bytes 393224 | tf_op jit(solution)/shard_map/ppermute | solution.py:597
  74.9 12.6 %collective-permute-done.1 = bf16[64,1024]{1,0:T(8,128)(2,1)S(1)} collective-permute-done((bf16[64,1024]{1,0:T(8,128)(2,1)S(1)}, bf16[64,1024]{1,0:T(8,128)(2,1)S(1)}, u32[]{:S(2)}, u32[]{:S(2)}) %collective-permute-start.1) | collective-permute-done | bytes 131104 | tf_op jit(solution)/shard_map/ppermute | solution.py:598
  87.6 0.5 collective-permute-done
  88.1 0.7 pad_maximum_fusion.2
  88.8 0.0 all-to-all-done.1.att_ref
  88.8 9.2 %middle.1 = (bf16[128,1024]{1,0:T(8,128)(2,1)}, f32[128,1024]{1,0:T(8,128)}, bf16[16,96,128]{2,1,0:T(8,128)(2,1)}, bf16[128,1280]{1,0:T(8,128)(2,1)}, bf16[128,1...) custom-call(s32[5]{0:T(128)} %stack.15.scalars, ...), custom_call_target="tpu_custom_call" | custom-call | tf_op jit(solution)/shard_map/middle/pallas_call | solution.py:285
  98.0 6.9 %all-to-all-start.2 = ((bf16[16,96,128]{2,1,0:T(8,128)(2,1)}), bf16[16,96,128]{2,1,0:T(8,128)(2,1)S(1)}, u32[]{:S(2)}, u32[]{:S(2)}) async-start(bf16[16,96,128]{2,1,0:T(8,128)(2,1)} %get-tuple-element.38), calls=%async_computation.2 | async-start | bytes 786432 | tf_op jit(solution)/shard_map/all_to_all | solution.py:609
  104.9 1.8 collective-permute-start.2
  106.7 2.8 %collective-permute-start.3 = (bf16[128,1280]{1,0:T(8,128)(2,1)}, bf16[128,1280]{1,0:T(8,128)(2,1)S(1)}, u32[]{:S(2)}, u32[]{:S(2)}) collective-permute-start(bf16[128,1280]{1,0:T(8,128)(2,1)} %get-tuple-element.41), channel_id=1, source_target_pairs={{0,128},{16,144},{32,160},{48,176},{64,192},{80,208},{96,224},{112... | collective-permute-start | bytes 983048 | tf_op jit(solution)/shard_map/ppermute | solution.py:576
  109.5 0.1 collective-permute-start.4
  109.6 6.2 %collective-permute-done.2.two = bf16[128,1280]{1,0:T(8,128)(2,1)S(1)} collective-permute-done((bf16[128,1280]{1,0:T(8,128)(2,1)}, bf16[128,1280]{1,0:T(8,128)(2,1)S(1)}, u32[]{:S(2)}, u32[]{:S(2)}) %collective-permute-start.2) | collective-permute-done | bytes 327712 | tf_op jit(solution)/shard_map/ppermute | solution.py:576
  115.7 6.7 %collective-permute-done.3.three = bf16[128,1280]{1,0:T(8,128)(2,1)S(1)} collective-permute-done((bf16[128,1280]{1,0:T(8,128)(2,1)}, bf16[128,1280]{1,0:T(8,128)(2,1)S(1)}, u32[]{:S(2)}, u32[]{:S(2)}) %collective-permute-start.3) | collective-permute-done | bytes 327712 | tf_op jit(solution)/shard_map/ppermute | solution.py:576
  122.4 2.6 %collective-permute-done.4.four = bf16[128,1280]{1,0:T(8,128)(2,1)S(1)} collective-permute-done((bf16[128,1280]{1,0:T(8,128)(2,1)}, bf16[128,1280]{1,0:T(8,128)(2,1)S(1)}, u32[]{:S(2)}, u32[]{:S(2)}) %collective-permute-start.4) | collective-permute-done | bytes 327712 | tf_op jit(solution)/shard_map/ppermute | solution.py:576
  125.0 0.0 all-to-all-done.2.grads_ref.back_ref
  125.0 14.7 %attend_back.1.grads_ref = bf16[16,192,128]{2,1,0:T(8,128)(2,1)} custom-call(s32[5]{0:T(128)} %stack.15.scalars, bf16[16,192,128]{2,1,0:T(8,128)(2,1)} %copy-done.1, bf16[16,96,128]{2,1,0:T(8,128)(2,1)S(1)} %all-to-all-done.2.grads_ref.back_ref, f32[64,2048]{1,0:T(8,128)} %get-tuple-element.44.out_ref, f32[1,2048]{1,0:T(1,128)} %get-tuple-element.45.lse_ref), custom_call_target="tpu_custom_call" | custom-call | flops 10737418240 | bytes 1572864 | tf_op jit(solution)/shard_map/attend_back/pallas_call | solution.py:356
  139.7 8.1 %all-to-all-start.3 = ((bf16[16,192,128]{2,1,0:T(8,128)(2,1)}), bf16[16,192,128]{2,1,0:T(8,128)(2,1)S(1)}, u32[]{:S(2)}, u32[]{:S(2)}) async-start(bf16[16,192,128]{2,1,0:T(8,128)(2,1)} %attend_back.1.grads_ref), calls=%async_computation.3 | async-start | bytes 1572864 | tf_op jit(solution)/shard_map/all_to_all | solution.py:612
  147.9 0.0 all-gather.2.cloned.1.call-done.normed_ref
  147.9 6.0 %gradient_parts.1 = (bf16[928,128]{1,0:T(8,128)(2,1)}, bf16[928,128]{1,0:T(8,128)(2,1)}, bf16[928,128]{1,0:T(8,128)(2,1)}, bf16[928,128]{1,0:T(8,128)(2,1)}) custom-call(s32[5]{0:T(128)} %stack.15.scalars, bf16[16,192,128]{2,1,0:T(8,128)(2,1)} %attend_back.1.grads_ref, bf16[16,96,128]{2,1,0:T(8,128)(2,1)} %copy-done, ...), custom_call_target="tpu_custom_call" | custom-call | tf_op jit(solution)/shard_map/gradient_parts/pallas_call | solution.py:460
  153.8 0.0 collective-permute-start.5
  153.8 3.0 %collective-permute-start.6 = (bf16[928,128]{1,0:T(8,128)(2,1)}, bf16[928,128]{1,0:T(8,128)(2,1)S(1)}, u32[]{:S(2)}, u32[]{:S(2)}) collective-permute-start(bf16[928,128]{1,0:T(8,128)(2,1)} %get-tuple-element.54), channel_id=1, source_target_pairs={{0,32},{16,48},{32,0},{48,16},{64,96},{80,112},{96,64},{112,80},{1... | collective-permute-start | bytes 712712 | tf_op jit(solution)/shard_map/ppermute | solution.py:576
  156.9 0.3 collective-permute-start.7
  157.2 10.6 %collective-permute-done.6.three = bf16[928,128]{1,0:T(8,128)(2,1)S(1)} collective-permute-done((bf16[928,128]{1,0:T(8,128)(2,1)}, bf16[928,128]{1,0:T(8,128)(2,1)S(1)}, u32[]{:S(2)}, u32[]{:S(2)}) %collective-permute-start.6) | collective-permute-done | bytes 237600 | tf_op jit(solution)/shard_map/ppermute | solution.py:576
  167.8 4.3 %collective-permute-done.7.four = bf16[928,128]{1,0:T(8,128)(2,1)S(1)} collective-permute-done((bf16[928,128]{1,0:T(8,128)(2,1)}, bf16[928,128]{1,0:T(8,128)(2,1)S(1)}, u32[]{:S(2)}, u32[]{:S(2)}) %collective-permute-start.7) | collective-permute-done | bytes 237600 | tf_op jit(solution)/shard_map/ppermute | solution.py:576
  172.1 1.9 fold_fast.1
  174.0 0.0 collective-permute-start.8
  174.0 1.8 collective-permute-start.9
  175.8 2.9 %collective-permute-start.10 = (bf16[128,128]{1,0:T(8,128)(2,1)}, bf16[128,128]{1,0:T(8,128)(2,1)S(1)}, u32[]{:S(2)}, u32[]{:S(2)}) collective-permute-start(bf16[128,128]{1,0:T(8,128)(2,1)} %get-tuple-element.59), channel_id=1, source_target_pairs={{0,192},{16,208},{32,224},{48,240},{64,128},{80,144},{96,160},{112... | collective-permute-start | bytes 98312 | tf_op jit(solution)/shard_map/ppermute | solution.py:576
  178.7 0.0 collective-permute-done.8.refs_1_
  178.7 0.9 collective-permute-done.9.refs_2_
  179.7 1.5 collective-permute-done.10.refs_3_
  181.2 1.9 fold_slow.1
  183.0 7.1 %all-to-all-start.4 = ((bf16[16,64,128]{2,1,0:T(8,128)(2,1)}), bf16[16,64,128]{2,1,0:T(8,128)(2,1)S(1)}, u32[]{:S(2)}, u32[]{:S(2)}) async-start(bf16[16,64,128]{2,1,0:T(8,128)(2,1)} %get-tuple-element.62), calls=%async_computation.4 | async-start | bytes 524288 | tf_op jit(solution)/shard_map/all_to_all | solution.py:618
  190.1 6.2 %input_gradient.1 = bf16[128,1024]{1,0:T(8,128)(2,1)} custom-call(bf16[16,192,128]{2,1,0:T(8,128)(2,1)S(1)} %all-to-all-done.3.joined_ref, bf16[1024,3072]{1,0:T(8,128)(2,1)} %weight_ref.3, bf16[128,1024]{1,0:T(8,128)(2,1)} %bitcast.18, f32[128,1024]{1,0:T(8,128)} %get-tuple-element.46.res_grad_ref), custom_call_target="tpu_custom_call" | custom-call | tf_op jit(solution)/shard_map/input_gradient/pallas_call | solution.py:402
  196.3 0.1 copy.12
  196.4 0.7 copy.13
  197.2 2.1 %all-to-all-done.4.refs_0_ = bf16[16,64,128]{2,1,0:T(8,128)(2,1)S(1)} async-done(((bf16[16,64,128]{2,1,0:T(8,128)(2,1)}), bf16[16,64,128]{2,1,0:T(8,128)(2,1)S(1)}, u32[]{:S(2)}, u32[]{:S(2)}) %all-to-all-start.4) | async-done | bytes 262176 | tf_op jit(solution)/shard_map/all_to_all | solution.py:618
  199.3 0.8 finish.1
  (16 shorter events, 0.1 us)
Async XLA Ops:
  7.2 140.7 %all-gather.2.cloned.1.call-start = ((), (), s32[]{:S(2)}) async-start(), calls=%async_computation.5 | async-start | bytes 4456448 | tf_op jit(solution)/shard_map/all_gather | solution.py:605
  7.2 17.8 %copy-start.2 = (bf16[1,128,1024]{2,1,0:T(8,128)(2,1)S(1)}, bf16[1,128,1024]{2,1,0:T(8,128)(2,1)}, u32[]{:S(2)}) copy-start(bf16[1,128,1024]{2,1,0:T(8,128)(2,1)} %param.6) | copy-start | bytes 786436
  7.2 17.8 %copy-start.3 = (bf16[1,128,1024]{2,1,0:T(8,128)(2,1)S(1)}, bf16[1,128,1024]{2,1,0:T(8,128)(2,1)}, u32[]{:S(2)}) copy-start(bf16[1,128,1024]{2,1,0:T(8,128)(2,1)} %param.7) | copy-start | bytes 786436
  14.2 35.5 %all-to-all-start = ((bf16[16,192,128]{2,1,0:T(8,128)(2,1)}), bf16[16,192,128]{2,1,0:T(8,128)(2,1)S(1)}, u32[]{:S(2)}, u32[]{:S(2)}) async-start(bf16[16,192,128]{2,1,0:T(8,128)(2,1)} %get-tuple-element.35), calls=%async_computation | async-start | bytes 1572864 | tf_op jit(solution)/shard_map/all_to_all | solution.py:603
  49.7 12.3 %copy-start.1 = (bf16[16,192,128]{2,1,0:T(8,128)(2,1)}, bf16[16,192,128]{2,1,0:T(8,128)(2,1)S(1)}, u32[]{:S(2)}) copy-start(bf16[16,192,128]{2,1,0:T(8,128)(2,1)S(1)} %all-to-all-done.heads_ref) | copy-start | bytes 2359300
  62.0 26.7 %all-to-all-start.1 = ((bf16[16,96,128]{2,1,0:T(8,128)(2,1)}), bf16[16,96,128]{2,1,0:T(8,128)(2,1)S(1)}, u32[]{:S(2)}, u32[]{:S(2)}) async-start(bf16[16,96,128]{2,1,0:T(8,128)(2,1)} %get-tuple-element.36), calls=%async_computation.1 | async-start | bytes 786432 | tf_op jit(solution)/shard_map/all_to_all | solution.py:607
  69.0 18.5 %collective-permute-start.1 = (bf16[64,1024]{1,0:T(8,128)(2,1)S(1)}, bf16[64,1024]{1,0:T(8,128)(2,1)S(1)}, u32[]{:S(2)}, u32[]{:S(2)}) collective-permute-start(bf16[64,1024]{1,0:T(8,128)(2,1)S(1)} %pad_maximum_fusion.1), channel_id=1, source_target_pairs={{1,0},{2,1},{3,2},{4,3},{5,4},{6,5},{7,6},{8,7},{9,8},{10,9},{11,1... | collective-permute-start | bytes 393224 | tf_op jit(solution)/shard_map/ppermute | solution.py:598
  71.1 17.0 %collective-permute-start = (bf16[64,1024]{1,0:T(8,128)(2,1)S(1)}, bf16[64,1024]{1,0:T(8,128)(2,1)S(1)}, u32[]{:S(2)}, u32[]{:S(2)}) collective-permute-start(bf16[64,1024]{1,0:T(8,128)(2,1)S(1)} %pad_maximum_fusion), channel_id=1, source_target_pairs={{0,1},{1,2},{2,3},{3,4},{4,5},{5,6},{6,7},{7,8},{8,9},{9,10},{10,1... | collective-permute-start | bytes 393224 | tf_op jit(solution)/shard_map/ppermute | solution.py:597
  98.0 27.0 %all-to-all-start.2 = ((bf16[16,96,128]{2,1,0:T(8,128)(2,1)}), bf16[16,96,128]{2,1,0:T(8,128)(2,1)S(1)}, u32[]{:S(2)}, u32[]{:S(2)}) async-start(bf16[16,96,128]{2,1,0:T(8,128)(2,1)} %get-tuple-element.38), calls=%async_computation.2 | async-start | bytes 786432 | tf_op jit(solution)/shard_map/all_to_all | solution.py:609
  104.9 10.9 %collective-permute-start.2 = (bf16[128,1280]{1,0:T(8,128)(2,1)}, bf16[128,1280]{1,0:T(8,128)(2,1)S(1)}, u32[]{:S(2)}, u32[]{:S(2)}) collective-permute-start(bf16[128,1280]{1,0:T(8,128)(2,1)} %get-tuple-element.40), channel_id=1, source_target_pairs={{0,64},{16,80},{32,96},{48,112},{64,0},{80,16},{96,32},{112,48},{1... | collective-permute-start | bytes 983048 | tf_op jit(solution)/shard_map/ppermute | solution.py:576
  106.7 15.8 %collective-permute-start.3 = (bf16[128,1280]{1,0:T(8,128)(2,1)}, bf16[128,1280]{1,0:T(8,128)(2,1)S(1)}, u32[]{:S(2)}, u32[]{:S(2)}) collective-permute-start(bf16[128,1280]{1,0:T(8,128)(2,1)} %get-tuple-element.41), channel_id=1, source_target_pairs={{0,128},{16,144},{32,160},{48,176},{64,192},{80,208},{96,224},{112... | collective-permute-start | bytes 983048 | tf_op jit(solution)/shard_map/ppermute | solution.py:576
  109.5 15.5 %collective-permute-start.4 = (bf16[128,1280]{1,0:T(8,128)(2,1)}, bf16[128,1280]{1,0:T(8,128)(2,1)S(1)}, u32[]{:S(2)}, u32[]{:S(2)}) collective-permute-start(bf16[128,1280]{1,0:T(8,128)(2,1)} %get-tuple-element.42), channel_id=1, source_target_pairs={{0,192},{16,208},{32,224},{48,240},{64,128},{80,144},{96,160},{112... | collective-permute-start | bytes 983048 | tf_op jit(solution)/shard_map/ppermute | solution.py:576
  125.0 14.7 %copy-start = (bf16[16,96,128]{2,1,0:T(8,128)(2,1)}, bf16[16,96,128]{2,1,0:T(8,128)(2,1)S(1)}, u32[]{:S(2)}) copy-start(bf16[16,96,128]{2,1,0:T(8,128)(2,1)S(1)} %all-to-all-done.2.grads_ref.back_ref) | copy-start | bytes 1179652
  139.7 43.3 %all-to-all-start.3 = ((bf16[16,192,128]{2,1,0:T(8,128)(2,1)}), bf16[16,192,128]{2,1,0:T(8,128)(2,1)S(1)}, u32[]{:S(2)}, u32[]{:S(2)}) async-start(bf16[16,192,128]{2,1,0:T(8,128)(2,1)} %attend_back.1.grads_ref), calls=%async_computation.3 | async-start | bytes 1572864 | tf_op jit(solution)/shard_map/all_to_all | solution.py:612
  153.8 3.4 %collective-permute-start.5 = (bf16[928,128]{1,0:T(8,128)(2,1)}, bf16[928,128]{1,0:T(8,128)(2,1)S(1)}, u32[]{:S(2)}, u32[]{:S(2)}) collective-permute-start(bf16[928,128]{1,0:T(8,128)(2,1)} %get-tuple-element.53), channel_id=1, source_target_pairs={{0,16},{16,0},{32,48},{48,32},{64,80},{80,64},{96,112},{112,96},{1... | collective-permute-start | bytes 712712 | tf_op jit(solution)/shard_map/ppermute | solution.py:576
  153.8 14.0 %collective-permute-start.6 = (bf16[928,128]{1,0:T(8,128)(2,1)}, bf16[928,128]{1,0:T(8,128)(2,1)S(1)}, u32[]{:S(2)}, u32[]{:S(2)}) collective-permute-start(bf16[928,128]{1,0:T(8,128)(2,1)} %get-tuple-element.54), channel_id=1, source_target_pairs={{0,32},{16,48},{32,0},{48,16},{64,96},{80,112},{96,64},{112,80},{1... | collective-permute-start | bytes 712712 | tf_op jit(solution)/shard_map/ppermute | solution.py:576
  156.9 15.2 %collective-permute-start.7 = (bf16[928,128]{1,0:T(8,128)(2,1)}, bf16[928,128]{1,0:T(8,128)(2,1)S(1)}, u32[]{:S(2)}, u32[]{:S(2)}) collective-permute-start(bf16[928,128]{1,0:T(8,128)(2,1)} %get-tuple-element.55), channel_id=1, source_target_pairs={{0,48},{16,32},{32,16},{48,0},{64,112},{80,96},{96,80},{112,64},{1... | collective-permute-start | bytes 712712 | tf_op jit(solution)/shard_map/ppermute | solution.py:576
  174.0 4.7 %collective-permute-start.8 = (bf16[128,128]{1,0:T(8,128)(2,1)}, bf16[128,128]{1,0:T(8,128)(2,1)S(1)}, u32[]{:S(2)}, u32[]{:S(2)}) collective-permute-start(bf16[128,128]{1,0:T(8,128)(2,1)} %get-tuple-element.57), channel_id=1, source_target_pairs={{0,64},{16,80},{32,96},{48,112},{64,0},{80,16},{96,32},{112,48},{1... | collective-permute-start | bytes 98312 | tf_op jit(solution)/shard_map/ppermute | solution.py:576
  174.0 5.6 %collective-permute-start.9 = (bf16[128,128]{1,0:T(8,128)(2,1)}, bf16[128,128]{1,0:T(8,128)(2,1)S(1)}, u32[]{:S(2)}, u32[]{:S(2)}) collective-permute-start(bf16[128,128]{1,0:T(8,128)(2,1)} %get-tuple-element.58), channel_id=1, source_target_pairs={{0,128},{16,144},{32,160},{48,176},{64,192},{80,208},{96,224},{112... | collective-permute-start | bytes 98312 | tf_op jit(solution)/shard_map/ppermute | solution.py:576
  175.8 5.3 %collective-permute-start.10 = (bf16[128,128]{1,0:T(8,128)(2,1)}, bf16[128,128]{1,0:T(8,128)(2,1)S(1)}, u32[]{:S(2)}, u32[]{:S(2)}) collective-permute-start(bf16[128,128]{1,0:T(8,128)(2,1)} %get-tuple-element.59), channel_id=1, source_target_pairs={{0,192},{16,208},{32,224},{48,240},{64,128},{80,144},{96,160},{112... | collective-permute-start | bytes 98312 | tf_op jit(solution)/shard_map/ppermute | solution.py:576
  183.0 16.3 %all-to-all-start.4 = ((bf16[16,64,128]{2,1,0:T(8,128)(2,1)}), bf16[16,64,128]{2,1,0:T(8,128)(2,1)S(1)}, u32[]{:S(2)}, u32[]{:S(2)}) async-start(bf16[16,64,128]{2,1,0:T(8,128)(2,1)} %get-tuple-element.62), calls=%async_computation.4 | async-start | bytes 524288 | tf_op jit(solution)/shard_map/all_to_all | solution.py:618
  190.1 6.2 %copy-start.4 = (f32[64,192]{1,0:T(8,128)S(1)}, f32[64,192]{1,0:T(8,128)}, u32[]{:S(2)}) copy-start(f32[64,192]{1,0:T(8,128)} %get-tuple-element.61) | copy-start | bytes 147460
Sparse Core Ops, SparseCore 0:
  14.3 94.6 all-gather.1

commit v7 on v5

--- a/solution.py
+++ b/solution.py
@@ -191,10 +191,7 @@
     output_ref,
     res_grad_ref,
     send_ref,
-    pack_one,
-    pack_two,
-    pack_three,
-    pack_four,
+    pack_ref,
     taps_ref,
     conv_in,
     grad_all,
@@ -267,10 +264,8 @@
     res_grad = grads_ref[...].astype(F32) + normalize_back(unit, scale, conv_grad[...] * keep)
     res_grad_ref[...] = res_grad
     rounded = res_grad.astype(BF16)
-    for k, pack_ref in enumerate((pack_one, pack_two, pack_three, pack_four)):
-        pack_ref[:, 0:width] = rounded
-        picked = [att_ref[FAST * i + (scalars[3] ^ k), 0:HD, :] for i in range(SLOW)]
-        pack_ref[:, width:] = jnp.concatenate(picked, axis=0).T
+    pack_ref[:, 0:width] = rounded
+    pack_ref[:, width:] = attended
     back = dot(w_out_ref[...], rounded, 1, 1).astype(BF16)
     send_ref[:, 0:HD, :] = back.reshape(heads, HD, rows)
     for h in range(heads):
@@ -287,8 +282,8 @@
             jax.ShapeDtypeStruct((rows, width), BF16),
             jax.ShapeDtypeStruct((rows, width), F32),
             jax.ShapeDtypeStruct((HEADS, HD + KW + 1, rows), BF16),
-        ]
-        + [jax.ShapeDtypeStruct((rows, width + SLOW * HD), BF16)] * FAST,
+            jax.ShapeDtypeStruct((rows, 2 * width), BF16),
+        ],
         scratch_shapes=[
             pltpu.VMEM((KW + 1, width), F32),
             pltpu.VMEM((rows + 2 * HALO, width), F32),
@@ -417,30 +412,29 @@
     )(local_memory(joined), w_qkv, frames, res_grad)
 
 
-def out_part_kernel(scalars, one, two, three, four, *rest):
-    send_refs, part = rest[:SLOW], rest[SLOW]
-    width = send_refs[0].shape[0] // HD * 128
-    packs = (one, two, three, four)
-    left = jnp.concatenate([ref[:, width:] for ref in packs], axis=0)
-    right = jnp.concatenate([ref[:, 0:width] for ref in packs], axis=0)
-    part[...] = dot(left.T, right)
+def out_part_kernel(scalars, pack_ref, *rest):
+    send_refs, part = rest[:FAST], rest[FAST]
+    width = pack_ref.shape[1] // 2
+    block = FAST * HD
+    first = pl.multiple_of(width + scalars[4] * block, block)
+    part[...] = dot(pack_ref[:, pl.ds(first, block)].T, pack_ref[:, 0:width])
     for k, send_ref in enumerate(send_refs):
-        rows = pl.ds(pl.multiple_of((scalars[4] ^ k) * HD, HD), HD)
+        rows = pl.ds(pl.multiple_of((scalars[3] ^ k) * HD, HD), HD)
         for c in range(width // 128):
             send_ref[c * HD : (c + 1) * HD, :] = part[rows, c * 128 : (c + 1) * 128].astype(BF16)
 
 
 def out_part(scalars, packs):
-    rows, wide = packs[0].shape
+    width = packs.shape[1] // 2
     vmem = pl.BlockSpec(memory_space=pltpu.VMEM)
     return pl.pallas_call(
         out_part_kernel,
-        in_specs=[SMEM] + [vmem] * 4,
-        out_shape=[jax.ShapeDtypeStruct((OUT, 128), BF16)] * SLOW,
-        scratch_shapes=[pltpu.VMEM((SLOW * HD, wide - SLOW * HD), F32)],
+        in_specs=[SMEM, vmem],
+        out_shape=[jax.ShapeDtypeStruct((OUT, 128), BF16)] * FAST,
+        scratch_shapes=[pltpu.VMEM((FAST * HD, width), F32)],
         compiler_params=params(),
         name="out_part",
-    )(scalars, *packs)
+    )(scalars, packs)
 
 
 def parts_kernel(scalars, grads_ref, back_ref, normed_ref, *rest):
@@ -611,13 +605,14 @@
     normed_all = lax.all_gather(normed, "seq", axis=0, tiled=True)
     send, out, lse = attend(scalars, heads_near)
     att = local_memory(lax.all_to_all(send, "seq", 0, 0, tiled=True))
-    output, res_grad, send, *packs = middle(scalars, att, x, x_side, g, g_side, w_out, w_conv)
+    output, res_grad, send, pack = middle(scalars, att, x, x_side, g, g_side, w_out, w_conv)
     back = lax.all_to_all(send, "seq", 0, 0, tiled=True)
-    back, packs = lax.optimization_barrier((back, exchange(packs, 1)))
+    far = [[FAST * i + j for i in range(SLOW)] for j in range(FAST)]
+    packs = lax.all_gather(pack, "dp", axis=0, axis_index_groups=far, tiled=True)
     send = attend_back(scalars, heads, local_memory(back), out, lse)
     joined = lax.all_to_all(send, "seq", 0, 0, tiled=True)
     parts = exchange(gradient_parts(scalars, send, back, normed_all), 1)
-    outer = exchange(out_part(scalars, packs), FAST)
+    outer = exchange(out_part(scalars, packs), 1)
     parts = exchange(fold_fast(scalars, parts), FAST)
     qkv, send = fold_slow(parts, outer, seq_count, grad_scale)
     input_grad = input_gradient(joined, w_qkv, x, res_grad)

time: 208 us -> 197 us (0.947)
  blocking collectives: 0 us -> 19 us
  starting transfers between devices: 60.7 us -> 45.4 us
  waiting for transfers between devices: 67.1 us -> 52.9 us
    ppermute x12 -> x9, waiting for transfers between devices: 27.2 us -> 7.97 us  [exchange(): lax.ppermute(block, 'dp', pairs(k))]
    all_to_all x0 -> x1, blocking collectives: none -> 19 us  [local(): back = lax.all_to_all(send, 'seq', 0, 0, tiled=True)]
    ppermute x1, waiting for transfers between devices: 13.1 us -> 0.17 us  [local(): lax.ppermute(jnp.concatenate([x[-HALO:], g[-HALO:]], axis=0), 'seq', forw...]
    ppermute x1, waiting for transfers between devices: 0.01 us -> 12.6 us  [local(): lax.ppermute(jnp.concatenate([x[:HALO], g[:HALO]], axis=0), 'seq', backward)]
    all_to_all x1 -> x0, starting transfers between devices: 6.88 us -> none  [local(): back = lax.all_to_all(send, 'seq', 0, 0, tiled=True)]
    all_gather x0 -> x1, waiting for transfers between devices: none -> 5.46 us  [local(): lax.all_gather(pack, 'dp', axis=0, axis_index_groups=far, tiled=True)]
    ppermute x12 -> x9, starting transfers between devices: 15.9 us -> 11.2 us  [exchange(): lax.ppermute(block, 'dp', pairs(k))]
    all_to_all x1, starting transfers between devices: 7.66 us -> 5.04 us  [local(): joined = lax.all_to_all(send, 'seq', 0, 0, tiled=True)]
  transfers between devices with their start and end apart: 20 -> 17, of which waited for: 10 -> 9; matrix products, arithmetic and copies ran while one was open for 1% -> 1% of each run, Pallas kernels for 26% -> 28%
where the time goes in v7:
time: 197 us; the launch traced here: 196 us
  Pallas kernels  62 us (31%)
  waiting for transfers between devices  52.9 us (27%)
  starting transfers between devices  45.4 us (23%)
  blocking collectives  19 us (10%)
  between operations  14.8 us (8%)
    all_to_all x1, waiting for transfers between devices, local(): heads = lax.all_to_all(send, 'seq', 0, 0, tiled=True)  24.7 us
    all_to_all x1, blocking collectives, local(): back = lax.all_to_all(send, 'seq', 0, 0, tiled=True)  19 us
    pallas_call x1, Pallas kernels, attend_back(): pl.pallas_call(attend_back_kernel, in_specs=[SMEM] + [vmem] * 4, out_shap...  14.7 us
    ppermute x1, waiting for transfers between devices, local(): lax.ppermute(jnp.concatenate([x[:HALO], g[:HALO]], axis=0), 'seq', backward)  12.6 us
    pallas_call x1, Pallas kernels, attend(): pl.pallas_call(attend_kernel, in_specs=[SMEM, pl.BlockSpec(memory_space=p...  12.3 us
    ppermute x9, starting transfers between devices, exchange(): lax.ppermute(block, 'dp', pairs(k))  11.2 us
    all_to_all x1, starting transfers between devices, local(): heads = lax.all_to_all(send, 'seq', 0, 0, tiled=True)  9.52 us
    pallas_call x1, Pallas kernels, middle(): pl.pallas_call(middle_kernel, in_specs=[SMEM] + [vmem] * 7, out_shape=[ja...  8.99 us
  transfers between devices with their start and end apart: 17, of which 9 were waited for; matrix products, arithmetic and copies ran while one was open for 1% of the time, Pallas kernels for 28%

profile of v7, /device:TPU:32, one launch (start us, length us, event | category | flops | bytes accessed | tf_op | source)
XLA Modules:
  0.0 196.3 jit_solution(15110126406540740334)
XLA Ops:
  7.2 0.0 all-gather.3.cloned.1.call-start
  7.2 0.0 copy-start.2
  7.2 0.0 copy-start.3
  7.2 7.0 %project.1 = (bf16[128,1024]{1,0:T(8,128)(2,1)}, bf16[16,192,128]{2,1,0:T(8,128)(2,1)}) custom-call(bf16[128,1024]{1,0:T(8,128)(2,1)} %bitcast.16, bf16[1024,3072]{1,0:T(8,128)(2,1)} %weight_ref.3), custom_call_target="tpu_custom_call" | custom-call | tf_op jit(solution)/shard_map/project/pallas_call | solution.py:88
  14.2 0.0 all-gather.3.cloned.1.call-update
  14.2 9.5 %all-to-all-start = ((bf16[16,192,128]{2,1,0:T(8,128)(2,1)}), bf16[16,192,128]{2,1,0:T(8,128)(2,1)S(1)}, u32[]{:S(2)}, u32[]{:S(2)}) async-start(bf16[16,192,128]{2,1,0:T(8,128)(2,1)} %get-tuple-element.30), calls=%async_computation | async-start | bytes 1572864 | tf_op jit(solution)/shard_map/all_to_all | solution.py:603
  24.4 0.6 stack.15.scalars
  25.1 24.7 %all-to-all-done.heads_ref = bf16[16,192,128]{2,1,0:T(8,128)(2,1)S(1)} async-done(((bf16[16,192,128]{2,1,0:T(8,128)(2,1)}), bf16[16,192,128]{2,1,0:T(8,128)(2,1)S(1)}, u32[]{:S(2)}, u32[]{:S(2)}) %all-to-all-start) | async-done | bytes 786464 | tf_op jit(solution)/shard_map/all_to_all | solution.py:603
  49.7 12.3 %attend.1 = (bf16[16,96,128]{2,1,0:T(8,128)(2,1)}, f32[64,2048]{1,0:T(8,128)}, f32[1,2048]{1,0:T(1,128)}) custom-call(s32[5]{0:T(128)} %stack.15.scalars, bf16[16,192,128]{2,1,0:T(8,128)(2,1)S(1)} %all-to-all-done.heads_ref), custom_call_target="tpu_custom_call" | custom-call | flops 4294967296 | bytes 786432 | tf_op jit(solution)/shard_map/attend/pallas_call | solution.py:162
  62.1 7.0 %all-to-all-start.1 = ((bf16[16,96,128]{2,1,0:T(8,128)(2,1)}), bf16[16,96,128]{2,1,0:T(8,128)(2,1)S(1)}, u32[]{:S(2)}, u32[]{:S(2)}) async-start(bf16[16,96,128]{2,1,0:T(8,128)(2,1)} %get-tuple-element.31), calls=%async_computation.1 | async-start | bytes 786432 | tf_op jit(solution)/shard_map/all_to_all | solution.py:607
  69.1 0.0 all-gather.5.cloned.1.call-start
  69.1 2.0 %collective-permute-start.1 = (bf16[64,1024]{1,0:T(8,128)(2,1)S(1)}, bf16[64,1024]{1,0:T(8,128)(2,1)S(1)}, u32[]{:S(2)}, u32[]{:S(2)}) collective-permute-start(bf16[64,1024]{1,0:T(8,128)(2,1)S(1)} %pad_maximum_fusion.1), channel_id=1, source_target_pairs={{1,0},{2,1},{3,2},{4,3},{5,4},{6,5},{7,6},{8,7},{9,8},{10,9},{11,1... | collective-permute-start | bytes 393224 | tf_op jit(solution)/shard_map/ppermute | solution.py:598
  71.2 3.8 %collective-permute-start = (bf16[64,1024]{1,0:T(8,128)(2,1)S(1)}, bf16[64,1024]{1,0:T(8,128)(2,1)S(1)}, u32[]{:S(2)}, u32[]{:S(2)}) collective-permute-start(bf16[64,1024]{1,0:T(8,128)(2,1)S(1)} %pad_maximum_fusion), channel_id=1, source_target_pairs={{0,1},{1,2},{2,3},{3,4},{4,5},{5,6},{6,7},{7,8},{8,9},{9,10},{10,1... | collective-permute-start | bytes 393224 | tf_op jit(solution)/shard_map/ppermute | solution.py:597
  75.0 12.6 %collective-permute-done.1 = bf16[64,1024]{1,0:T(8,128)(2,1)S(1)} collective-permute-done((bf16[64,1024]{1,0:T(8,128)(2,1)S(1)}, bf16[64,1024]{1,0:T(8,128)(2,1)S(1)}, u32[]{:S(2)}, u32[]{:S(2)}) %collective-permute-start.1) | collective-permute-done | bytes 131104 | tf_op jit(solution)/shard_map/ppermute | solution.py:598
  87.6 0.2 collective-permute-done
  87.8 0.7 pad_maximum_fusion.2
  88.5 0.0 all-to-all-done.1.att_ref
  88.5 9.0 %middle.1 = (bf16[128,1024]{1,0:T(8,128)(2,1)}, f32[128,1024]{1,0:T(8,128)}, bf16[16,96,128]{2,1,0:T(8,128)(2,1)}, bf16[128,2048]{1,0:T(8,128)(2,1)}) custom-call(s32[5]{0:T(128)} %stack.15.scalars, bf16[16,96,128]{2,1,0:T(8,128)(2,1)S(1)} %all-to-all-done.1.att_ref, bf16[128,1024]{1,0:T(8,128)(2,1)} %bitcast.17, ...), custom_call_target="tpu_custom_call" | custom-call | tf_op jit(solution)/shard_map/middle/pallas_call | solution.py:278
  97.5 0.0 all-gather.5.cloned.1.call-update
  97.6 19.0 %all_to_all.25.grads_ref.back_ref = bf16[16,96,128]{2,1,0:T(8,128)(2,1)S(1)} all-to-all(bf16[16,96,128]{2,1,0:T(8,128)(2,1)} %get-tuple-element.33), channel_id=1, replica_groups=mesh['dp'=16,'seq'=16] {'seq'}, dimensions={0} | all-to-all | bytes 786432 | tf_op jit(solution)/shard_map/all_to_all | solution.py:609
  116.5 14.7 %attend_back.1.grads_ref = bf16[16,192,128]{2,1,0:T(8,128)(2,1)} custom-call(s32[5]{0:T(128)} %stack.15.scalars, bf16[16,192,128]{2,1,0:T(8,128)(2,1)} %copy-done.1, bf16[16,96,128]{2,1,0:T(8,128)(2,1)S(1)} %all_to_all.25.grads_ref.back_ref, f32[64,2048]{1,0:T(8,128)} %get-tuple-element.34.out_ref, f32[1,2048]{1,0:T(1,128)} %get-tuple-element.35.lse_ref), custom_call_target="tpu_custom_call" | custom-call | flops 10737418240 | bytes 1572864 | tf_op jit(solution)/shard_map/attend_back/pallas_call | solution.py:349
  131.2 5.0 %all-to-all-start.3 = ((bf16[16,192,128]{2,1,0:T(8,128)(2,1)}), bf16[16,192,128]{2,1,0:T(8,128)(2,1)S(1)}, u32[]{:S(2)}, u32[]{:S(2)}) async-start(bf16[16,192,128]{2,1,0:T(8,128)(2,1)} %attend_back.1.grads_ref), calls=%async_computation.3 | async-start | bytes 1572864 | tf_op jit(solution)/shard_map/all_to_all | solution.py:613
  136.2 0.0 all-gather.3.cloned.1.call-done.normed_ref
  136.3 5.5 %gradient_parts.1 = (bf16[416,128]{1,0:T(8,128)(2,1)}, bf16[416,128]{1,0:T(8,128)(2,1)}, bf16[416,128]{1,0:T(8,128)(2,1)}, bf16[416,128]{1,0:T(8,128)(2,1)}) custom-call(s32[5]{0:T(128)} %stack.15.scalars, bf16[16,192,128]{2,1,0:T(8,128)(2,1)} %attend_back.1.grads_ref, bf16[16,96,128]{2,1,0:T(8,128)(2,1)} %copy-done, ...), custom_call_target="tpu_custom_call" | custom-call | flops 1073741824 | bytes 4194304 | tf_op jit(solution)/shard_map/gradient_parts/pallas_call | solution.py:467
  141.7 0.0 collective-permute-start.2
  141.7 5.5 %all-gather.5.cloned.1.call-done.pack_ref = bf16[512,2048]{1,0:T(8,128)(2,1)} async-done(((bf16[128,2048]{1,0:T(8,128)(2,1)}), bf16[512,2048]{1,0:T(8,128)(2,1)}) %all-gather.5.cloned.1.call-update) | async-done | bytes 2097168 | tf_op jit(solution)/shard_map/all_gather | solution.py:611
  147.2 2.9 %out_part.1 = (bf16[512,128]{1,0:T(8,128)(2,1)}, bf16[512,128]{1,0:T(8,128)(2,1)}, bf16[512,128]{1,0:T(8,128)(2,1)}, bf16[512,128]{1,0:T(8,128)(2,1)}) custom-call(s32[5]{0:T(128)} %stack.15.scalars, bf16[512,2048]{1,0:T(8,128)(2,1)} %all-gather.5.cloned.1.call-done.pack_ref), custom_call_target="tpu_custom_call" | custom-call | tf_op jit(solution)/shard_map/out_part/pallas_call | solution.py:430
  150.1 3.0 %collective-permute-start.3 = (bf16[416,128]{1,0:T(8,128)(2,1)}, bf16[416,128]{1,0:T(8,128)(2,1)S(1)}, u32[]{:S(2)}, u32[]{:S(2)}) collective-permute-start(bf16[416,128]{1,0:T(8,128)(2,1)} %get-tuple-element.40), channel_id=1, source_target_pairs={{0,32},{16,48},{32,0},{48,16},{64,96},{80,112},{96,64},{112,80},{1... | collective-permute-start | bytes 319496 | tf_op jit(solution)/shard_map/ppermute | solution.py:576
  153.1 0.4 collective-permute-start.4
  153.4 3.0 %collective-permute-start.9 = (bf16[512,128]{1,0:T(8,128)(2,1)}, bf16[512,128]{1,0:T(8,128)(2,1)S(1)}, u32[]{:S(2)}, u32[]{:S(2)}) collective-permute-start(bf16[512,128]{1,0:T(8,128)(2,1)} %get-tuple-element.49), channel_id=1, source_target_pairs={{0,32},{16,48},{32,0},{48,16},{64,96},{80,112},{96,64},{112,80},{1... | collective-permute-start | bytes 393224 | tf_op jit(solution)/shard_map/ppermute | solution.py:576
  156.4 0.2 collective-permute-start.10
  156.6 1.1 collective-permute-done.3.three
  157.7 2.0 %collective-permute-done.4.four = bf16[416,128]{1,0:T(8,128)(2,1)S(1)} collective-permute-done((bf16[416,128]{1,0:T(8,128)(2,1)}, bf16[416,128]{1,0:T(8,128)(2,1)S(1)}, u32[]{:S(2)}, u32[]{:S(2)}) %collective-permute-start.4) | collective-permute-done | bytes 106528 | tf_op jit(solution)/shard_map/ppermute | solution.py:576
  159.7 1.7 fold_fast.1
  161.4 1.5 collective-permute-start.5
  163.0 2.7 %collective-permute-start.6 = (bf16[128,128]{1,0:T(8,128)(2,1)}, bf16[128,128]{1,0:T(8,128)(2,1)S(1)}, u32[]{:S(2)}, u32[]{:S(2)}) collective-permute-start(bf16[128,128]{1,0:T(8,128)(2,1)} %get-tuple-element.44), channel_id=1, source_target_pairs={{0,128},{16,144},{32,160},{48,176},{64,192},{80,208},{96,224},{112... | collective-permute-start | bytes 98312 | tf_op jit(solution)/shard_map/ppermute | solution.py:576
  165.6 0.0 collective-permute-done.8.refs_5_
  165.6 0.5 collective-permute-start.7
  166.1 0.0 collective-permute-done.9.refs_6_
  166.1 2.4 %collective-permute-done.6.refs_2_ = bf16[128,128]{1,0:T(8,128)(2,1)S(1)} collective-permute-done((bf16[128,128]{1,0:T(8,128)(2,1)}, bf16[128,128]{1,0:T(8,128)(2,1)S(1)}, u32[]{:S(2)}, u32[]{:S(2)}) %collective-permute-start.6) | collective-permute-done | bytes 32800 | tf_op jit(solution)/shard_map/ppermute | solution.py:576
  168.6 2.4 %collective-permute-done.7.refs_3_ = bf16[128,128]{1,0:T(8,128)(2,1)S(1)} collective-permute-done((bf16[128,128]{1,0:T(8,128)(2,1)}, bf16[128,128]{1,0:T(8,128)(2,1)S(1)}, u32[]{:S(2)}, u32[]{:S(2)}) %collective-permute-start.7) | collective-permute-done | bytes 32800 | tf_op jit(solution)/shard_map/ppermute | solution.py:576
  171.0 1.9 fold_slow.1
  172.9 6.7 %all-to-all-start.4 = ((bf16[16,64,128]{2,1,0:T(8,128)(2,1)}), bf16[16,64,128]{2,1,0:T(8,128)(2,1)S(1)}, u32[]{:S(2)}, u32[]{:S(2)}) async-start(bf16[16,64,128]{2,1,0:T(8,128)(2,1)} %get-tuple-element.52), calls=%async_computation.4 | async-start | bytes 524288 | tf_op jit(solution)/shard_map/all_to_all | solution.py:619
  179.6 6.2 %input_gradient.1 = bf16[128,1024]{1,0:T(8,128)(2,1)} custom-call(bf16[16,192,128]{2,1,0:T(8,128)(2,1)S(1)} %all-to-all-done.3.joined_ref, bf16[1024,3072]{1,0:T(8,128)(2,1)} %weight_ref.3, bf16[128,1024]{1,0:T(8,128)(2,1)} %bitcast.18, f32[128,1024]{1,0:T(8,128)} %get-tuple-element.36.res_grad_ref), custom_call_target="tpu_custom_call" | custom-call | tf_op jit(solution)/shard_map/input_gradient/pallas_call | solution.py:395
  185.8 0.1 copy.12
  185.9 0.7 copy.13
  186.6 2.0 %all-to-all-done.4.refs_0_ = bf16[16,64,128]{2,1,0:T(8,128)(2,1)S(1)} async-done(((bf16[16,64,128]{2,1,0:T(8,128)(2,1)}), bf16[16,64,128]{2,1,0:T(8,128)(2,1)S(1)}, u32[]{:S(2)}, u32[]{:S(2)}) %all-to-all-start.4) | async-done | bytes 262176 | tf_op jit(solution)/shard_map/all_to_all | solution.py:619
  188.6 0.8 finish.1
  (19 shorter events, 0.1 us)
Async XLA Ops:
  7.2 129.1 %all-gather.3.cloned.1.call-start = ((), (), s32[]{:S(2)}) async-start(), calls=%async_computation.5 | async-start | bytes 4456448 | tf_op jit(solution)/shard_map/all_gather | solution.py:605
  7.2 17.8 %copy-start.2 = (bf16[1,128,1024]{2,1,0:T(8,128)(2,1)S(1)}, bf16[1,128,1024]{2,1,0:T(8,128)(2,1)}, u32[]{:S(2)}) copy-start(bf16[1,128,1024]{2,1,0:T(8,128)(2,1)} %param.6) | copy-start | bytes 786436
  7.2 17.8 %copy-start.3 = (bf16[1,128,1024]{2,1,0:T(8,128)(2,1)S(1)}, bf16[1,128,1024]{2,1,0:T(8,128)(2,1)}, u32[]{:S(2)}) copy-start(bf16[1,128,1024]{2,1,0:T(8,128)(2,1)} %param.7) | copy-start | bytes 786436
  14.2 35.5 %all-to-all-start = ((bf16[16,192,128]{2,1,0:T(8,128)(2,1)}), bf16[16,192,128]{2,1,0:T(8,128)(2,1)S(1)}, u32[]{:S(2)}, u32[]{:S(2)}) async-start(bf16[16,192,128]{2,1,0:T(8,128)(2,1)} %get-tuple-element.30), calls=%async_computation | async-start | bytes 1572864 | tf_op jit(solution)/shard_map/all_to_all | solution.py:603
  49.7 12.4 %copy-start.1 = (bf16[16,192,128]{2,1,0:T(8,128)(2,1)}, bf16[16,192,128]{2,1,0:T(8,128)(2,1)S(1)}, u32[]{:S(2)}) copy-start(bf16[16,192,128]{2,1,0:T(8,128)(2,1)S(1)} %all-to-all-done.heads_ref) | copy-start | bytes 2359300
  62.1 26.4 %all-to-all-start.1 = ((bf16[16,96,128]{2,1,0:T(8,128)(2,1)}), bf16[16,96,128]{2,1,0:T(8,128)(2,1)S(1)}, u32[]{:S(2)}, u32[]{:S(2)}) async-start(bf16[16,96,128]{2,1,0:T(8,128)(2,1)} %get-tuple-element.31), calls=%async_computation.1 | async-start | bytes 786432 | tf_op jit(solution)/shard_map/all_to_all | solution.py:607
  69.1 78.1 %all-gather.5.cloned.1.call-start = ((), (), s32[]{:S(2)}) async-start(), calls=%async_computation.6 | async-start | bytes 2621440 | tf_op jit(solution)/shard_map/all_gather | solution.py:611
  69.1 18.5 %collective-permute-start.1 = (bf16[64,1024]{1,0:T(8,128)(2,1)S(1)}, bf16[64,1024]{1,0:T(8,128)(2,1)S(1)}, u32[]{:S(2)}, u32[]{:S(2)}) collective-permute-start(bf16[64,1024]{1,0:T(8,128)(2,1)S(1)} %pad_maximum_fusion.1), channel_id=1, source_target_pairs={{1,0},{2,1},{3,2},{4,3},{5,4},{6,5},{7,6},{8,7},{9,8},{10,9},{11,1... | collective-permute-start | bytes 393224 | tf_op jit(solution)/shard_map/ppermute | solution.py:598
  71.2 16.6 %collective-permute-start = (bf16[64,1024]{1,0:T(8,128)(2,1)S(1)}, bf16[64,1024]{1,0:T(8,128)(2,1)S(1)}, u32[]{:S(2)}, u32[]{:S(2)}) collective-permute-start(bf16[64,1024]{1,0:T(8,128)(2,1)S(1)} %pad_maximum_fusion), channel_id=1, source_target_pairs={{0,1},{1,2},{2,3},{3,4},{4,5},{5,6},{6,7},{7,8},{8,9},{9,10},{10,1... | collective-permute-start | bytes 393224 | tf_op jit(solution)/shard_map/ppermute | solution.py:597
  116.5 14.7 %copy-start = (bf16[16,96,128]{2,1,0:T(8,128)(2,1)}, bf16[16,96,128]{2,1,0:T(8,128)(2,1)S(1)}, u32[]{:S(2)}) copy-start(bf16[16,96,128]{2,1,0:T(8,128)(2,1)S(1)} %all_to_all.25.grads_ref.back_ref) | copy-start | bytes 1179652
  131.2 41.7 %all-to-all-start.3 = ((bf16[16,192,128]{2,1,0:T(8,128)(2,1)}), bf16[16,192,128]{2,1,0:T(8,128)(2,1)S(1)}, u32[]{:S(2)}, u32[]{:S(2)}) async-start(bf16[16,192,128]{2,1,0:T(8,128)(2,1)} %attend_back.1.grads_ref), calls=%async_computation.3 | async-start | bytes 1572864 | tf_op jit(solution)/shard_map/all_to_all | solution.py:613
  141.7 14.7 %collective-permute-start.2 = (bf16[416,128]{1,0:T(8,128)(2,1)}, bf16[416,128]{1,0:T(8,128)(2,1)S(1)}, u32[]{:S(2)}, u32[]{:S(2)}) collective-permute-start(bf16[416,128]{1,0:T(8,128)(2,1)} %get-tuple-element.39), channel_id=1, source_target_pairs={{0,16},{16,0},{32,48},{48,32},{64,80},{80,64},{96,112},{112,96},{1... | collective-permute-start | bytes 319496 | tf_op jit(solution)/shard_map/ppermute | solution.py:576
  150.1 15.5 %collective-permute-start.8 = (bf16[512,128]{1,0:T(8,128)(2,1)}, bf16[512,128]{1,0:T(8,128)(2,1)S(1)}, u32[]{:S(2)}, u32[]{:S(2)}) collective-permute-start(bf16[512,128]{1,0:T(8,128)(2,1)} %get-tuple-element.48), channel_id=1, source_target_pairs={{0,16},{16,0},{32,48},{48,32},{64,80},{80,64},{96,112},{112,96},{1... | collective-permute-start | bytes 393224 | tf_op jit(solution)/shard_map/ppermute | solution.py:576
  150.1 7.6 %collective-permute-start.3 = (bf16[416,128]{1,0:T(8,128)(2,1)}, bf16[416,128]{1,0:T(8,128)(2,1)S(1)}, u32[]{:S(2)}, u32[]{:S(2)}) collective-permute-start(bf16[416,128]{1,0:T(8,128)(2,1)} %get-tuple-element.40), channel_id=1, source_target_pairs={{0,32},{16,48},{32,0},{48,16},{64,96},{80,112},{96,64},{112,80},{1... | collective-permute-start | bytes 319496 | tf_op jit(solution)/shard_map/ppermute | solution.py:576
  153.1 6.7 %collective-permute-start.4 = (bf16[416,128]{1,0:T(8,128)(2,1)}, bf16[416,128]{1,0:T(8,128)(2,1)S(1)}, u32[]{:S(2)}, u32[]{:S(2)}) collective-permute-start(bf16[416,128]{1,0:T(8,128)(2,1)} %get-tuple-element.41), channel_id=1, source_target_pairs={{0,48},{16,32},{32,16},{48,0},{64,112},{80,96},{96,80},{112,64},{1... | collective-permute-start | bytes 319496 | tf_op jit(solution)/shard_map/ppermute | solution.py:576
  153.4 12.7 %collective-permute-start.9 = (bf16[512,128]{1,0:T(8,128)(2,1)}, bf16[512,128]{1,0:T(8,128)(2,1)S(1)}, u32[]{:S(2)}, u32[]{:S(2)}) collective-permute-start(bf16[512,128]{1,0:T(8,128)(2,1)} %get-tuple-element.49), channel_id=1, source_target_pairs={{0,32},{16,48},{32,0},{48,16},{64,96},{80,112},{96,64},{112,80},{1... | collective-permute-start | bytes 393224 | tf_op jit(solution)/shard_map/ppermute | solution.py:576
  156.4 9.7 %collective-permute-start.10 = (bf16[512,128]{1,0:T(8,128)(2,1)}, bf16[512,128]{1,0:T(8,128)(2,1)S(1)}, u32[]{:S(2)}, u32[]{:S(2)}) collective-permute-start(bf16[512,128]{1,0:T(8,128)(2,1)} %get-tuple-element.50), channel_id=1, source_target_pairs={{0,48},{16,32},{32,16},{48,0},{64,112},{80,96},{96,80},{112,64},{1... | collective-permute-start | bytes 393224 | tf_op jit(solution)/shard_map/ppermute | solution.py:576
  161.4 4.7 %collective-permute-start.5 = (bf16[128,128]{1,0:T(8,128)(2,1)}, bf16[128,128]{1,0:T(8,128)(2,1)S(1)}, u32[]{:S(2)}, u32[]{:S(2)}) collective-permute-start(bf16[128,128]{1,0:T(8,128)(2,1)} %get-tuple-element.43), channel_id=1, source_target_pairs={{0,64},{16,80},{32,96},{48,112},{64,0},{80,16},{96,32},{112,48},{1... | collective-permute-start | bytes 98312 | tf_op jit(solution)/shard_map/ppermute | solution.py:576
  163.0 5.6 %collective-permute-start.6 = (bf16[128,128]{1,0:T(8,128)(2,1)}, bf16[128,128]{1,0:T(8,128)(2,1)S(1)}, u32[]{:S(2)}, u32[]{:S(2)}) collective-permute-start(bf16[128,128]{1,0:T(8,128)(2,1)} %get-tuple-element.44), channel_id=1, source_target_pairs={{0,128},{16,144},{32,160},{48,176},{64,192},{80,208},{96,224},{112... | collective-permute-start | bytes 98312 | tf_op jit(solution)/shard_map/ppermute | solution.py:576
  165.6 5.3 %collective-permute-start.7 = (bf16[128,128]{1,0:T(8,128)(2,1)}, bf16[128,128]{1,0:T(8,128)(2,1)S(1)}, u32[]{:S(2)}, u32[]{:S(2)}) collective-permute-start(bf16[128,128]{1,0:T(8,128)(2,1)} %get-tuple-element.45), channel_id=1, source_target_pairs={{0,192},{16,208},{32,224},{48,240},{64,128},{80,144},{96,160},{112... | collective-permute-start | bytes 98312 | tf_op jit(solution)/shard_map/ppermute | solution.py:576
  172.9 15.8 %all-to-all-start.4 = ((bf16[16,64,128]{2,1,0:T(8,128)(2,1)}), bf16[16,64,128]{2,1,0:T(8,128)(2,1)S(1)}, u32[]{:S(2)}, u32[]{:S(2)}) async-start(bf16[16,64,128]{2,1,0:T(8,128)(2,1)} %get-tuple-element.52), calls=%async_computation.4 | async-start | bytes 524288 | tf_op jit(solution)/shard_map/all_to_all | solution.py:619
  179.6 6.2 %copy-start.4 = (f32[64,192]{1,0:T(8,128)S(1)}, f32[64,192]{1,0:T(8,128)}, u32[]{:S(2)}) copy-start(f32[64,192]{1,0:T(8,128)} %get-tuple-element.51) | copy-start | bytes 147460
Sparse Core Ops, SparseCore 0:
  14.3 95.3 all-gather.2
  111.6 35.5 all-gather.4

commit v8 on v7

--- a/solution.py
+++ b/solution.py
@@ -269,7 +269,10 @@
     back = dot(w_out_ref[...], rounded, 1, 1).astype(BF16)
     send_ref[:, 0:HD, :] = back.reshape(heads, HD, rows)
     for h in range(heads):
-        send_ref[h, HD:, :] = halves(taps_ref[:, h * HD : (h + 1) * HD])
+        own = taps_ref[:, h * HD : (h + 1) * HD]
+        middle_row = (KW + 1) // 2
+        own = jnp.concatenate([own[0:middle_row], own[middle_row:]], axis=1)
+        send_ref[h, HD:, :] = own.astype(BF16)
 
 
 def middle(scalars, att, frames, frames_side, grads, grads_side, w_out, w_conv):
@@ -281,7 +284,7 @@
         out_shape=[
             jax.ShapeDtypeStruct((rows, width), BF16),
             jax.ShapeDtypeStruct((rows, width), F32),
-            jax.ShapeDtypeStruct((HEADS, HD + KW + 1, rows), BF16),
+            jax.ShapeDtypeStruct((HEADS, HD + (KW + 1) // 2, rows), BF16),
             jax.ShapeDtypeStruct((rows, 2 * width), BF16),
         ],
         scratch_shapes=[
@@ -444,11 +447,11 @@
 
     @pl.when(slow == 0)
     def _():
-        taps = jnp.zeros((KW + 1, rows), F32)
+        taps = jnp.zeros(((KW + 1) // 2, rows), F32)
         for i in range(count):
             columns[:, i * rows : (i + 1) * rows] = grads_ref[i]
             taps = taps + back_ref[i, HD:, :].astype(F32)
-        pair = halves(joined_halves(taps))
+        pair = halves(jnp.concatenate([taps[:, 0:HD], taps[:, HD:]], axis=0))
         for send_ref in send_refs:
             send_ref[TAPS:, :] = pair
 
@@ -612,8 +615,9 @@
     send = attend_back(scalars, heads, local_memory(back), out, lse)
     joined = lax.all_to_all(send, "seq", 0, 0, tiled=True)
     parts = exchange(gradient_parts(scalars, send, back, normed_all), 1)
+    parts, packs = lax.optimization_barrier((fold_fast(scalars, parts), packs))
+    parts = exchange(parts, FAST)
     outer = exchange(out_part(scalars, packs), 1)
-    parts = exchange(fold_fast(scalars, parts), FAST)
     qkv, send = fold_slow(parts, outer, seq_count, grad_scale)
     input_grad = input_gradient(joined, w_qkv, x, res_grad)
     recv = lax.all_to_all(send, "seq", 0, 0, tiled=True)

time: 197 us -> 199 us (1.010)
  starting transfers between devices: 45.4 us -> 50 us
    all_gather x1, waiting for transfers between devices: 5.46 us -> 0.01 us  [local(): lax.all_gather(pack, 'dp', axis=0, axis_index_groups=far, tiled=True)]
    ppermute x9, waiting for transfers between devices: 7.97 us -> 12 us  [exchange(): lax.ppermute(block, 'dp', pairs(k))]
    ppermute x9, starting transfers between devices: 11.2 us -> 15.1 us  [exchange(): lax.ppermute(block, 'dp', pairs(k))]
  transfers between devices with their start and end apart: 17 -> 17, of which waited for: 9 -> 7; matrix products, arithmetic and copies ran while one was open for 1% -> 1% of each run, Pallas kernels for 28% -> 27%
where the time goes in v8:
time: 199 us; the launch traced here: 198 us
  Pallas kernels  61.8 us (31%)
  waiting for transfers between devices  51.5 us (26%)
  starting transfers between devices  50 us (25%)
  blocking collectives  17.8 us (9%)
  between operations  14.8 us (7%)
    all_to_all x1, waiting for transfers between devices, local(): heads = lax.all_to_all(send, 'seq', 0, 0, tiled=True)  24.6 us
    all_to_all x1, blocking collectives, local(): back = lax.all_to_all(send, 'seq', 0, 0, tiled=True)  17.8 us
    ppermute x9, starting transfers between devices, exchange(): lax.ppermute(block, 'dp', pairs(k))  15.1 us
    pallas_call x1, Pallas kernels, attend_back(): pl.pallas_call(attend_back_kernel, in_specs=[SMEM] + [vmem] * 4, out_shap...  14.7 us
    ppermute x1, waiting for transfers between devices, local(): lax.ppermute(jnp.concatenate([x[:HALO], g[:HALO]], axis=0), 'seq', backward)  12.6 us
    pallas_call x1, Pallas kernels, attend(): pl.pallas_call(attend_kernel, in_specs=[SMEM, pl.BlockSpec(memory_space=p...  12.3 us
    ppermute x9, waiting for transfers between devices, exchange(): lax.ppermute(block, 'dp', pairs(k))  12 us
    all_to_all x1, starting transfers between devices, local(): heads = lax.all_to_all(send, 'seq', 0, 0, tiled=True)  9.52 us
  transfers between devices with their start and end apart: 17, of which 7 were waited for; matrix products, arithmetic and copies ran while one was open for 1% of the time, Pallas kernels for 27%

profile of v8, /device:TPU:32, one launch (start us, length us, event | category | flops | bytes accessed | tf_op | source)
XLA Modules:
  0.0 198.2 jit_solution(16806437910143081626)
XLA Ops:
  7.2 0.0 all-gather.3.cloned.1.call-start
  7.2 0.0 copy-start.2
  7.2 0.0 copy-start.3
  7.2 7.0 %project.1 = (bf16[128,1024]{1,0:T(8,128)(2,1)}, bf16[16,192,128]{2,1,0:T(8,128)(2,1)}) custom-call(bf16[128,1024]{1,0:T(8,128)(2,1)} %bitcast.16, bf16[1024,3072]{1,0:T(8,128)(2,1)} %weight_ref.3), custom_call_target="tpu_custom_call" | custom-call | tf_op jit(solution)/shard_map/project/pallas_call | solution.py:88
  14.2 0.0 all-gather.3.cloned.1.call-update
  14.2 9.5 %all-to-all-start = ((bf16[16,192,128]{2,1,0:T(8,128)(2,1)}), bf16[16,192,128]{2,1,0:T(8,128)(2,1)S(1)}, u32[]{:S(2)}, u32[]{:S(2)}) async-start(bf16[16,192,128]{2,1,0:T(8,128)(2,1)} %get-tuple-element.35), calls=%async_computation | async-start | bytes 1572864 | tf_op jit(solution)/shard_map/all_to_all | solution.py:606
  24.4 0.7 stack.15.scalars
  25.1 24.6 %all-to-all-done.heads_ref = bf16[16,192,128]{2,1,0:T(8,128)(2,1)S(1)} async-done(((bf16[16,192,128]{2,1,0:T(8,128)(2,1)}), bf16[16,192,128]{2,1,0:T(8,128)(2,1)S(1)}, u32[]{:S(2)}, u32[]{:S(2)}) %all-to-all-start) | async-done | bytes 786464 | tf_op jit(solution)/shard_map/all_to_all | solution.py:606
  49.7 12.3 %attend.1 = (bf16[16,96,128]{2,1,0:T(8,128)(2,1)}, f32[64,2048]{1,0:T(8,128)}, f32[1,2048]{1,0:T(1,128)}) custom-call(s32[5]{0:T(128)} %stack.15.scalars, bf16[16,192,128]{2,1,0:T(8,128)(2,1)S(1)} %all-to-all-done.heads_ref), custom_call_target="tpu_custom_call" | custom-call | flops 4294967296 | bytes 786432 | tf_op jit(solution)/shard_map/attend/pallas_call | solution.py:162
  62.1 7.0 %all-to-all-start.1 = ((bf16[16,96,128]{2,1,0:T(8,128)(2,1)}), bf16[16,96,128]{2,1,0:T(8,128)(2,1)S(1)}, u32[]{:S(2)}, u32[]{:S(2)}) async-start(bf16[16,96,128]{2,1,0:T(8,128)(2,1)} %get-tuple-element.36), calls=%async_computation.1 | async-start | bytes 786432 | tf_op jit(solution)/shard_map/all_to_all | solution.py:610
  69.1 0.0 all-gather.5.cloned.1.call-start
  69.1 2.0 %collective-permute-start.1 = (bf16[64,1024]{1,0:T(8,128)(2,1)S(1)}, bf16[64,1024]{1,0:T(8,128)(2,1)S(1)}, u32[]{:S(2)}, u32[]{:S(2)}) collective-permute-start(bf16[64,1024]{1,0:T(8,128)(2,1)S(1)} %pad_maximum_fusion.1), channel_id=1, source_target_pairs={{1,0},{2,1},{3,2},{4,3},{5,4},{6,5},{7,6},{8,7},{9,8},{10,9},{11,1... | collective-permute-start | bytes 393224 | tf_op jit(solution)/shard_map/ppermute | solution.py:601
  71.2 3.8 %collective-permute-start = (bf16[64,1024]{1,0:T(8,128)(2,1)S(1)}, bf16[64,1024]{1,0:T(8,128)(2,1)S(1)}, u32[]{:S(2)}, u32[]{:S(2)}) collective-permute-start(bf16[64,1024]{1,0:T(8,128)(2,1)S(1)} %pad_maximum_fusion), channel_id=1, source_target_pairs={{0,1},{1,2},{2,3},{3,4},{4,5},{5,6},{6,7},{7,8},{8,9},{9,10},{10,1... | collective-permute-start | bytes 393224 | tf_op jit(solution)/shard_map/ppermute | solution.py:600
  75.0 12.6 %collective-permute-done.1 = bf16[64,1024]{1,0:T(8,128)(2,1)S(1)} collective-permute-done((bf16[64,1024]{1,0:T(8,128)(2,1)S(1)}, bf16[64,1024]{1,0:T(8,128)(2,1)S(1)}, u32[]{:S(2)}, u32[]{:S(2)}) %collective-permute-start.1) | collective-permute-done | bytes 131104 | tf_op jit(solution)/shard_map/ppermute | solution.py:601
  87.6 0.2 collective-permute-done
  87.8 0.7 pad_maximum_fusion.2
  88.5 0.0 all-to-all-done.1.att_ref
  88.5 9.0 %middle.1 = (bf16[128,1024]{1,0:T(8,128)(2,1)}, f32[128,1024]{1,0:T(8,128)}, bf16[16,80,128]{2,1,0:T(8,128)(2,1)}, bf16[128,2048]{1,0:T(8,128)(2,1)}) custom-call(s32[5]{0:T(128)} %stack.15.scalars, bf16[16,96,128]{2,1,0:T(8,128)(2,1)S(1)} %all-to-all-done.1.att_ref, bf16[128,1024]{1,0:T(8,128)(2,1)} %bitcast.17, ...), custom_call_target="tpu_custom_call" | custom-call | tf_op jit(solution)/shard_map/middle/pallas_call | solution.py:281
  97.5 0.0 all-gather.5.cloned.1.call-update
  97.5 17.8 %all_to_all.25.grads_ref.back_ref = bf16[16,80,128]{2,1,0:T(8,128)(2,1)S(1)} all-to-all(bf16[16,80,128]{2,1,0:T(8,128)(2,1)} %get-tuple-element.38), channel_id=1, replica_groups=mesh['dp'=16,'seq'=16] {'seq'}, dimensions={0} | all-to-all | bytes 655360 | tf_op jit(solution)/shard_map/all_to_all | solution.py:612
  115.3 14.7 %attend_back.1.grads_ref = bf16[16,192,128]{2,1,0:T(8,128)(2,1)} custom-call(s32[5]{0:T(128)} %stack.15.scalars, bf16[16,192,128]{2,1,0:T(8,128)(2,1)} %copy-done.1, bf16[16,80,128]{2,1,0:T(8,128)(2,1)S(1)} %all_to_all.25.grads_ref.back_ref, f32[64,2048]{1,0:T(8,128)} %get-tuple-element.39.out_ref, f32[1,2048]{1,0:T(1,128)} %get-tuple-element.40.lse_ref), custom_call_target="tpu_custom_call" | custom-call | flops 10737418240 | bytes 1572864 | tf_op jit(solution)/shard_map/attend_back/pallas_call | solution.py:352
  130.0 4.9 %all-to-all-start.3 = ((bf16[16,192,128]{2,1,0:T(8,128)(2,1)}), bf16[16,192,128]{2,1,0:T(8,128)(2,1)S(1)}, u32[]{:S(2)}, u32[]{:S(2)}) async-start(bf16[16,192,128]{2,1,0:T(8,128)(2,1)} %attend_back.1.grads_ref), calls=%async_computation.3 | async-start | bytes 1572864 | tf_op jit(solution)/shard_map/all_to_all | solution.py:616
  134.9 0.0 all-gather.3.cloned.1.call-done.normed_ref
  134.9 5.3 %gradient_parts.1 = (bf16[416,128]{1,0:T(8,128)(2,1)}, bf16[416,128]{1,0:T(8,128)(2,1)}, bf16[416,128]{1,0:T(8,128)(2,1)}, bf16[416,128]{1,0:T(8,128)(2,1)}) custom-call(s32[5]{0:T(128)} %stack.15.scalars, bf16[16,192,128]{2,1,0:T(8,128)(2,1)} %attend_back.1.grads_ref, bf16[16,80,128]{2,1,0:T(8,128)(2,1)} %copy-done, ...), custom_call_target="tpu_custom_call" | custom-call | flops 1073741824 | bytes 4194304 | tf_op jit(solution)/shard_map/gradient_parts/pallas_call | solution.py:470
  140.3 3.0 %collective-permute-start.3 = (bf16[416,128]{1,0:T(8,128)(2,1)}, bf16[416,128]{1,0:T(8,128)(2,1)S(1)}, u32[]{:S(2)}, u32[]{:S(2)}) collective-permute-start(bf16[416,128]{1,0:T(8,128)(2,1)} %get-tuple-element.45), channel_id=1, source_target_pairs={{0,32},{16,48},{32,0},{48,16},{64,96},{80,112},{96,64},{112,80},{1... | collective-permute-start | bytes 319496 | tf_op jit(solution)/shard_map/ppermute | solution.py:579
  143.3 0.4 collective-permute-start.4
  143.6 0.0 collective-permute-done.2.two
  143.6 5.6 %collective-permute-done.3.three = bf16[416,128]{1,0:T(8,128)(2,1)S(1)} collective-permute-done((bf16[416,128]{1,0:T(8,128)(2,1)}, bf16[416,128]{1,0:T(8,128)(2,1)S(1)}, u32[]{:S(2)}, u32[]{:S(2)}) %collective-permute-start.3) | collective-permute-done | bytes 106528 | tf_op jit(solution)/shard_map/ppermute | solution.py:579
  149.3 3.9 %collective-permute-done.4.four = bf16[416,128]{1,0:T(8,128)(2,1)S(1)} collective-permute-done((bf16[416,128]{1,0:T(8,128)(2,1)}, bf16[416,128]{1,0:T(8,128)(2,1)S(1)}, u32[]{:S(2)}, u32[]{:S(2)}) %collective-permute-start.4) | collective-permute-done | bytes 106528 | tf_op jit(solution)/shard_map/ppermute | solution.py:579
  153.1 1.7 fold_fast.1
  154.8 2.9 %out_part.1 = (bf16[512,128]{1,0:T(8,128)(2,1)}, bf16[512,128]{1,0:T(8,128)(2,1)}, bf16[512,128]{1,0:T(8,128)(2,1)}, bf16[512,128]{1,0:T(8,128)(2,1)}) custom-call(s32[5]{0:T(128)} %stack.15.scalars, bf16[512,2048]{1,0:T(8,128)(2,1)} %all-gather.5.cloned.1.call-done.pack_ref), custom_call_target="tpu_custom_call" | custom-call | tf_op jit(solution)/shard_map/out_part/pallas_call | solution.py:433
  157.7 0.3 collective-permute-start.8
  158.1 2.4 %collective-permute-start.9 = (bf16[512,128]{1,0:T(8,128)(2,1)}, bf16[512,128]{1,0:T(8,128)(2,1)S(1)}, u32[]{:S(2)}, u32[]{:S(2)}) collective-permute-start(bf16[512,128]{1,0:T(8,128)(2,1)} %get-tuple-element.59), channel_id=1, source_target_pairs={{0,32},{16,48},{32,0},{48,16},{64,96},{80,112},{96,64},{112,80},{1... | collective-permute-start | bytes 393224 | tf_op jit(solution)/shard_map/ppermute | solution.py:579
  160.4 0.7 collective-permute-start.10
  161.1 2.3 %collective-permute-start.5 = (bf16[128,128]{1,0:T(8,128)(2,1)}, bf16[128,128]{1,0:T(8,128)(2,1)S(1)}, u32[]{:S(2)}, u32[]{:S(2)}) collective-permute-start(bf16[128,128]{1,0:T(8,128)(2,1)} %get-tuple-element.53), channel_id=1, source_target_pairs={{0,64},{16,80},{32,96},{48,112},{64,0},{80,16},{96,32},{112,48},{1... | collective-permute-start | bytes 98312 | tf_op jit(solution)/shard_map/ppermute | solution.py:579
  163.4 3.2 %collective-permute-start.6 = (bf16[128,128]{1,0:T(8,128)(2,1)}, bf16[128,128]{1,0:T(8,128)(2,1)S(1)}, u32[]{:S(2)}, u32[]{:S(2)}) collective-permute-start(bf16[128,128]{1,0:T(8,128)(2,1)} %get-tuple-element.54), channel_id=1, source_target_pairs={{0,128},{16,144},{32,160},{48,176},{64,192},{80,208},{96,224},{112... | collective-permute-start | bytes 98312 | tf_op jit(solution)/shard_map/ppermute | solution.py:579
  166.6 0.0 collective-permute-done.5.refs_1_
  166.6 2.8 %collective-permute-start.7 = (bf16[128,128]{1,0:T(8,128)(2,1)}, bf16[128,128]{1,0:T(8,128)(2,1)S(1)}, u32[]{:S(2)}, u32[]{:S(2)}) collective-permute-start(bf16[128,128]{1,0:T(8,128)(2,1)} %get-tuple-element.55), channel_id=1, source_target_pairs={{0,192},{16,208},{32,224},{48,240},{64,128},{80,144},{96,160},{112... | collective-permute-start | bytes 98312 | tf_op jit(solution)/shard_map/ppermute | solution.py:579
  169.4 0.0 collective-permute-done.6.refs_2_
  169.4 2.5 %collective-permute-done.7.refs_3_ = bf16[128,128]{1,0:T(8,128)(2,1)S(1)} collective-permute-done((bf16[128,128]{1,0:T(8,128)(2,1)}, bf16[128,128]{1,0:T(8,128)(2,1)S(1)}, u32[]{:S(2)}, u32[]{:S(2)}) %collective-permute-start.7) | collective-permute-done | bytes 32800 | tf_op jit(solution)/shard_map/ppermute | solution.py:579
  171.9 0.0 collective-permute-done.8.refs_5_
  172.0 1.9 fold_slow.1
  173.9 7.6 %all-to-all-start.4 = ((bf16[16,64,128]{2,1,0:T(8,128)(2,1)}), bf16[16,64,128]{2,1,0:T(8,128)(2,1)S(1)}, u32[]{:S(2)}, u32[]{:S(2)}) async-start(bf16[16,64,128]{2,1,0:T(8,128)(2,1)} %get-tuple-element.62), calls=%async_computation.4 | async-start | bytes 524288 | tf_op jit(solution)/shard_map/all_to_all | solution.py:623
  181.4 6.2 %input_gradient.1 = bf16[128,1024]{1,0:T(8,128)(2,1)} custom-call(bf16[16,192,128]{2,1,0:T(8,128)(2,1)S(1)} %all-to-all-done.3.joined_ref, bf16[1024,3072]{1,0:T(8,128)(2,1)} %weight_ref.3, bf16[128,1024]{1,0:T(8,128)(2,1)} %bitcast.18, f32[128,1024]{1,0:T(8,128)} %get-tuple-element.41.res_grad_ref), custom_call_target="tpu_custom_call" | custom-call | tf_op jit(solution)/shard_map/input_gradient/pallas_call | solution.py:398
  187.7 0.1 copy.12
  187.8 0.7 copy.13
  188.5 2.0 %all-to-all-done.4.refs_0_ = bf16[16,64,128]{2,1,0:T(8,128)(2,1)S(1)} async-done(((bf16[16,64,128]{2,1,0:T(8,128)(2,1)}), bf16[16,64,128]{2,1,0:T(8,128)(2,1)S(1)}, u32[]{:S(2)}, u32[]{:S(2)}) %all-to-all-start.4) | async-done | bytes 262176 | tf_op jit(solution)/shard_map/all_to_all | solution.py:623
  190.6 0.8 finish.1
  (19 shorter events, 0.1 us)
Async XLA Ops:
  7.2 127.8 %all-gather.3.cloned.1.call-start = ((), (), s32[]{:S(2)}) async-start(), calls=%async_computation.5 | async-start | bytes 4456448 | tf_op jit(solution)/shard_map/all_gather | solution.py:608
  7.2 17.9 %copy-start.2 = (bf16[1,128,1024]{2,1,0:T(8,128)(2,1)S(1)}, bf16[1,128,1024]{2,1,0:T(8,128)(2,1)}, u32[]{:S(2)}) copy-start(bf16[1,128,1024]{2,1,0:T(8,128)(2,1)} %param.6) | copy-start | bytes 786436
  7.2 17.9 %copy-start.3 = (bf16[1,128,1024]{2,1,0:T(8,128)(2,1)S(1)}, bf16[1,128,1024]{2,1,0:T(8,128)(2,1)}, u32[]{:S(2)}) copy-start(bf16[1,128,1024]{2,1,0:T(8,128)(2,1)} %param.7) | copy-start | bytes 786436
  14.2 35.5 %all-to-all-start = ((bf16[16,192,128]{2,1,0:T(8,128)(2,1)}), bf16[16,192,128]{2,1,0:T(8,128)(2,1)S(1)}, u32[]{:S(2)}, u32[]{:S(2)}) async-start(bf16[16,192,128]{2,1,0:T(8,128)(2,1)} %get-tuple-element.35), calls=%async_computation | async-start | bytes 1572864 | tf_op jit(solution)/shard_map/all_to_all | solution.py:606
  49.7 12.4 %copy-start.1 = (bf16[16,192,128]{2,1,0:T(8,128)(2,1)}, bf16[16,192,128]{2,1,0:T(8,128)(2,1)S(1)}, u32[]{:S(2)}) copy-start(bf16[16,192,128]{2,1,0:T(8,128)(2,1)S(1)} %all-to-all-done.heads_ref) | copy-start | bytes 2359300
  62.1 26.4 %all-to-all-start.1 = ((bf16[16,96,128]{2,1,0:T(8,128)(2,1)}), bf16[16,96,128]{2,1,0:T(8,128)(2,1)S(1)}, u32[]{:S(2)}, u32[]{:S(2)}) async-start(bf16[16,96,128]{2,1,0:T(8,128)(2,1)} %get-tuple-element.36), calls=%async_computation.1 | async-start | bytes 786432 | tf_op jit(solution)/shard_map/all_to_all | solution.py:610
  69.1 85.8 %all-gather.5.cloned.1.call-start = ((), (), s32[]{:S(2)}) async-start(), calls=%async_computation.6 | async-start | bytes 2621440 | tf_op jit(solution)/shard_map/all_gather | solution.py:614
  69.1 18.5 %collective-permute-start.1 = (bf16[64,1024]{1,0:T(8,128)(2,1)S(1)}, bf16[64,1024]{1,0:T(8,128)(2,1)S(1)}, u32[]{:S(2)}, u32[]{:S(2)}) collective-permute-start(bf16[64,1024]{1,0:T(8,128)(2,1)S(1)} %pad_maximum_fusion.1), channel_id=1, source_target_pairs={{1,0},{2,1},{3,2},{4,3},{5,4},{6,5},{7,6},{8,7},{9,8},{10,9},{11,1... | collective-permute-start | bytes 393224 | tf_op jit(solution)/shard_map/ppermute | solution.py:601
  71.2 16.6 %collective-permute-start = (bf16[64,1024]{1,0:T(8,128)(2,1)S(1)}, bf16[64,1024]{1,0:T(8,128)(2,1)S(1)}, u32[]{:S(2)}, u32[]{:S(2)}) collective-permute-start(bf16[64,1024]{1,0:T(8,128)(2,1)S(1)} %pad_maximum_fusion), channel_id=1, source_target_pairs={{0,1},{1,2},{2,3},{3,4},{4,5},{5,6},{6,7},{7,8},{8,9},{9,10},{10,1... | collective-permute-start | bytes 393224 | tf_op jit(solution)/shard_map/ppermute | solution.py:600
  115.3 14.7 %copy-start = (bf16[16,80,128]{2,1,0:T(8,128)(2,1)}, bf16[16,80,128]{2,1,0:T(8,128)(2,1)S(1)}, u32[]{:S(2)}) copy-start(bf16[16,80,128]{2,1,0:T(8,128)(2,1)S(1)} %all_to_all.25.grads_ref.back_ref) | copy-start | bytes 983044
  130.0 43.9 %all-to-all-start.3 = ((bf16[16,192,128]{2,1,0:T(8,128)(2,1)}), bf16[16,192,128]{2,1,0:T(8,128)(2,1)S(1)}, u32[]{:S(2)}, u32[]{:S(2)}) async-start(bf16[16,192,128]{2,1,0:T(8,128)(2,1)} %attend_back.1.grads_ref), calls=%async_computation.3 | async-start | bytes 1572864 | tf_op jit(solution)/shard_map/all_to_all | solution.py:616
  140.3 3.4 %collective-permute-start.2 = (bf16[416,128]{1,0:T(8,128)(2,1)}, bf16[416,128]{1,0:T(8,128)(2,1)S(1)}, u32[]{:S(2)}, u32[]{:S(2)}) collective-permute-start(bf16[416,128]{1,0:T(8,128)(2,1)} %get-tuple-element.44), channel_id=1, source_target_pairs={{0,16},{16,0},{32,48},{48,32},{64,80},{80,64},{96,112},{112,96},{1... | collective-permute-start | bytes 319496 | tf_op jit(solution)/shard_map/ppermute | solution.py:579
  140.3 9.0 %collective-permute-start.3 = (bf16[416,128]{1,0:T(8,128)(2,1)}, bf16[416,128]{1,0:T(8,128)(2,1)S(1)}, u32[]{:S(2)}, u32[]{:S(2)}) collective-permute-start(bf16[416,128]{1,0:T(8,128)(2,1)} %get-tuple-element.45), channel_id=1, source_target_pairs={{0,32},{16,48},{32,0},{48,16},{64,96},{80,112},{96,64},{112,80},{1... | collective-permute-start | bytes 319496 | tf_op jit(solution)/shard_map/ppermute | solution.py:579
  143.3 9.9 %collective-permute-start.4 = (bf16[416,128]{1,0:T(8,128)(2,1)}, bf16[416,128]{1,0:T(8,128)(2,1)S(1)}, u32[]{:S(2)}, u32[]{:S(2)}) collective-permute-start(bf16[416,128]{1,0:T(8,128)(2,1)} %get-tuple-element.46), channel_id=1, source_target_pairs={{0,48},{16,32},{32,16},{48,0},{64,112},{80,96},{96,80},{112,64},{1... | collective-permute-start | bytes 319496 | tf_op jit(solution)/shard_map/ppermute | solution.py:579
  157.7 14.2 %collective-permute-start.8 = (bf16[512,128]{1,0:T(8,128)(2,1)}, bf16[512,128]{1,0:T(8,128)(2,1)S(1)}, u32[]{:S(2)}, u32[]{:S(2)}) collective-permute-start(bf16[512,128]{1,0:T(8,128)(2,1)} %get-tuple-element.58), channel_id=1, source_target_pairs={{0,16},{16,0},{32,48},{48,32},{64,80},{80,64},{96,112},{112,96},{1... | collective-permute-start | bytes 393224 | tf_op jit(solution)/shard_map/ppermute | solution.py:579
  158.1 13.9 %collective-permute-start.9 = (bf16[512,128]{1,0:T(8,128)(2,1)}, bf16[512,128]{1,0:T(8,128)(2,1)S(1)}, u32[]{:S(2)}, u32[]{:S(2)}) collective-permute-start(bf16[512,128]{1,0:T(8,128)(2,1)} %get-tuple-element.59), channel_id=1, source_target_pairs={{0,32},{16,48},{32,0},{48,16},{64,96},{80,112},{96,64},{112,80},{1... | collective-permute-start | bytes 393224 | tf_op jit(solution)/shard_map/ppermute | solution.py:579
  160.4 11.5 %collective-permute-start.10 = (bf16[512,128]{1,0:T(8,128)(2,1)}, bf16[512,128]{1,0:T(8,128)(2,1)S(1)}, u32[]{:S(2)}, u32[]{:S(2)}) collective-permute-start(bf16[512,128]{1,0:T(8,128)(2,1)} %get-tuple-element.60), channel_id=1, source_target_pairs={{0,48},{16,32},{32,16},{48,0},{64,112},{80,96},{96,80},{112,64},{1... | collective-permute-start | bytes 393224 | tf_op jit(solution)/shard_map/ppermute | solution.py:579
  161.1 5.5 %collective-permute-start.5 = (bf16[128,128]{1,0:T(8,128)(2,1)}, bf16[128,128]{1,0:T(8,128)(2,1)S(1)}, u32[]{:S(2)}, u32[]{:S(2)}) collective-permute-start(bf16[128,128]{1,0:T(8,128)(2,1)} %get-tuple-element.53), channel_id=1, source_target_pairs={{0,64},{16,80},{32,96},{48,112},{64,0},{80,16},{96,32},{112,48},{1... | collective-permute-start | bytes 98312 | tf_op jit(solution)/shard_map/ppermute | solution.py:579
  163.4 6.0 %collective-permute-start.6 = (bf16[128,128]{1,0:T(8,128)(2,1)}, bf16[128,128]{1,0:T(8,128)(2,1)S(1)}, u32[]{:S(2)}, u32[]{:S(2)}) collective-permute-start(bf16[128,128]{1,0:T(8,128)(2,1)} %get-tuple-element.54), channel_id=1, source_target_pairs={{0,128},{16,144},{32,160},{48,176},{64,192},{80,208},{96,224},{112... | collective-permute-start | bytes 98312 | tf_op jit(solution)/shard_map/ppermute | solution.py:579
  166.6 5.3 %collective-permute-start.7 = (bf16[128,128]{1,0:T(8,128)(2,1)}, bf16[128,128]{1,0:T(8,128)(2,1)S(1)}, u32[]{:S(2)}, u32[]{:S(2)}) collective-permute-start(bf16[128,128]{1,0:T(8,128)(2,1)} %get-tuple-element.55), channel_id=1, source_target_pairs={{0,192},{16,208},{32,224},{48,240},{64,128},{80,144},{96,160},{112... | collective-permute-start | bytes 98312 | tf_op jit(solution)/shard_map/ppermute | solution.py:579
  173.9 16.7 %all-to-all-start.4 = ((bf16[16,64,128]{2,1,0:T(8,128)(2,1)}), bf16[16,64,128]{2,1,0:T(8,128)(2,1)S(1)}, u32[]{:S(2)}, u32[]{:S(2)}) async-start(bf16[16,64,128]{2,1,0:T(8,128)(2,1)} %get-tuple-element.62), calls=%async_computation.4 | async-start | bytes 524288 | tf_op jit(solution)/shard_map/all_to_all | solution.py:623
  181.4 6.2 %copy-start.4 = (f32[64,192]{1,0:T(8,128)S(1)}, f32[64,192]{1,0:T(8,128)}, u32[]{:S(2)}) copy-start(f32[64,192]{1,0:T(8,128)} %get-tuple-element.61) | copy-start | bytes 147460
Sparse Core Ops, SparseCore 0:
  14.3 94.6 all-gather.2
  110.9 35.9 all-gather.4

commit v9 on v8

--- a/solution.py
+++ b/solution.py
@@ -19,7 +19,8 @@
 CUT = 96
 FAST = 4
 SLOW = 4
-TAPS = SLOW * CUT
+TAPS = FAST * CUT
+LAST = CUT + KW + 1
 OUT = 8 * HD
 
 
@@ -415,37 +416,11 @@
     )(local_memory(joined), w_qkv, frames, res_grad)
 
 
-def out_part_kernel(scalars, pack_ref, *rest):
-    send_refs, part = rest[:FAST], rest[FAST]
-    width = pack_ref.shape[1] // 2
-    block = FAST * HD
-    first = pl.multiple_of(width + scalars[4] * block, block)
-    part[...] = dot(pack_ref[:, pl.ds(first, block)].T, pack_ref[:, 0:width])
-    for k, send_ref in enumerate(send_refs):
-        rows = pl.ds(pl.multiple_of((scalars[3] ^ k) * HD, HD), HD)
-        for c in range(width // 128):
-            send_ref[c * HD : (c + 1) * HD, :] = part[rows, c * 128 : (c + 1) * 128].astype(BF16)
-
-
-def out_part(scalars, packs):
-    width = packs.shape[1] // 2
-    vmem = pl.BlockSpec(memory_space=pltpu.VMEM)
-    return pl.pallas_call(
-        out_part_kernel,
-        in_specs=[SMEM, vmem],
-        out_shape=[jax.ShapeDtypeStruct((OUT, 128), BF16)] * FAST,
-        scratch_shapes=[pltpu.VMEM((FAST * HD, width), F32)],
-        compiler_params=params(),
-        name="out_part",
-    )(scalars, packs)
-
-
 def parts_kernel(scalars, grads_ref, back_ref, normed_ref, *rest):
-    send_refs, columns, pieces = rest[:FAST], rest[FAST], rest[FAST + 1]
+    send_refs, columns = rest[:SLOW], rest[SLOW]
     count, wide, rows = grads_ref.shape
-    slow = pl.program_id(0)
-
-    @pl.when(slow == 0)
+
+    @pl.when(pl.program_id(0) == 0)
     def _():
         taps = jnp.zeros(((KW + 1) // 2, rows), F32)
         for i in range(count):
@@ -457,11 +432,16 @@
 
     part = dot(columns[...], normed_ref[...])
     each = part.shape[1] // FAST
+    pieces = []
     for i in range(FAST):
         piece = part[:, i * each : (i + 1) * each]
-        pieces[i] = jnp.concatenate([piece[0:CUT], piece[CUT:]], axis=1).astype(BF16)
+        pieces.append(jnp.concatenate([piece[0:CUT], piece[CUT:]], axis=1).astype(BF16))
     for k, send_ref in enumerate(send_refs):
-        send_ref[pl.ds(pl.multiple_of(slow * CUT, CUT), CUT), :] = pieces[scalars[3] ^ k]
+
+        @pl.when(pl.program_id(0) == k)
+        def _():
+            for i, piece in enumerate(pieces):
+                send_ref[i * CUT : (i + 1) * CUT, :] = piece
 
 
 def gradient_parts(scalars, grads, back, normed_all):
@@ -469,18 +449,19 @@
     total, width = normed_all.shape
     return pl.pallas_call(
         parts_kernel,
-        grid=(SLOW,),
-        in_specs=[
-            SMEM,
-            whole(grads.shape),
-            whole(back.shape),
-            pl.BlockSpec((total, width // SLOW), lambda j: (0, j)),
-        ],
-        out_specs=[whole((TAPS + KW + 1, 128))] * FAST,
-        out_shape=[jax.ShapeDtypeStruct((TAPS + KW + 1, 128), BF16)] * FAST,
-        scratch_shapes=[pltpu.VMEM((wide, total), BF16), pltpu.VMEM((FAST, CUT, 128), BF16)],
-        compiler_params=params(),
-        cost_estimate=cost(2 * 256 * total * width, total * width * 2),
+        grid_spec=pltpu.PrefetchScalarGridSpec(
+            num_scalar_prefetch=1,
+            grid=(SLOW,),
+            in_specs=[
+                pl.BlockSpec(grads.shape, lambda j, place: (0, 0, 0)),
+                pl.BlockSpec(back.shape, lambda j, place: (0, 0, 0)),
+                pl.BlockSpec((total, width // SLOW), lambda j, place: (0, place[4] ^ j)),
+            ],
+            out_specs=[pl.BlockSpec((TAPS + KW + 1, 128), lambda j, place: (0, 0))] * SLOW,
+            scratch_shapes=[pltpu.VMEM((wide, total), BF16)],
+        ),
+        out_shape=[jax.ShapeDtypeStruct((TAPS + KW + 1, 128), BF16)] * SLOW,
+        compiler_params=params(),
         name="gradient_parts",
     )(scalars, grads, back, normed_all)
 
@@ -489,37 +470,48 @@
     return (own.astype(F32) + one.astype(F32)) + (two.astype(F32) + three.astype(F32))
 
 
-def fold_fast_kernel(scalars, one, two, three, four, *rest):
-    send_refs, pieces = rest[:SLOW], rest[SLOW]
+def fold_first_kernel(scalars, one, two, three, four, pack_ref, *rest):
+    send_refs, pieces, outer = rest[:FAST], *rest[FAST:]
+    width = pack_ref.shape[1] // 2
+    block = FAST * HD
+    first = pl.multiple_of(width + scalars[4] * block, block)
+    outer[...] = dot(pack_ref[:, pl.ds(first, block)].T, pack_ref[:, 0:width])
     total = sum_four(one[...], two[...], three[...], four[...])
     pair = halves(joined_halves(total[TAPS:]))
-    for i in range(SLOW):
+    for i in range(FAST):
         pieces[i] = total[i * CUT : (i + 1) * CUT].astype(BF16)
     for k, send_ref in enumerate(send_refs):
-        send_ref[0:CUT, :] = pieces[scalars[4] ^ k]
-        send_ref[CUT:, :] = pair
-
-
-def fold_fast(scalars, blocks):
+        send_ref[0:CUT, :] = pieces[scalars[3] ^ k]
+        send_ref[CUT:LAST, :] = pair
+        own = pl.ds(pl.multiple_of((scalars[3] ^ k) * HD, HD), HD)
+        for c in range(width // 128):
+            at = LAST + c * HD
+            send_ref[at : at + HD, :] = outer[own, c * 128 : (c + 1) * 128].astype(BF16)
+
+
+def fold_first(scalars, blocks, packs):
     vmem = pl.BlockSpec(memory_space=pltpu.VMEM)
     return pl.pallas_call(
-        fold_fast_kernel,
-        in_specs=[SMEM] + [vmem] * 4,
-        out_shape=[jax.ShapeDtypeStruct((CUT + KW + 1, 128), BF16)] * SLOW,
-        scratch_shapes=[pltpu.VMEM((SLOW, CUT, 128), BF16)],
-        compiler_params=params(),
-        name="fold_fast",
-    )(scalars, *blocks)
-
-
-def fold_slow_kernel(*refs, scale):
-    qkv_ref, send_ref = refs[8:]
+        fold_first_kernel,
+        in_specs=[SMEM] + [vmem] * 5,
+        out_shape=[jax.ShapeDtypeStruct((LAST + OUT, 128), BF16)] * FAST,
+        scratch_shapes=[
+            pltpu.VMEM((FAST, CUT, 128), BF16),
+            pltpu.VMEM((FAST * HD, packs.shape[1] // 2), F32),
+        ],
+        compiler_params=params(),
+        name="fold_first",
+    )(scalars, *blocks, packs)
+
+
+def fold_last_kernel(*refs, scale):
+    qkv_ref, send_ref = refs[4:]
     total = sum_four(*(ref[...] for ref in refs[0:4]))
     model_rows = (total[0:CUT] * scale).T
     qkv_ref[:, 0:CUT] = model_rows[0:HD]
     qkv_ref[:, CUT:] = model_rows[HD:]
-    pair = halves(joined_halves(total[CUT:]))
-    outer = sum_four(*(ref[...] for ref in refs[4:8]))
+    pair = halves(joined_halves(total[CUT:LAST]))
+    outer = total[LAST:]
     count = send_ref.shape[0]
     each = HD // count
     for i in range(count):
@@ -528,18 +520,18 @@
         send_ref[i, OUT // count :, :] = pair
 
 
-def fold_slow(blocks, out_blocks, seq_count, scale):
+def fold_last(blocks, seq_count, scale):
     vmem = pl.BlockSpec(memory_space=pltpu.VMEM)
     return pl.pallas_call(
-        lambda *refs: fold_slow_kernel(*refs, scale=scale),
-        in_specs=[vmem] * 8,
+        lambda *refs: fold_last_kernel(*refs, scale=scale),
+        in_specs=[vmem] * 4,
         out_shape=[
             jax.ShapeDtypeStruct((HD, 3 * HD), F32),
             jax.ShapeDtypeStruct((seq_count, OUT // seq_count + KW + 1, 128), BF16),
         ],
         compiler_params=params(),
-        name="fold_slow",
-    )(*blocks, *out_blocks)
+        name="fold_last",
+    )(*blocks)
 
 
 def finish_kernel(recv_ref, out_ref, taps_ref, *, scale):
@@ -614,11 +606,9 @@
     packs = lax.all_gather(pack, "dp", axis=0, axis_index_groups=far, tiled=True)
     send = attend_back(scalars, heads, local_memory(back), out, lse)
     joined = lax.all_to_all(send, "seq", 0, 0, tiled=True)
-    parts = exchange(gradient_parts(scalars, send, back, normed_all), 1)
-    parts, packs = lax.optimization_barrier((fold_fast(scalars, parts), packs))
-    parts = exchange(parts, FAST)
-    outer = exchange(out_part(scalars, packs), 1)
-    qkv, send = fold_slow(parts, outer, seq_count, grad_scale)
+    parts = exchange(gradient_parts(scalars, send, back, normed_all), FAST)
+    parts = exchange(fold_first(scalars, parts, packs), 1)
+    qkv, send = fold_last(parts, seq_count, grad_scale)
     input_grad = input_gradient(joined, w_qkv, x, res_grad)
     recv = lax.all_to_all(send, "seq", 0, 0, tiled=True)
     out_total, taps_total = finish(local_memory(recv), width, grad_scale)

time: 199 us -> 196 us (0.985)
  starting transfers between devices: 50 us -> 43.9 us
  waiting for transfers between devices: 51.5 us -> 55.8 us
    ppermute x9 -> x6, starting transfers between devices: 15.1 us -> 8.06 us  [exchange(): lax.ppermute(block, 'dp', pairs(k))]
    all_gather x1, waiting for transfers between devices: 0.01 us -> 2.55 us  [local(): lax.all_gather(pack, 'dp', axis=0, axis_index_groups=far, tiled=True)]
    pallas_call x4 -> x3, Pallas kernels: 11.8 us -> 10.9 us  [the longest x1 6.03 us: gradient_parts(): pl.pallas_call(parts_kernel, grid_spec=pltpu.PrefetchScalarGridSpec(num_s...]
    ppermute x9 -> x6, waiting for transfers between devices: 12 us -> 12.1 us  [exchange(): lax.ppermute(block, 'dp', pairs(k))]
  transfers between devices with their start and end apart: 17 -> 14, of which waited for: 7 -> 10; matrix products, arithmetic and copies ran while one was open for 1% -> 1% of each run, Pallas kernels for 27% -> 27%
where the time goes in v9:
time: 196 us; the launch traced here: 195 us
  Pallas kernels  60.9 us (31%)
  waiting for transfers between devices  55.8 us (28%)
  starting transfers between devices  43.9 us (22%)
  blocking collectives  17.4 us (9%)
  between operations  14.8 us (8%)
    all_to_all x1, waiting for transfers between devices, local(): heads = lax.all_to_all(send, 'seq', 0, 0, tiled=True)  24.7 us
    all_to_all x1, blocking collectives, local(): back = lax.all_to_all(send, 'seq', 0, 0, tiled=True)  17.4 us
    pallas_call x1, Pallas kernels, attend_back(): pl.pallas_call(attend_back_kernel, in_specs=[SMEM] + [vmem] * 4, out_shap...  14.7 us
    ppermute x1, waiting for transfers between devices, local(): lax.ppermute(jnp.concatenate([x[:HALO], g[:HALO]], axis=0), 'seq', backward)  12.6 us
    pallas_call x1, Pallas kernels, attend(): pl.pallas_call(attend_kernel, in_specs=[SMEM, pl.BlockSpec(memory_space=p...  12.4 us
    ppermute x6, waiting for transfers between devices, exchange(): lax.ppermute(block, 'dp', pairs(k))  12.1 us
    all_to_all x1, starting transfers between devices, local(): heads = lax.all_to_all(send, 'seq', 0, 0, tiled=True)  9.52 us
    pallas_call x1, Pallas kernels, middle(): pl.pallas_call(middle_kernel, in_specs=[SMEM] + [vmem] * 7, out_shape=[ja...  8.96 us
  transfers between devices with their start and end apart: 14, of which 10 were waited for; matrix products, arithmetic and copies ran while one was open for 1% of the time, Pallas kernels for 27%

profile of v9, /device:TPU:32, one launch (start us, length us, event | category | flops | bytes accessed | tf_op | source)
XLA Modules:
  0.0 195.2 jit_solution(2403305370779905183)
XLA Ops:
  7.2 0.0 all-gather.3.cloned.1.call-start
  7.2 0.0 copy-start.2
  7.2 0.0 copy-start.3
  7.2 7.0 %project.1 = (bf16[128,1024]{1,0:T(8,128)(2,1)}, bf16[16,192,128]{2,1,0:T(8,128)(2,1)}) custom-call(bf16[128,1024]{1,0:T(8,128)(2,1)} %bitcast.16, bf16[1024,3072]{1,0:T(8,128)(2,1)} %weight_ref.3), custom_call_target="tpu_custom_call" | custom-call | tf_op jit(solution)/shard_map/project/pallas_call | solution.py:89
  14.2 0.0 all-gather.3.cloned.1.call-update
  14.2 9.5 %all-to-all-start = ((bf16[16,192,128]{2,1,0:T(8,128)(2,1)}), bf16[16,192,128]{2,1,0:T(8,128)(2,1)S(1)}, u32[]{:S(2)}, u32[]{:S(2)}) async-start(bf16[16,192,128]{2,1,0:T(8,128)(2,1)} %get-tuple-element.26), calls=%async_computation | async-start | bytes 1572864 | tf_op jit(solution)/shard_map/all_to_all | solution.py:598
  24.4 0.6 stack.15.scalars
  25.0 0.0 copy-done.3
  25.1 24.7 %all-to-all-done.heads_ref = bf16[16,192,128]{2,1,0:T(8,128)(2,1)S(1)} async-done(((bf16[16,192,128]{2,1,0:T(8,128)(2,1)}), bf16[16,192,128]{2,1,0:T(8,128)(2,1)S(1)}, u32[]{:S(2)}, u32[]{:S(2)}) %all-to-all-start) | async-done | bytes 786464 | tf_op jit(solution)/shard_map/all_to_all | solution.py:598
  49.7 12.4 %attend.1 = (bf16[16,96,128]{2,1,0:T(8,128)(2,1)}, f32[64,2048]{1,0:T(8,128)}, f32[1,2048]{1,0:T(1,128)}) custom-call(s32[5]{0:T(128)} %stack.15.scalars, bf16[16,192,128]{2,1,0:T(8,128)(2,1)S(1)} %all-to-all-done.heads_ref), custom_call_target="tpu_custom_call" | custom-call | flops 4294967296 | bytes 786432 | tf_op jit(solution)/shard_map/attend/pallas_call | solution.py:163
  62.1 7.0 %all-to-all-start.1 = ((bf16[16,96,128]{2,1,0:T(8,128)(2,1)}), bf16[16,96,128]{2,1,0:T(8,128)(2,1)S(1)}, u32[]{:S(2)}, u32[]{:S(2)}) async-start(bf16[16,96,128]{2,1,0:T(8,128)(2,1)} %get-tuple-element.27), calls=%async_computation.1 | async-start | bytes 786432 | tf_op jit(solution)/shard_map/all_to_all | solution.py:602
  69.1 0.0 all-gather.5.cloned.1.call-start
  69.2 2.0 %collective-permute-start.1 = (bf16[64,1024]{1,0:T(8,128)(2,1)S(1)}, bf16[64,1024]{1,0:T(8,128)(2,1)S(1)}, u32[]{:S(2)}, u32[]{:S(2)}) collective-permute-start(bf16[64,1024]{1,0:T(8,128)(2,1)S(1)} %pad_maximum_fusion.1), channel_id=1, source_target_pairs={{1,0},{2,1},{3,2},{4,3},{5,4},{6,5},{7,6},{8,7},{9,8},{10,9},{11,1... | collective-permute-start | bytes 393224 | tf_op jit(solution)/shard_map/ppermute | solution.py:593
  71.2 3.8 %collective-permute-start = (bf16[64,1024]{1,0:T(8,128)(2,1)S(1)}, bf16[64,1024]{1,0:T(8,128)(2,1)S(1)}, u32[]{:S(2)}, u32[]{:S(2)}) collective-permute-start(bf16[64,1024]{1,0:T(8,128)(2,1)S(1)} %pad_maximum_fusion), channel_id=1, source_target_pairs={{0,1},{1,2},{2,3},{3,4},{4,5},{5,6},{6,7},{7,8},{8,9},{9,10},{10,1... | collective-permute-start | bytes 393224 | tf_op jit(solution)/shard_map/ppermute | solution.py:592
  75.0 12.6 %collective-permute-done.1 = bf16[64,1024]{1,0:T(8,128)(2,1)S(1)} collective-permute-done((bf16[64,1024]{1,0:T(8,128)(2,1)S(1)}, bf16[64,1024]{1,0:T(8,128)(2,1)S(1)}, u32[]{:S(2)}, u32[]{:S(2)}) %collective-permute-start.1) | collective-permute-done | bytes 131104 | tf_op jit(solution)/shard_map/ppermute | solution.py:593
  87.7 0.4 collective-permute-done
  88.1 0.7 pad_maximum_fusion.2
  88.8 0.0 all-to-all-done.1.att_ref
  88.8 9.0 %middle.1 = (bf16[128,1024]{1,0:T(8,128)(2,1)}, f32[128,1024]{1,0:T(8,128)}, bf16[16,80,128]{2,1,0:T(8,128)(2,1)}, bf16[128,2048]{1,0:T(8,128)(2,1)}) custom-call(s32[5]{0:T(128)} %stack.15.scalars, bf16[16,96,128]{2,1,0:T(8,128)(2,1)S(1)} %all-to-all-done.1.att_ref, bf16[128,1024]{1,0:T(8,128)(2,1)} %bitcast.17, ...), custom_call_target="tpu_custom_call" | custom-call | tf_op jit(solution)/shard_map/middle/pallas_call | solution.py:282
  97.8 0.0 all-gather.5.cloned.1.call-update
  97.8 17.4 %all_to_all.25.grads_ref.back_ref = bf16[16,80,128]{2,1,0:T(8,128)(2,1)S(1)} all-to-all(bf16[16,80,128]{2,1,0:T(8,128)(2,1)} %get-tuple-element.29), channel_id=1, replica_groups=mesh['dp'=16,'seq'=16] {'seq'}, dimensions={0} | all-to-all | bytes 655360 | tf_op jit(solution)/shard_map/all_to_all | solution.py:604
  115.3 14.7 %attend_back.1.grads_ref = bf16[16,192,128]{2,1,0:T(8,128)(2,1)} custom-call(s32[5]{0:T(128)} %stack.15.scalars, bf16[16,192,128]{2,1,0:T(8,128)(2,1)} %copy-done.1, bf16[16,80,128]{2,1,0:T(8,128)(2,1)S(1)} %all_to_all.25.grads_ref.back_ref, f32[64,2048]{1,0:T(8,128)} %get-tuple-element.30.out_ref, f32[1,2048]{1,0:T(1,128)} %get-tuple-element.31.lse_ref), custom_call_target="tpu_custom_call" | custom-call | flops 10737418240 | bytes 1572864 | tf_op jit(solution)/shard_map/attend_back/pallas_call | solution.py:353
  129.9 0.0 copy-done
  130.0 5.0 %all-to-all-start.3 = ((bf16[16,192,128]{2,1,0:T(8,128)(2,1)}), bf16[16,192,128]{2,1,0:T(8,128)(2,1)S(1)}, u32[]{:S(2)}, u32[]{:S(2)}) async-start(bf16[16,192,128]{2,1,0:T(8,128)(2,1)} %attend_back.1.grads_ref), calls=%async_computation.3 | async-start | bytes 1572864 | tf_op jit(solution)/shard_map/all_to_all | solution.py:608
  135.0 0.0 all-gather.3.cloned.1.call-done.normed_ref
  135.0 6.0 %gradient_parts.1 = (bf16[416,128]{1,0:T(8,128)(2,1)}, bf16[416,128]{1,0:T(8,128)(2,1)}, bf16[416,128]{1,0:T(8,128)(2,1)}, bf16[416,128]{1,0:T(8,128)(2,1)}) custom-call(s32[5]{0:T(128)} %stack.15.scalars, bf16[16,192,128]{2,1,0:T(8,128)(2,1)} %attend_back.1.grads_ref, bf16[16,80,128]{2,1,0:T(8,128)(2,1)} %copy-done, ...), custom_call_target="tpu_custom_call" | custom-call | tf_op jit(solution)/shard_map/gradient_parts/pallas_call | solution.py:450
  141.0 1.6 collective-permute-start.2
  142.6 2.9 %collective-permute-start.3 = (bf16[416,128]{1,0:T(8,128)(2,1)}, bf16[416,128]{1,0:T(8,128)(2,1)S(1)}, u32[]{:S(2)}, u32[]{:S(2)}) collective-permute-start(bf16[416,128]{1,0:T(8,128)(2,1)} %get-tuple-element.36), channel_id=1, source_target_pairs={{0,128},{16,144},{32,160},{48,176},{64,192},{80,208},{96,224},{112... | collective-permute-start | bytes 319496 | tf_op jit(solution)/shard_map/ppermute | solution.py:571
  145.5 0.2 collective-permute-start.4
  145.7 2.6 %all-gather.5.cloned.1.call-done.pack_ref = bf16[512,2048]{1,0:T(8,128)(2,1)} async-done(((bf16[128,2048]{1,0:T(8,128)(2,1)}), bf16[512,2048]{1,0:T(8,128)(2,1)}) %all-gather.5.cloned.1.call-update) | async-done | bytes 2097168 | tf_op jit(solution)/shard_map/all_gather | solution.py:606
  148.3 0.2 collective-permute-done.2.two
  148.5 2.7 %collective-permute-done.3.three = bf16[416,128]{1,0:T(8,128)(2,1)S(1)} collective-permute-done((bf16[416,128]{1,0:T(8,128)(2,1)}, bf16[416,128]{1,0:T(8,128)(2,1)S(1)}, u32[]{:S(2)}, u32[]{:S(2)}) %collective-permute-start.3) | collective-permute-done | bytes 106528 | tf_op jit(solution)/shard_map/ppermute | solution.py:571
  151.2 1.1 collective-permute-done.4.four
  152.3 3.0 %fold_first.1 = (bf16[640,128]{1,0:T(8,128)(2,1)}, bf16[640,128]{1,0:T(8,128)(2,1)}, bf16[640,128]{1,0:T(8,128)(2,1)}, bf16[640,128]{1,0:T(8,128)(2,1)}) custom-call(s32[5]{0:T(128)} %stack.15.scalars, bf16[416,128]{1,0:T(8,128)(2,1)} %get-tuple-element.34.one, bf16[416,128]{1,0:T(8,128)(2,1)S(1)} %collective-permute-done.2.two, ...), custom_call_target="tpu_custom_call" | custom-call | tf_op jit(solution)/shard_map/fold_first/pallas_call | solution.py:494
  155.3 0.0 collective-permute-start.5
  155.3 3.0 %collective-permute-start.6 = (bf16[640,128]{1,0:T(8,128)(2,1)}, bf16[640,128]{1,0:T(8,128)(2,1)S(1)}, u32[]{:S(2)}, u32[]{:S(2)}) collective-permute-start(bf16[640,128]{1,0:T(8,128)(2,1)} %get-tuple-element.41), channel_id=1, source_target_pairs={{0,32},{16,48},{32,0},{48,16},{64,96},{80,112},{96,64},{112,80},{1... | collective-permute-start | bytes 491528 | tf_op jit(solution)/shard_map/ppermute | solution.py:571
  158.3 0.4 collective-permute-start.7
  158.7 0.0 collective-permute-done.5.refs_1_
  158.7 5.3 %collective-permute-done.6.refs_2_ = bf16[640,128]{1,0:T(8,128)(2,1)S(1)} collective-permute-done((bf16[640,128]{1,0:T(8,128)(2,1)}, bf16[640,128]{1,0:T(8,128)(2,1)S(1)}, u32[]{:S(2)}, u32[]{:S(2)}) %collective-permute-start.6) | collective-permute-done | bytes 163872 | tf_op jit(solution)/shard_map/ppermute | solution.py:571
  164.0 2.7 %collective-permute-done.7.refs_3_ = bf16[640,128]{1,0:T(8,128)(2,1)S(1)} collective-permute-done((bf16[640,128]{1,0:T(8,128)(2,1)}, bf16[640,128]{1,0:T(8,128)(2,1)S(1)}, u32[]{:S(2)}, u32[]{:S(2)}) %collective-permute-start.7) | collective-permute-done | bytes 163872 | tf_op jit(solution)/shard_map/ppermute | solution.py:571
  166.8 1.9 fold_last.1
  168.6 0.0 all-to-all-done.3.joined_ref
  168.6 8.4 %all-to-all-start.4 = ((bf16[16,64,128]{2,1,0:T(8,128)(2,1)}), bf16[16,64,128]{2,1,0:T(8,128)(2,1)S(1)}, u32[]{:S(2)}, u32[]{:S(2)}) async-start(bf16[16,64,128]{2,1,0:T(8,128)(2,1)} %get-tuple-element.44), calls=%async_computation.4 | async-start | bytes 524288 | tf_op jit(solution)/shard_map/all_to_all | solution.py:613
  177.1 6.2 %input_gradient.1 = bf16[128,1024]{1,0:T(8,128)(2,1)} custom-call(bf16[16,192,128]{2,1,0:T(8,128)(2,1)S(1)} %all-to-all-done.3.joined_ref, bf16[1024,3072]{1,0:T(8,128)(2,1)} %weight_ref.3, bf16[128,1024]{1,0:T(8,128)(2,1)} %bitcast.18, f32[128,1024]{1,0:T(8,128)} %get-tuple-element.32.res_grad_ref), custom_call_target="tpu_custom_call" | custom-call | tf_op jit(solution)/shard_map/input_gradient/pallas_call | solution.py:399
  183.3 0.1 copy.12
  183.4 0.7 copy.13
  184.1 3.4 %all-to-all-done.4.refs_0_ = bf16[16,64,128]{2,1,0:T(8,128)(2,1)S(1)} async-done(((bf16[16,64,128]{2,1,0:T(8,128)(2,1)}), bf16[16,64,128]{2,1,0:T(8,128)(2,1)S(1)}, u32[]{:S(2)}, u32[]{:S(2)}) %all-to-all-start.4) | async-done | bytes 262176 | tf_op jit(solution)/shard_map/all_to_all | solution.py:613
  187.5 0.8 finish.1
  (12 shorter events, 0.1 us)
Async XLA Ops:
  7.2 127.8 %all-gather.3.cloned.1.call-start = ((), (), s32[]{:S(2)}) async-start(), calls=%async_computation.5 | async-start | bytes 4456448 | tf_op jit(solution)/shard_map/all_gather | solution.py:600
  7.2 17.8 %copy-start.2 = (bf16[1,128,1024]{2,1,0:T(8,128)(2,1)S(1)}, bf16[1,128,1024]{2,1,0:T(8,128)(2,1)}, u32[]{:S(2)}) copy-start(bf16[1,128,1024]{2,1,0:T(8,128)(2,1)} %param.6) | copy-start | bytes 786436
  7.2 17.8 %copy-start.3 = (bf16[1,128,1024]{2,1,0:T(8,128)(2,1)S(1)}, bf16[1,128,1024]{2,1,0:T(8,128)(2,1)}, u32[]{:S(2)}) copy-start(bf16[1,128,1024]{2,1,0:T(8,128)(2,1)} %param.7) | copy-start | bytes 786436
  14.2 35.5 %all-to-all-start = ((bf16[16,192,128]{2,1,0:T(8,128)(2,1)}), bf16[16,192,128]{2,1,0:T(8,128)(2,1)S(1)}, u32[]{:S(2)}, u32[]{:S(2)}) async-start(bf16[16,192,128]{2,1,0:T(8,128)(2,1)} %get-tuple-element.26), calls=%async_computation | async-start | bytes 1572864 | tf_op jit(solution)/shard_map/all_to_all | solution.py:598
  49.7 12.4 %copy-start.1 = (bf16[16,192,128]{2,1,0:T(8,128)(2,1)}, bf16[16,192,128]{2,1,0:T(8,128)(2,1)S(1)}, u32[]{:S(2)}) copy-start(bf16[16,192,128]{2,1,0:T(8,128)(2,1)S(1)} %all-to-all-done.heads_ref) | copy-start | bytes 2359300
  62.1 26.7 %all-to-all-start.1 = ((bf16[16,96,128]{2,1,0:T(8,128)(2,1)}), bf16[16,96,128]{2,1,0:T(8,128)(2,1)S(1)}, u32[]{:S(2)}, u32[]{:S(2)}) async-start(bf16[16,96,128]{2,1,0:T(8,128)(2,1)} %get-tuple-element.27), calls=%async_computation.1 | async-start | bytes 786432 | tf_op jit(solution)/shard_map/all_to_all | solution.py:602
  69.1 79.2 %all-gather.5.cloned.1.call-start = ((), (), s32[]{:S(2)}) async-start(), calls=%async_computation.6 | async-start | bytes 2621440 | tf_op jit(solution)/shard_map/all_gather | solution.py:606
  69.2 18.5 %collective-permute-start.1 = (bf16[64,1024]{1,0:T(8,128)(2,1)S(1)}, bf16[64,1024]{1,0:T(8,128)(2,1)S(1)}, u32[]{:S(2)}, u32[]{:S(2)}) collective-permute-start(bf16[64,1024]{1,0:T(8,128)(2,1)S(1)} %pad_maximum_fusion.1), channel_id=1, source_target_pairs={{1,0},{2,1},{3,2},{4,3},{5,4},{6,5},{7,6},{8,7},{9,8},{10,9},{11,1... | collective-permute-start | bytes 393224 | tf_op jit(solution)/shard_map/ppermute | solution.py:593
  71.2 16.9 %collective-permute-start = (bf16[64,1024]{1,0:T(8,128)(2,1)S(1)}, bf16[64,1024]{1,0:T(8,128)(2,1)S(1)}, u32[]{:S(2)}, u32[]{:S(2)}) collective-permute-start(bf16[64,1024]{1,0:T(8,128)(2,1)S(1)} %pad_maximum_fusion), channel_id=1, source_target_pairs={{0,1},{1,2},{2,3},{3,4},{4,5},{5,6},{6,7},{7,8},{8,9},{9,10},{10,1... | collective-permute-start | bytes 393224 | tf_op jit(solution)/shard_map/ppermute | solution.py:592
  115.3 14.7 %copy-start = (bf16[16,80,128]{2,1,0:T(8,128)(2,1)}, bf16[16,80,128]{2,1,0:T(8,128)(2,1)S(1)}, u32[]{:S(2)}) copy-start(bf16[16,80,128]{2,1,0:T(8,128)(2,1)S(1)} %all_to_all.25.grads_ref.back_ref) | copy-start | bytes 983044
  130.0 38.7 %all-to-all-start.3 = ((bf16[16,192,128]{2,1,0:T(8,128)(2,1)}), bf16[16,192,128]{2,1,0:T(8,128)(2,1)S(1)}, u32[]{:S(2)}, u32[]{:S(2)}) async-start(bf16[16,192,128]{2,1,0:T(8,128)(2,1)} %attend_back.1.grads_ref), calls=%async_computation.3 | async-start | bytes 1572864 | tf_op jit(solution)/shard_map/all_to_all | solution.py:608
  141.0 7.5 %collective-permute-start.2 = (bf16[416,128]{1,0:T(8,128)(2,1)}, bf16[416,128]{1,0:T(8,128)(2,1)S(1)}, u32[]{:S(2)}, u32[]{:S(2)}) collective-permute-start(bf16[416,128]{1,0:T(8,128)(2,1)} %get-tuple-element.35), channel_id=1, source_target_pairs={{0,64},{16,80},{32,96},{48,112},{64,0},{80,16},{96,32},{112,48},{1... | collective-permute-start | bytes 319496 | tf_op jit(solution)/shard_map/ppermute | solution.py:571
  142.6 8.6 %collective-permute-start.3 = (bf16[416,128]{1,0:T(8,128)(2,1)}, bf16[416,128]{1,0:T(8,128)(2,1)S(1)}, u32[]{:S(2)}, u32[]{:S(2)}) collective-permute-start(bf16[416,128]{1,0:T(8,128)(2,1)} %get-tuple-element.36), channel_id=1, source_target_pairs={{0,128},{16,144},{32,160},{48,176},{64,192},{80,208},{96,224},{112... | collective-permute-start | bytes 319496 | tf_op jit(solution)/shard_map/ppermute | solution.py:571
  145.5 6.8 %collective-permute-start.4 = (bf16[416,128]{1,0:T(8,128)(2,1)}, bf16[416,128]{1,0:T(8,128)(2,1)S(1)}, u32[]{:S(2)}, u32[]{:S(2)}) collective-permute-start(bf16[416,128]{1,0:T(8,128)(2,1)} %get-tuple-element.37), channel_id=1, source_target_pairs={{0,192},{16,208},{32,224},{48,240},{64,128},{80,144},{96,160},{112... | collective-permute-start | bytes 319496 | tf_op jit(solution)/shard_map/ppermute | solution.py:571
  155.3 3.4 %collective-permute-start.5 = (bf16[640,128]{1,0:T(8,128)(2,1)}, bf16[640,128]{1,0:T(8,128)(2,1)S(1)}, u32[]{:S(2)}, u32[]{:S(2)}) collective-permute-start(bf16[640,128]{1,0:T(8,128)(2,1)} %get-tuple-element.40), channel_id=1, source_target_pairs={{0,16},{16,0},{32,48},{48,32},{64,80},{80,64},{96,112},{112,96},{1... | collective-permute-start | bytes 491528 | tf_op jit(solution)/shard_map/ppermute | solution.py:571
  155.3 8.7 %collective-permute-start.6 = (bf16[640,128]{1,0:T(8,128)(2,1)}, bf16[640,128]{1,0:T(8,128)(2,1)S(1)}, u32[]{:S(2)}, u32[]{:S(2)}) collective-permute-start(bf16[640,128]{1,0:T(8,128)(2,1)} %get-tuple-element.41), channel_id=1, source_target_pairs={{0,32},{16,48},{32,0},{48,16},{64,96},{80,112},{96,64},{112,80},{1... | collective-permute-start | bytes 491528 | tf_op jit(solution)/shard_map/ppermute | solution.py:571
  158.3 8.5 %collective-permute-start.7 = (bf16[640,128]{1,0:T(8,128)(2,1)}, bf16[640,128]{1,0:T(8,128)(2,1)S(1)}, u32[]{:S(2)}, u32[]{:S(2)}) collective-permute-start(bf16[640,128]{1,0:T(8,128)(2,1)} %get-tuple-element.42), channel_id=1, source_target_pairs={{0,48},{16,32},{32,16},{48,0},{64,112},{80,96},{96,80},{112,64},{1... | collective-permute-start | bytes 491528 | tf_op jit(solution)/shard_map/ppermute | solution.py:571
  168.6 18.9 %all-to-all-start.4 = ((bf16[16,64,128]{2,1,0:T(8,128)(2,1)}), bf16[16,64,128]{2,1,0:T(8,128)(2,1)S(1)}, u32[]{:S(2)}, u32[]{:S(2)}) async-start(bf16[16,64,128]{2,1,0:T(8,128)(2,1)} %get-tuple-element.44), calls=%async_computation.4 | async-start | bytes 524288 | tf_op jit(solution)/shard_map/all_to_all | solution.py:613
  177.0 6.2 %copy-start.4 = (f32[64,192]{1,0:T(8,128)S(1)}, f32[64,192]{1,0:T(8,128)}, u32[]{:S(2)}) copy-start(f32[64,192]{1,0:T(8,128)} %get-tuple-element.43) | copy-start | bytes 147460
Sparse Core Ops, SparseCore 0:
  14.3 94.5 all-gather.2
  110.8 37.4 all-gather.4

commit v10 on v9

--- a/solution.py
+++ b/solution.py
@@ -11,8 +11,10 @@
 KW = 31
 HD = 64
 HALO = 32
+QUERIES = 512
+KEYS = 256
 QB = 256
-KB = 256
+KB = 512
 F32 = jnp.float32
 BF16 = jnp.bfloat16
 LIMIT = 56 * 1024 * 1024
@@ -83,7 +85,7 @@
 
 def project(frames, w_qkv):
     rows, width = frames.shape
-    cols = 512
+    cols = 1024
     per = cols // HD
     groups = HEADS // per
     return pl.pallas_call(
@@ -126,27 +128,27 @@
         value[:, i * rows : (i + 1) * rows] = heads_ref[i, 2 * HD : 3 * HD, :]
 
     def one_block(block, carry):
-        cols = pl.ds(pl.multiple_of(block * QB, QB), QB)
+        cols = pl.ds(pl.multiple_of(block * QUERIES, QUERIES), QUERIES)
         query_cols = query[:, cols]
         peak = None
-        for k in range(total // KB):
-            part = dot(keys[k * KB : (k + 1) * KB, :], query_cols)
-            scores[k * KB : (k + 1) * KB, :] = part
-            top = jnp.max(part.reshape(KB // 8, 8, QB), axis=0)
+        for k in range(total // KEYS):
+            part = dot(keys[k * KEYS : (k + 1) * KEYS, :], query_cols)
+            scores[k * KEYS : (k + 1) * KEYS, :] = part
+            top = jnp.max(part.reshape(KEYS // 8, 8, QUERIES), axis=0)
             peak = top if peak is None else jnp.maximum(peak, top)
         peak = jnp.max(peak, axis=0, keepdims=True)
-        total_row = jnp.zeros((8, QB), F32)
-        acc = jnp.zeros((HD, QB), F32)
-        for k in range(total // KB):
-            expo = jnp.exp(scores[k * KB : (k + 1) * KB, :] - peak)
-            total_row = total_row + jnp.sum(expo.reshape(KB // 8, 8, QB), axis=0)
-            acc = acc + dot(value[:, k * KB : (k + 1) * KB], expo.astype(BF16))
+        total_row = jnp.zeros((8, QUERIES), F32)
+        acc = jnp.zeros((HD, QUERIES), F32)
+        for k in range(total // KEYS):
+            expo = jnp.exp(scores[k * KEYS : (k + 1) * KEYS, :] - peak)
+            total_row = total_row + jnp.sum(expo.reshape(KEYS // 8, 8, QUERIES), axis=0)
+            acc = acc + dot(value[:, k * KEYS : (k + 1) * KEYS], expo.astype(BF16))
         total_row = jnp.sum(total_row, axis=0, keepdims=True)
         out_ref[:, cols] = acc / total_row
         lse_ref[:, cols] = peak + jnp.log(total_row)
         return carry
 
-    lax.fori_loop(0, total // QB, one_block, 0)
+    lax.fori_loop(0, total // QUERIES, one_block, 0, unroll=True)
     none = jnp.zeros((HD, HALO), F32)
     for i in range(count):
         send_ref[i, 0:HD, :] = out_ref[:, i * rows : (i + 1) * rows].astype(BF16)
@@ -172,7 +174,7 @@
             pltpu.VMEM((2 * HD, total), BF16),
             pltpu.VMEM((total, 2 * HD), BF16),
             pltpu.VMEM((HD, total), BF16),
-            pltpu.VMEM((total, QB), F32),
+            pltpu.VMEM((total, QUERIES), F32),
         ],
         compiler_params=params(),
         cost_estimate=cost(2 * 2 * total * total * 256, heads.size * 2, total * total),
@@ -192,7 +194,11 @@
     output_ref,
     res_grad_ref,
     send_ref,
-    pack_ref,
+    round_ref,
+    pick_one,
+    pick_two,
+    pick_three,
+    pick_four,
     taps_ref,
     conv_in,
     grad_all,
@@ -265,8 +271,10 @@
     res_grad = grads_ref[...].astype(F32) + normalize_back(unit, scale, conv_grad[...] * keep)
     res_grad_ref[...] = res_grad
     rounded = res_grad.astype(BF16)
-    pack_ref[:, 0:width] = rounded
-    pack_ref[:, width:] = attended
+    round_ref[...] = rounded
+    for k, pick_ref in enumerate((pick_one, pick_two, pick_three, pick_four)):
+        first_head = pl.multiple_of((scalars[4] ^ k) * FAST, FAST)
+        pick_ref[...] = att_ref[pl.ds(first_head, FAST), 0:HD, :].reshape(FAST * HD, rows)
     back = dot(w_out_ref[...], rounded, 1, 1).astype(BF16)
     send_ref[:, 0:HD, :] = back.reshape(heads, HD, rows)
     for h in range(heads):
@@ -286,8 +294,9 @@
             jax.ShapeDtypeStruct((rows, width), BF16),
             jax.ShapeDtypeStruct((rows, width), F32),
             jax.ShapeDtypeStruct((HEADS, HD + (KW + 1) // 2, rows), BF16),
-            jax.ShapeDtypeStruct((rows, 2 * width), BF16),
-        ],
+            jax.ShapeDtypeStruct((rows, width), BF16),
+        ]
+        + [jax.ShapeDtypeStruct((FAST * HD, rows), BF16)] * SLOW,
         scratch_shapes=[
             pltpu.VMEM((KW + 1, width), F32),
             pltpu.VMEM((rows + 2 * HALO, width), F32),
@@ -340,7 +349,7 @@
             send_ref[block * (KB // rows) + i, HD : 3 * HD, :] = joined[:, i * rows : (i + 1) * rows]
         return carry
 
-    lax.fori_loop(0, total // KB, one_block, 0)
+    lax.fori_loop(0, total // KB, one_block, 0, unroll=True)
     for i in range(count):
         cols = slice(i * rows, (i + 1) * rows)
         send_ref[i, 0:HD, :] = (query_grad[:, cols] * 0.125).astype(BF16)
@@ -395,7 +404,7 @@
 
 def input_gradient(joined, w_qkv, frames, res_grad):
     rows, width = frames.shape
-    block = 256
+    block = 512
     return pl.pallas_call(
         input_grad_kernel,
         grid=(width // block,),
@@ -470,12 +479,17 @@
     return (own.astype(F32) + one.astype(F32)) + (two.astype(F32) + three.astype(F32))
 
 
-def fold_first_kernel(scalars, one, two, three, four, pack_ref, *rest):
-    send_refs, pieces, outer = rest[:FAST], *rest[FAST:]
-    width = pack_ref.shape[1] // 2
-    block = FAST * HD
-    first = pl.multiple_of(width + scalars[4] * block, block)
-    outer[...] = dot(pack_ref[:, pl.ds(first, block)].T, pack_ref[:, 0:width])
+def fold_first_kernel(scalars, one, two, three, four, round_ref, *rest):
+    picks, send_refs = rest[:SLOW], rest[SLOW : SLOW + FAST]
+    pieces, outer = rest[SLOW + FAST :]
+    width = round_ref.shape[1]
+    rows = picks[0].shape[1]
+    right = []
+    for k in range(SLOW):
+        first = pl.multiple_of((scalars[4] ^ k) * rows, rows)
+        right.append(round_ref[pl.ds(first, rows), :])
+    left = jnp.concatenate([ref[...] for ref in picks], axis=1)
+    outer[...] = dot(left, jnp.concatenate(right, axis=0))
     total = sum_four(one[...], two[...], three[...], four[...])
     pair = halves(joined_halves(total[TAPS:]))
     for i in range(FAST):
@@ -489,19 +503,19 @@
             send_ref[at : at + HD, :] = outer[own, c * 128 : (c + 1) * 128].astype(BF16)
 
 
-def fold_first(scalars, blocks, packs):
+def fold_first(scalars, blocks, rounded_all, picks):
     vmem = pl.BlockSpec(memory_space=pltpu.VMEM)
     return pl.pallas_call(
         fold_first_kernel,
-        in_specs=[SMEM] + [vmem] * 5,
+        in_specs=[SMEM] + [vmem] * (5 + SLOW),
         out_shape=[jax.ShapeDtypeStruct((LAST + OUT, 128), BF16)] * FAST,
         scratch_shapes=[
             pltpu.VMEM((FAST, CUT, 128), BF16),
-            pltpu.VMEM((FAST * HD, packs.shape[1] // 2), F32),
+            pltpu.VMEM((FAST * HD, rounded_all.shape[1]), F32),
         ],
         compiler_params=params(),
         name="fold_first",
-    )(scalars, *blocks, packs)
+    )(scalars, *blocks, rounded_all, *picks)
 
 
 def fold_last_kernel(*refs, scale):
@@ -600,14 +614,15 @@
     normed_all = lax.all_gather(normed, "seq", axis=0, tiled=True)
     send, out, lse = attend(scalars, heads_near)
     att = local_memory(lax.all_to_all(send, "seq", 0, 0, tiled=True))
-    output, res_grad, send, pack = middle(scalars, att, x, x_side, g, g_side, w_out, w_conv)
+    output, res_grad, send, rounded, *picks = middle(scalars, att, x, x_side, g, g_side, w_out, w_conv)
     back = lax.all_to_all(send, "seq", 0, 0, tiled=True)
     far = [[FAST * i + j for i in range(SLOW)] for j in range(FAST)]
-    packs = lax.all_gather(pack, "dp", axis=0, axis_index_groups=far, tiled=True)
+    rounded_all = lax.all_gather(rounded, "dp", axis=0, axis_index_groups=far, tiled=True)
+    back, picks = lax.optimization_barrier((back, exchange(picks, FAST)))
     send = attend_back(scalars, heads, local_memory(back), out, lse)
     joined = lax.all_to_all(send, "seq", 0, 0, tiled=True)
     parts = exchange(gradient_parts(scalars, send, back, normed_all), FAST)
-    parts = exchange(fold_first(scalars, parts, packs), 1)
+    parts = exchange(fold_first(scalars, parts, rounded_all, picks), 1)
     qkv, send = fold_last(parts, seq_count, grad_scale)
     input_grad = input_gradient(joined, w_qkv, x, res_grad)
     recv = lax.all_to_all(send, "seq", 0, 0, tiled=True)

time: 196 us -> 188 us (0.959)
  blocking collectives: 17.4 us -> 0 us
  starting transfers between devices: 43.9 us -> 59.6 us
  Pallas kernels: 60.9 us -> 51.4 us
  waiting for transfers between devices: 55.8 us -> 59.4 us
    all_to_all x1 -> x0, blocking collectives: 17.4 us -> none  [local(): back = lax.all_to_all(send, 'seq', 0, 0, tiled=True)]
    all_to_all x0 -> x1, starting transfers between devices: none -> 8.07 us  [local(): back = lax.all_to_all(send, 'seq', 0, 0, tiled=True)]
    ppermute x6 -> x9, waiting for transfers between devices: 12.1 us -> 17.3 us  [exchange(): lax.ppermute(block, 'dp', pairs(k))]
    ppermute x6 -> x9, starting transfers between devices: 8.06 us -> 12.9 us  [exchange(): lax.ppermute(block, 'dp', pairs(k))]
    pallas_call x1, Pallas kernels: 12.4 us -> 7.65 us  [attend(): pl.pallas_call(attend_kernel, in_specs=[SMEM, pl.BlockSpec(memory_space=p...]
    all_to_all x1, starting transfers between devices: 5.02 us -> 8.11 us  [local(): joined = lax.all_to_all(send, 'seq', 0, 0, tiled=True)]
    all_gather x1, waiting for transfers between devices: 2.55 us -> 0.01 us  [local(): lax.all_gather(rounded, 'dp', axis=0, axis_index_groups=far, tiled=True)]
    pallas_call x1, Pallas kernels: 14.7 us -> 12.7 us  [attend_back(): pl.pallas_call(attend_back_kernel, in_specs=[SMEM] + [vmem] * 4, out_shap...]
  transfers between devices with their start and end apart: 14 -> 18, of which waited for: 10 -> 11; matrix products, arithmetic and copies ran while one was open for 1% -> 1% of each run, Pallas kernels for 27% -> 24%
where the time goes in v10:
time: 188 us; the launch traced here: 187 us
  starting transfers between devices  59.6 us (32%)
  waiting for transfers between devices  59.4 us (32%)
  Pallas kernels  51.4 us (27%)
  between operations  14.8 us (8%)
    all_to_all x1, waiting for transfers between devices, local(): heads = lax.all_to_all(send, 'seq', 0, 0, tiled=True)  24.7 us
    ppermute x9, waiting for transfers between devices, exchange(): lax.ppermute(block, 'dp', pairs(k))  17.3 us
    ppermute x9, starting transfers between devices, exchange(): lax.ppermute(block, 'dp', pairs(k))  12.9 us
    ppermute x1, waiting for transfers between devices, local(): lax.ppermute(jnp.concatenate([x[:HALO], g[:HALO]], axis=0), 'seq', backward)  12.8 us
    pallas_call x1, Pallas kernels, attend_back(): pl.pallas_call(attend_back_kernel, in_specs=[SMEM] + [vmem] * 4, out_shap...  12.7 us
    all_to_all x1, starting transfers between devices, local(): heads = lax.all_to_all(send, 'seq', 0, 0, tiled=True)  9.52 us
    pallas_call x1, Pallas kernels, middle(): pl.pallas_call(middle_kernel, in_specs=[SMEM] + [vmem] * 7, out_shape=[ja...  8.85 us
    all_to_all x1, starting transfers between devices, local(): recv = lax.all_to_all(send, 'seq', 0, 0, tiled=True)  8.12 us
  transfers between devices with their start and end apart: 18, of which 11 were waited for; matrix products, arithmetic and copies ran while one was open for 1% of the time, Pallas kernels for 24%

profile of v10, /device:TPU:32, one launch (start us, length us, event | category | flops | bytes accessed | tf_op | source)
XLA Modules:
  0.0 187.5 jit_solution(14792587452101761310)
XLA Ops:
  7.2 0.0 all-gather.3.cloned.1.call-start
  7.2 0.0 copy-start.2
  7.2 0.0 copy-start.3
  7.2 5.5 %project.1 = (bf16[128,1024]{1,0:T(8,128)(2,1)}, bf16[16,192,128]{2,1,0:T(8,128)(2,1)}) custom-call(bf16[128,1024]{1,0:T(8,128)(2,1)} %bitcast.16, bf16[1024,3072]{1,0:T(8,128)(2,1)} %weight_ref.3), custom_call_target="tpu_custom_call" | custom-call | tf_op jit(solution)/shard_map/project/pallas_call | solution.py:91
  12.7 0.0 all-gather.3.cloned.1.call-update
  12.7 9.5 %all-to-all-start = ((bf16[16,192,128]{2,1,0:T(8,128)(2,1)}), bf16[16,192,128]{2,1,0:T(8,128)(2,1)S(1)}, u32[]{:S(2)}, u32[]{:S(2)}) async-start(bf16[16,192,128]{2,1,0:T(8,128)(2,1)} %get-tuple-element.35), calls=%async_computation | async-start | bytes 1572864 | tf_op jit(solution)/shard_map/all_to_all | solution.py:612
  22.9 0.6 stack.15.scalars
  23.6 24.7 %all-to-all-done.heads_ref = bf16[16,192,128]{2,1,0:T(8,128)(2,1)S(1)} async-done(((bf16[16,192,128]{2,1,0:T(8,128)(2,1)}), bf16[16,192,128]{2,1,0:T(8,128)(2,1)S(1)}, u32[]{:S(2)}, u32[]{:S(2)}) %all-to-all-start) | async-done | bytes 786464 | tf_op jit(solution)/shard_map/all_to_all | solution.py:612
  48.3 7.7 %attend.1 = (bf16[16,96,128]{2,1,0:T(8,128)(2,1)}, f32[64,2048]{1,0:T(8,128)}, f32[1,2048]{1,0:T(1,128)}) custom-call(s32[5]{0:T(128)} %stack.15.scalars, bf16[16,192,128]{2,1,0:T(8,128)(2,1)S(1)} %all-to-all-done.heads_ref), custom_call_target="tpu_custom_call" | custom-call | flops 4294967296 | bytes 786432 | tf_op jit(solution)/shard_map/attend/pallas_call | solution.py:165
  55.9 7.0 %all-to-all-start.1 = ((bf16[16,96,128]{2,1,0:T(8,128)(2,1)}), bf16[16,96,128]{2,1,0:T(8,128)(2,1)S(1)}, u32[]{:S(2)}, u32[]{:S(2)}) async-start(bf16[16,96,128]{2,1,0:T(8,128)(2,1)} %get-tuple-element.36), calls=%async_computation.1 | async-start | bytes 786432 | tf_op jit(solution)/shard_map/all_to_all | solution.py:616
  62.9 2.0 %collective-permute-start.1 = (bf16[64,1024]{1,0:T(8,128)(2,1)S(1)}, bf16[64,1024]{1,0:T(8,128)(2,1)S(1)}, u32[]{:S(2)}, u32[]{:S(2)}) collective-permute-start(bf16[64,1024]{1,0:T(8,128)(2,1)S(1)} %pad_maximum_fusion.1), channel_id=1, source_target_pairs={{1,0},{2,1},{3,2},{4,3},{5,4},{6,5},{7,6},{8,7},{9,8},{10,9},{11,1... | collective-permute-start | bytes 393224 | tf_op jit(solution)/shard_map/ppermute | solution.py:607
  65.0 3.8 %collective-permute-start = (bf16[64,1024]{1,0:T(8,128)(2,1)S(1)}, bf16[64,1024]{1,0:T(8,128)(2,1)S(1)}, u32[]{:S(2)}, u32[]{:S(2)}) collective-permute-start(bf16[64,1024]{1,0:T(8,128)(2,1)S(1)} %pad_maximum_fusion), channel_id=1, source_target_pairs={{0,1},{1,2},{2,3},{3,4},{4,5},{5,6},{6,7},{7,8},{8,9},{9,10},{10,1... | collective-permute-start | bytes 393224 | tf_op jit(solution)/shard_map/ppermute | solution.py:606
  68.8 12.8 %collective-permute-done.1 = bf16[64,1024]{1,0:T(8,128)(2,1)S(1)} collective-permute-done((bf16[64,1024]{1,0:T(8,128)(2,1)S(1)}, bf16[64,1024]{1,0:T(8,128)(2,1)S(1)}, u32[]{:S(2)}, u32[]{:S(2)}) %collective-permute-start.1) | collective-permute-done | bytes 131104 | tf_op jit(solution)/shard_map/ppermute | solution.py:607
  81.6 0.3 collective-permute-done
  81.9 0.7 pad_maximum_fusion.2
  82.7 0.0 all-to-all-done.1.att_ref
  82.7 8.9 %middle.1 = (bf16[128,1024]{1,0:T(8,128)(2,1)}, f32[128,1024]{1,0:T(8,128)}, bf16[16,80,128]{2,1,0:T(8,128)(2,1)}, bf16[128,1024]{1,0:T(8,128)(2,1)}, bf16[256,1...) custom-call(s32[5]{0:T(128)} %stack.15.scalars, ...), custom_call_target="tpu_custom_call" | custom-call | tf_op jit(solution)/shard_map/middle/pallas_call | solution.py:290
  91.5 8.1 %all-to-all-start.2 = ((bf16[16,80,128]{2,1,0:T(8,128)(2,1)}), bf16[16,80,128]{2,1,0:T(8,128)(2,1)S(1)}, u32[]{:S(2)}, u32[]{:S(2)}) async-start(bf16[16,80,128]{2,1,0:T(8,128)(2,1)} %get-tuple-element.38), calls=%async_computation.2 | async-start | bytes 655360 | tf_op jit(solution)/shard_map/all_to_all | solution.py:618
  99.6 0.0 all-gather.5.cloned.1.call-start
  99.6 1.8 collective-permute-start.2
  101.4 3.1 %collective-permute-start.3 = (bf16[256,128]{1,0:T(8,128)(2,1)}, bf16[256,128]{1,0:T(8,128)(2,1)S(1)}, u32[]{:S(2)}, u32[]{:S(2)}) collective-permute-start(bf16[256,128]{1,0:T(8,128)(2,1)} %get-tuple-element.41), channel_id=1, source_target_pairs={{0,128},{16,144},{32,160},{48,176},{64,192},{80,208},{96,224},{112... | collective-permute-start | bytes 196616 | tf_op jit(solution)/shard_map/ppermute | solution.py:585
  104.5 0.0 collective-permute-start.4
  104.5 0.0 all-gather.5.cloned.1.call-update
  104.5 3.1 %collective-permute-done.3.rest_2_ = bf16[256,128]{1,0:T(8,128)(2,1)S(1)} collective-permute-done((bf16[256,128]{1,0:T(8,128)(2,1)}, bf16[256,128]{1,0:T(8,128)(2,1)S(1)}, u32[]{:S(2)}, u32[]{:S(2)}) %collective-permute-start.3) | collective-permute-done | bytes 65568 | tf_op jit(solution)/shard_map/ppermute | solution.py:585
  107.6 2.5 %collective-permute-done.4.rest_3_ = bf16[256,128]{1,0:T(8,128)(2,1)S(1)} collective-permute-done((bf16[256,128]{1,0:T(8,128)(2,1)}, bf16[256,128]{1,0:T(8,128)(2,1)S(1)}, u32[]{:S(2)}, u32[]{:S(2)}) %collective-permute-start.4) | collective-permute-done | bytes 65568 | tf_op jit(solution)/shard_map/ppermute | solution.py:585
  110.2 0.0 all-to-all-done.2.grads_ref.back_ref
  110.2 12.7 %attend_back.1.grads_ref = bf16[16,192,128]{2,1,0:T(8,128)(2,1)} custom-call(s32[5]{0:T(128)} %stack.15.scalars, bf16[16,192,128]{2,1,0:T(8,128)(2,1)} %copy-done.1, bf16[16,80,128]{2,1,0:T(8,128)(2,1)S(1)} %all-to-all-done.2.grads_ref.back_ref, f32[64,2048]{1,0:T(8,128)} %get-tuple-element.44.out_ref, f32[1,2048]{1,0:T(1,128)} %get-tuple-element.45.lse_ref), custom_call_target="tpu_custom_call" | custom-call | flops 10737418240 | bytes 1572864 | tf_op jit(solution)/shard_map/attend_back/pallas_call | solution.py:362
  122.9 8.1 %all-to-all-start.3 = ((bf16[16,192,128]{2,1,0:T(8,128)(2,1)}), bf16[16,192,128]{2,1,0:T(8,128)(2,1)S(1)}, u32[]{:S(2)}, u32[]{:S(2)}) async-start(bf16[16,192,128]{2,1,0:T(8,128)(2,1)} %attend_back.1.grads_ref), calls=%async_computation.3 | async-start | bytes 1572864 | tf_op jit(solution)/shard_map/all_to_all | solution.py:623
  131.0 0.0 all-gather.3.cloned.1.call-done.normed_ref
  131.0 6.0 %gradient_parts.1 = (bf16[416,128]{1,0:T(8,128)(2,1)}, bf16[416,128]{1,0:T(8,128)(2,1)}, bf16[416,128]{1,0:T(8,128)(2,1)}, bf16[416,128]{1,0:T(8,128)(2,1)}) custom-call(s32[5]{0:T(128)} %stack.15.scalars, bf16[16,192,128]{2,1,0:T(8,128)(2,1)} %attend_back.1.grads_ref, bf16[16,80,128]{2,1,0:T(8,128)(2,1)} %copy-done, ...), custom_call_target="tpu_custom_call" | custom-call | tf_op jit(solution)/shard_map/gradient_parts/pallas_call | solution.py:459
  137.0 2.2 %collective-permute-start.6 = (bf16[416,128]{1,0:T(8,128)(2,1)}, bf16[416,128]{1,0:T(8,128)(2,1)S(1)}, u32[]{:S(2)}, u32[]{:S(2)}) collective-permute-start(bf16[416,128]{1,0:T(8,128)(2,1)} %get-tuple-element.50), channel_id=1, source_target_pairs={{0,128},{16,144},{32,160},{48,176},{64,192},{80,208},{96,224},{112... | collective-permute-start | bytes 319496 | tf_op jit(solution)/shard_map/ppermute | solution.py:585
  139.2 2.5 %collective-permute-start.7 = (bf16[416,128]{1,0:T(8,128)(2,1)}, bf16[416,128]{1,0:T(8,128)(2,1)S(1)}, u32[]{:S(2)}, u32[]{:S(2)}) collective-permute-start(bf16[416,128]{1,0:T(8,128)(2,1)} %get-tuple-element.51), channel_id=1, source_target_pairs={{0,192},{16,208},{32,224},{48,240},{64,128},{80,144},{96,160},{112... | collective-permute-start | bytes 319496 | tf_op jit(solution)/shard_map/ppermute | solution.py:585
  141.7 0.2 collective-permute-done.5.two
  141.9 1.6 collective-permute-done.6.three
  143.5 1.8 collective-permute-done.7.four
  145.3 2.6 %fold_first.1 = (bf16[640,128]{1,0:T(8,128)(2,1)}, bf16[640,128]{1,0:T(8,128)(2,1)}, bf16[640,128]{1,0:T(8,128)(2,1)}, bf16[640,128]{1,0:T(8,128)(2,1)}) custom-call(s32[5]{0:T(128)} %stack.15.scalars, bf16[416,128]{1,0:T(8,128)(2,1)} %get-tuple-element.48.one, bf16[416,128]{1,0:T(8,128)(2,1)S(1)} %collective-permute-done.5.two, ...), custom_call_target="tpu_custom_call" | custom-call | tf_op jit(solution)/shard_map/fold_first/pallas_call | solution.py:508
  147.8 0.0 collective-permute-start.8
  147.9 2.9 %collective-permute-start.9 = (bf16[640,128]{1,0:T(8,128)(2,1)}, bf16[640,128]{1,0:T(8,128)(2,1)S(1)}, u32[]{:S(2)}, u32[]{:S(2)}) collective-permute-start(bf16[640,128]{1,0:T(8,128)(2,1)} %get-tuple-element.59), channel_id=1, source_target_pairs={{0,32},{16,48},{32,0},{48,16},{64,96},{80,112},{96,64},{112,80},{1... | collective-permute-start | bytes 491528 | tf_op jit(solution)/shard_map/ppermute | solution.py:585
  150.7 0.5 collective-permute-start.10
  151.2 5.4 %collective-permute-done.9.refs_2_ = bf16[640,128]{1,0:T(8,128)(2,1)S(1)} collective-permute-done((bf16[640,128]{1,0:T(8,128)(2,1)}, bf16[640,128]{1,0:T(8,128)(2,1)S(1)}, u32[]{:S(2)}, u32[]{:S(2)}) %collective-permute-start.9) | collective-permute-done | bytes 163872 | tf_op jit(solution)/shard_map/ppermute | solution.py:585
  156.6 2.7 %collective-permute-done.10.refs_3_ = bf16[640,128]{1,0:T(8,128)(2,1)S(1)} collective-permute-done((bf16[640,128]{1,0:T(8,128)(2,1)}, bf16[640,128]{1,0:T(8,128)(2,1)S(1)}, u32[]{:S(2)}, u32[]{:S(2)}) %collective-permute-start.10) | collective-permute-done | bytes 163872 | tf_op jit(solution)/shard_map/ppermute | solution.py:585
  159.3 1.9 %fold_last.1 = (f32[64,192]{1,0:T(8,128)}, bf16[16,64,128]{2,1,0:T(8,128)(2,1)}) custom-call(bf16[640,128]{1,0:T(8,128)(2,1)} %get-tuple-element.57.refs_0_, bf16[640,128]{1,0:T(8,128)(2,1)S(1)} %collective-permute-done.8.refs_1_, bf16[640,128]{1,0:T(8,128)(2,1)S(1)} %collective-permute-done.9.refs_2_, bf16[640,128]{1,0:T(8,128)(2,1)S(1)} %collective-permute-done.10.refs_3_), custom_call_target="tpu_custom_call" | custom-call | tf_op jit(solution)/shard_map/fold_last/pallas_call | solution.py:539
  161.2 8.1 %all-to-all-start.4 = ((bf16[16,64,128]{2,1,0:T(8,128)(2,1)}), bf16[16,64,128]{2,1,0:T(8,128)(2,1)S(1)}, u32[]{:S(2)}, u32[]{:S(2)}) async-start(bf16[16,64,128]{2,1,0:T(8,128)(2,1)} %get-tuple-element.62), calls=%async_computation.4 | async-start | bytes 524288 | tf_op jit(solution)/shard_map/all_to_all | solution.py:628
  169.3 5.4 %input_gradient.1 = bf16[128,1024]{1,0:T(8,128)(2,1)} custom-call(bf16[16,192,128]{2,1,0:T(8,128)(2,1)S(1)} %all-to-all-done.3.joined_ref, bf16[1024,3072]{1,0:T(8,128)(2,1)} %weight_ref.3, bf16[128,1024]{1,0:T(8,128)(2,1)} %bitcast.18, f32[128,1024]{1,0:T(8,128)} %get-tuple-element.46.res_grad_ref), custom_call_target="tpu_custom_call" | custom-call | tf_op jit(solution)/shard_map/input_gradient/pallas_call | solution.py:408
  174.7 0.1 copy.12
  174.8 0.7 copy.13
  175.6 4.3 %all-to-all-done.4.refs_0_ = bf16[16,64,128]{2,1,0:T(8,128)(2,1)S(1)} async-done(((bf16[16,64,128]{2,1,0:T(8,128)(2,1)}), bf16[16,64,128]{2,1,0:T(8,128)(2,1)S(1)}, u32[]{:S(2)}, u32[]{:S(2)}) %all-to-all-start.4) | async-done | bytes 262176 | tf_op jit(solution)/shard_map/all_to_all | solution.py:628
  179.8 0.8 finish.1
  (19 shorter events, 0.1 us)
Async XLA Ops:
  7.2 123.8 %all-gather.3.cloned.1.call-start = ((), (), s32[]{:S(2)}) async-start(), calls=%async_computation.5 | async-start | bytes 4456448 | tf_op jit(solution)/shard_map/all_gather | solution.py:614
  7.2 16.3 %copy-start.2 = (bf16[1,128,1024]{2,1,0:T(8,128)(2,1)S(1)}, bf16[1,128,1024]{2,1,0:T(8,128)(2,1)}, u32[]{:S(2)}) copy-start(bf16[1,128,1024]{2,1,0:T(8,128)(2,1)} %param.6) | copy-start | bytes 786436
  7.2 16.3 %copy-start.3 = (bf16[1,128,1024]{2,1,0:T(8,128)(2,1)S(1)}, bf16[1,128,1024]{2,1,0:T(8,128)(2,1)}, u32[]{:S(2)}) copy-start(bf16[1,128,1024]{2,1,0:T(8,128)(2,1)} %param.7) | copy-start | bytes 786436
  12.7 35.5 %all-to-all-start = ((bf16[16,192,128]{2,1,0:T(8,128)(2,1)}), bf16[16,192,128]{2,1,0:T(8,128)(2,1)S(1)}, u32[]{:S(2)}, u32[]{:S(2)}) async-start(bf16[16,192,128]{2,1,0:T(8,128)(2,1)} %get-tuple-element.35), calls=%async_computation | async-start | bytes 1572864 | tf_op jit(solution)/shard_map/all_to_all | solution.py:612
  48.3 7.7 %copy-start.1 = (bf16[16,192,128]{2,1,0:T(8,128)(2,1)}, bf16[16,192,128]{2,1,0:T(8,128)(2,1)S(1)}, u32[]{:S(2)}) copy-start(bf16[16,192,128]{2,1,0:T(8,128)(2,1)S(1)} %all-to-all-done.heads_ref) | copy-start | bytes 2359300
  55.9 26.7 %all-to-all-start.1 = ((bf16[16,96,128]{2,1,0:T(8,128)(2,1)}), bf16[16,96,128]{2,1,0:T(8,128)(2,1)S(1)}, u32[]{:S(2)}, u32[]{:S(2)}) async-start(bf16[16,96,128]{2,1,0:T(8,128)(2,1)} %get-tuple-element.36), calls=%async_computation.1 | async-start | bytes 786432 | tf_op jit(solution)/shard_map/all_to_all | solution.py:616
  62.9 18.7 %collective-permute-start.1 = (bf16[64,1024]{1,0:T(8,128)(2,1)S(1)}, bf16[64,1024]{1,0:T(8,128)(2,1)S(1)}, u32[]{:S(2)}, u32[]{:S(2)}) collective-permute-start(bf16[64,1024]{1,0:T(8,128)(2,1)S(1)} %pad_maximum_fusion.1), channel_id=1, source_target_pairs={{1,0},{2,1},{3,2},{4,3},{5,4},{6,5},{7,6},{8,7},{9,8},{10,9},{11,1... | collective-permute-start | bytes 393224 | tf_op jit(solution)/shard_map/ppermute | solution.py:607
  65.0 17.0 %collective-permute-start = (bf16[64,1024]{1,0:T(8,128)(2,1)S(1)}, bf16[64,1024]{1,0:T(8,128)(2,1)S(1)}, u32[]{:S(2)}, u32[]{:S(2)}) collective-permute-start(bf16[64,1024]{1,0:T(8,128)(2,1)S(1)} %pad_maximum_fusion), channel_id=1, source_target_pairs={{0,1},{1,2},{2,3},{3,4},{4,5},{5,6},{6,7},{7,8},{8,9},{9,10},{10,1... | collective-permute-start | bytes 393224 | tf_op jit(solution)/shard_map/ppermute | solution.py:606
  91.5 18.7 %all-to-all-start.2 = ((bf16[16,80,128]{2,1,0:T(8,128)(2,1)}), bf16[16,80,128]{2,1,0:T(8,128)(2,1)S(1)}, u32[]{:S(2)}, u32[]{:S(2)}) async-start(bf16[16,80,128]{2,1,0:T(8,128)(2,1)} %get-tuple-element.38), calls=%async_computation.2 | async-start | bytes 655360 | tf_op jit(solution)/shard_map/all_to_all | solution.py:618
  99.6 42.1 %all-gather.5.cloned.1.call-start = ((), (), s32[]{:S(2)}) async-start(), calls=%async_computation.6 | async-start | bytes 1310720 | tf_op jit(solution)/shard_map/all_gather | solution.py:620
  99.6 4.9 %collective-permute-start.2 = (bf16[256,128]{1,0:T(8,128)(2,1)}, bf16[256,128]{1,0:T(8,128)(2,1)S(1)}, u32[]{:S(2)}, u32[]{:S(2)}) collective-permute-start(bf16[256,128]{1,0:T(8,128)(2,1)} %get-tuple-element.40), channel_id=1, source_target_pairs={{0,64},{16,80},{32,96},{48,112},{64,0},{80,16},{96,32},{112,48},{1... | collective-permute-start | bytes 196616 | tf_op jit(solution)/shard_map/ppermute | solution.py:585
  101.4 6.2 %collective-permute-start.3 = (bf16[256,128]{1,0:T(8,128)(2,1)}, bf16[256,128]{1,0:T(8,128)(2,1)S(1)}, u32[]{:S(2)}, u32[]{:S(2)}) collective-permute-start(bf16[256,128]{1,0:T(8,128)(2,1)} %get-tuple-element.41), channel_id=1, source_target_pairs={{0,128},{16,144},{32,160},{48,176},{64,192},{80,208},{96,224},{112... | collective-permute-start | bytes 196616 | tf_op jit(solution)/shard_map/ppermute | solution.py:585
  104.5 5.7 %collective-permute-start.4 = (bf16[256,128]{1,0:T(8,128)(2,1)}, bf16[256,128]{1,0:T(8,128)(2,1)S(1)}, u32[]{:S(2)}, u32[]{:S(2)}) collective-permute-start(bf16[256,128]{1,0:T(8,128)(2,1)} %get-tuple-element.42), channel_id=1, source_target_pairs={{0,192},{16,208},{32,224},{48,240},{64,128},{80,144},{96,160},{112... | collective-permute-start | bytes 196616 | tf_op jit(solution)/shard_map/ppermute | solution.py:585
  110.2 12.7 %copy-start = (bf16[16,80,128]{2,1,0:T(8,128)(2,1)}, bf16[16,80,128]{2,1,0:T(8,128)(2,1)S(1)}, u32[]{:S(2)}) copy-start(bf16[16,80,128]{2,1,0:T(8,128)(2,1)S(1)} %all-to-all-done.2.grads_ref.back_ref) | copy-start | bytes 983044
  122.9 38.3 %all-to-all-start.3 = ((bf16[16,192,128]{2,1,0:T(8,128)(2,1)}), bf16[16,192,128]{2,1,0:T(8,128)(2,1)S(1)}, u32[]{:S(2)}, u32[]{:S(2)}) async-start(bf16[16,192,128]{2,1,0:T(8,128)(2,1)} %attend_back.1.grads_ref), calls=%async_computation.3 | async-start | bytes 1572864 | tf_op jit(solution)/shard_map/all_to_all | solution.py:623
  137.0 4.9 %collective-permute-start.5 = (bf16[416,128]{1,0:T(8,128)(2,1)}, bf16[416,128]{1,0:T(8,128)(2,1)S(1)}, u32[]{:S(2)}, u32[]{:S(2)}) collective-permute-start(bf16[416,128]{1,0:T(8,128)(2,1)} %get-tuple-element.49), channel_id=1, source_target_pairs={{0,64},{16,80},{32,96},{48,112},{64,0},{80,16},{96,32},{112,48},{1... | collective-permute-start | bytes 319496 | tf_op jit(solution)/shard_map/ppermute | solution.py:585
  137.0 6.5 %collective-permute-start.6 = (bf16[416,128]{1,0:T(8,128)(2,1)}, bf16[416,128]{1,0:T(8,128)(2,1)S(1)}, u32[]{:S(2)}, u32[]{:S(2)}) collective-permute-start(bf16[416,128]{1,0:T(8,128)(2,1)} %get-tuple-element.50), channel_id=1, source_target_pairs={{0,128},{16,144},{32,160},{48,176},{64,192},{80,208},{96,224},{112... | collective-permute-start | bytes 319496 | tf_op jit(solution)/shard_map/ppermute | solution.py:585
  139.2 6.1 %collective-permute-start.7 = (bf16[416,128]{1,0:T(8,128)(2,1)}, bf16[416,128]{1,0:T(8,128)(2,1)S(1)}, u32[]{:S(2)}, u32[]{:S(2)}) collective-permute-start(bf16[416,128]{1,0:T(8,128)(2,1)} %get-tuple-element.51), channel_id=1, source_target_pairs={{0,192},{16,208},{32,224},{48,240},{64,128},{80,144},{96,160},{112... | collective-permute-start | bytes 319496 | tf_op jit(solution)/shard_map/ppermute | solution.py:585
  147.8 3.4 %collective-permute-start.8 = (bf16[640,128]{1,0:T(8,128)(2,1)}, bf16[640,128]{1,0:T(8,128)(2,1)S(1)}, u32[]{:S(2)}, u32[]{:S(2)}) collective-permute-start(bf16[640,128]{1,0:T(8,128)(2,1)} %get-tuple-element.58), channel_id=1, source_target_pairs={{0,16},{16,0},{32,48},{48,32},{64,80},{80,64},{96,112},{112,96},{1... | collective-permute-start | bytes 491528 | tf_op jit(solution)/shard_map/ppermute | solution.py:585
  147.9 8.7 %collective-permute-start.9 = (bf16[640,128]{1,0:T(8,128)(2,1)}, bf16[640,128]{1,0:T(8,128)(2,1)S(1)}, u32[]{:S(2)}, u32[]{:S(2)}) collective-permute-start(bf16[640,128]{1,0:T(8,128)(2,1)} %get-tuple-element.59), channel_id=1, source_target_pairs={{0,32},{16,48},{32,0},{48,16},{64,96},{80,112},{96,64},{112,80},{1... | collective-permute-start | bytes 491528 | tf_op jit(solution)/shard_map/ppermute | solution.py:585
  150.7 8.5 %collective-permute-start.10 = (bf16[640,128]{1,0:T(8,128)(2,1)}, bf16[640,128]{1,0:T(8,128)(2,1)S(1)}, u32[]{:S(2)}, u32[]{:S(2)}) collective-permute-start(bf16[640,128]{1,0:T(8,128)(2,1)} %get-tuple-element.60), channel_id=1, source_target_pairs={{0,48},{16,32},{32,16},{48,0},{64,112},{80,96},{96,80},{112,64},{1... | collective-permute-start | bytes 491528 | tf_op jit(solution)/shard_map/ppermute | solution.py:585
  161.2 18.7 %all-to-all-start.4 = ((bf16[16,64,128]{2,1,0:T(8,128)(2,1)}), bf16[16,64,128]{2,1,0:T(8,128)(2,1)S(1)}, u32[]{:S(2)}, u32[]{:S(2)}) async-start(bf16[16,64,128]{2,1,0:T(8,128)(2,1)} %get-tuple-element.62), calls=%async_computation.4 | async-start | bytes 524288 | tf_op jit(solution)/shard_map/all_to_all | solution.py:628
  169.3 5.4 %copy-start.4 = (f32[64,192]{1,0:T(8,128)S(1)}, f32[64,192]{1,0:T(8,128)}, u32[]{:S(2)}) copy-start(f32[64,192]{1,0:T(8,128)} %get-tuple-element.61) | copy-start | bytes 147460
Sparse Core Ops, SparseCore 0:
  12.9 96.2 all-gather.2
  110.9 30.3 all-gather.4

commit v11 on v10

--- a/solution.py
+++ b/solution.py
@@ -186,9 +186,9 @@
     scalars,
     att_ref,
     frames_ref,
-    frames_side,
     grads_ref,
-    grads_side,
+    low_ref,
+    high_ref,
     w_out_ref,
     w_conv_ref,
     output_ref,
@@ -221,7 +221,7 @@
     split_w = w_out_ref[...].reshape(heads, 2, half, width)
     side = dot(packed[0 : 2 * HALO], split_w[:, 0].reshape(heads * half, width))
     side = side + dot(packed[2 * HALO :], split_w[:, 1].reshape(heads * half, width))
-    side = frames_side[...].astype(F32) + side
+    side = jnp.concatenate([low_ref[0:HALO, :], high_ref[0:HALO, :]], axis=0).astype(F32) + side
 
     def keep_of(count, start):
         frame = lax.broadcasted_iota(jnp.int32, (count, 1), 0) + start
@@ -237,12 +237,11 @@
     high = unit_side[HALO:] * keep_of(HALO, first + rows)
     conv_in[0:HALO, :] = low.astype(BF16).astype(F32)
     conv_in[HALO + rows :, :] = high.astype(BF16).astype(F32)
-    grad_all[0:HALO, :] = grads_side[0:HALO, :].astype(F32)
-    grad_all[body, :] = grads_ref[...].astype(F32)
-    grad_all[HALO + rows :, :] = grads_side[HALO:, :].astype(F32)
-
     reach = rows + HALO
     edge = HALO // 2
+    grad_all[edge:HALO, :] = low_ref[HALO:, :].astype(F32)
+    grad_all[body, :] = grads_ref[...].astype(F32)
+    grad_all[HALO + rows : edge + reach, :] = high_ref[HALO:, :].astype(F32)
 
     def one_chunk(chunk, carry):
         lanes = pl.ds(pl.multiple_of(chunk * 128, 128), 128)
@@ -284,7 +283,7 @@
         send_ref[h, HD:, :] = own.astype(BF16)
 
 
-def middle(scalars, att, frames, frames_side, grads, grads_side, w_out, w_conv):
+def middle(scalars, att, frames, grads, low, high, w_out, w_conv):
     rows, width = frames.shape
     vmem = pl.BlockSpec(memory_space=pltpu.VMEM)
     return pl.pallas_call(
@@ -308,7 +307,7 @@
         ],
         compiler_params=params(),
         name="middle",
-    )(scalars, att, frames, frames_side, grads, grads_side, w_out, w_conv)
+    )(scalars, att, frames, grads, low, high, w_out, w_conv)
 
 
 def attend_back_kernel(
@@ -524,7 +523,9 @@
     model_rows = (total[0:CUT] * scale).T
     qkv_ref[:, 0:CUT] = model_rows[0:HD]
     qkv_ref[:, CUT:] = model_rows[HD:]
-    pair = halves(joined_halves(total[CUT:LAST]))
+    taps = joined_halves(total[CUT:LAST])
+    half = (KW + 1) // 2
+    pair = jnp.concatenate([taps[0:half], taps[half:]], axis=1).astype(BF16)
     outer = total[LAST:]
     count = send_ref.shape[0]
     each = HD // count
@@ -541,7 +542,7 @@
         in_specs=[vmem] * 4,
         out_shape=[
             jax.ShapeDtypeStruct((HD, 3 * HD), F32),
-            jax.ShapeDtypeStruct((seq_count, OUT // seq_count + KW + 1, 128), BF16),
+            jax.ShapeDtypeStruct((seq_count, OUT // seq_count + (KW + 1) // 2, 128), BF16),
         ],
         compiler_params=params(),
         name="fold_last",
@@ -559,9 +560,13 @@
     for c in range(OUT // HD):
         out_ref[:, c * 128 : (c + 1) * 128] = total[c * each : (c + 1) * each]
     for i in range(count // 2):
-        both = [joined_halves(recv_ref[2 * i + k, wide:, :].astype(F32)) for k in range(2)]
-        both = jnp.concatenate(both, axis=1) * scale
-        taps_ref[:, i * 2 * HD : (i + 1) * 2 * HD] = both[0:KW]
+        a = recv_ref[2 * i, wide:, :].astype(F32) * scale
+        b = recv_ref[2 * i + 1, wide:, :].astype(F32) * scale
+        lanes = slice(i * 2 * HD, (i + 1) * 2 * HD)
+        half = (KW + 1) // 2
+        taps_ref[0:half, lanes] = jnp.concatenate([a[:, 0:HD], b[:, 0:HD]], axis=1)
+        upper = jnp.concatenate([a[:, HD:], b[:, HD:]], axis=1)
+        taps_ref[half:KW, lanes] = upper[0 : KW - half]
 
 
 def finish(recv, width, scale):
@@ -603,10 +608,10 @@
 
     forward = [(i, i + 1) for i in range(seq_count - 1)]
     backward = [(i + 1, i) for i in range(seq_count - 1)]
-    low = lax.ppermute(jnp.concatenate([x[-HALO:], g[-HALO:]], axis=0), "seq", forward)
-    high = lax.ppermute(jnp.concatenate([x[:HALO], g[:HALO]], axis=0), "seq", backward)
-    x_side = jnp.concatenate([low[:HALO], high[:HALO]], axis=0)
-    g_side = jnp.concatenate([low[HALO:], high[HALO:]], axis=0)
+    edge = HALO // 2
+    low = lax.ppermute(jnp.concatenate([x[-HALO:], g[-edge:]], axis=0), "seq", forward)
+    high = lax.ppermute(jnp.concatenate([x[:HALO], g[:edge]], axis=0), "seq", backward)
+    low, high = local_memory(low), local_memory(high)
 
     normed, send = project(x, w_qkv)
     heads = lax.all_to_all(send, "seq", 0, 0, tiled=True)
@@ -614,7 +619,7 @@
     normed_all = lax.all_gather(normed, "seq", axis=0, tiled=True)
     send, out, lse = attend(scalars, heads_near)
     att = local_memory(lax.all_to_all(send, "seq", 0, 0, tiled=True))
-    output, res_grad, send, rounded, *picks = middle(scalars, att, x, x_side, g, g_side, w_out, w_conv)
+    output, res_grad, send, rounded, *picks = middle(scalars, att, x, g, low, high, w_out, w_conv)
     back = lax.all_to_all(send, "seq", 0, 0, tiled=True)
     far = [[FAST * i + j for i in range(SLOW)] for j in range(FAST)]
     rounded_all = lax.all_gather(rounded, "dp", axis=0, axis_index_groups=far, tiled=True)

time: 188 us -> 186 us (0.989)
    ppermute x2, waiting for transfers between devices: 13.1 us -> 10.9 us  [the longest x1 10.9 us: local(): lax.ppermute(jnp.concatenate([x[-HALO:], g[-edge:]], axis=0), 'seq', forw...]
where the time goes in v11:
time: 186 us; the launch traced here: 185 us
  starting transfers between devices  58.5 us (31%)
  waiting for transfers between devices  58.3 us (31%)
  Pallas kernels  51 us (27%)
  between operations  14.8 us (8%)
  local copies, waits for them, and re-layouts  2.31 us (1%)
    all_to_all x1, waiting for transfers between devices, local(): heads = lax.all_to_all(send, 'seq', 0, 0, tiled=True)  24.7 us
    ppermute x9, waiting for transfers between devices, exchange(): lax.ppermute(block, 'dp', pairs(k))  17.1 us
    ppermute x9, starting transfers between devices, exchange(): lax.ppermute(block, 'dp', pairs(k))  12.9 us
    pallas_call x1, Pallas kernels, attend_back(): pl.pallas_call(attend_back_kernel, in_specs=[SMEM] + [vmem] * 4, out_shap...  12.7 us
    ppermute x1, waiting for transfers between devices, local(): lax.ppermute(jnp.concatenate([x[-HALO:], g[-edge:]], axis=0), 'seq', forw...  10.9 us
    all_to_all x1, starting transfers between devices, local(): heads = lax.all_to_all(send, 'seq', 0, 0, tiled=True)  9.53 us
    pallas_call x1, Pallas kernels, middle(): pl.pallas_call(middle_kernel, in_specs=[SMEM] + [vmem] * 7, out_shape=[ja...  8.72 us
    all_to_all x1, starting transfers between devices, local(): recv = lax.all_to_all(send, 'seq', 0, 0, tiled=True)  8.26 us
  transfers between devices with their start and end apart: 18, of which 11 were waited for; matrix products, arithmetic and copies ran while one was open for 1% of the time, Pallas kernels for 24%

profile of v11, /device:TPU:32, one launch (start us, length us, event | category | flops | bytes accessed | tf_op | source)
XLA Modules:
  0.0 184.9 jit_solution(7357968592674027934)
XLA Ops:
  7.2 0.0 all-gather.3.cloned.1.call-start
  7.2 5.4 %project.1 = (bf16[128,1024]{1,0:T(8,128)(2,1)}, bf16[16,192,128]{2,1,0:T(8,128)(2,1)}) custom-call(bf16[128,1024]{1,0:T(8,128)(2,1)} %bitcast.16, bf16[1024,3072]{1,0:T(8,128)(2,1)} %weight_ref.3), custom_call_target="tpu_custom_call" | custom-call | tf_op jit(solution)/shard_map/project/pallas_call | solution.py:91
  12.7 0.0 all-gather.3.cloned.1.call-update
  12.7 9.5 %all-to-all-start = ((bf16[16,192,128]{2,1,0:T(8,128)(2,1)}), bf16[16,192,128]{2,1,0:T(8,128)(2,1)S(1)}, u32[]{:S(2)}, u32[]{:S(2)}) async-start(bf16[16,192,128]{2,1,0:T(8,128)(2,1)} %get-tuple-element.35), calls=%async_computation | async-start | bytes 1572864 | tf_op jit(solution)/shard_map/all_to_all | solution.py:617
  22.9 0.7 stack.15.scalars
  23.5 24.7 %all-to-all-done.heads_ref = bf16[16,192,128]{2,1,0:T(8,128)(2,1)S(1)} async-done(((bf16[16,192,128]{2,1,0:T(8,128)(2,1)}), bf16[16,192,128]{2,1,0:T(8,128)(2,1)S(1)}, u32[]{:S(2)}, u32[]{:S(2)}) %all-to-all-start) | async-done | bytes 786464 | tf_op jit(solution)/shard_map/all_to_all | solution.py:617
  48.2 7.6 %attend.1 = (bf16[16,96,128]{2,1,0:T(8,128)(2,1)}, f32[64,2048]{1,0:T(8,128)}, f32[1,2048]{1,0:T(1,128)}) custom-call(s32[5]{0:T(128)} %stack.15.scalars, bf16[16,192,128]{2,1,0:T(8,128)(2,1)S(1)} %all-to-all-done.heads_ref), custom_call_target="tpu_custom_call" | custom-call | flops 4294967296 | bytes 786432 | tf_op jit(solution)/shard_map/attend/pallas_call | solution.py:165
  55.8 7.0 %all-to-all-start.1 = ((bf16[16,96,128]{2,1,0:T(8,128)(2,1)}), bf16[16,96,128]{2,1,0:T(8,128)(2,1)S(1)}, u32[]{:S(2)}, u32[]{:S(2)}) async-start(bf16[16,96,128]{2,1,0:T(8,128)(2,1)} %get-tuple-element.36), calls=%async_computation.1 | async-start | bytes 786432 | tf_op jit(solution)/shard_map/all_to_all | solution.py:621
  62.8 0.8 slice_bitcast_fusion.2
  63.6 3.4 %collective-permute-start = (bf16[48,1024]{1,0:T(8,128)(2,1)S(1)}, bf16[48,1024]{1,0:T(8,128)(2,1)S(1)}, u32[]{:S(2)}, u32[]{:S(2)}) collective-permute-start(bf16[48,1024]{1,0:T(8,128)(2,1)S(1)} %pad_maximum_fusion), channel_id=1, source_target_pairs={{0,1},{1,2},{2,3},{3,4},{4,5},{5,6},{6,7},{7,8},{8,9},{9,10},{10,1... | collective-permute-start | bytes 294920 | tf_op jit(solution)/shard_map/ppermute | solution.py:612
  67.0 2.5 %collective-permute-start.1 = (bf16[48,1024]{1,0:T(8,128)(2,1)S(1)}, bf16[48,1024]{1,0:T(8,128)(2,1)S(1)}, u32[]{:S(2)}, u32[]{:S(2)}) collective-permute-start(bf16[48,1024]{1,0:T(8,128)(2,1)S(1)} %pad_maximum_fusion.1), channel_id=1, source_target_pairs={{1,0},{2,1},{3,2},{4,3},{5,4},{6,5},{7,6},{8,7},{9,8},{10,9},{11,1... | collective-permute-start | bytes 294920 | tf_op jit(solution)/shard_map/ppermute | solution.py:613
  69.5 10.9 %collective-permute-done.low_ref = bf16[48,1024]{1,0:T(8,128)(2,1)S(1)} collective-permute-done((bf16[48,1024]{1,0:T(8,128)(2,1)S(1)}, bf16[48,1024]{1,0:T(8,128)(2,1)S(1)}, u32[]{:S(2)}, u32[]{:S(2)}) %collective-permute-start) | collective-permute-done | bytes 98336 | tf_op jit(solution)/shard_map/ppermute | solution.py:612
  80.5 8.7 %middle.1 = (bf16[128,1024]{1,0:T(8,128)(2,1)}, f32[128,1024]{1,0:T(8,128)}, bf16[16,80,128]{2,1,0:T(8,128)(2,1)}, bf16[128,1024]{1,0:T(8,128)(2,1)}, bf16[256,1...) custom-call(s32[5]{0:T(128)} %stack.15.scalars, ...), custom_call_target="tpu_custom_call" | custom-call | tf_op jit(solution)/shard_map/middle/pallas_call | solution.py:289
  89.2 8.0 %all-to-all-start.2 = ((bf16[16,80,128]{2,1,0:T(8,128)(2,1)}), bf16[16,80,128]{2,1,0:T(8,128)(2,1)S(1)}, u32[]{:S(2)}, u32[]{:S(2)}) async-start(bf16[16,80,128]{2,1,0:T(8,128)(2,1)} %get-tuple-element.38), calls=%async_computation.2 | async-start | bytes 655360 | tf_op jit(solution)/shard_map/all_to_all | solution.py:623
  97.2 0.0 all-gather.5.cloned.1.call-start
  97.3 1.8 collective-permute-start.2
  99.0 3.1 %collective-permute-start.3 = (bf16[256,128]{1,0:T(8,128)(2,1)}, bf16[256,128]{1,0:T(8,128)(2,1)S(1)}, u32[]{:S(2)}, u32[]{:S(2)}) collective-permute-start(bf16[256,128]{1,0:T(8,128)(2,1)} %get-tuple-element.41), channel_id=1, source_target_pairs={{0,128},{16,144},{32,160},{48,176},{64,192},{80,208},{96,224},{112... | collective-permute-start | bytes 196616 | tf_op jit(solution)/shard_map/ppermute | solution.py:590
  102.1 0.0 collective-permute-start.4
  102.1 0.0 all-gather.5.cloned.1.call-update
  102.2 0.0 collective-permute-done.2.rest_1_
  102.2 3.1 %collective-permute-done.3.rest_2_ = bf16[256,128]{1,0:T(8,128)(2,1)S(1)} collective-permute-done((bf16[256,128]{1,0:T(8,128)(2,1)}, bf16[256,128]{1,0:T(8,128)(2,1)S(1)}, u32[]{:S(2)}, u32[]{:S(2)}) %collective-permute-start.3) | collective-permute-done | bytes 65568 | tf_op jit(solution)/shard_map/ppermute | solution.py:590
  105.3 2.5 %collective-permute-done.4.rest_3_ = bf16[256,128]{1,0:T(8,128)(2,1)S(1)} collective-permute-done((bf16[256,128]{1,0:T(8,128)(2,1)}, bf16[256,128]{1,0:T(8,128)(2,1)S(1)}, u32[]{:S(2)}, u32[]{:S(2)}) %collective-permute-start.4) | collective-permute-done | bytes 65568 | tf_op jit(solution)/shard_map/ppermute | solution.py:590
  107.8 1.3 all-to-all-done.2.grads_ref.back_ref
  109.1 12.7 %attend_back.1.grads_ref = bf16[16,192,128]{2,1,0:T(8,128)(2,1)} custom-call(s32[5]{0:T(128)} %stack.15.scalars, bf16[16,192,128]{2,1,0:T(8,128)(2,1)} %copy-done.1, bf16[16,80,128]{2,1,0:T(8,128)(2,1)S(1)} %all-to-all-done.2.grads_ref.back_ref, f32[64,2048]{1,0:T(8,128)} %get-tuple-element.44.out_ref, f32[1,2048]{1,0:T(1,128)} %get-tuple-element.45.lse_ref), custom_call_target="tpu_custom_call" | custom-call | flops 10737418240 | bytes 1572864 | tf_op jit(solution)/shard_map/attend_back/pallas_call | solution.py:361
  121.8 6.9 %all-to-all-start.3 = ((bf16[16,192,128]{2,1,0:T(8,128)(2,1)}), bf16[16,192,128]{2,1,0:T(8,128)(2,1)S(1)}, u32[]{:S(2)}, u32[]{:S(2)}) async-start(bf16[16,192,128]{2,1,0:T(8,128)(2,1)} %attend_back.1.grads_ref), calls=%async_computation.3 | async-start | bytes 1572864 | tf_op jit(solution)/shard_map/all_to_all | solution.py:628
  128.6 0.0 all-gather.3.cloned.1.call-done.normed_ref
  128.7 6.0 %gradient_parts.1 = (bf16[416,128]{1,0:T(8,128)(2,1)}, bf16[416,128]{1,0:T(8,128)(2,1)}, bf16[416,128]{1,0:T(8,128)(2,1)}, bf16[416,128]{1,0:T(8,128)(2,1)}) custom-call(s32[5]{0:T(128)} %stack.15.scalars, bf16[16,192,128]{2,1,0:T(8,128)(2,1)} %attend_back.1.grads_ref, bf16[16,80,128]{2,1,0:T(8,128)(2,1)} %copy-done, ...), custom_call_target="tpu_custom_call" | custom-call | tf_op jit(solution)/shard_map/gradient_parts/pallas_call | solution.py:458
  134.6 0.1 collective-permute-start.5
  134.7 3.1 %collective-permute-start.6 = (bf16[416,128]{1,0:T(8,128)(2,1)}, bf16[416,128]{1,0:T(8,128)(2,1)S(1)}, u32[]{:S(2)}, u32[]{:S(2)}) collective-permute-start(bf16[416,128]{1,0:T(8,128)(2,1)} %get-tuple-element.50), channel_id=1, source_target_pairs={{0,128},{16,144},{32,160},{48,176},{64,192},{80,208},{96,224},{112... | collective-permute-start | bytes 319496 | tf_op jit(solution)/shard_map/ppermute | solution.py:590
  137.8 1.5 collective-permute-start.7
  139.3 1.2 all-gather.5.cloned.1.call-done.round_ref
  140.5 1.4 collective-permute-done.6.three
  141.9 2.0 %collective-permute-done.7.four = bf16[416,128]{1,0:T(8,128)(2,1)S(1)} collective-permute-done((bf16[416,128]{1,0:T(8,128)(2,1)}, bf16[416,128]{1,0:T(8,128)(2,1)S(1)}, u32[]{:S(2)}, u32[]{:S(2)}) %collective-permute-start.7) | collective-permute-done | bytes 106528 | tf_op jit(solution)/shard_map/ppermute | solution.py:590
  143.9 2.5 %fold_first.1 = (bf16[640,128]{1,0:T(8,128)(2,1)}, bf16[640,128]{1,0:T(8,128)(2,1)}, bf16[640,128]{1,0:T(8,128)(2,1)}, bf16[640,128]{1,0:T(8,128)(2,1)}) custom-call(s32[5]{0:T(128)} %stack.15.scalars, bf16[416,128]{1,0:T(8,128)(2,1)} %get-tuple-element.48.one, bf16[416,128]{1,0:T(8,128)(2,1)S(1)} %collective-permute-done.5.two, ...), custom_call_target="tpu_custom_call" | custom-call | tf_op jit(solution)/shard_map/fold_first/pallas_call | solution.py:507
  146.5 0.0 collective-permute-start.8
  146.5 2.4 %collective-permute-start.9 = (bf16[640,128]{1,0:T(8,128)(2,1)}, bf16[640,128]{1,0:T(8,128)(2,1)S(1)}, u32[]{:S(2)}, u32[]{:S(2)}) collective-permute-start(bf16[640,128]{1,0:T(8,128)(2,1)} %get-tuple-element.59), channel_id=1, source_target_pairs={{0,32},{16,48},{32,0},{48,16},{64,96},{80,112},{96,64},{112,80},{1... | collective-permute-start | bytes 491528 | tf_op jit(solution)/shard_map/ppermute | solution.py:590
  148.9 1.0 collective-permute-start.10
  149.8 0.0 collective-permute-done.8.refs_1_
  149.8 5.4 %collective-permute-done.9.refs_2_ = bf16[640,128]{1,0:T(8,128)(2,1)S(1)} collective-permute-done((bf16[640,128]{1,0:T(8,128)(2,1)}, bf16[640,128]{1,0:T(8,128)(2,1)S(1)}, u32[]{:S(2)}, u32[]{:S(2)}) %collective-permute-start.9) | collective-permute-done | bytes 163872 | tf_op jit(solution)/shard_map/ppermute | solution.py:590
  155.2 2.6 %collective-permute-done.10.refs_3_ = bf16[640,128]{1,0:T(8,128)(2,1)S(1)} collective-permute-done((bf16[640,128]{1,0:T(8,128)(2,1)}, bf16[640,128]{1,0:T(8,128)(2,1)S(1)}, u32[]{:S(2)}, u32[]{:S(2)}) %collective-permute-start.10) | collective-permute-done | bytes 163872 | tf_op jit(solution)/shard_map/ppermute | solution.py:590
  157.9 1.8 fold_last.1
  159.7 0.0 all-to-all-done.3.joined_ref
  159.7 8.3 %all-to-all-start.4 = ((bf16[16,48,128]{2,1,0:T(8,128)(2,1)}), bf16[16,48,128]{2,1,0:T(8,128)(2,1)S(1)}, u32[]{:S(2)}, u32[]{:S(2)}) async-start(bf16[16,48,128]{2,1,0:T(8,128)(2,1)} %get-tuple-element.62), calls=%async_computation.4 | async-start | bytes 393216 | tf_op jit(solution)/shard_map/all_to_all | solution.py:633
  167.9 5.4 %input_gradient.1 = bf16[128,1024]{1,0:T(8,128)(2,1)} custom-call(bf16[16,192,128]{2,1,0:T(8,128)(2,1)S(1)} %all-to-all-done.3.joined_ref, bf16[1024,3072]{1,0:T(8,128)(2,1)} %weight_ref.3, bf16[128,1024]{1,0:T(8,128)(2,1)} %bitcast.18, f32[128,1024]{1,0:T(8,128)} %get-tuple-element.46.res_grad_ref), custom_call_target="tpu_custom_call" | custom-call | tf_op jit(solution)/shard_map/input_gradient/pallas_call | solution.py:407
  173.3 0.1 copy.12
  173.4 0.7 copy.13
  174.2 3.1 %all-to-all-done.4.refs_0_ = bf16[16,48,128]{2,1,0:T(8,128)(2,1)S(1)} async-done(((bf16[16,48,128]{2,1,0:T(8,128)(2,1)}), bf16[16,48,128]{2,1,0:T(8,128)(2,1)S(1)}, u32[]{:S(2)}, u32[]{:S(2)}) %all-to-all-start.4) | async-done | bytes 196640 | tf_op jit(solution)/shard_map/all_to_all | solution.py:633
  177.3 0.8 finish.1
  (14 shorter events, 0.0 us)
Async XLA Ops:
  7.2 121.5 %all-gather.3.cloned.1.call-start = ((), (), s32[]{:S(2)}) async-start(), calls=%async_computation.5 | async-start | bytes 4456448 | tf_op jit(solution)/shard_map/all_gather | solution.py:619
  12.7 35.5 %all-to-all-start = ((bf16[16,192,128]{2,1,0:T(8,128)(2,1)}), bf16[16,192,128]{2,1,0:T(8,128)(2,1)S(1)}, u32[]{:S(2)}, u32[]{:S(2)}) async-start(bf16[16,192,128]{2,1,0:T(8,128)(2,1)} %get-tuple-element.35), calls=%async_computation | async-start | bytes 1572864 | tf_op jit(solution)/shard_map/all_to_all | solution.py:617
  23.5 40.1 %copy-start.2 = (bf16[1,128,1024]{2,1,0:T(8,128)(2,1)S(1)}, bf16[1,128,1024]{2,1,0:T(8,128)(2,1)}, u32[]{:S(2)}) copy-start(bf16[1,128,1024]{2,1,0:T(8,128)(2,1)} %param.6) | copy-start | bytes 786436
  48.2 7.6 %copy-start.1 = (bf16[16,192,128]{2,1,0:T(8,128)(2,1)}, bf16[16,192,128]{2,1,0:T(8,128)(2,1)S(1)}, u32[]{:S(2)}) copy-start(bf16[16,192,128]{2,1,0:T(8,128)(2,1)S(1)} %all-to-all-done.heads_ref) | copy-start | bytes 2359300
  55.8 24.6 %all-to-all-start.1 = ((bf16[16,96,128]{2,1,0:T(8,128)(2,1)}), bf16[16,96,128]{2,1,0:T(8,128)(2,1)S(1)}, u32[]{:S(2)}, u32[]{:S(2)}) async-start(bf16[16,96,128]{2,1,0:T(8,128)(2,1)} %get-tuple-element.36), calls=%async_computation.1 | async-start | bytes 786432 | tf_op jit(solution)/shard_map/all_to_all | solution.py:621
  63.6 16.8 %collective-permute-start = (bf16[48,1024]{1,0:T(8,128)(2,1)S(1)}, bf16[48,1024]{1,0:T(8,128)(2,1)S(1)}, u32[]{:S(2)}, u32[]{:S(2)}) collective-permute-start(bf16[48,1024]{1,0:T(8,128)(2,1)S(1)} %pad_maximum_fusion), channel_id=1, source_target_pairs={{0,1},{1,2},{2,3},{3,4},{4,5},{5,6},{6,7},{7,8},{8,9},{9,10},{10,1... | collective-permute-start | bytes 294920 | tf_op jit(solution)/shard_map/ppermute | solution.py:612
  67.0 13.4 %collective-permute-start.1 = (bf16[48,1024]{1,0:T(8,128)(2,1)S(1)}, bf16[48,1024]{1,0:T(8,128)(2,1)S(1)}, u32[]{:S(2)}, u32[]{:S(2)}) collective-permute-start(bf16[48,1024]{1,0:T(8,128)(2,1)S(1)} %pad_maximum_fusion.1), channel_id=1, source_target_pairs={{1,0},{2,1},{3,2},{4,3},{5,4},{6,5},{7,6},{8,7},{9,8},{10,9},{11,1... | collective-permute-start | bytes 294920 | tf_op jit(solution)/shard_map/ppermute | solution.py:613
  89.2 19.9 %all-to-all-start.2 = ((bf16[16,80,128]{2,1,0:T(8,128)(2,1)}), bf16[16,80,128]{2,1,0:T(8,128)(2,1)S(1)}, u32[]{:S(2)}, u32[]{:S(2)}) async-start(bf16[16,80,128]{2,1,0:T(8,128)(2,1)} %get-tuple-element.38), calls=%async_computation.2 | async-start | bytes 655360 | tf_op jit(solution)/shard_map/all_to_all | solution.py:623
  97.2 43.3 %all-gather.5.cloned.1.call-start = ((), (), s32[]{:S(2)}) async-start(), calls=%async_computation.6 | async-start | bytes 1310720 | tf_op jit(solution)/shard_map/all_gather | solution.py:625
  97.3 4.9 %collective-permute-start.2 = (bf16[256,128]{1,0:T(8,128)(2,1)}, bf16[256,128]{1,0:T(8,128)(2,1)S(1)}, u32[]{:S(2)}, u32[]{:S(2)}) collective-permute-start(bf16[256,128]{1,0:T(8,128)(2,1)} %get-tuple-element.40), channel_id=1, source_target_pairs={{0,64},{16,80},{32,96},{48,112},{64,0},{80,16},{96,32},{112,48},{1... | collective-permute-start | bytes 196616 | tf_op jit(solution)/shard_map/ppermute | solution.py:590
  99.0 6.3 %collective-permute-start.3 = (bf16[256,128]{1,0:T(8,128)(2,1)}, bf16[256,128]{1,0:T(8,128)(2,1)S(1)}, u32[]{:S(2)}, u32[]{:S(2)}) collective-permute-start(bf16[256,128]{1,0:T(8,128)(2,1)} %get-tuple-element.41), channel_id=1, source_target_pairs={{0,128},{16,144},{32,160},{48,176},{64,192},{80,208},{96,224},{112... | collective-permute-start | bytes 196616 | tf_op jit(solution)/shard_map/ppermute | solution.py:590
  102.1 5.7 %collective-permute-start.4 = (bf16[256,128]{1,0:T(8,128)(2,1)}, bf16[256,128]{1,0:T(8,128)(2,1)S(1)}, u32[]{:S(2)}, u32[]{:S(2)}) collective-permute-start(bf16[256,128]{1,0:T(8,128)(2,1)} %get-tuple-element.42), channel_id=1, source_target_pairs={{0,192},{16,208},{32,224},{48,240},{64,128},{80,144},{96,160},{112... | collective-permute-start | bytes 196616 | tf_op jit(solution)/shard_map/ppermute | solution.py:590
  109.1 12.7 %copy-start = (bf16[16,80,128]{2,1,0:T(8,128)(2,1)}, bf16[16,80,128]{2,1,0:T(8,128)(2,1)S(1)}, u32[]{:S(2)}) copy-start(bf16[16,80,128]{2,1,0:T(8,128)(2,1)S(1)} %all-to-all-done.2.grads_ref.back_ref) | copy-start | bytes 983044
  121.8 37.9 %all-to-all-start.3 = ((bf16[16,192,128]{2,1,0:T(8,128)(2,1)}), bf16[16,192,128]{2,1,0:T(8,128)(2,1)S(1)}, u32[]{:S(2)}, u32[]{:S(2)}) async-start(bf16[16,192,128]{2,1,0:T(8,128)(2,1)} %attend_back.1.grads_ref), calls=%async_computation.3 | async-start | bytes 1572864 | tf_op jit(solution)/shard_map/all_to_all | solution.py:628
  134.6 5.9 %collective-permute-start.5 = (bf16[416,128]{1,0:T(8,128)(2,1)}, bf16[416,128]{1,0:T(8,128)(2,1)S(1)}, u32[]{:S(2)}, u32[]{:S(2)}) collective-permute-start(bf16[416,128]{1,0:T(8,128)(2,1)} %get-tuple-element.49), channel_id=1, source_target_pairs={{0,64},{16,80},{32,96},{48,112},{64,0},{80,16},{96,32},{112,48},{1... | collective-permute-start | bytes 319496 | tf_op jit(solution)/shard_map/ppermute | solution.py:590
  134.7 7.2 %collective-permute-start.6 = (bf16[416,128]{1,0:T(8,128)(2,1)}, bf16[416,128]{1,0:T(8,128)(2,1)S(1)}, u32[]{:S(2)}, u32[]{:S(2)}) collective-permute-start(bf16[416,128]{1,0:T(8,128)(2,1)} %get-tuple-element.50), channel_id=1, source_target_pairs={{0,128},{16,144},{32,160},{48,176},{64,192},{80,208},{96,224},{112... | collective-permute-start | bytes 319496 | tf_op jit(solution)/shard_map/ppermute | solution.py:590
  137.8 6.1 %collective-permute-start.7 = (bf16[416,128]{1,0:T(8,128)(2,1)}, bf16[416,128]{1,0:T(8,128)(2,1)S(1)}, u32[]{:S(2)}, u32[]{:S(2)}) collective-permute-start(bf16[416,128]{1,0:T(8,128)(2,1)} %get-tuple-element.51), channel_id=1, source_target_pairs={{0,192},{16,208},{32,224},{48,240},{64,128},{80,144},{96,160},{112... | collective-permute-start | bytes 319496 | tf_op jit(solution)/shard_map/ppermute | solution.py:590
  146.5 3.4 %collective-permute-start.8 = (bf16[640,128]{1,0:T(8,128)(2,1)}, bf16[640,128]{1,0:T(8,128)(2,1)S(1)}, u32[]{:S(2)}, u32[]{:S(2)}) collective-permute-start(bf16[640,128]{1,0:T(8,128)(2,1)} %get-tuple-element.58), channel_id=1, source_target_pairs={{0,16},{16,0},{32,48},{48,32},{64,80},{80,64},{96,112},{112,96},{1... | collective-permute-start | bytes 491528 | tf_op jit(solution)/shard_map/ppermute | solution.py:590
  146.5 8.8 %collective-permute-start.9 = (bf16[640,128]{1,0:T(8,128)(2,1)}, bf16[640,128]{1,0:T(8,128)(2,1)S(1)}, u32[]{:S(2)}, u32[]{:S(2)}) collective-permute-start(bf16[640,128]{1,0:T(8,128)(2,1)} %get-tuple-element.59), channel_id=1, source_target_pairs={{0,32},{16,48},{32,0},{48,16},{64,96},{80,112},{96,64},{112,80},{1... | collective-permute-start | bytes 491528 | tf_op jit(solution)/shard_map/ppermute | solution.py:590
  148.9 9.0 %collective-permute-start.10 = (bf16[640,128]{1,0:T(8,128)(2,1)}, bf16[640,128]{1,0:T(8,128)(2,1)S(1)}, u32[]{:S(2)}, u32[]{:S(2)}) collective-permute-start(bf16[640,128]{1,0:T(8,128)(2,1)} %get-tuple-element.60), channel_id=1, source_target_pairs={{0,48},{16,32},{32,16},{48,0},{64,112},{80,96},{96,80},{112,64},{1... | collective-permute-start | bytes 491528 | tf_op jit(solution)/shard_map/ppermute | solution.py:590
  159.7 13.7 %copy-start.3 = (f32[64,192]{1,0:T(8,128)S(1)}, f32[64,192]{1,0:T(8,128)}, u32[]{:S(2)}) copy-start(f32[64,192]{1,0:T(8,128)} %get-tuple-element.61) | copy-start | bytes 147460
  159.7 17.6 %all-to-all-start.4 = ((bf16[16,48,128]{2,1,0:T(8,128)(2,1)}), bf16[16,48,128]{2,1,0:T(8,128)(2,1)S(1)}, u32[]{:S(2)}, u32[]{:S(2)}) async-start(bf16[16,48,128]{2,1,0:T(8,128)(2,1)} %get-tuple-element.62), calls=%async_computation.4 | async-start | bytes 393216 | tf_op jit(solution)/shard_map/all_to_all | solution.py:633
Sparse Core Ops, SparseCore 0:
  12.8 96.3 all-gather.2
  111.0 29.4 all-gather.4

commit v12 on v11

--- a/solution.py
+++ b/solution.py
@@ -611,11 +611,12 @@
     edge = HALO // 2
     low = lax.ppermute(jnp.concatenate([x[-HALO:], g[-edge:]], axis=0), "seq", forward)
     high = lax.ppermute(jnp.concatenate([x[:HALO], g[:edge]], axis=0), "seq", backward)
-    low, high = local_memory(low), local_memory(high)
 
     normed, send = project(x, w_qkv)
     heads = lax.all_to_all(send, "seq", 0, 0, tiled=True)
+    heads, low, high = lax.optimization_barrier((heads, low, high))
     heads_near = local_memory(heads)
+    low, high = local_memory(low), local_memory(high)
     normed_all = lax.all_gather(normed, "seq", axis=0, tiled=True)
     send, out, lse = attend(scalars, heads_near)
     att = local_memory(lax.all_to_all(send, "seq", 0, 0, tiled=True))

time: 186 us -> 186 us (level)
  blocking collectives: 0 us -> 24.1 us
  waiting for transfers between devices: 58.3 us -> 43.5 us
  starting transfers between devices: 58.5 us -> 49.4 us
    all_to_all x1, waiting for transfers between devices: 24.7 us -> 0.01 us  [local(): heads = lax.all_to_all(send, 'seq', 0, 0, tiled=True)]
    all_to_all x0 -> x1, blocking collectives: none -> 24.1 us  [local(): att = local_memory(lax.all_to_all(send, 'seq', 0, 0, tiled=True))]
    ppermute x1, waiting for transfers between devices: 10.9 us -> 19.4 us  [local(): lax.ppermute(jnp.concatenate([x[-HALO:], g[-edge:]], axis=0), 'seq', forw...]
    all_to_all x1 -> x0, starting transfers between devices: 6.98 us -> none  [local(): att = local_memory(lax.all_to_all(send, 'seq', 0, 0, tiled=True))]
  transfers between devices with their start and end apart: 18 -> 17, of which waited for: 11 -> 12; matrix products, arithmetic and copies ran while one was open for 1% -> 1% of each run, Pallas kernels for 24% -> 24%
where the time goes in v12:
time: 186 us; the launch traced here: 185 us
  Pallas kernels  51 us (27%)
  starting transfers between devices  49.4 us (27%)
  waiting for transfers between devices  43.5 us (23%)
  blocking collectives  24.1 us (13%)
  between operations  14.8 us (8%)
  local copies, waits for them, and re-layouts  2.21 us (1%)
    all_to_all x1, blocking collectives, local(): att = local_memory(lax.all_to_all(send, 'seq', 0, 0, tiled=True))  24.1 us
    ppermute x1, waiting for transfers between devices, local(): lax.ppermute(jnp.concatenate([x[-HALO:], g[-edge:]], axis=0), 'seq', forw...  19.4 us
    ppermute x9, waiting for transfers between devices, exchange(): lax.ppermute(block, 'dp', pairs(k))  17.8 us
    ppermute x9, starting transfers between devices, exchange(): lax.ppermute(block, 'dp', pairs(k))  12.9 us
    pallas_call x1, Pallas kernels, attend_back(): pl.pallas_call(attend_back_kernel, in_specs=[SMEM] + [vmem] * 4, out_shap...  12.7 us
    all_to_all x1, starting transfers between devices, local(): heads = lax.all_to_all(send, 'seq', 0, 0, tiled=True)  9.53 us
    pallas_call x1, Pallas kernels, middle(): pl.pallas_call(middle_kernel, in_specs=[SMEM] + [vmem] * 7, out_shape=[ja...  8.68 us
    all_to_all x1, starting transfers between devices, local(): recv = lax.all_to_all(send, 'seq', 0, 0, tiled=True)  8.26 us
  transfers between devices with their start and end apart: 17, of which 12 were waited for; matrix products, arithmetic and copies ran while one was open for 1% of the time, Pallas kernels for 24%

profile of v12, /device:TPU:32, one launch (start us, length us, event | category | flops | bytes accessed | tf_op | source)
XLA Modules:
  0.0 184.9 jit_solution(7670269866841393547)
XLA Ops:
  7.2 0.0 all-gather.3.cloned.1.call-start
  7.2 0.0 copy-start.2
  7.2 5.5 %project.1 = (bf16[128,1024]{1,0:T(8,128)(2,1)}, bf16[16,192,128]{2,1,0:T(8,128)(2,1)}) custom-call(bf16[128,1024]{1,0:T(8,128)(2,1)} %bitcast.16, bf16[1024,3072]{1,0:T(8,128)(2,1)} %weight_ref.3), custom_call_target="tpu_custom_call" | custom-call | tf_op jit(solution)/shard_map/project/pallas_call | solution.py:91
  12.7 0.0 all-gather.3.cloned.1.call-update
  12.7 9.5 %all-to-all-start = ((bf16[16,192,128]{2,1,0:T(8,128)(2,1)}), bf16[16,192,128]{2,1,0:T(8,128)(2,1)S(1)}, u32[]{:S(2)}, u32[]{:S(2)}) async-start(bf16[16,192,128]{2,1,0:T(8,128)(2,1)} %get-tuple-element.38), calls=%async_computation | async-start | bytes 1572864 | tf_op jit(solution)/shard_map/all_to_all | solution.py:616
  22.3 0.8 slice_bitcast_fusion.2
  23.1 3.4 %collective-permute-start = (bf16[48,1024]{1,0:T(8,128)(2,1)S(1)}, bf16[48,1024]{1,0:T(8,128)(2,1)S(1)}, u32[]{:S(2)}, u32[]{:S(2)}) collective-permute-start(bf16[48,1024]{1,0:T(8,128)(2,1)S(1)} %pad_maximum_fusion), channel_id=1, source_target_pairs={{0,1},{1,2},{2,3},{3,4},{4,5},{5,6},{6,7},{7,8},{8,9},{9,10},{10,1... | collective-permute-start | bytes 294920 | tf_op jit(solution)/shard_map/ppermute | solution.py:612
  26.5 2.5 %collective-permute-start.1 = (bf16[48,1024]{1,0:T(8,128)(2,1)S(1)}, bf16[48,1024]{1,0:T(8,128)(2,1)S(1)}, u32[]{:S(2)}, u32[]{:S(2)}) collective-permute-start(bf16[48,1024]{1,0:T(8,128)(2,1)S(1)} %pad_maximum_fusion.1), channel_id=1, source_target_pairs={{1,0},{2,1},{3,2},{4,3},{5,4},{6,5},{7,6},{8,7},{9,8},{10,9},{11,1... | collective-permute-start | bytes 294920 | tf_op jit(solution)/shard_map/ppermute | solution.py:613
  29.6 0.6 stack.15.scalars
  30.2 19.4 %collective-permute-done.low_ref = bf16[48,1024]{1,0:T(8,128)(2,1)S(1)} collective-permute-done((bf16[48,1024]{1,0:T(8,128)(2,1)S(1)}, bf16[48,1024]{1,0:T(8,128)(2,1)S(1)}, u32[]{:S(2)}, u32[]{:S(2)}) %collective-permute-start) | collective-permute-done | bytes 98336 | tf_op jit(solution)/shard_map/ppermute | solution.py:612
  49.5 1.0 collective-permute-done.1.high_ref
  50.5 7.6 %attend.1 = (bf16[16,96,128]{2,1,0:T(8,128)(2,1)}, f32[64,2048]{1,0:T(8,128)}, f32[1,2048]{1,0:T(1,128)}) custom-call(s32[5]{0:T(128)} %stack.15.scalars, bf16[16,192,128]{2,1,0:T(8,128)(2,1)S(1)} %all-to-all-done.heads_ref), custom_call_target="tpu_custom_call" | custom-call | flops 4294967296 | bytes 786432 | tf_op jit(solution)/shard_map/attend/pallas_call | solution.py:165
  58.1 24.1 %all_to_all.25.att_ref = bf16[16,96,128]{2,1,0:T(8,128)(2,1)S(1)} all-to-all(bf16[16,96,128]{2,1,0:T(8,128)(2,1)} %get-tuple-element.40), channel_id=1, replica_groups=mesh['dp'=16,'seq'=16] {'seq'}, dimensions={0} | all-to-all | bytes 786432 | tf_op jit(solution)/shard_map/all_to_all | solution.py:622
  82.2 8.7 %middle.1 = (bf16[128,1024]{1,0:T(8,128)(2,1)}, f32[128,1024]{1,0:T(8,128)}, bf16[16,80,128]{2,1,0:T(8,128)(2,1)}, bf16[128,1024]{1,0:T(8,128)(2,1)}, bf16[256,1...) custom-call(s32[5]{0:T(128)} %stack.15.scalars, ...), custom_call_target="tpu_custom_call" | custom-call | tf_op jit(solution)/shard_map/middle/pallas_call | solution.py:289
  90.9 6.2 %all-to-all-start.2 = ((bf16[16,80,128]{2,1,0:T(8,128)(2,1)}), bf16[16,80,128]{2,1,0:T(8,128)(2,1)S(1)}, u32[]{:S(2)}, u32[]{:S(2)}) async-start(bf16[16,80,128]{2,1,0:T(8,128)(2,1)} %get-tuple-element.44), calls=%async_computation.2 | async-start | bytes 655360 | tf_op jit(solution)/shard_map/all_to_all | solution.py:624
  97.1 0.0 all-gather.5.cloned.1.call-start
  97.1 1.7 collective-permute-start.2
  98.8 3.1 %collective-permute-start.3 = (bf16[256,128]{1,0:T(8,128)(2,1)}, bf16[256,128]{1,0:T(8,128)(2,1)S(1)}, u32[]{:S(2)}, u32[]{:S(2)}) collective-permute-start(bf16[256,128]{1,0:T(8,128)(2,1)} %get-tuple-element.47), channel_id=1, source_target_pairs={{0,128},{16,144},{32,160},{48,176},{64,192},{80,208},{96,224},{112... | collective-permute-start | bytes 196616 | tf_op jit(solution)/shard_map/ppermute | solution.py:590
  101.9 0.0 collective-permute-start.4
  101.9 0.0 all-gather.5.cloned.1.call-update
  102.0 0.0 collective-permute-done.2.rest_1_
  102.0 3.1 %collective-permute-done.3.rest_2_ = bf16[256,128]{1,0:T(8,128)(2,1)S(1)} collective-permute-done((bf16[256,128]{1,0:T(8,128)(2,1)}, bf16[256,128]{1,0:T(8,128)(2,1)S(1)}, u32[]{:S(2)}, u32[]{:S(2)}) %collective-permute-start.3) | collective-permute-done | bytes 65568 | tf_op jit(solution)/shard_map/ppermute | solution.py:590
  105.1 2.5 %collective-permute-done.4.rest_3_ = bf16[256,128]{1,0:T(8,128)(2,1)S(1)} collective-permute-done((bf16[256,128]{1,0:T(8,128)(2,1)}, bf16[256,128]{1,0:T(8,128)(2,1)S(1)}, u32[]{:S(2)}, u32[]{:S(2)}) %collective-permute-start.4) | collective-permute-done | bytes 65568 | tf_op jit(solution)/shard_map/ppermute | solution.py:590
  107.6 1.5 all-to-all-done.2.grads_ref.back_ref
  109.2 12.7 %attend_back.1.grads_ref = bf16[16,192,128]{2,1,0:T(8,128)(2,1)} custom-call(s32[5]{0:T(128)} %stack.15.scalars, bf16[16,192,128]{2,1,0:T(8,128)(2,1)} %copy-done.1, bf16[16,80,128]{2,1,0:T(8,128)(2,1)S(1)} %all-to-all-done.2.grads_ref.back_ref, f32[64,2048]{1,0:T(8,128)} %get-tuple-element.50.out_ref, f32[1,2048]{1,0:T(1,128)} %get-tuple-element.51.lse_ref), custom_call_target="tpu_custom_call" | custom-call | flops 10737418240 | bytes 1572864 | tf_op jit(solution)/shard_map/attend_back/pallas_call | solution.py:361
  121.8 6.6 %all-to-all-start.3 = ((bf16[16,192,128]{2,1,0:T(8,128)(2,1)}), bf16[16,192,128]{2,1,0:T(8,128)(2,1)S(1)}, u32[]{:S(2)}, u32[]{:S(2)}) async-start(bf16[16,192,128]{2,1,0:T(8,128)(2,1)} %attend_back.1.grads_ref), calls=%async_computation.3 | async-start | bytes 1572864 | tf_op jit(solution)/shard_map/all_to_all | solution.py:629
  128.4 0.0 all-gather.3.cloned.1.call-done.normed_ref
  128.5 6.0 %gradient_parts.1 = (bf16[416,128]{1,0:T(8,128)(2,1)}, bf16[416,128]{1,0:T(8,128)(2,1)}, bf16[416,128]{1,0:T(8,128)(2,1)}, bf16[416,128]{1,0:T(8,128)(2,1)}) custom-call(s32[5]{0:T(128)} %stack.15.scalars, bf16[16,192,128]{2,1,0:T(8,128)(2,1)} %attend_back.1.grads_ref, bf16[16,80,128]{2,1,0:T(8,128)(2,1)} %copy-done, ...), custom_call_target="tpu_custom_call" | custom-call | tf_op jit(solution)/shard_map/gradient_parts/pallas_call | solution.py:458
  134.5 0.0 collective-permute-start.5
  134.5 3.2 %collective-permute-start.6 = (bf16[416,128]{1,0:T(8,128)(2,1)}, bf16[416,128]{1,0:T(8,128)(2,1)S(1)}, u32[]{:S(2)}, u32[]{:S(2)}) collective-permute-start(bf16[416,128]{1,0:T(8,128)(2,1)} %get-tuple-element.56), channel_id=1, source_target_pairs={{0,128},{16,144},{32,160},{48,176},{64,192},{80,208},{96,224},{112... | collective-permute-start | bytes 319496 | tf_op jit(solution)/shard_map/ppermute | solution.py:590
  137.8 1.4 collective-permute-start.7
  139.2 0.6 all-gather.5.cloned.1.call-done.round_ref
  139.8 0.3 collective-permute-done.5.two
  140.1 2.0 %collective-permute-done.6.three = bf16[416,128]{1,0:T(8,128)(2,1)S(1)} collective-permute-done((bf16[416,128]{1,0:T(8,128)(2,1)}, bf16[416,128]{1,0:T(8,128)(2,1)S(1)}, u32[]{:S(2)}, u32[]{:S(2)}) %collective-permute-start.6) | collective-permute-done | bytes 106528 | tf_op jit(solution)/shard_map/ppermute | solution.py:590
  142.1 1.8 collective-permute-done.7.four
  143.9 2.5 %fold_first.1 = (bf16[640,128]{1,0:T(8,128)(2,1)}, bf16[640,128]{1,0:T(8,128)(2,1)}, bf16[640,128]{1,0:T(8,128)(2,1)}, bf16[640,128]{1,0:T(8,128)(2,1)}) custom-call(s32[5]{0:T(128)} %stack.15.scalars, bf16[416,128]{1,0:T(8,128)(2,1)} %get-tuple-element.54.one, bf16[416,128]{1,0:T(8,128)(2,1)S(1)} %collective-permute-done.5.two, ...), custom_call_target="tpu_custom_call" | custom-call | tf_op jit(solution)/shard_map/fold_first/pallas_call | solution.py:507
  146.4 0.0 collective-permute-start.8
  146.4 2.7 %collective-permute-start.9 = (bf16[640,128]{1,0:T(8,128)(2,1)}, bf16[640,128]{1,0:T(8,128)(2,1)S(1)}, u32[]{:S(2)}, u32[]{:S(2)}) collective-permute-start(bf16[640,128]{1,0:T(8,128)(2,1)} %get-tuple-element.65), channel_id=1, source_target_pairs={{0,32},{16,48},{32,0},{48,16},{64,96},{80,112},{96,64},{112,80},{1... | collective-permute-start | bytes 491528 | tf_op jit(solution)/shard_map/ppermute | solution.py:590
  149.1 0.7 collective-permute-start.10
  149.8 5.4 %collective-permute-done.9.refs_2_ = bf16[640,128]{1,0:T(8,128)(2,1)S(1)} collective-permute-done((bf16[640,128]{1,0:T(8,128)(2,1)}, bf16[640,128]{1,0:T(8,128)(2,1)S(1)}, u32[]{:S(2)}, u32[]{:S(2)}) %collective-permute-start.9) | collective-permute-done | bytes 163872 | tf_op jit(solution)/shard_map/ppermute | solution.py:590
  155.2 2.6 %collective-permute-done.10.refs_3_ = bf16[640,128]{1,0:T(8,128)(2,1)S(1)} collective-permute-done((bf16[640,128]{1,0:T(8,128)(2,1)}, bf16[640,128]{1,0:T(8,128)(2,1)S(1)}, u32[]{:S(2)}, u32[]{:S(2)}) %collective-permute-start.10) | collective-permute-done | bytes 163872 | tf_op jit(solution)/shard_map/ppermute | solution.py:590
  157.8 1.8 fold_last.1
  159.6 8.3 %all-to-all-start.4 = ((bf16[16,48,128]{2,1,0:T(8,128)(2,1)}), bf16[16,48,128]{2,1,0:T(8,128)(2,1)S(1)}, u32[]{:S(2)}, u32[]{:S(2)}) async-start(bf16[16,48,128]{2,1,0:T(8,128)(2,1)} %get-tuple-element.68), calls=%async_computation.4 | async-start | bytes 393216 | tf_op jit(solution)/shard_map/all_to_all | solution.py:634
  167.9 5.4 %input_gradient.1 = bf16[128,1024]{1,0:T(8,128)(2,1)} custom-call(bf16[16,192,128]{2,1,0:T(8,128)(2,1)S(1)} %all-to-all-done.3.joined_ref, bf16[1024,3072]{1,0:T(8,128)(2,1)} %weight_ref.3, bf16[128,1024]{1,0:T(8,128)(2,1)} %bitcast.18, f32[128,1024]{1,0:T(8,128)} %get-tuple-element.52.res_grad_ref), custom_call_target="tpu_custom_call" | custom-call | tf_op jit(solution)/shard_map/input_gradient/pallas_call | solution.py:407
  173.3 0.1 copy.12
  173.4 0.7 copy.13
  174.1 3.1 %all-to-all-done.4.refs_0_ = bf16[16,48,128]{2,1,0:T(8,128)(2,1)S(1)} async-done(((bf16[16,48,128]{2,1,0:T(8,128)(2,1)}), bf16[16,48,128]{2,1,0:T(8,128)(2,1)S(1)}, u32[]{:S(2)}, u32[]{:S(2)}) %all-to-all-start.4) | async-done | bytes 196640 | tf_op jit(solution)/shard_map/all_to_all | solution.py:634
  177.3 0.8 finish.1
  (13 shorter events, 0.0 us)
Async XLA Ops:
  7.2 121.3 %all-gather.3.cloned.1.call-start = ((), (), s32[]{:S(2)}) async-start(), calls=%async_computation.5 | async-start | bytes 4456448 | tf_op jit(solution)/shard_map/all_gather | solution.py:620
  7.2 15.8 %copy-start.2 = (bf16[1,128,1024]{2,1,0:T(8,128)(2,1)S(1)}, bf16[1,128,1024]{2,1,0:T(8,128)(2,1)}, u32[]{:S(2)}) copy-start(bf16[1,128,1024]{2,1,0:T(8,128)(2,1)} %param.6) | copy-start | bytes 786436
  12.7 37.8 %all-to-all-start = ((bf16[16,192,128]{2,1,0:T(8,128)(2,1)}), bf16[16,192,128]{2,1,0:T(8,128)(2,1)S(1)}, u32[]{:S(2)}, u32[]{:S(2)}) async-start(bf16[16,192,128]{2,1,0:T(8,128)(2,1)} %get-tuple-element.38), calls=%async_computation | async-start | bytes 1572864 | tf_op jit(solution)/shard_map/all_to_all | solution.py:616
  23.1 26.5 %collective-permute-start = (bf16[48,1024]{1,0:T(8,128)(2,1)S(1)}, bf16[48,1024]{1,0:T(8,128)(2,1)S(1)}, u32[]{:S(2)}, u32[]{:S(2)}) collective-permute-start(bf16[48,1024]{1,0:T(8,128)(2,1)S(1)} %pad_maximum_fusion), channel_id=1, source_target_pairs={{0,1},{1,2},{2,3},{3,4},{4,5},{5,6},{6,7},{7,8},{8,9},{9,10},{10,1... | collective-permute-start | bytes 294920 | tf_op jit(solution)/shard_map/ppermute | solution.py:612
  26.5 24.0 %collective-permute-start.1 = (bf16[48,1024]{1,0:T(8,128)(2,1)S(1)}, bf16[48,1024]{1,0:T(8,128)(2,1)S(1)}, u32[]{:S(2)}, u32[]{:S(2)}) collective-permute-start(bf16[48,1024]{1,0:T(8,128)(2,1)S(1)} %pad_maximum_fusion.1), channel_id=1, source_target_pairs={{1,0},{2,1},{3,2},{4,3},{5,4},{6,5},{7,6},{8,7},{9,8},{10,9},{11,1... | collective-permute-start | bytes 294920 | tf_op jit(solution)/shard_map/ppermute | solution.py:613
  50.5 7.6 %copy-start.1 = (bf16[16,192,128]{2,1,0:T(8,128)(2,1)}, bf16[16,192,128]{2,1,0:T(8,128)(2,1)S(1)}, u32[]{:S(2)}) copy-start(bf16[16,192,128]{2,1,0:T(8,128)(2,1)S(1)} %all-to-all-done.heads_ref) | copy-start | bytes 2359300
  90.9 18.3 %all-to-all-start.2 = ((bf16[16,80,128]{2,1,0:T(8,128)(2,1)}), bf16[16,80,128]{2,1,0:T(8,128)(2,1)S(1)}, u32[]{:S(2)}, u32[]{:S(2)}) async-start(bf16[16,80,128]{2,1,0:T(8,128)(2,1)} %get-tuple-element.44), calls=%async_computation.2 | async-start | bytes 655360 | tf_op jit(solution)/shard_map/all_to_all | solution.py:624
  97.1 42.7 %all-gather.5.cloned.1.call-start = ((), (), s32[]{:S(2)}) async-start(), calls=%async_computation.6 | async-start | bytes 1310720 | tf_op jit(solution)/shard_map/all_gather | solution.py:626
  97.1 4.8 %collective-permute-start.2 = (bf16[256,128]{1,0:T(8,128)(2,1)}, bf16[256,128]{1,0:T(8,128)(2,1)S(1)}, u32[]{:S(2)}, u32[]{:S(2)}) collective-permute-start(bf16[256,128]{1,0:T(8,128)(2,1)} %get-tuple-element.46), channel_id=1, source_target_pairs={{0,64},{16,80},{32,96},{48,112},{64,0},{80,16},{96,32},{112,48},{1... | collective-permute-start | bytes 196616 | tf_op jit(solution)/shard_map/ppermute | solution.py:590
  98.8 6.2 %collective-permute-start.3 = (bf16[256,128]{1,0:T(8,128)(2,1)}, bf16[256,128]{1,0:T(8,128)(2,1)S(1)}, u32[]{:S(2)}, u32[]{:S(2)}) collective-permute-start(bf16[256,128]{1,0:T(8,128)(2,1)} %get-tuple-element.47), channel_id=1, source_target_pairs={{0,128},{16,144},{32,160},{48,176},{64,192},{80,208},{96,224},{112... | collective-permute-start | bytes 196616 | tf_op jit(solution)/shard_map/ppermute | solution.py:590
  101.9 5.7 %collective-permute-start.4 = (bf16[256,128]{1,0:T(8,128)(2,1)}, bf16[256,128]{1,0:T(8,128)(2,1)S(1)}, u32[]{:S(2)}, u32[]{:S(2)}) collective-permute-start(bf16[256,128]{1,0:T(8,128)(2,1)} %get-tuple-element.48), channel_id=1, source_target_pairs={{0,192},{16,208},{32,224},{48,240},{64,128},{80,144},{96,160},{112... | collective-permute-start | bytes 196616 | tf_op jit(solution)/shard_map/ppermute | solution.py:590
  109.2 12.7 %copy-start = (bf16[16,80,128]{2,1,0:T(8,128)(2,1)}, bf16[16,80,128]{2,1,0:T(8,128)(2,1)S(1)}, u32[]{:S(2)}) copy-start(bf16[16,80,128]{2,1,0:T(8,128)(2,1)S(1)} %all-to-all-done.2.grads_ref.back_ref) | copy-start | bytes 983044
  121.8 37.8 %all-to-all-start.3 = ((bf16[16,192,128]{2,1,0:T(8,128)(2,1)}), bf16[16,192,128]{2,1,0:T(8,128)(2,1)S(1)}, u32[]{:S(2)}, u32[]{:S(2)}) async-start(bf16[16,192,128]{2,1,0:T(8,128)(2,1)} %attend_back.1.grads_ref), calls=%async_computation.3 | async-start | bytes 1572864 | tf_op jit(solution)/shard_map/all_to_all | solution.py:629
  134.5 5.6 %collective-permute-start.5 = (bf16[416,128]{1,0:T(8,128)(2,1)}, bf16[416,128]{1,0:T(8,128)(2,1)S(1)}, u32[]{:S(2)}, u32[]{:S(2)}) collective-permute-start(bf16[416,128]{1,0:T(8,128)(2,1)} %get-tuple-element.55), channel_id=1, source_target_pairs={{0,64},{16,80},{32,96},{48,112},{64,0},{80,16},{96,32},{112,48},{1... | collective-permute-start | bytes 319496 | tf_op jit(solution)/shard_map/ppermute | solution.py:590
  134.5 7.6 %collective-permute-start.6 = (bf16[416,128]{1,0:T(8,128)(2,1)}, bf16[416,128]{1,0:T(8,128)(2,1)S(1)}, u32[]{:S(2)}, u32[]{:S(2)}) collective-permute-start(bf16[416,128]{1,0:T(8,128)(2,1)} %get-tuple-element.56), channel_id=1, source_target_pairs={{0,128},{16,144},{32,160},{48,176},{64,192},{80,208},{96,224},{112... | collective-permute-start | bytes 319496 | tf_op jit(solution)/shard_map/ppermute | solution.py:590
  137.8 6.1 %collective-permute-start.7 = (bf16[416,128]{1,0:T(8,128)(2,1)}, bf16[416,128]{1,0:T(8,128)(2,1)S(1)}, u32[]{:S(2)}, u32[]{:S(2)}) collective-permute-start(bf16[416,128]{1,0:T(8,128)(2,1)} %get-tuple-element.57), channel_id=1, source_target_pairs={{0,192},{16,208},{32,224},{48,240},{64,128},{80,144},{96,160},{112... | collective-permute-start | bytes 319496 | tf_op jit(solution)/shard_map/ppermute | solution.py:590
  146.4 3.4 %collective-permute-start.8 = (bf16[640,128]{1,0:T(8,128)(2,1)}, bf16[640,128]{1,0:T(8,128)(2,1)S(1)}, u32[]{:S(2)}, u32[]{:S(2)}) collective-permute-start(bf16[640,128]{1,0:T(8,128)(2,1)} %get-tuple-element.64), channel_id=1, source_target_pairs={{0,16},{16,0},{32,48},{48,32},{64,80},{80,64},{96,112},{112,96},{1... | collective-permute-start | bytes 491528 | tf_op jit(solution)/shard_map/ppermute | solution.py:590
  146.4 8.8 %collective-permute-start.9 = (bf16[640,128]{1,0:T(8,128)(2,1)}, bf16[640,128]{1,0:T(8,128)(2,1)S(1)}, u32[]{:S(2)}, u32[]{:S(2)}) collective-permute-start(bf16[640,128]{1,0:T(8,128)(2,1)} %get-tuple-element.65), channel_id=1, source_target_pairs={{0,32},{16,48},{32,0},{48,16},{64,96},{80,112},{96,64},{112,80},{1... | collective-permute-start | bytes 491528 | tf_op jit(solution)/shard_map/ppermute | solution.py:590
  149.1 8.7 %collective-permute-start.10 = (bf16[640,128]{1,0:T(8,128)(2,1)}, bf16[640,128]{1,0:T(8,128)(2,1)S(1)}, u32[]{:S(2)}, u32[]{:S(2)}) collective-permute-start(bf16[640,128]{1,0:T(8,128)(2,1)} %get-tuple-element.66), channel_id=1, source_target_pairs={{0,48},{16,32},{32,16},{48,0},{64,112},{80,96},{96,80},{112,64},{1... | collective-permute-start | bytes 491528 | tf_op jit(solution)/shard_map/ppermute | solution.py:590
  159.6 13.7 %copy-start.3 = (f32[64,192]{1,0:T(8,128)S(1)}, f32[64,192]{1,0:T(8,128)}, u32[]{:S(2)}) copy-start(f32[64,192]{1,0:T(8,128)} %get-tuple-element.67) | copy-start | bytes 147460
  159.6 17.6 %all-to-all-start.4 = ((bf16[16,48,128]{2,1,0:T(8,128)(2,1)}), bf16[16,48,128]{2,1,0:T(8,128)(2,1)S(1)}, u32[]{:S(2)}, u32[]{:S(2)}) async-start(bf16[16,48,128]{2,1,0:T(8,128)(2,1)} %get-tuple-element.68), calls=%async_computation.4 | async-start | bytes 393216 | tf_op jit(solution)/shard_map/all_to_all | solution.py:634
Sparse Core Ops, SparseCore 0:
  12.8 99.6 all-gather.2
  114.3 25.4 all-gather.4
